TPU v7x, 32 devices: a whole 2x2x4 slice. The times are simulated.
32 devices in a mesh: dp: 16 (over z, x, core), tensor: 2 (over y).
Axes of the slice: x: 2, y: 2, z: 4, core: 2. Of those that a mesh axis runs over, the one named last changes fastest.
Arguments:
- block_in: bfloat16 [16384, 1024], P('dp'), may hold values from -6 to 6
- cotangent: bfloat16 [16384, 1024], P('dp'), may hold values from -8 to 8
- lengths: int32 [16, 4], P('dp'), may hold values from 1 to 512, 1024 in all within a row
- pad_count: int32 [16], P('dp'), may hold values from 0 to 255
- norm_in_attn: float32 [1024], replicated, may hold values from 0.5 to 1.5
- w_query: bfloat16 [1024, 1024], P(None, 'tensor'), may hold values from -0.1875 to 0.1875
- w_key: bfloat16 [1024, 1024], P(None, 'tensor'), may hold values from -0.1875 to 0.1875
- w_value: bfloat16 [1024, 1024], P(None, 'tensor'), may hold values from -0.1875 to 0.1875
- w_out: bfloat16 [1024, 1024], P('tensor'), may hold values from -0.1875 to 0.1875
- norm_out_attn: float32 [1024], replicated, may hold values from 0.5 to 1.5
- norm_in_mlp: float32 [1024], replicated, may hold values from 0.5 to 1.5
- w_up: bfloat16 [1024, 4096], P(None, 'tensor'), may hold values from -0.1875 to 0.1875
- w_down: bfloat16 [4096, 1024], P('tensor'), may hold values from -0.09375 to 0.09375
- norm_out_mlp: float32 [1024], replicated, may hold values from 0.5 to 1.5
Outputs:
- block_out: bfloat16 [16384, 1024], P('dp')
- grad_in: float32 [16384, 1024], P('dp')
- grad_norm_in_attn: float32 [1024], P('dp')
- grad_query: float32 [1024, 1024], P('dp', 'tensor')
- grad_key: float32 [1024, 1024], P('dp', 'tensor')
- grad_value: float32 [1024, 1024], P('dp', 'tensor')
- grad_out_proj: float32 [1024, 1024], P('tensor', 'dp')
- grad_norm_out_attn: float32 [1024], P('dp')
- grad_norm_in_mlp: float32 [1024], P('dp')
- grad_up: float32 [1024, 4096], P('dp', 'tensor')
- grad_down: float32 [4096, 1024], P('tensor', 'dp')
- grad_norm_out_mlp: float32 [1024], P('dp')
Inputs may be any that keep to these rules, and one draw needn't show every extreme that they name: Each row's 4 lengths sum to 1024, and the longest document of every row has exactly half of 1024 tokens. The last pad_count positions of a row are padding; they may cut into the last documents.
All inputs are finite; a program needn't handle non-finite values.
Results may differ from a plain program's by a relative error of at most 0.014.
Values sent between devices are 32-bit elements; how exact they have to be, the bound alone decides.
No kernel may reach another device: no remote copies, remote signals or barrier semaphores. Data moves between devices by JAX's collectives and lax.ppermute only.
A program may use at most 192 MiB of HBM per device.

v0:
```python
from functools import partial
import math

import jax
import jax.numpy as jnp
from jax import lax
from jax.sharding import PartitionSpec as P

HEAD_DIM = 64


def norm_parts(values):
    average = jnp.mean(values, axis=-1, keepdims=True)
    centered = values - average
    inverse = lax.rsqrt(jnp.mean(centered * centered, axis=-1, keepdims=True) + 1e-05)
    return (centered * inverse, inverse)


def norm_back(grad_output, gain, normed, inverse):
    scaled = grad_output * gain
    mean_scaled = jnp.mean(scaled, axis=-1, keepdims=True)
    mean_cross = jnp.mean(scaled * normed, axis=-1, keepdims=True)
    return (
        inverse * (scaled - mean_scaled - normed * mean_cross),
        jnp.sum(grad_output * normed, axis=0),
    )


def row_layout(lengths, pad_count, row_len):
    doc_ends = jnp.cumsum(lengths, axis=-1)
    doc_starts = doc_ends - lengths
    indices = jnp.arange(row_len, dtype=jnp.int32)
    segment = jnp.sum((indices[None, :, None] >= doc_ends[:, None, :]).astype(jnp.int32), axis=-1)
    labels = jnp.arange(lengths.shape[-1], dtype=jnp.int32)
    offset = jnp.sum(
        jnp.where(segment[:, :, None] == labels[None, None, :], doc_starts[:, None, :], 0), axis=-1
    )
    position = indices[None, :] - offset
    padded = indices[None, :] >= (row_len - pad_count)[:, None]
    return (segment, position, padded)


def rotate(values, position, direction):
    head_dim = values.shape[-1]
    half_dim = head_dim // 2
    frequency = 10000.0 ** (-2.0 * jnp.arange(half_dim, dtype=jnp.float32) / head_dim)
    angles = position.astype(jnp.float32)[..., None] * frequency
    cosine = jnp.cos(angles)[..., None, :]
    sine_part = direction * jnp.sin(angles)[..., None, :]
    first = values[..., :half_dim]
    second = values[..., half_dim:]
    return jnp.concatenate(
        [first * cosine - second * sine_part, second * cosine + first * sine_part], axis=-1
    )


def allowed_block(segment, padded, row_start, query_count, key_count):
    query_index = row_start + jnp.arange(query_count, dtype=jnp.int32)
    key_index = jnp.arange(key_count, dtype=jnp.int32)
    query_segment = segment[:, row_start : row_start + query_count]
    allowed = (query_segment[:, :, None] == segment[:, None, :key_count]) & (
        key_index[None, None, :] <= query_index[None, :, None]
    )
    allowed = (
        allowed
        & jnp.logical_not(padded[:, None, :key_count])
        & jnp.logical_not(padded[:, row_start : row_start + query_count, None])
    )
    allowed = allowed | (key_index[None, None, :] == query_index[None, :, None])
    return allowed[:, None]


def masked_scores(query_block, key_block, allowed, scale):
    scores = (
        jnp.einsum("rqhd,rkhd->rhqk", query_block, key_block, preferred_element_type=jnp.float32)
        * scale
    )
    return jnp.where(allowed, scores, -1e30)


def body(
    block_in,
    cotangent,
    lengths,
    pad_count,
    norm_in_attn,
    w_query,
    w_key,
    w_value,
    w_out,
    norm_out_attn,
    norm_in_mlp,
    w_up,
    w_down,
    norm_out_mlp,
):
    row_count = lengths.shape[0]
    tokens_here = block_in.shape[0]
    row_len = tokens_here // row_count
    head_dim = HEAD_DIM
    local_heads = w_query.shape[1] // head_dim
    scale = 1.0 / math.sqrt(head_dim)
    block_rows = min(512, row_len)
    block_count = row_len // block_rows
    segment, position, padded = row_layout(lengths, pad_count, row_len)
    allowed_list = [
        allowed_block(segment, padded, number * block_rows, block_rows, (number + 1) * block_rows)
        for number in range(block_count)
    ]
    inputs = block_in.astype(jnp.float32)
    input_hat, input_inv = norm_parts(inputs)
    attn_in = (input_hat * norm_in_attn).astype(jnp.bfloat16)

    def project(weight):
        return jnp.dot(attn_in, weight, preferred_element_type=jnp.float32).reshape(
            row_count, row_len, local_heads, head_dim
        )

    query_rows = rotate(project(w_query), position, 1.0).astype(jnp.bfloat16)
    key_rows = rotate(project(w_key), position, 1.0).astype(jnp.bfloat16)
    value_rows = project(w_value).astype(jnp.bfloat16)
    log_totals = []
    head_outputs = []
    for number in range(block_count):
        row_start = number * block_rows
        row_stop = row_start + block_rows
        scores = masked_scores(
            query_rows[:, row_start:row_stop], key_rows[:, :row_stop], allowed_list[number], scale
        )
        highest = jnp.max(scores, axis=-1, keepdims=True)
        log_total = highest + jnp.log(jnp.sum(jnp.exp(scores - highest), axis=-1, keepdims=True))
        softmax_block = jnp.exp(scores - log_total)
        log_totals.append(log_total)
        head_outputs.append(
            jnp.einsum(
                "rhqk,rkhd->rqhd",
                softmax_block.astype(jnp.bfloat16),
                value_rows[:, :row_stop],
                preferred_element_type=jnp.float32,
            )
        )
    attended = (
        jnp.concatenate(head_outputs, axis=1)
        .reshape(tokens_here, local_heads * head_dim)
        .astype(jnp.bfloat16)
    )
    attn_part = jnp.dot(attended, w_out, preferred_element_type=jnp.float32)
    attn_total = lax.psum(attn_part, "tensor")
    attn_hat, attn_inv = norm_parts(attn_total)
    hidden_res = inputs + attn_hat * norm_out_attn
    mlp_hat, mlp_inv = norm_parts(hidden_res)
    mlp_in = (mlp_hat * norm_in_mlp).astype(jnp.bfloat16)
    up_pre = jnp.dot(mlp_in, w_up, preferred_element_type=jnp.float32)
    activated = jax.nn.gelu(up_pre, approximate=True).astype(jnp.bfloat16)
    mlp_part = jnp.dot(activated, w_down, preferred_element_type=jnp.float32)
    mlp_total = lax.psum(mlp_part, "tensor")
    out_hat, out_inv = norm_parts(mlp_total)
    block_out = (hidden_res + out_hat * norm_out_mlp).astype(jnp.bfloat16)
    grad_output = cotangent.astype(jnp.float32)
    grad_mlp, gain_out_mlp = norm_back(grad_output, norm_out_mlp, out_hat, out_inv)
    grad_mlp_low = grad_mlp.astype(jnp.bfloat16)
    grad_act = jnp.einsum("td,fd->tf", grad_mlp_low, w_down, preferred_element_type=jnp.float32)
    gelu_value, gelu_pull = jax.vjp(partial(jax.nn.gelu, approximate=True), up_pre)
    grad_up_pre = gelu_pull(grad_act)[0].astype(jnp.bfloat16)
    weight_down = jnp.einsum(
        "tf,td->fd", activated, grad_mlp_low, preferred_element_type=jnp.float32
    )
    weight_up = jnp.einsum("td,tf->df", mlp_in, grad_up_pre, preferred_element_type=jnp.float32)
    grad_mlp_part = jnp.einsum("tf,df->td", grad_up_pre, w_up, preferred_element_type=jnp.float32)
    grad_mlp_in = lax.psum(grad_mlp_part, "tensor")
    grad_res_extra, gain_in_mlp = norm_back(grad_mlp_in, norm_in_mlp, mlp_hat, mlp_inv)
    grad_res = grad_output + grad_res_extra
    grad_attn, gain_out_attn = norm_back(grad_res, norm_out_attn, attn_hat, attn_inv)
    grad_attn_low = grad_attn.astype(jnp.bfloat16)
    weight_out = jnp.einsum(
        "te,td->ed", attended, grad_attn_low, preferred_element_type=jnp.float32
    )
    grad_heads = jnp.einsum("td,ed->te", grad_attn_low, w_out, preferred_element_type=jnp.float32)
    grad_heads = grad_heads.astype(jnp.bfloat16).reshape(row_count, row_len, local_heads, head_dim)
    grad_query_blocks = []
    grad_key_total = jnp.zeros((row_count, row_len, local_heads, head_dim), jnp.float32)
    grad_value_total = jnp.zeros((row_count, row_len, local_heads, head_dim), jnp.float32)
    for number in range(block_count):
        row_start = number * block_rows
        row_stop = row_start + block_rows
        scores = masked_scores(
            query_rows[:, row_start:row_stop], key_rows[:, :row_stop], allowed_list[number], scale
        )
        softmax_block = jnp.exp(scores - log_totals[number])
        grad_block = grad_heads[:, row_start:row_stop]
        grad_soft = jnp.einsum(
            "rqhd,rkhd->rhqk",
            grad_block,
            value_rows[:, :row_stop],
            preferred_element_type=jnp.float32,
        )
        grad_scores = softmax_block * (
            grad_soft - jnp.sum(grad_soft * softmax_block, axis=-1, keepdims=True)
        )
        grad_scores = grad_scores.astype(jnp.bfloat16)
        grad_query_blocks.append(
            jnp.einsum(
                "rhqk,rkhd->rqhd",
                grad_scores,
                key_rows[:, :row_stop],
                preferred_element_type=jnp.float32,
            )
            * scale
        )
        key_term = (
            jnp.einsum(
                "rhqk,rqhd->rkhd",
                grad_scores,
                query_rows[:, row_start:row_stop],
                preferred_element_type=jnp.float32,
            )
            * scale
        )
        grad_key_total = grad_key_total.at[:, :row_stop].add(key_term)
        value_term = jnp.einsum(
            "rhqk,rqhd->rkhd",
            softmax_block.astype(jnp.bfloat16),
            grad_block,
            preferred_element_type=jnp.float32,
        )
        grad_value_total = grad_value_total.at[:, :row_stop].add(value_term)
    width_here = local_heads * head_dim
    grad_q = (
        rotate(jnp.concatenate(grad_query_blocks, axis=1), position, -1.0)
        .reshape(tokens_here, width_here)
        .astype(jnp.bfloat16)
    )
    grad_k = (
        rotate(grad_key_total, position, -1.0).reshape(tokens_here, width_here).astype(jnp.bfloat16)
    )
    grad_v = grad_value_total.reshape(tokens_here, width_here).astype(jnp.bfloat16)
    weight_query = jnp.einsum("td,te->de", attn_in, grad_q, preferred_element_type=jnp.float32)
    weight_key = jnp.einsum("td,te->de", attn_in, grad_k, preferred_element_type=jnp.float32)
    weight_value = jnp.einsum("td,te->de", attn_in, grad_v, preferred_element_type=jnp.float32)
    grad_attn_part = jnp.einsum("te,de->td", grad_q, w_query, preferred_element_type=jnp.float32)
    grad_attn_part = grad_attn_part + jnp.einsum(
        "te,de->td", grad_k, w_key, preferred_element_type=jnp.float32
    )
    grad_attn_part = grad_attn_part + jnp.einsum(
        "te,de->td", grad_v, w_value, preferred_element_type=jnp.float32
    )
    grad_attn_in = lax.psum(grad_attn_part, "tensor")
    grad_in_extra, gain_in_attn = norm_back(grad_attn_in, norm_in_attn, input_hat, input_inv)
    grad_in = grad_res + grad_in_extra
    summed = (
        lax.psum_scatter(weight_query, "dp", scatter_dimension=0, tiled=True),
        lax.psum_scatter(weight_key, "dp", scatter_dimension=0, tiled=True),
        lax.psum_scatter(weight_value, "dp", scatter_dimension=0, tiled=True),
        lax.psum_scatter(weight_out, "dp", scatter_dimension=1, tiled=True),
        lax.psum_scatter(weight_up, "dp", scatter_dimension=0, tiled=True),
        lax.psum_scatter(weight_down, "dp", scatter_dimension=1, tiled=True),
        lax.psum_scatter(gain_in_attn, "dp", scatter_dimension=0, tiled=True),
        lax.psum_scatter(gain_out_attn, "dp", scatter_dimension=0, tiled=True),
        lax.psum_scatter(gain_in_mlp, "dp", scatter_dimension=0, tiled=True),
        lax.psum_scatter(gain_out_mlp, "dp", scatter_dimension=0, tiled=True),
    )
    return (
        block_out,
        grad_in,
        summed[6],
        summed[0],
        summed[1],
        summed[2],
        summed[3],
        summed[7],
        summed[8],
        summed[4],
        summed[5],
        summed[9],
    )


def solution(mesh):
    placed = (
        P("dp", None),
        P("dp", None),
        P("dp", None),
        P("dp"),
        P(),
        P(None, "tensor"),
        P(None, "tensor"),
        P(None, "tensor"),
        P("tensor", None),
        P(),
        P(),
        P(None, "tensor"),
        P("tensor", None),
        P(),
    )
    return jax.shard_map(
        body,
        mesh=mesh,
        in_specs=placed,
        out_specs=(
            P("dp", None),
            P("dp", None),
            P("dp"),
            P("dp", "tensor"),
            P("dp", "tensor"),
            P("dp", "tensor"),
            P("tensor", "dp"),
            P("dp"),
            P("dp"),
            P("dp", "tensor"),
            P("tensor", "dp"),
            P("dp"),
        ),
        check_vma=False,
    )
```

profile of v0, /device:TPU:1, one launch (start us, length us, event | category | flops | bytes accessed | tf_op | source)
XLA Modules:
  0.0 1110.3 jit_solution(16160604327030551473)
XLA Ops:
  9.9 2.0 convert_reduce_fusion
  11.9 2.3 fusion.26
  15.0 1.3 convolution_convert_fusion.1
  16.9 1.3 fusion.80
  18.5 1.3 fusion.79
  20.1 1.2 broadcast_multiply_fusion
  22.1 1.5 fusion.9
  23.7 1.7 exponential_reduce_fusion.1
  25.4 1.5 copy-done.3
  27.9 3.2 fusion
  31.1 4.2 exponential_reduce_fusion
  35.4 5.0 copy-done.4
  40.5 2.1 fusion.41
  42.6 4.7 fusion.40
  48.4 3.3 fusion.81
  52.1 109.8 %all-reduce.12.cloned.1.call-done = f32[1024,1024]{1,0:T(8,128)} async-done(((f32[1024,1024]{1,0:T(8,128)}), f32[1024,1024]{1,0:T(8,128)}) %all-reduce.12.cloned.1.call-update) | async-done | bytes 4194320 | tf_op jit(solution)/shard_map/psum | solution.py:148
  161.8 2.4 reduce_sum.243
  164.3 2.9 multiply_reduce_fusion.8
  169.6 3.0 copy-done.66
  172.6 4.7 fusion.74
  177.3 3.2 copy-done.73
  180.5 6.7 fusion.76
  187.8 107.5 %all-reduce.14.cloned.1.call-done = f32[1024,1024]{1,0:T(8,128)} async-done(((f32[1024,1024]{1,0:T(8,128)}), f32[1024,1024]{1,0:T(8,128)}) %all-reduce.14.cloned.1.call-update) | async-done | bytes 4194320 | tf_op jit(solution)/shard_map/psum | solution.py:156
  295.3 2.4 reduce_sum.247
  297.8 2.9 multiply_reduce_fusion.6
  301.2 2.7 fusion.31
  303.9 2.8 fusion.29
  306.8 3.3 copy-done.74
  310.1 9.6 fusion.8
  319.8 1.9 copy-done.75
  321.7 6.1 fusion.82
  328.0 107.8 %all-reduce.16.cloned.1.call-done = f32[1024,1024]{1,0:T(8,128)} async-done(((f32[1024,1024]{1,0:T(8,128)}), f32[1024,1024]{1,0:T(8,128)}) %all-reduce.16.cloned.1.call-update) | async-done | bytes 4194320 | tf_op jit(solution)/shard_map/psum | solution.py:170
  435.8 5.5 multiply_reduce_fusion.2
  441.7 6.3 multiply_reduce_fusion.3
  448.0 1.4 multiply_convert_fusion.3
  450.2 1.3 convolution_convert_fusion
  452.6 3.3 convolution_bitcast_fusion
  455.9 4.9 multiply_reduce_fusion.1
  460.8 4.7 multiply_convert_fusion.1
  465.6 2.4 fusion.37
  468.0 1.8 fusion.38
  470.7 11.6 %multiply_reduce_fusion = (f32[8,512]{1,0:T(8,128)}, f32[8,512,1024]{2,1,0:T(8,128)}) fusion(f32[8,512,1024]{2,1,0:T(8,128)S(1)} %bitcast.128, f32[8,512]{1,0:T(8,128)} %copy-done.49, pred[512,1024]{1,0:T(8,128)(4,1)S(1)} %copy-done.17, bf16[1024,8,64]{0,2,1:T(8,128)(2,1)} %bitcast.139, bf16[1,1024,8,64]{1,3,2,0:T(8,128)(2,1)} %bitcast.145), kind=kOutput, calls=%fused_computation.1 | convolution fusion | flops 557838336 | bytes 35684352 | tf_op jit(solution)/shard_map/rqhd,rkhd->rhqk/dot_general | solution.py:191
  482.3 6.9 fusion.32
  489.2 11.1 %multiply_convert_fusion = bf16[8,512,1024]{2,1,0:T(8,128)(2,1)} fusion(f32[8,512,1024]{2,1,0:T(8,128)} %get-tuple-element.123, f32[8,512,1024]{2,1,0:T(8,128)S(1)} %bitcast.128, f32[8,512]{1,0:T(8,128)S(1)} %copy-done.53, f32[8,512]{1,0:T(8,128)S(1)} %copy-done.50, pred[512,1024]{1,0:T(8,128)(4,1)S(1)} %copy-done.17), kind=kLoop, calls=%fused_computation | loop fusion | flops 25165824 | bytes 42500096 | tf_op jit(solution)/shard_map/convert_element_type | solution.py:200
  500.4 6.5 fusion.39
  507.0 1.6 bitcast_add_fusion.1
  509.8 1.3 fusion.84
  511.3 1.3 fusion.83
  513.2 3.2 add_add_fusion
  518.3 2.6 fusion.88
  521.0 5.2 fusion.87
  526.4 4.0 fusion.86
  530.6 4.5 fusion.85
  535.2 11.6 %fusion.75 = f32[2048,1024]{0,1:T(8,128)} fusion(bf16[1024,1024]{1,0:T(8,128)(2,1)S(1)} %copy-done.34, f32[1024,2048]{1,0:T(8,128)} %copy-done.73), kind=kOutput, calls=%fused_computation.170 | convolution fusion | flops 4313841664 | bytes 18874368 | tf_op jit(solution)/shard_map/tf,td->fd/dot_general | solution.py:165
  546.8 11.8 %fusion.73 = f32[1024,2048]{1,0:T(8,128)} fusion(bf16[1024,2048]{1,0:T(8,128)(2,1)} %copy-done.75, f32[1024,1024]{1,0:T(8,128)} %copy-done.5, f32[1024]{0:T(1024)S(1)} %copy-done.59, f32[1024]{0:T(1024)S(1)} %add_rsqrt_fusion.1, f32[1024]{0:T(1024)S(1)} %broadcast_multiply_fusion.10), kind=kOutput, calls=%fused_computation.168 | convolution fusion | flops 4299161600 | bytes 16789504 | tf_op jit(solution)/shard_map/td,tf->df/dot_general | solution.py:168
  560.5 64.0 %all-reduce.18.cloned.1.call-done = f32[1024,1024]{1,0:T(8,128)} async-done(((f32[1024,1024]{1,0:T(8,128)}), f32[1024,1024]{1,0:T(8,128)}) %all-reduce.18.cloned.1.call-update) | async-done | bytes 4194320 | tf_op jit(solution)/shard_map/psum | solution.py:247
  624.5 3.6 fusion.25
  628.1 57.3 %all-reduce.6 = (f32[1024]{0:T(1024)S(1)}, f32[1024]{0:T(1024)S(1)}, f32[1024]{0:T(1024)S(1)}, f32[1024]{0:T(1024)S(1)}) all-reduce(f32[1024]{0:T(1024)S(1)} %get-tuple-element.82, f32[1024]{0:T(1024)S(1)} %copy-done.63, f32[1024]{0:T(1024)S(1)} %copy-done.60, f32[1024]{0:T(1024)S(1)} %copy-done.62), channel_id=2, replica_groups=mesh['dp'=16,'tensor'=2] {'dp'}, use_global_device_ids=true, to_apply=%region_30.31.clone | all-reduce | flops 4096 | bytes 32768
  687.7 5.6 fusion.24
  693.3 60.7 %reduce-scatter.11.cloned.1.call-done = f32[64,512]{1,0:T(8,128)} async-done(((f32[1024,512]{1,0:T(8,128)}), f32[64,512]{1,0:T(8,128)}) %reduce-scatter.11.cloned.1.call-update) | async-done | bytes 131088 | tf_op jit(solution)/shard_map/reduce_scatter | solution.py:253
  754.0 64.9 %reduce-scatter.9.cloned.1.call-done = f32[64,512]{1,0:T(8,128)} async-done(((f32[1024,512]{1,0:T(8,128)}), f32[64,512]{1,0:T(8,128)}) %reduce-scatter.9.cloned.1.call-update) | async-done | bytes 131088 | tf_op jit(solution)/shard_map/reduce_scatter | solution.py:252
  818.9 65.4 %reduce-scatter.7.cloned.1.call-done = f32[64,512]{1,0:T(8,128)} async-done(((f32[1024,512]{1,0:T(8,128)}), f32[64,512]{1,0:T(8,128)}) %reduce-scatter.7.cloned.1.call-update) | async-done | bytes 131088 | tf_op jit(solution)/shard_map/reduce_scatter | solution.py:251
  884.3 110.0 %reduce-scatter.17.cloned.1.call-done = f32[2048,64]{0,1:T(8,128)} async-done(((f32[2048,1024]{0,1:T(8,128)}), f32[2048,64]{0,1:T(8,128)}) %reduce-scatter.17.cloned.1.call-update) | async-done | bytes 524304 | tf_op jit(solution)/shard_map/reduce_scatter | solution.py:256
  994.3 109.0 %reduce-scatter.15.cloned.1.call-done = f32[64,2048]{1,0:T(8,128)} async-done(((f32[1024,2048]{1,0:T(8,128)}), f32[64,2048]{1,0:T(8,128)}) %reduce-scatter.15.cloned.1.call-update) | async-done | bytes 524304 | tf_op jit(solution)/shard_map/reduce_scatter | solution.py:255
  (224 shorter events, 21.6 us)
Async XLA Ops:
  7.2 41.2 %copy-start = (bf16[512,1024]{1,0:T(8,128)(2,1)S(1)}, bf16[512,1024]{1,0:T(8,128)(2,1)}, u32[]{:S(2)}) copy-start(bf16[512,1024]{1,0:T(8,128)(2,1)} %param.34) | copy-start | bytes 3145732
  7.2 7.0 copy-start.11
  7.2 7.0 copy-start.57
  7.2 154.6 %all-reduce.12.cloned.1.call-start = ((), (), s32[]{:S(2)}) async-start(), calls=%async_computation.6 | async-start | bytes 8388608 | tf_op jit(solution)/shard_map/psum | solution.py:148
  9.9 5.1 copy-start.42
  11.9 4.4 copy-start.51
  14.9 3.3 copy-start.37
  16.9 25.6 %copy-start.31 = (bf16[1024,512]{0,1:T(8,128)(2,1)}, bf16[1024,512]{0,1:T(8,128)(2,1)S(1)}, u32[]{:S(2)}) copy-start(bf16[1024,512]{0,1:T(8,128)(2,1)S(1)} %convolution_convert_fusion.1) | copy-start | bytes 3145732
  22.1 5.8 copy-start.18
  22.1 5.8 copy-start.20
  22.1 5.8 copy-start.23
  22.1 5.8 copy-start.25
  27.8 14.7 %copy-start.16 = (pred[512,1024]{1,0:T(8,128)(4,1)}, pred[512,1024]{1,0:T(8,128)(4,1)S(1)}, u32[]{:S(2)}) copy-start(pred[512,1024]{1,0:T(8,128)(4,1)S(1)} %fusion.36) | copy-start | bytes 1572868
  31.1 11.4 %copy-start.2 = (f32[8,512,1024]{2,1,0:T(8,128)}, f32[8,512,1024]{2,1,0:T(8,128)S(1)}, u32[]{:S(2)}) copy-start(f32[8,512,1024]{2,1,0:T(8,128)S(1)} %get-tuple-element.117) | copy-start | bytes 50331652
  31.1 9.3 copy-start.4
  35.4 7.2 copy-start.49
  51.7 115.5 %copy-start.56 = (f32[1024]{0:T(1024)S(1)}, f32[1024]{0:T(1024)}, u32[]{:S(2)}) copy-start(f32[1024]{0:T(1024)} %param.35) | copy-start | bytes 12292
  51.7 243.6 %all-reduce.14.cloned.1.call-start = ((), (), s32[]{:S(2)}) async-start(), calls=%async_computation.7 | async-start | bytes 8388608 | tf_op jit(solution)/shard_map/psum | solution.py:156
  164.3 3.5 copy-start.8
  168.9 8.4 copy-start.5
  168.9 3.7 copy-start.66
  172.6 7.9 copy-start.64
  187.3 113.4 %copy-start.15 = (bf16[1024,1024]{1,0:T(8,128)(2,1)S(1)}, bf16[1024,1024]{1,0:T(8,128)(2,1)}, u32[]{:S(2)}) copy-start(bf16[1024,1024]{1,0:T(8,128)(2,1)} %param.27) | copy-start | bytes 6291460
  187.3 113.4 %copy-start.61 = (f32[1024]{0:T(1024)S(1)}, f32[1024]{0:T(1024)}, u32[]{:S(2)}) copy-start(f32[1024]{0:T(1024)} %param.39) | copy-start | bytes 12292
  187.3 248.5 %all-reduce.16.cloned.1.call-start = ((), (), s32[]{:S(2)}) async-start(), calls=%async_computation.8 | async-start | bytes 8388608 | tf_op jit(solution)/shard_map/psum | solution.py:170
  297.8 3.5 copy-start.13
  303.9 6.2 copy-start.74
  306.8 12.9 %copy-start.33 = (bf16[1024,1024]{1,0:T(8,128)(2,1)}, bf16[1024,1024]{1,0:T(8,128)(2,1)S(1)}, u32[]{:S(2)}) copy-start(bf16[1024,1024]{1,0:T(8,128)(2,1)S(1)} %get-tuple-element.97) | copy-start | bytes 6291460
  310.1 11.6 %copy-start.67 = (bf16[1024,2048]{1,0:T(8,128)(2,1)S(1)}, bf16[1024,2048]{1,0:T(8,128)(2,1)}, u32[]{:S(2)}) copy-start(bf16[1024,2048]{1,0:T(8,128)(2,1)} %param.37) | copy-start | bytes 12582916
  327.8 296.7 %all-reduce.18.cloned.1.call-start = ((), (), s32[]{:S(2)}) async-start(), calls=%async_computation.9 | async-start | bytes 8388608 | tf_op jit(solution)/shard_map/psum | solution.py:247
  435.8 5.6 copy-start.7
  435.8 5.9 copy-start.9
  441.7 9.8 slice-start.4
  448.0 4.6 slice-start.5
  451.5 4.4 copy-start.41
  452.6 3.3 copy-start.32
  460.8 4.8 copy-start.19
  460.8 4.8 copy-start.21
  460.8 9.0 slice-start
  460.8 9.0 slice-start.1
  460.8 9.0 slice-start.2
  465.6 5.1 slice-start.3
  482.3 6.9 copy-start.50
  482.3 6.9 copy-start.53
  500.4 6.5 copy-start.10
  500.4 6.5 copy-start.22
  500.4 6.5 copy-start.30
  516.4 176.9 %reduce-scatter.13.cloned.1.call-start = ((), (), s32[]{:S(2)}) async-start(), calls=%async_computation.13 | async-start | bytes 2228224 | tf_op jit(solution)/shard_map/reduce_scatter | solution.py:254
  521.0 5.4 copy-start.38
  521.0 233.0 %reduce-scatter.11.cloned.1.call-start = ((), (), s32[]{:S(2)}) async-start(), calls=%async_computation.12 | async-start | bytes 2228224 | tf_op jit(solution)/shard_map/reduce_scatter | solution.py:253
  526.3 4.3 copy-start.46
  526.3 292.6 %reduce-scatter.9.cloned.1.call-start = ((), (), s32[]{:S(2)}) async-start(), calls=%async_computation.11 | async-start | bytes 2228224 | tf_op jit(solution)/shard_map/reduce_scatter | solution.py:252
  530.3 4.8 copy-start.34
  530.4 354.0 %reduce-scatter.7.cloned.1.call-start = ((), (), s32[]{:S(2)}) async-start(), calls=%async_computation.10 | async-start | bytes 2228224 | tf_op jit(solution)/shard_map/reduce_scatter | solution.py:251
  535.1 459.2 %reduce-scatter.17.cloned.1.call-start = ((), (), s32[]{:S(2)}) async-start(), calls=%async_computation.15 | async-start | bytes 8912896 | tf_op jit(solution)/shard_map/reduce_scatter | solution.py:256
  546.8 556.5 %reduce-scatter.15.cloned.1.call-start = ((), (), s32[]{:S(2)}) async-start(), calls=%async_computation.14 | async-start | bytes 8912896 | tf_op jit(solution)/shard_map/reduce_scatter | solution.py:255
  558.6 65.8 %copy-start.12 = (bf16[1024,1024]{1,0:T(8,128)(2,1)S(1)}, bf16[1024,1024]{1,0:T(8,128)(2,1)}, u32[]{:S(2)}) copy-start(bf16[1024,1024]{1,0:T(8,128)(2,1)} %param.26) | copy-start | bytes 6291460
  558.6 65.8 %copy-start.52 = (f32[1024]{0:T(1024)S(1)}, f32[1024]{0:T(1024)}, u32[]{:S(2)}) copy-start(f32[1024]{0:T(1024)} %copy-done.51) | copy-start | bytes 12292
  558.6 65.8 %copy-start.55 = (f32[1024]{0:T(1024)S(1)}, f32[1024]{0:T(1024)}, u32[]{:S(2)}) copy-start(f32[1024]{0:T(1024)} %copy-done.54) | copy-start | bytes 12292
  558.6 65.8 %copy-start.58 = (f32[1024]{0:T(1024)S(1)}, f32[1024]{0:T(1024)}, u32[]{:S(2)}) copy-start(f32[1024]{0:T(1024)} %param.30) | copy-start | bytes 12292
  558.7 69.4 %copy-start.60 = (f32[1024]{0:T(1024)S(1)}, f32[1024]{0:T(1024)}, u32[]{:S(2)}) copy-start(f32[1024]{0:T(1024)} %get-tuple-element.76) | copy-start | bytes 12292
  558.7 69.4 %copy-start.62 = (f32[1024]{0:T(1024)S(1)}, f32[1024]{0:T(1024)}, u32[]{:S(2)}) copy-start(f32[1024]{0:T(1024)} %get-tuple-element.80) | copy-start | bytes 12292
  558.7 69.4 %copy-start.63 = (f32[1024]{0:T(1024)S(1)}, f32[1024]{0:T(1024)}, u32[]{:S(2)}) copy-start(f32[1024]{0:T(1024)} %get-tuple-element.78) | copy-start | bytes 12292
  687.7 415.5 %copy-start.1 = (bf16[512,1024]{1,0:T(8,128)(2,1)S(1)}, bf16[512,1024]{1,0:T(8,128)(2,1)}, u32[]{:S(2)}) copy-start(bf16[512,1024]{1,0:T(8,128)(2,1)} %param.34) | copy-start | bytes 3145732
  (28 other events, 53.2 us)
Sparse Core Ops, SparseCore 0:
  51.9 109.9 all-reduce.11
  187.4 107.8 all-reduce.13
  327.9 107.8 all-reduce.15
  516.6 107.8 all-reduce.17
  628.6 60.0 reduce-scatter.12
  693.4 60.6 reduce-scatter.10
  758.3 60.5 reduce-scatter.8
  823.7 60.5 reduce-scatter.6
  889.0 105.2 reduce-scatter.16
  998.8 104.4 reduce-scatter.14
where the time goes:
time: 1120 us; the launch traced here: 1110 us
  waiting for transfers between devices  799 us (71%)
  matrix products  132 us (12%)
  other arithmetic  73.1 us (7%)
  blocking collectives  57.3 us (5%)
  local copies, waits for them, and re-layouts  30.9 us (3%)
  between operations  16.9 us (2%)
    reduce_scatter x1, waiting for transfers between devices, body(): lax.psum_scatter(weight_down, 'dp', scatter_dimension=1, tiled=True)  110 us
    psum x1, waiting for transfers between devices, body(): attn_total = lax.psum(attn_part, 'tensor')  110 us
    reduce_scatter x1, waiting for transfers between devices, body(): lax.psum_scatter(weight_up, 'dp', scatter_dimension=0, tiled=True)  109 us
    psum x1, waiting for transfers between devices, body(): grad_mlp_in = lax.psum(grad_mlp_part, 'tensor')  108 us
    psum x1, waiting for transfers between devices, body(): mlp_total = lax.psum(mlp_part, 'tensor')  107 us
    reduce_scatter x1, waiting for transfers between devices, body(): lax.psum_scatter(weight_query, 'dp', scatter_dimension=0, tiled=True)  65.4 us
    reduce_scatter x1, waiting for transfers between devices, body(): lax.psum_scatter(weight_key, 'dp', scatter_dimension=0, tiled=True)  64.9 us
    psum x1, waiting for transfers between devices, body(): grad_attn_in = lax.psum(grad_attn_part, 'tensor')  64 us
  transfers between devices with their start and end apart: 10, of which 9 were waited for; matrix products, arithmetic and copies ran while one was open for 5% of the time, Pallas kernels for 0%

commit v1 on v0

--- a/solution.py
+++ b/solution.py
@@ -27,7 +27,10 @@
 
 
 def row_layout(lengths, pad_count, row_len):
-    doc_ends = jnp.cumsum(lengths, axis=-1)
+    ends = [lengths[:, 0]]
+    for number in range(1, lengths.shape[-1]):
+        ends.append(ends[-1] + lengths[:, number])
+    doc_ends = jnp.stack(ends, axis=-1)
     doc_starts = doc_ends - lengths
     indices = jnp.arange(row_len, dtype=jnp.int32)
     segment = jnp.sum((indices[None, :, None] >= doc_ends[:, None, :]).astype(jnp.int32), axis=-1)
@@ -76,6 +79,10 @@
         * scale
     )
     return jnp.where(allowed, scores, -1e30)
+
+
+def pair_sum(values):
+    return values + lax.ppermute(values, "tensor", [(0, 1), (1, 0)])
 
 
 def body(
@@ -145,7 +152,7 @@
         .astype(jnp.bfloat16)
     )
     attn_part = jnp.dot(attended, w_out, preferred_element_type=jnp.float32)
-    attn_total = lax.psum(attn_part, "tensor")
+    attn_total = pair_sum(attn_part)
     attn_hat, attn_inv = norm_parts(attn_total)
     hidden_res = inputs + attn_hat * norm_out_attn
     mlp_hat, mlp_inv = norm_parts(hidden_res)
@@ -153,7 +160,7 @@
     up_pre = jnp.dot(mlp_in, w_up, preferred_element_type=jnp.float32)
     activated = jax.nn.gelu(up_pre, approximate=True).astype(jnp.bfloat16)
     mlp_part = jnp.dot(activated, w_down, preferred_element_type=jnp.float32)
-    mlp_total = lax.psum(mlp_part, "tensor")
+    mlp_total = pair_sum(mlp_part)
     out_hat, out_inv = norm_parts(mlp_total)
     block_out = (hidden_res + out_hat * norm_out_mlp).astype(jnp.bfloat16)
     grad_output = cotangent.astype(jnp.float32)
@@ -163,17 +170,17 @@
     gelu_value, gelu_pull = jax.vjp(partial(jax.nn.gelu, approximate=True), up_pre)
     grad_up_pre = gelu_pull(grad_act)[0].astype(jnp.bfloat16)
     weight_down = jnp.einsum(
-        "tf,td->fd", activated, grad_mlp_low, preferred_element_type=jnp.float32
+        "tf,td->df", activated, grad_mlp_low, preferred_element_type=jnp.float32
     )
     weight_up = jnp.einsum("td,tf->df", mlp_in, grad_up_pre, preferred_element_type=jnp.float32)
     grad_mlp_part = jnp.einsum("tf,df->td", grad_up_pre, w_up, preferred_element_type=jnp.float32)
-    grad_mlp_in = lax.psum(grad_mlp_part, "tensor")
+    grad_mlp_in = pair_sum(grad_mlp_part)
     grad_res_extra, gain_in_mlp = norm_back(grad_mlp_in, norm_in_mlp, mlp_hat, mlp_inv)
     grad_res = grad_output + grad_res_extra
     grad_attn, gain_out_attn = norm_back(grad_res, norm_out_attn, attn_hat, attn_inv)
     grad_attn_low = grad_attn.astype(jnp.bfloat16)
     weight_out = jnp.einsum(
-        "te,td->ed", attended, grad_attn_low, preferred_element_type=jnp.float32
+        "te,td->de", attended, grad_attn_low, preferred_element_type=jnp.float32
     )
     grad_heads = jnp.einsum("td,ed->te", grad_attn_low, w_out, preferred_element_type=jnp.float32)
     grad_heads = grad_heads.astype(jnp.bfloat16).reshape(row_count, row_len, local_heads, head_dim)
@@ -244,20 +251,33 @@
     grad_attn_part = grad_attn_part + jnp.einsum(
         "te,de->td", grad_v, w_value, preferred_element_type=jnp.float32
     )
-    grad_attn_in = lax.psum(grad_attn_part, "tensor")
+    grad_attn_in = pair_sum(grad_attn_part)
     grad_in_extra, gain_in_attn = norm_back(grad_attn_in, norm_in_attn, input_hat, input_inv)
     grad_in = grad_res + grad_in_extra
+    wide = w_query.shape[1]
+    hidden = w_up.shape[1]
+    gains = jnp.stack([gain_in_attn, gain_out_attn, gain_in_mlp, gain_out_mlp], axis=1)
+    mlp_grads = lax.psum_scatter(
+        jnp.concatenate([weight_up, weight_down], axis=1), "dp", scatter_dimension=0, tiled=True
+    )
+    attn_grads = lax.psum_scatter(
+        jnp.concatenate([weight_query, weight_key, weight_value, weight_out, jnp.pad(gains, ((0, 0), (0, 124)))], axis=1),
+        "dp",
+        scatter_dimension=0,
+        tiled=True,
+    )
+    gain_sums = attn_grads[:, 4 * wide :]
     summed = (
-        lax.psum_scatter(weight_query, "dp", scatter_dimension=0, tiled=True),
-        lax.psum_scatter(weight_key, "dp", scatter_dimension=0, tiled=True),
-        lax.psum_scatter(weight_value, "dp", scatter_dimension=0, tiled=True),
-        lax.psum_scatter(weight_out, "dp", scatter_dimension=1, tiled=True),
-        lax.psum_scatter(weight_up, "dp", scatter_dimension=0, tiled=True),
-        lax.psum_scatter(weight_down, "dp", scatter_dimension=1, tiled=True),
-        lax.psum_scatter(gain_in_attn, "dp", scatter_dimension=0, tiled=True),
-        lax.psum_scatter(gain_out_attn, "dp", scatter_dimension=0, tiled=True),
-        lax.psum_scatter(gain_in_mlp, "dp", scatter_dimension=0, tiled=True),
-        lax.psum_scatter(gain_out_mlp, "dp", scatter_dimension=0, tiled=True),
+        attn_grads[:, :wide],
+        attn_grads[:, wide : 2 * wide],
+        attn_grads[:, 2 * wide : 3 * wide],
+        attn_grads[:, 3 * wide : 4 * wide].T,
+        mlp_grads[:, :hidden],
+        mlp_grads[:, hidden:].T,
+        gain_sums[:, 0],
+        gain_sums[:, 1],
+        gain_sums[:, 2],
+        gain_sums[:, 3],
     )
     return (
         block_out,

time: 1120 us -> 865 us (0.77)
  waiting for transfers between devices: 799 us -> 594 us
  blocking collectives: 57.3 us -> 0 us
  local copies, waits for them, and re-layouts: 30.9 us -> 49.2 us
  matrix products: 132 us -> 116 us
    psum x4 -> x0, waiting for transfers between devices: 389 us -> none  [the longest x1 110 us: body(): attn_total = lax.psum(attn_part, 'tensor')]
    ppermute x0 -> x4, waiting for transfers between devices: none -> 344 us  [pair_sum(): return values + lax.ppermute(values, 'tensor', [(0, 1), (1, 0)])]
    reduce_scatter x6 -> x1, waiting for transfers between devices: 410 us -> 178 us  [body(): lax.psum_scatter(jnp.concatenate([weight_up, weight_down], axis=1), 'dp',...]
    unnamed x10 -> x3, waiting for transfers between devices: 0.16 us -> 72.6 us
    unnamed x1 -> x0, blocking collectives: 57.3 us -> none
    unnamed x169 -> x155, local copies, waits for them, and re-layouts: 30.9 us -> 42.6 us
  transfers between devices with their start and end apart: 10 -> 6, of which waited for: 9 -> 6; matrix products, arithmetic and copies ran while one was open for 5% -> 7% of each run, Pallas kernels for 0% -> 0%
where the time goes in v1:
time: 865 us; the launch traced here: 854 us
  waiting for transfers between devices  594 us (69%)
  matrix products  116 us (13%)
  other arithmetic  71.3 us (8%)
  local copies, waits for them, and re-layouts  49.2 us (6%)
  between operations  18.5 us (2%)
    ppermute x4, waiting for transfers between devices, pair_sum(): return values + lax.ppermute(values, 'tensor', [(0, 1), (1, 0)])  344 us
    reduce_scatter x1, waiting for transfers between devices, body(): lax.psum_scatter(jnp.concatenate([weight_up, weight_down], axis=1), 'dp',...  178 us
    unnamed x3, waiting for transfers between devices  72.6 us
    unnamed x155, local copies, waits for them, and re-layouts  42.6 us
    convert_element_type x2, other arithmetic, body(): grad_scores = grad_scores.astype(jnp.bfloat16)  18 us
  transfers between devices with their start and end apart: 6, of which 6 were waited for; matrix products, arithmetic and copies ran while one was open for 7% of the time, Pallas kernels for 0%

profile of v1, /device:TPU:1, one launch (start us, length us, event | category | flops | bytes accessed | tf_op | source)
XLA Modules:
  0.0 853.9 jit_solution(13509049382918222154)
XLA Ops:
  8.0 1.4 fusion.91
  12.0 1.4 subtract_bitcast_fusion
  13.6 2.9 copy.50
  18.5 1.4 convolution_convert_fusion.1
  19.9 1.4 fusion.81
  21.5 1.4 fusion.83
  23.2 1.2 broadcast_multiply_fusion
  25.2 1.5 fusion.9
  26.7 1.7 exponential_reduce_fusion.1
  28.5 1.5 copy-done.5
  31.0 3.4 fusion
  34.3 4.2 exponential_reduce_fusion
  38.6 5.0 copy-done.6
  43.7 2.1 fusion.41
  45.8 4.7 fusion.40
  50.6 1.4 fusion.92
  52.0 2.1 collective-permute-start
  54.1 90.3 %collective-permute-done = f32[1024,1024]{0,1:T(8,128)S(1)} collective-permute-done((f32[1024,1024]{0,1:T(8,128)S(1)}, f32[1024,1024]{0,1:T(8,128)S(1)}, u32[]{:S(2)}, u32[]{:S(2)}) %collective-permute-start) | collective-permute-done | bytes 4194336 | tf_op jit(solution)/shard_map/ppermute | solution.py:85
  144.4 1.3 fusion.88
  148.3 1.6 copy-done.3
  149.9 1.6 copy-done.29
  151.5 4.9 fusion.75
  156.4 6.3 fusion.77
  163.9 3.0 copy.52
  166.9 87.0 %collective-permute-done.1 = f32[1024,1024]{0,1:T(8,128)} collective-permute-done((f32[1024,1024]{0,1:T(8,128)}, f32[1024,1024]{0,1:T(8,128)}, u32[]{:S(2)}, u32[]{:S(2)}) %collective-permute-start.1) | collective-permute-done | bytes 4194336 | tf_op jit(solution)/shard_map/ppermute | solution.py:85
  253.9 4.5 fusion.86
  259.1 2.3 fusion.31
  261.4 3.3 fusion.29
  265.8 10.9 %fusion.8 = bf16[1024,2048]{1,0:T(8,128)(2,1)} fusion(f32[1024,2048]{1,0:T(8,128)S(1)} %bitcast.143, bf16[1024,1024]{0,1:T(8,128)(2,1)S(1)} %get-tuple-element.137, bf16[2048,1024]{1,0:T(8,128)(2,1)S(1)} %copy-done.60), kind=kOutput, calls=%fused_computation.16 | convolution fusion | flops 4336910336 | bytes 18874368 | tf_op jit(solution)/shard_map/td,fd->tf/dot_general | solution.py:169
  276.7 6.4 fusion.93
  284.0 89.1 %collective-permute-done.2 = f32[1024,1024]{0,1:T(8,128)S(1)} collective-permute-done((f32[1024,1024]{0,1:T(8,128)S(1)}, f32[1024,1024]{0,1:T(8,128)S(1)}, u32[]{:S(2)}, u32[]{:S(2)}) %collective-permute-start.2) | collective-permute-done | bytes 4194336 | tf_op jit(solution)/shard_map/ppermute | solution.py:85
  373.1 2.7 multiply_reduce_fusion.2
  375.8 4.1 multiply_reduce_fusion.3
  382.0 1.3 convolution_convert_fusion
  383.3 3.3 convolution_bitcast_fusion
  386.6 4.9 multiply_reduce_fusion.1
  391.5 7.1 multiply_convert_fusion.1
  398.7 2.4 fusion.37
  401.1 1.8 fusion.38
  403.8 11.5 %multiply_reduce_fusion = (f32[8,512]{1,0:T(8,128)}, f32[8,512,1024]{2,1,0:T(8,128)}) fusion(f32[8,512,1024]{2,1,0:T(8,128)S(1)} %bitcast.135, f32[8,512]{1,0:T(8,128)} %copy-done.45, pred[512,1024]{1,0:T(8,128)(4,1)S(1)} %copy-done.14, bf16[1024,8,64]{0,2,1:T(8,128)(2,1)} %bitcast.148, bf16[1,1024,8,64]{1,3,2,0:T(8,128)(2,1)} %bitcast.154), kind=kOutput, calls=%fused_computation.2 | convolution fusion | flops 557838336 | bytes 35684352 | tf_op jit(solution)/shard_map/rqhd,rkhd->rhqk/dot_general | solution.py:198
  415.3 6.9 fusion.32
  422.2 10.9 %multiply_convert_fusion = bf16[8,512,1024]{2,1,0:T(8,128)(2,1)} fusion(f32[8,512,1024]{2,1,0:T(8,128)} %get-tuple-element.177, f32[8,512,1024]{2,1,0:T(8,128)S(1)} %bitcast.135, f32[8,512]{1,0:T(8,128)S(1)} %copy-done.47, f32[8,512]{1,0:T(8,128)S(1)} %copy-done.46, pred[512,1024]{1,0:T(8,128)(4,1)S(1)} %copy-done.14), kind=kLoop, calls=%fused_computation.1 | loop fusion | flops 25165824 | bytes 42500096 | tf_op jit(solution)/shard_map/convert_element_type | solution.py:207
  433.2 6.5 fusion.39
  439.7 1.6 bitcast_add_fusion.1
  442.6 1.2 fusion.94
  443.9 1.3 fusion.95
  445.5 1.3 add_add_fusion
  447.4 2.8 convolution_dynamic-update-slice_fusion.3
  450.1 2.7 convolution_dynamic-update-slice_fusion.2
  452.9 2.8 convolution_dynamic-update-slice_fusion.1
  455.7 2.7 convolution_dynamic-update-slice_fusion
  458.4 77.5 %collective-permute-done.3 = f32[1024,1024]{0,1:T(8,128)S(1)} collective-permute-done((f32[1024,1024]{0,1:T(8,128)S(1)}, f32[1024,1024]{0,1:T(8,128)S(1)}, u32[]{:S(2)}, u32[]{:S(2)}) %collective-permute-start.3) | collective-permute-done | bytes 4194336 | tf_op jit(solution)/shard_map/ppermute | solution.py:85
  535.9 3.6 fusion.25
  540.4 9.3 %copy.66 = f32[1024,2176]{1,0:T(8,128)} copy(f32[1024,2176]{0,1:T(8,128)} %fusion.50) | data formatting | bytes 17825792
  549.8 7.8 fusion.74
  557.6 7.4 fusion.76
  565.0 7.4 pad_maximum_fusion
  572.4 4.1 copy.56
  576.5 7.0 fusion.24
  583.5 5.4 copy.57
  589.0 72.5 %reduce-scatter.7.cloned.1.call-done = f32[64,2176]{1,0:T(8,128)} async-done(((f32[1024,2176]{1,0:T(8,128)}), f32[64,2176]{1,0:T(8,128)}) %reduce-scatter.7.cloned.1.call-update) | async-done | bytes 557072
  664.8 1.9 slice_bitcast_fusion.10
  666.7 177.8 %reduce-scatter.5.cloned.1.call-done = f32[64,4096]{1,0:T(8,128)} async-done(((f32[1024,4096]{1,0:T(8,128)}), f32[64,4096]{1,0:T(8,128)}) %reduce-scatter.5.cloned.1.call-update) | async-done | bytes 1048592 | tf_op jit(solution)/shard_map/reduce_scatter | solution.py:260
  844.6 2.3 slice_bitcast_fusion
  (198 shorter events, 20.4 us)
Async XLA Ops:
  7.2 43.5 %copy-start = (bf16[512,1024]{1,0:T(8,128)(2,1)S(1)}, bf16[512,1024]{1,0:T(8,128)(2,1)}, u32[]{:S(2)}) copy-start(bf16[512,1024]{1,0:T(8,128)(2,1)} %param.34) | copy-start | bytes 3145732
  7.2 654.3 %reduce-scatter.7.cloned.1.call-start = ((), (), s32[]{:S(2)}) async-start(), calls=%async_computation.3 | async-start | bytes 9469952
  13.6 3.9 copy-start.57
  16.5 129.7 %copy-start.10 = (bf16[1024,1024]{0,1:T(8,128)(2,1)}, bf16[1024,1024]{0,1:T(8,128)(2,1)S(1)}, u32[]{:S(2)}) copy-start(bf16[1024,1024]{0,1:T(8,128)(2,1)S(1)} %copy.50) | copy-start | bytes 6291460
  16.5 2.0 copy-start.40
  16.9 4.5 copy-start.48
  18.5 2.9 copy-start.51
  19.9 25.8 %copy-start.31 = (bf16[1024,512]{0,1:T(8,128)(2,1)}, bf16[1024,512]{0,1:T(8,128)(2,1)S(1)}, u32[]{:S(2)}) copy-start(bf16[1024,512]{0,1:T(8,128)(2,1)S(1)} %convolution_convert_fusion.1) | copy-start | bytes 3145732
  24.4 2.3 copy-start.37
  25.1 5.8 copy-start.15
  25.2 5.8 copy-start.17
  25.2 5.8 copy-start.20
  25.2 5.8 copy-start.22
  26.7 3.2 copy-start.5
  30.9 14.9 %copy-start.13 = (pred[512,1024]{1,0:T(8,128)(4,1)}, pred[512,1024]{1,0:T(8,128)(4,1)S(1)}, u32[]{:S(2)}) copy-start(pred[512,1024]{1,0:T(8,128)(4,1)S(1)} %fusion.36) | copy-start | bytes 1572868
  34.3 11.4 %copy-start.2 = (f32[8,512,1024]{2,1,0:T(8,128)}, f32[8,512,1024]{2,1,0:T(8,128)S(1)}, u32[]{:S(2)}) copy-start(f32[8,512,1024]{2,1,0:T(8,128)S(1)} %get-tuple-element.171) | copy-start | bytes 50331652
  34.3 9.3 %copy-start.6 = (f32[8,512,512]{1,2,0:T(8,128)S(1)}, f32[8,512,512]{1,2,0:T(8,128)}, u32[]{:S(2)}) copy-start(f32[8,512,512]{1,2,0:T(8,128)} %copy-done.5) | copy-start | bytes 25165828
  38.6 7.2 copy-start.45
  50.6 3.5 copy-start.25
  52.0 92.4 %collective-permute-start = (f32[1024,1024]{0,1:T(8,128)S(1)}, f32[1024,1024]{0,1:T(8,128)S(1)}, u32[]{:S(2)}, u32[]{:S(2)}) collective-permute-start(f32[1024,1024]{0,1:T(8,128)S(1)} %fusion.92), channel_id=1, source_target_pairs={{0,1},{1,0},{2,3},{3,2},{4,5},{5,4},{6,7},{7,6},{8,9},{9,8},{10,11... | collective-permute-start | bytes 12582920 | tf_op jit(solution)/shard_map/ppermute | solution.py:85
  145.7 2.1 copy-start.7
  147.8 2.1 copy-start.3
  147.8 3.7 copy-start.29
  147.8 3.7 copy-start.44
  151.5 4.9 copy-start.59
  156.4 6.3 copy-start.24
  162.7 91.2 %collective-permute-start.1 = (f32[1024,1024]{0,1:T(8,128)}, f32[1024,1024]{0,1:T(8,128)}, u32[]{:S(2)}, u32[]{:S(2)}) collective-permute-start(f32[1024,1024]{0,1:T(8,128)} %fusion.77), channel_id=1, source_target_pairs={{0,1},{1,0},{2,3},{3,2},{4,5},{5,4},{6,7},{7,6},{8,9},{9,8},{10,11... | collective-permute-start | bytes 12582920 | tf_op jit(solution)/shard_map/ppermute | solution.py:85
  258.9 2.5 copy-start.4
  259.1 5.6 slice-start.6
  261.4 3.3 slice-start.7
  261.4 4.4 copy-start.60
  264.7 12.0 %copy-start.33 = (bf16[1024,1024]{0,1:T(8,128)(2,1)}, bf16[1024,1024]{0,1:T(8,128)(2,1)S(1)}, u32[]{:S(2)}) copy-start(bf16[1024,1024]{0,1:T(8,128)(2,1)S(1)} %get-tuple-element.137) | copy-start | bytes 6291460
  265.8 10.9 %copy-start.30 = (bf16[1024,2048]{1,0:T(8,128)(2,1)S(1)}, bf16[1024,2048]{1,0:T(8,128)(2,1)}, u32[]{:S(2)}) copy-start(bf16[1024,2048]{1,0:T(8,128)(2,1)} %param.37) | copy-start | bytes 12582916
  283.1 92.7 %copy-start.8 = (f32[1024,1024]{0,1:T(8,128)S(1)}, f32[1024,1024]{0,1:T(8,128)}, u32[]{:S(2)}) copy-start(f32[1024,1024]{0,1:T(8,128)} %copy-done.7) | copy-start | bytes 12582916
  283.1 90.0 %collective-permute-start.2 = (f32[1024,1024]{0,1:T(8,128)S(1)}, f32[1024,1024]{0,1:T(8,128)S(1)}, u32[]{:S(2)}, u32[]{:S(2)}) collective-permute-start(f32[1024,1024]{0,1:T(8,128)S(1)} %fusion.93), channel_id=1, source_target_pairs={{0,1},{1,0},{2,3},{3,2},{4,5},{5,4},{6,7},{7,6},{8,9},{9,8},{10,11... | collective-permute-start | bytes 12582920 | tf_op jit(solution)/shard_map/ppermute | solution.py:85
  373.1 10.2 %slice-start.4 = ((s8[8388608]{0:T(1024)(128)(4,1)}), s8[4194304]{0:T(1024)(128)(4,1)S(1)}, s32[]{:S(2)}) async-start(s8[8388608]{0:T(1024)(128)(4,1)} %bitcast.136), calls=%async_computation.8 | async-start | bytes 8388608
  375.8 7.4 slice-start.5
  380.0 2.0 copy-start.12
  382.0 4.6 copy-start.35
  383.2 3.3 copy-start.39
  383.3 3.3 copy-start.32
  391.5 7.2 copy-start.16
  391.5 7.2 copy-start.18
  391.5 11.4 %slice-start = ((s8[16777216]{0:T(1024)(128)(4,1)}), s8[4194304]{0:T(1024)(128)(4,1)S(1)}, s32[]{:S(2)}) async-start(s8[16777216]{0:T(1024)(128)(4,1)} %bitcast.134), calls=%async_computation.4 | async-start | bytes 8388608
  391.5 11.4 %slice-start.1 = ((s8[16777216]{0:T(1024)(128)(4,1)}), s8[4194304]{0:T(1024)(128)(4,1)S(1)}, s32[]{:S(2)}) async-start(s8[16777216]{0:T(1024)(128)(4,1)} %bitcast.134), calls=%async_computation.5 | async-start | bytes 8388608
  391.5 11.3 %slice-start.2 = ((s8[16777216]{0:T(1024)(128)(4,1)}), s8[4194304]{0:T(1024)(128)(4,1)S(1)}, s32[]{:S(2)}) async-start(s8[16777216]{0:T(1024)(128)(4,1)} %bitcast.134), calls=%async_computation.6 | async-start | bytes 8388608
  398.7 2.4 copy-start.21
  398.7 2.4 copy-start.23
  398.7 5.1 slice-start.3
  401.1 2.7 copy-start.14
  415.3 6.9 copy-start.46
  415.3 6.9 copy-start.47
  433.1 6.5 copy-start.9
  433.1 6.5 copy-start.19
  433.1 6.5 copy-start.28
  446.8 89.1 %collective-permute-start.3 = (f32[1024,1024]{0,1:T(8,128)S(1)}, f32[1024,1024]{0,1:T(8,128)S(1)}, u32[]{:S(2)}, u32[]{:S(2)}) collective-permute-start(f32[1024,1024]{0,1:T(8,128)S(1)} %add_add_fusion), channel_id=1, source_target_pairs={{0,1},{1,0},{2,3},{3,2},{4,5},{5,4},{6,7},{7,6},{8,9},{9,8},{10,11... | collective-permute-start | bytes 12582920 | tf_op jit(solution)/shard_map/ppermute | solution.py:85
  452.9 2.8 copy-start.26
  452.9 2.8 copy-start.36
  458.4 81.2 %copy-start.54 = (f32[1024]{0:T(1024)S(1)}, f32[1024]{0:T(1024)}, u32[]{:S(2)}) copy-start(f32[1024]{0:T(1024)} %get-tuple-element.118) | copy-start | bytes 12292
  458.4 81.2 %copy-start.55 = (f32[1024]{0:T(1024)S(1)}, f32[1024]{0:T(1024)}, u32[]{:S(2)}) copy-start(f32[1024]{0:T(1024)} %get-tuple-element.114) | copy-start | bytes 12292
  458.4 81.2 %copy-start.56 = (f32[1024]{0:T(1024)S(1)}, f32[1024]{0:T(1024)}, u32[]{:S(2)}) copy-start(f32[1024]{0:T(1024)} %get-tuple-element.112) | copy-start | bytes 12292
  549.7 294.9 %reduce-scatter.5.cloned.1.call-start = ((), (), s32[]{:S(2)}) async-start(), calls=%async_computation.2 | async-start | bytes 17825792 | tf_op jit(solution)/shard_map/reduce_scatter | solution.py:260
  549.8 7.8 copy-start.34
  576.5 270.3 %copy-start.1 = (bf16[512,1024]{1,0:T(8,128)(2,1)S(1)}, bf16[512,1024]{1,0:T(8,128)(2,1)}, u32[]{:S(2)}) copy-start(bf16[512,1024]{1,0:T(8,128)(2,1)} %param.34) | copy-start | bytes 3145732
  (15 other events, 22.3 us)
Sparse Core Ops, SparseCore 0:
  549.8 111.6 reduce-scatter.6
  666.2 178.3 reduce-scatter.4

commit v2 on v0

v2 whole, which is shorter than its diff:
```python
from functools import partial
import math

import jax
import jax.numpy as jnp
from jax import lax
from jax.experimental import pallas as pl
from jax.experimental.pallas import tpu as pltpu
from jax.sharding import PartitionSpec as P
import numpy as np

HEAD_DIM = 64


def half_columns(values, which, size):
    return lax.dynamic_slice_in_dim(values, which * size, size, axis=1)


def flat_pairs(count, target):
    pairs = []
    for row in range(count):
        for side in range(2):
            goal = target(row, row % 2, side)
            if goal is not None:
                pairs.append((row * 2 + side, goal[0] * 2 + goal[1]))
    return pairs


def send(values, pairs):
    return lax.ppermute(values, ("dp", "tensor"), pairs)


def half_of(values, which, size):
    return lax.dynamic_slice_in_dim(values, which * size, size, axis=0)


BLOCK = 256
LANES = 128
VMEM_LIMIT = 56 * 1024 * 1024


def doc_ends(lengths_ref, docs):
    ends = [lengths_ref[0, 0]]
    for number in range(1, docs):
        ends.append(ends[-1] + lengths_ref[0, number])
    return ends


def doc_start(index, ends):
    start = jnp.zeros_like(index)
    for end in ends:
        start = jnp.where(index >= end, end, start)
    return start


def first_key(index, ends, real):
    return jnp.where(index >= real, index, doc_start(index, ends))


def rope_tables(ends, row_len, freq_ref, cos_ref, sin_ref):
    index = lax.broadcasted_iota(jnp.int32, (1, row_len), 1)
    position = (index - doc_start(index, ends)).astype(jnp.float32)
    angles = freq_ref[...] * position
    cosine, sine = jnp.cos(angles), jnp.sin(angles)
    cos_ref[...] = jnp.concatenate([cosine] * 4, axis=0).T
    sin_ref[...] = jnp.concatenate([-sine, sine] * 2, axis=0).T


def turned(values, cosine, sine, low_half):
    ahead = pltpu.roll(values, LANES - HEAD_DIM // 2, 1)
    behind = pltpu.roll(values, HEAD_DIM // 2, 1)
    return values * cosine + jnp.where(low_half, ahead, behind) * sine


def normed(values):
    average = jnp.mean(values, axis=-1, keepdims=True)
    centered = values - average
    return centered * lax.rsqrt(jnp.mean(centered * centered, axis=-1, keepdims=True) + 1e-05)


def contract(left, right, left_dim, right_dim):
    return lax.dot_general(
        left, right, (((left_dim,), (right_dim,)), ((), ())), preferred_element_type=jnp.float32
    )


def prepare(docs, lengths_ref, freq_ref, rows_of, gain_ref, attn_in_ref, cos_ref, sin_ref):
    row_len = attn_in_ref.shape[0]

    @pl.when(pl.program_id(0) == 0)
    def _():
        rope_tables(doc_ends(lengths_ref, docs), row_len, freq_ref, cos_ref, sin_ref)
        for number in range(row_len // BLOCK):
            rows = pl.ds(number * BLOCK, BLOCK)
            attn_in_ref[rows, :] = (
                normed(rows_of(rows)) * gain_ref[...]
            ).astype(jnp.bfloat16)


def head_masks():
    lane = lax.broadcasted_iota(jnp.int32, (1, LANES), 1)
    return (lax.rem(lane, HEAD_DIM) < HEAD_DIM // 2, lane < HEAD_DIM)


def forward_kernel(docs, first, lengths_ref, pad_ref, freq_ref, gain_ref, *refs):
    if first:
        x_ref, wq_ref, wk_ref, wv_ref, out_ref, attn_in_ref, cos_ref, sin_ref, q_ref, k_ref, v_ref = refs
        row_len = x_ref.shape[0]
        prepare(
            docs, lengths_ref, freq_ref, lambda rows: x_ref[rows, :].astype(jnp.float32), gain_ref, attn_in_ref, cos_ref, sin_ref
        )
    else:
        attn_in_ref, cos_ref, sin_ref, wq_ref, wk_ref, wv_ref, out_ref, q_ref, k_ref, v_ref = refs
        row_len = attn_in_ref.shape[0]
    low_half, even = head_masks()
    group = wq_ref.shape[1]
    scale = 1.0 / math.sqrt(HEAD_DIM)
    for number in range(row_len // BLOCK):
        rows = pl.ds(number * BLOCK, BLOCK)
        block = attn_in_ref[rows, :]
        query = jnp.dot(block, wq_ref[...], preferred_element_type=jnp.float32)
        key = jnp.dot(block, wk_ref[...], preferred_element_type=jnp.float32)
        v_ref[rows, :] = jnp.dot(block, wv_ref[...], preferred_element_type=jnp.float32).astype(jnp.bfloat16)
        cosine, sine = cos_ref[rows, :], sin_ref[rows, :]
        for pair in range(group // LANES):
            cols = slice(pair * LANES, (pair + 1) * LANES)
            q_ref[rows, cols] = (turned(query[:, cols], cosine, sine, low_half) * scale).astype(jnp.bfloat16)
            k_ref[rows, cols] = turned(key[:, cols], cosine, sine, low_half).astype(jnp.bfloat16)
    ends = doc_ends(lengths_ref, docs)
    real = row_len - pad_ref[0]
    for number in range(row_len // BLOCK):
        rows = pl.ds(number * BLOCK, BLOCK)
        keys = (number + 1) * BLOCK
        query_index = number * BLOCK + lax.broadcasted_iota(jnp.int32, (BLOCK, 1), 0)
        start = first_key(query_index, ends, real)
        key_index = lax.broadcasted_iota(jnp.int32, (1, keys), 1)
        allowed = (key_index >= start) & (key_index <= query_index)
        for pair in range(group // LANES):
            cols = slice(pair * LANES, (pair + 1) * LANES)
            query = q_ref[rows, cols]
            key, value = k_ref[:keys, cols], v_ref[:keys, cols]
            results = []
            for chosen in (even, jnp.logical_not(even)):
                one = query * chosen.astype(jnp.bfloat16)
                scores = jnp.where(allowed, contract(one, key, 1, 1), -1e30)
                weights = jnp.exp(scores - jnp.max(scores, axis=-1, keepdims=True))
                total = jnp.sum(weights, axis=-1, keepdims=True)
                results.append(
                    jnp.dot(weights.astype(jnp.bfloat16), value, preferred_element_type=jnp.float32) / total
                )
            out_ref[rows, cols] = jnp.where(even, results[0], results[1]).astype(jnp.bfloat16).astype(jnp.float32)


def ready_kernel(
    docs, where_ref, lengths_ref, pad_ref, freq_ref, here_ref, there_ref, gain_ref, wq_ref, wk_ref, wv_ref,
    q_ref, k_ref, v_ref, log_ref, attn_in_ref, cos_ref, sin_ref,
):
    row_len = here_ref.shape[0]
    flag = where_ref[1]
    prepare(
        docs,
        lengths_ref,
        freq_ref,
        lambda rows: jnp.where(flag != 0, here_ref[rows, :].astype(jnp.float32), there_ref[rows, :]),
        gain_ref,
        attn_in_ref,
        cos_ref,
        sin_ref,
    )
    low_half, even = head_masks()
    group = wq_ref.shape[1]
    scale = 1.0 / math.sqrt(HEAD_DIM)
    for number in range(row_len // BLOCK):
        rows = pl.ds(number * BLOCK, BLOCK)
        block = attn_in_ref[rows, :]
        query = jnp.dot(block, wq_ref[...], preferred_element_type=jnp.float32)
        key = jnp.dot(block, wk_ref[...], preferred_element_type=jnp.float32)
        v_ref[rows, :] = jnp.dot(block, wv_ref[...], preferred_element_type=jnp.float32).astype(jnp.bfloat16)
        cosine, sine = cos_ref[rows, :], sin_ref[rows, :]
        for pair in range(group // LANES):
            cols = slice(pair * LANES, (pair + 1) * LANES)
            q_ref[rows, cols] = (turned(query[:, cols], cosine, sine, low_half) * scale).astype(jnp.bfloat16)
            k_ref[rows, cols] = turned(key[:, cols], cosine, sine, low_half).astype(jnp.bfloat16)
    ends = doc_ends(lengths_ref, docs)
    real = row_len - pad_ref[0]
    for number in range(row_len // BLOCK):
        rows = pl.ds(number * BLOCK, BLOCK)
        keys = (number + 1) * BLOCK
        query_index = number * BLOCK + lax.broadcasted_iota(jnp.int32, (1, BLOCK), 1)
        start = first_key(query_index, ends, real)
        key_index = lax.broadcasted_iota(jnp.int32, (keys, 1), 0)
        allowed = (key_index >= start) & (key_index <= query_index)
        for pair in range(group // LANES):
            cols = slice(pair * LANES, (pair + 1) * LANES)
            query, key = q_ref[rows, cols], k_ref[:keys, cols]
            for side, chosen in enumerate((even, jnp.logical_not(even))):
                one = query * chosen.astype(jnp.bfloat16)
                scores = jnp.where(allowed, contract(key, one, 1, 1), -1e30)
                highest = jnp.max(scores, axis=0, keepdims=True)
                total = jnp.sum(jnp.exp(scores - highest), axis=0, keepdims=True)
                head = pair * 2 + side
                log_ref[0, head : head + 1, rows] = highest + jnp.log(total)


def backward_kernel(
    docs, lengths_ref, pad_ref, cos_ref, sin_ref, q_ref, k_ref, v_ref, log_ref, grad_ref,
    gq_ref, gk_ref, gv_ref, key_sum, value_sum,
):
    row_len = q_ref.shape[0]
    low_half, even = head_masks()
    scale = 1.0 / math.sqrt(HEAD_DIM)
    ends = doc_ends(lengths_ref, docs)
    real = row_len - pad_ref[0]
    blocks = row_len // BLOCK
    for number in range(blocks - 1, -1, -1):
        rows = pl.ds(number * BLOCK, BLOCK)
        keys = (number + 1) * BLOCK
        query_index = number * BLOCK + lax.broadcasted_iota(jnp.int32, (1, BLOCK), 1)
        start = first_key(query_index, ends, real)
        key_index = lax.broadcasted_iota(jnp.int32, (keys, 1), 0)
        allowed = (key_index >= start) & (key_index <= query_index)
        query, grad = q_ref[rows, :], grad_ref[rows, :]
        key, value = k_ref[:keys, :], v_ref[:keys, :]
        parts = []
        for side, chosen in enumerate((even, jnp.logical_not(even))):
            mask = chosen.astype(jnp.bfloat16)
            one_query, one_grad = query * mask, grad * mask
            scores = jnp.where(allowed, contract(key, one_query, 1, 1), -1e30)
            weights = jnp.exp(scores - log_ref[0, side : side + 1, rows])
            soft = contract(value, one_grad, 1, 1)
            cross = jnp.sum(soft * weights, axis=0, keepdims=True)
            grad_scores = (weights * (soft - cross)).astype(jnp.bfloat16)
            low_weights = weights.astype(jnp.bfloat16)
            parts.append((
                contract(grad_scores, key, 0, 0),
                jnp.dot(grad_scores, one_query, preferred_element_type=jnp.float32),
                jnp.dot(low_weights, one_grad, preferred_element_type=jnp.float32),
            ))
        grad_query = jnp.where(even, parts[0][0], parts[1][0]) * scale
        gq_ref[rows, :] = turned(grad_query, cos_ref[rows, :], -sin_ref[rows, :], low_half).astype(jnp.bfloat16)
        if number == blocks - 1:
            key_sum[...] = parts[0][1] + parts[1][1]
            value_sum[...] = parts[0][2] + parts[1][2]
        else:
            key_sum[:keys, :] += parts[0][1] + parts[1][1]
            value_sum[:keys, :] += parts[0][2] + parts[1][2]
    for number in range(blocks):
        rows = pl.ds(number * BLOCK, BLOCK)
        gk_ref[rows, :] = turned(
            key_sum[rows, :], cos_ref[rows, :], -sin_ref[rows, :], low_half
        ).astype(jnp.bfloat16)
        gv_ref[rows, :] = value_sum[rows, :].astype(jnp.bfloat16)


def smem():
    return pl.BlockSpec(memory_space=pltpu.SMEM)


def whole(shape):
    return pl.BlockSpec(shape, lambda step: (0,) * len(shape))


def frequencies():
    half_dim = HEAD_DIM // 2
    return (10000.0 ** (-2.0 * np.arange(half_dim) / HEAD_DIM)).astype(np.float32)[:, None]


def attention_forward(number, sources, lengths, pad_count, gain, w_query, w_key, w_value):
    row_len, width = sources[0].shape
    first = number == 0
    group = w_query.shape[1] // 2
    weight = pl.BlockSpec((width, group), lambda step: (0, number))
    table = jax.ShapeDtypeStruct((row_len, LANES), jnp.float32)
    outs = [jax.ShapeDtypeStruct((row_len, group), jnp.float32)]
    if first:
        outs += [jax.ShapeDtypeStruct((row_len, width), jnp.bfloat16), table, table]
    return pl.pallas_call(
        partial(forward_kernel, lengths.shape[1], first),
        grid=(1,),
        in_specs=[
            smem(), smem(), whole((HEAD_DIM // 2, 1)), whole((1, width)),
            *(whole(source.shape) for source in sources), weight, weight, weight,
        ],
        out_specs=[whole(out.shape) for out in outs],
        out_shape=outs,
        scratch_shapes=[pltpu.VMEM((row_len, group), jnp.bfloat16)] * 3,
        compiler_params=pltpu.CompilerParams(vmem_limit_bytes=VMEM_LIMIT),
        cost_estimate=pl.CostEstimate(
            flops=6 * row_len * width * group + 16 * row_len * row_len * group,
            bytes_accessed=4 * row_len * width + 6 * width * group,
            transcendentals=row_len * row_len * group // HEAD_DIM,
        ),
        name="attention_forward",
    )(lengths, pad_count, jnp.asarray(frequencies()), gain[None], *sources, w_query, w_key, w_value)


def attention_ready(where, block_in, there, lengths, pad_count, gain, weights):
    row_len, width = block_in.shape
    wide = weights.shape[1] // 3
    group = 2 * LANES
    heads = group // HEAD_DIM
    steps = wide // group
    weight = [pl.BlockSpec((width, group), lambda step, part=part: (0, part * steps + step)) for part in range(3)]
    part = pl.BlockSpec((row_len, group), lambda step: (0, step))
    table = jax.ShapeDtypeStruct((row_len, LANES), jnp.float32)
    rows = jax.ShapeDtypeStruct((row_len, wide), jnp.bfloat16)
    return pl.pallas_call(
        partial(ready_kernel, lengths.shape[1]),
        grid=(wide // group,),
        in_specs=[
            smem(), smem(), smem(), whole((HEAD_DIM // 2, 1)), whole((row_len, width)), whole((row_len, width)), whole((1, width)), *weight,
        ],
        out_specs=[
            part, part, part,
            pl.BlockSpec((1, heads, row_len), lambda step: (step, 0, 0)),
            whole((row_len, width)), whole((row_len, LANES)), whole((row_len, LANES)),
        ],
        out_shape=[
            rows, rows, rows,
            jax.ShapeDtypeStruct((wide // group, heads, row_len), jnp.float32),
            jax.ShapeDtypeStruct((row_len, width), jnp.bfloat16), table, table,
        ],
        compiler_params=pltpu.CompilerParams(vmem_limit_bytes=VMEM_LIMIT),
        cost_estimate=pl.CostEstimate(
            flops=6 * row_len * width * wide + 8 * row_len * row_len * wide,
            bytes_accessed=6 * row_len * width + 6 * width * wide + 6 * row_len * wide,
            transcendentals=row_len * row_len * wide // HEAD_DIM,
        ),
        name="attention_ready",
    )(where, lengths, pad_count, jnp.asarray(frequencies()), block_in, there, gain[None], weights, weights, weights)


def attention_backward(ready, lengths, pad_count, grad_heads):
    query, key, value, logs, _, cosine, sine = ready
    row_len, wide = query.shape
    pairs = wide // LANES
    logs = logs.reshape(pairs, LANES // HEAD_DIM, row_len)
    part = pl.BlockSpec((row_len, LANES), lambda step: (0, step))
    rows = jax.ShapeDtypeStruct((row_len, wide), jnp.bfloat16)
    return pl.pallas_call(
        partial(backward_kernel, lengths.shape[1]),
        grid=(pairs,),
        in_specs=[
            smem(), smem(), whole((row_len, LANES)), whole((row_len, LANES)), part, part, part,
            pl.BlockSpec((1, LANES // HEAD_DIM, row_len), lambda step: (step, 0, 0)), part,
        ],
        out_specs=[part, part, part],
        out_shape=[rows, rows, rows],
        scratch_shapes=[pltpu.VMEM((row_len, LANES), jnp.float32), pltpu.VMEM((row_len, LANES), jnp.float32)],
        compiler_params=pltpu.CompilerParams(vmem_limit_bytes=VMEM_LIMIT),
        cost_estimate=pl.CostEstimate(
            flops=40 * row_len * row_len * wide,
            bytes_accessed=14 * row_len * wide,
            transcendentals=row_len * row_len * wide // HEAD_DIM,
        ),
        name="attention_backward",
    )(lengths, pad_count, cosine, sine, query, key, value, logs, grad_heads)


FF_STEPS = 4
PARTS = 2
TILE = 64


def chosen_rows(flag, here_ref, there_ref):
    return jnp.where(flag != 0, here_ref[...].astype(jnp.float32), there_ref[...])


def norm_stats(values):
    average = jnp.mean(values, axis=-1, keepdims=True)
    centered = values - average
    inverse = lax.rsqrt(jnp.mean(centered * centered, axis=-1, keepdims=True) + 1e-05)
    return (centered * inverse, inverse)


def norm_pull(grad, gain, hat, inverse):
    scaled = grad * gain
    mean_scaled = jnp.mean(scaled, axis=-1, keepdims=True)
    mean_cross = jnp.mean(scaled * hat, axis=-1, keepdims=True)
    return inverse * (scaled - mean_scaled - hat * mean_cross)


def add_gain(ref, step, row, value):
    @pl.when(step == 0)
    def _():
        ref[row : row + 1, :] = value

    @pl.when(step != 0)
    def _():
        ref[row : row + 1, :] += value


def hidden_kernel(where_ref, low_ref, high_ref, w_out_ref, arrived_ref, here_ref, there_ref, gain_ref, hidden_ref, total_ref):
    group = low_ref.shape[1]
    total = jnp.dot(low_ref[...], w_out_ref[:group, :], preferred_element_type=jnp.float32) + arrived_ref[...]
    total += jnp.dot(high_ref[...], w_out_ref[group:, :], preferred_element_type=jnp.float32)
    total_ref[...] = total
    hat, _ = norm_stats(total)
    hidden_ref[...] = chosen_rows(where_ref[1], here_ref, there_ref) + hat * gain_ref[...]


def mlp_forward_kernel(hidden_ref, gain_ref, up_ref, down_ref, *refs):
    mlp_in_ref, act_ref, slope_ref, part_ref = refs[-4:]
    step = pl.program_id(0)

    @pl.when(step == 0)
    def _():
        hat, _ = norm_stats(hidden_ref[...])
        mlp_in_ref[...] = (hat * gain_ref[...]).astype(jnp.bfloat16)

    factor = math.sqrt(2.0 / math.pi)
    size = up_ref.shape[1] // PARTS
    part = None
    for number in range(PARTS):
        cols = slice(number * size, (number + 1) * size)
        pre = jnp.dot(mlp_in_ref[...], up_ref[:, cols], preferred_element_type=jnp.float32)
        squared = pre * pre
        bent = jnp.tanh(factor * pre * (1.0 + 0.044715 * squared))
        gate = 0.5 * (1.0 + bent)
        act = (pre * gate).astype(jnp.bfloat16)
        act_ref[:, cols] = act
        slope_ref[:, cols] = gate + 0.5 * pre * (1.0 - bent * bent) * (factor + (3.0 * 0.044715 * factor) * squared)
        piece = jnp.dot(act, down_ref[cols, :], preferred_element_type=jnp.float32)
        part = piece if part is None else part + piece

    @pl.when(step == 0)
    def _():
        part_ref[...] = part

    @pl.when(step != 0)
    def _():
        part_ref[...] += part


def mlp_backward_kernel(
    where_ref, hidden_ref, total_ref, here_ref, there_ref, gain_ref, down_ref, up_ref, slope_ref, *refs
):
    block_ref, low_ref, gain_sum_ref, grad_up_ref, part_ref = refs[-5:]
    step = pl.program_id(0)

    @pl.when(step == 0)
    def _():
        hat, inverse = norm_stats(total_ref[...])
        cot = chosen_rows(where_ref[1], here_ref, there_ref)
        block_ref[...] = hidden_ref[...] + hat * gain_ref[...]
        low_ref[...] = norm_pull(cot, gain_ref[...], hat, inverse).astype(jnp.bfloat16)
        gain_sum_ref[...] = jnp.broadcast_to(jnp.sum(cot * hat, axis=0, keepdims=True), gain_sum_ref.shape)

    size = up_ref.shape[1] // PARTS
    part = None
    for number in range(PARTS):
        cols = slice(number * size, (number + 1) * size)
        grad_act = contract(low_ref[...], down_ref[cols, :], 1, 1)
        grad_up = (grad_act * slope_ref[:, cols]).astype(jnp.bfloat16)
        grad_up_ref[:, cols] = grad_up
        piece = contract(grad_up, up_ref[:, cols], 1, 1)
        part = piece if part is None else part + piece

    @pl.when(step == 0)
    def _():
        part_ref[...] = part

    @pl.when(step != 0)
    def _():
        part_ref[...] += part


def residual_kernel(
    where_ref, part_ref, arrived_ref, hidden_ref, attn_ref, here_ref, there_ref, gain_mlp_ref, gain_attn_ref, *refs
):
    res_ref, attn_grad_ref, gains_ref = refs[-3:]
    step = pl.program_id(0)
    grad = part_ref[...] + arrived_ref[...]
    hat, inverse = norm_stats(hidden_ref[...])
    cot = chosen_rows(where_ref[1], here_ref, there_ref)
    res = cot + norm_pull(grad, gain_mlp_ref[...], hat, inverse)
    res_ref[...] = res
    add_gain(gains_ref, step, 0, jnp.sum(grad * hat, axis=0, keepdims=True))
    hat, inverse = norm_stats(attn_ref[...])
    attn_grad_ref[...] = norm_pull(res, gain_attn_ref[...], hat, inverse)
    add_gain(gains_ref, step, 1, jnp.sum(res * hat, axis=0, keepdims=True))


def other_kernel(where_ref, grad_ref, weight_ref, out_ref):
    piece = contract(grad_ref[...], weight_ref[...], 1, 1)

    @pl.when(pl.program_id(0) == 0)
    def _():
        out_ref[...] = piece

    @pl.when(pl.program_id(0) != 0)
    def _():
        out_ref[...] += piece


def input_kernel(
    where_ref, grad_ref, weight_ref, arrived_ref, here_ref, there_ref, res_ref, gain_ref, out_ref, gain_sum_ref, sum_ref
):
    step = pl.program_id(0)
    piece = contract(grad_ref[...], weight_ref[...], 1, 1)

    @pl.when(step == 0)
    def _():
        sum_ref[...] = piece + arrived_ref[...]

    @pl.when(step != 0)
    def _():
        sum_ref[...] += piece

    @pl.when(step == pl.num_programs(0) - 1)
    def _():
        grad = sum_ref[...]
        hat, inverse = norm_stats(chosen_rows(where_ref[1], here_ref, there_ref))
        out_ref[...] = res_ref[...] + norm_pull(grad, gain_ref[...], hat, inverse)
        gain_sum_ref[...] = jnp.broadcast_to(jnp.sum(grad * hat, axis=0, keepdims=True), gain_sum_ref.shape)


def pack_kernel(where_ref, x_ref, cot_ref, out_ref):
    step = pl.program_id(0)

    @pl.when(step < 2)
    def _():
        out_ref[...] = x_ref[...].astype(jnp.float32)

    @pl.when(step == 2)
    def _():
        out_ref[...] = cot_ref[...].astype(jnp.float32)


def call(kernel, name, steps, where, arrays, specs, outs, aliases, flops):
    moved = sum(array.size * array.dtype.itemsize for array in arrays)
    return pl.pallas_call(
        kernel,
        grid_spec=pltpu.PrefetchScalarGridSpec(
            num_scalar_prefetch=0 if where is None else 1,
            grid=(steps,),
            in_specs=specs,
            out_specs=[spec for _, spec in outs],
        ),
        out_shape=[shape for shape, _ in outs],
        input_output_aliases=aliases,
        compiler_params=pltpu.CompilerParams(vmem_limit_bytes=VMEM_LIMIT),
        cost_estimate=pl.CostEstimate(flops=flops, bytes_accessed=moved, transcendentals=0),
        name=name,
    )(*(() if where is None else (where,)), *arrays)


def rows_spec(rows, width, place):
    return pl.BlockSpec((rows, width), lambda step, *where: (place(step, *where), 0))


def fixed_spec(shape):
    return pl.BlockSpec(shape, lambda *args: (0,) * len(shape))


def hidden_chunk(where, number, attended, w_out, arrived, block_in, there, gain):
    row_len, group = attended[0].shape
    width = w_out.shape[1]
    rows = row_len // 4
    mine = rows_spec(rows, width, lambda step, where: where[0] * 2 + number)
    mine_attended = rows_spec(rows, group, lambda step, where: where[0] * 2 + number)
    shape = jax.ShapeDtypeStruct((rows, width), jnp.float32)
    return call(
        hidden_kernel, "hidden", 1, where,
        (*attended, w_out, arrived, block_in, there, gain[None]),
        [
            mine_attended, mine_attended, fixed_spec(w_out.shape),
            rows_spec(rows, width, lambda step, where: number), mine, mine, fixed_spec((1, width)),
        ],
        [(shape, fixed_spec((rows, width))), (shape, fixed_spec((rows, width)))],
        {}, 4 * rows * group * width,
    )


def mlp_forward(number, hidden, gain, w_up, w_down, buffers):
    rows, width = hidden.shape
    inner = w_up.shape[1]
    size = inner // FF_STEPS
    spare = [pl.BlockSpec(memory_space=pl.ANY)] * len(buffers)
    return call(
        mlp_forward_kernel, "mlp_forward", FF_STEPS, None,
        (hidden, gain[None], w_up, w_down, *buffers),
        [
            fixed_spec((rows, width)), fixed_spec((1, width)),
            pl.BlockSpec((width, size), lambda step: (0, step)),
            pl.BlockSpec((size, width), lambda step: (step, 0)),
            *spare,
        ],
        [
            (jax.ShapeDtypeStruct((4 * rows, width), jnp.bfloat16), pl.BlockSpec((rows, width), lambda step: (number, 0))),
            (jax.ShapeDtypeStruct((4 * rows, inner), jnp.bfloat16), pl.BlockSpec((rows, size), lambda step: (number, step))),
            (jax.ShapeDtypeStruct((rows, inner), jnp.float32), pl.BlockSpec((rows, size), lambda step: (0, step))),
            (jax.ShapeDtypeStruct((rows, width), jnp.float32), fixed_spec((rows, width))),
        ],
        {4 + index: index for index in range(len(buffers))}, 4 * rows * width * inner,
    )


def mlp_backward(where, number, hidden, total, cotangent, there, gain, w_down, w_up, slope, buffers):
    rows, width = hidden.shape
    inner = w_up.shape[1]
    size = inner // FF_STEPS
    part = number % 2
    spare = [pl.BlockSpec(memory_space=pl.ANY)] * len(buffers)
    return call(
        mlp_backward_kernel, "mlp_backward", FF_STEPS, where,
        (hidden, total, cotangent, there, gain[None], w_down, w_up, slope, *buffers),
        [
            fixed_spec((rows, width)), fixed_spec((rows, width)),
            rows_spec(rows, width, lambda step, where: where[0] * 2 + part),
            rows_spec(rows, width, lambda step, where: 4 + part),
            fixed_spec((1, width)),
            pl.BlockSpec((size, width), lambda step, where: (step, 0)),
            pl.BlockSpec((width, size), lambda step, where: (0, step)),
            pl.BlockSpec((rows, size), lambda step, where: (0, step)),
            *spare,
        ],
        [
            (jax.ShapeDtypeStruct((rows, width), jnp.float32), fixed_spec((rows, width))),
            (jax.ShapeDtypeStruct((4 * rows, width), jnp.bfloat16), pl.BlockSpec((rows, width), lambda step, where: (number, 0))),
            (jax.ShapeDtypeStruct((8, width), jnp.float32), fixed_spec((8, width))),
            (jax.ShapeDtypeStruct((4 * rows, inner), jnp.bfloat16), pl.BlockSpec((rows, size), lambda step, where: (number, step))),
            (jax.ShapeDtypeStruct((rows, width), jnp.float32), fixed_spec((rows, width))),
        ],
        {9 + index: 1 + 2 * index for index in range(len(buffers))}, 4 * rows * width * inner,
    )


def residual_chunk(where, number, part, arrived, hidden, attn_total, cotangent, there, gain_mlp, gain_attn, buffers):
    rows, width = part.shape
    steps = rows // TILE
    local = rows_spec(TILE, width, lambda step, where: step)
    spare = [pl.BlockSpec(memory_space=pl.ANY)] * len(buffers)
    whole_half = jax.ShapeDtypeStruct((2 * rows, width), jnp.float32)
    place = rows_spec(TILE, width, lambda step, where: number * steps + step)
    return call(
        residual_kernel, "residual", steps, where,
        (part, arrived, hidden, attn_total, cotangent, there, gain_mlp[None], gain_attn[None], *buffers),
        [
            local, local, local, local,
            rows_spec(TILE, width, lambda step, where: (where[0] * 2 + number) * steps + step),
            rows_spec(TILE, width, lambda step, where: (4 + number) * steps + step),
            fixed_spec((1, width)), fixed_spec((1, width)),
            *spare,
        ],
        [(whole_half, place), (whole_half, place), (jax.ShapeDtypeStruct((8, width), jnp.float32), fixed_spec((8, width)))],
        {9 + index: index for index in range(len(buffers))}, 20 * rows * width,
    )


def packed(where, block_in, cotangent):
    row_len, width = block_in.shape
    half = row_len // 2
    return call(
        pack_kernel, "packed", 3, where, (block_in, cotangent),
        [
            rows_spec(half, width, lambda step, where: jnp.minimum(step, 1)),
            rows_spec(half, width, lambda step, where: 1 - where[0]),
        ],
        [(jax.ShapeDtypeStruct((3 * half, width), jnp.float32), rows_spec(half, width, lambda step, where: step))],
        {}, 0,
    )[0]


def input_specs(grads, weights, other):
    row_len, wide = grads.shape[0], grads.shape[1] // 3
    width = weights.shape[0]
    half = row_len // 2
    return [
        pl.BlockSpec((half, wide), lambda step, where: (1 - where[0] if other else where[0], step)),
        pl.BlockSpec((width, wide), lambda step, where: (0, step)),
    ], (half, width)


def input_other(where, grads, weights):
    specs, shape = input_specs(grads, weights, True)
    return call(
        other_kernel, "input_other", 3, where, (grads, weights), specs,
        [(jax.ShapeDtypeStruct(shape, jnp.float32), fixed_spec(shape))], {}, 2 * shape[0] * weights.size,
    )[0]


def input_own(where, grads, weights, arrived, block_in, there, res, gain):
    specs, shape = input_specs(grads, weights, False)
    mine = rows_spec(*shape, lambda step, where: where[0])
    moved = sum(array.size * array.dtype.itemsize for array in (grads, weights, arrived, block_in, there, res))
    return pl.pallas_call(
        input_kernel,
        grid_spec=pltpu.PrefetchScalarGridSpec(
            num_scalar_prefetch=1,
            grid=(3,),
            in_specs=specs + [fixed_spec(shape), mine, mine, fixed_spec(shape), fixed_spec((1, shape[1]))],
            out_specs=[fixed_spec(shape), fixed_spec((8, shape[1]))],
            scratch_shapes=[pltpu.VMEM(shape, jnp.float32)],
        ),
        out_shape=[jax.ShapeDtypeStruct(shape, jnp.float32), jax.ShapeDtypeStruct((8, shape[1]), jnp.float32)],
        compiler_params=pltpu.CompilerParams(vmem_limit_bytes=VMEM_LIMIT),
        cost_estimate=pl.CostEstimate(flops=2 * shape[0] * weights.size, bytes_accessed=moved, transcendentals=0),
        name="input_own",
    )(where, grads, weights, arrived, block_in, there, res, gain[None])


def after(values, *others):
    return lax.optimization_barrier((values, others))[0]


def ordered(mine, other, bit, axis):
    low = jnp.where(bit == 0, mine, other)
    high = jnp.where(bit == 0, other, mine)
    return jnp.concatenate([low, high], axis=axis)


def body(
    dp_size,
    block_in,
    cotangent,
    lengths,
    pad_count,
    norm_in_attn,
    w_query,
    w_key,
    w_value,
    w_out,
    norm_out_attn,
    norm_in_mlp,
    w_up,
    w_down,
    norm_out_mlp,
):
    f32, bf16 = jnp.float32, jnp.bfloat16
    place = lax.axis_index("dp")
    core = lax.rem(place, 2)
    chip = lax.div(place, 2)
    side = lax.axis_index("tensor")
    same = core == side
    keep = same.astype(f32)
    first = (core == 0).astype(f32)
    chips = dp_size // 2
    levels = chips.bit_length() - 1
    bits = [lax.rem(lax.div(chip, 1 << level), 2) for level in range(levels)]
    swap = flat_pairs(dp_size, lambda d, c, t: (d ^ 1, 1 - t) if c != t else None)
    cross = flat_pairs(dp_size, lambda d, c, t: (d ^ 1, t))
    over = flat_pairs(dp_size, lambda d, c, t: (d, 1 - t))
    flips = [flat_pairs(dp_size, lambda d, c, t: (d ^ (2 << level), t)) for level in range(levels)]
    row_len, width = block_in.shape
    half = row_len // 2
    chunk = half // 2
    wide = w_query.shape[1]
    hidden = w_up.shape[1]

    shares = min(2, levels)
    near = [flat_pairs(dp_size, lambda d, c, t: (d ^ (2 << level), t) if c != t else None) for level in range(shares)]

    where_own = jnp.stack([core, same.astype(jnp.int32)])
    where_peer = jnp.stack([core, 1 - same.astype(jnp.int32)])
    out_rows = wide // 2
    w_out_sent = send(half_of(w_out, bits[0], out_rows).astype(f32), swap)
    attended_low, *sources = attention_forward(0, (block_in,), lengths, pad_count, norm_in_attn, w_query, w_key, w_value)
    low_sent = send(attended_low, swap)
    sources = after(sources, w_out_sent)
    w_out_sent = ordered(w_out_sent, send(w_out_sent, near[0]), bits[0], 0)
    [attended_high] = attention_forward(1, sources, lengths, pad_count, norm_in_attn, w_query, w_key, w_value)
    high_sent = send(attended_high, swap)
    block_late, cot_late, facts = after((block_in, cotangent, jnp.pad(lengths, ((0, 0), (0, 1)))), attended_high)
    facts = facts.astype(f32) + jnp.pad(pad_count.astype(f32)[:, None], ((0, 0), (lengths.shape[1], 0)))
    there = send(packed(where_own, block_late, cot_late), cross)
    facts_there = send(facts, cross)
    low_sent = after(low_sent, attended_high)
    attended = [(attended_low * keep + low_sent).astype(bf16), (attended_high * keep + high_sent).astype(bf16)]
    weights_here = jnp.concatenate([w_query, w_key, w_value], axis=1)
    part_rows = width >> shares
    which = sum(bits[level] << level for level in range(shares))
    weights_sent = send(half_of(after(weights_here, attended[1]), which, part_rows).astype(f32), swap)
    w_out_mine = (w_out.astype(f32) * keep + w_out_sent).astype(bf16)
    facts_row = jnp.where(same, facts, facts_there).astype(jnp.int32)
    docs = lengths.shape[1]
    lengths_row, pad_row = facts_row[:, :docs], facts_row[:, docs]
    part_other = sum(
        jnp.dot(half_of(values, 1 - core, half), w_out_mine[start : start + out_rows], preferred_element_type=f32)
        for values, start in zip(attended, (0, out_rows))
    )
    arrived = send(part_other, cross)
    hidden_own, attn_total, hidden_peer = [], [], []
    for number in range(2):
        one, total = hidden_chunk(where_own, number, attended, w_out_mine, arrived, block_in, there, norm_out_attn)
        hidden_own.append(one)
        attn_total.append(total)
        hidden_peer.append(send(one, over))

    buffers, slopes, parts, sums_own = (), [], [], []
    for number in range(4):
        piece = hidden_own[number] if number < 2 else hidden_peer[number - 2]
        if number == 3:
            piece = after(piece, parts[2], weights_sent)
        *buffers, slope, part = mlp_forward(number, piece, norm_in_mlp, w_up, w_down, buffers)
        slopes.append(slope)
        parts.append(part)
        if number >= 2:
            sums_own.append(send(part, over))
            if number - 2 < shares:
                weights_sent = after(weights_sent, part)
                weights_sent = ordered(weights_sent, send(weights_sent, near[number - 2]), bits[number - 2], 0)
    mlp_in_all, activated_all = buffers
    weights_late = after(weights_sent, parts[3])
    weights_mine = (weights_here.astype(f32) * keep + weights_late).astype(bf16)
    ready = attention_ready(where_own, block_in, there, lengths_row, pad_row, norm_in_attn, weights_mine)
    totals, blocks, back_parts, gain_out_mlp = [], [], [], []
    buffers = ()
    for number in range(4):
        if number < 2:
            total = parts[number] + (sums_own[0] if number == 0 else after(sums_own[1], back_parts[0]))
            totals.append(total)
            totals_peer = send(total, over)
            totals.append(totals_peer)
        total = totals[2 * number] if number < 2 else totals[2 * (number - 2) + 1]
        if number >= 2:
            total = after(total, back_parts[number - 1], ready)
        hidden_piece = hidden_own[number] if number < 2 else hidden_peer[number - 2]
        block, low_all, gain_sum, up_all, part = mlp_backward(
            where_own if number < 2 else where_peer,
            number,
            hidden_piece,
            total,
            cotangent,
            there,
            norm_out_mlp,
            w_down,
            w_up,
            slopes[number],
            buffers,
        )
        buffers = (low_all, up_all)
        blocks.append(block)
        back_parts.append(part)
        gain_out_mlp.append(gain_sum[0])
    grad_low_all, grad_up_all = buffers
    sums_own = [send(part, over) for part in back_parts[2:]]

    small = width // chips // 2

    def halved(held, arrived, level):
        group = (-1, 2, width // chips, held.shape[-1])
        parts = [held.reshape(group)] + ([] if arrived is None else [arrived.reshape(group)])
        results = []
        for which in (bits[level], 1 - bits[level]):
            results.append(sum(lax.dynamic_index_in_dim(part, which, 1, keepdims=False) for part in parts))
        return results

    def to_chip(held, arrived, level, gate=None):
        for number in range(level, levels):
            held, leaving = halved(held, arrived, number)
            arrived = send(leaving, flips[number])
        return (held + arrived).reshape(width // chips, -1)

    def to_core(held):
        arrived = send(half_of(held, 1 - core, small), cross)
        return ordered(half_of(held, core, small), arrived, core, 1)

    def weight_part(left, right, columns):
        return jnp.einsum("td,tf->df", left, half_columns(right, columns, hidden // 2), preferred_element_type=f32)

    down_sent = send(weight_part(grad_low_all, activated_all, 1 - core), cross)
    weight_up = jnp.einsum("td,tf->df", mlp_in_all, grad_up_all, preferred_element_type=f32)
    grad_up = lax.psum_scatter(weight_up, "dp", scatter_dimension=0, tiled=True)
    down_kept = weight_part(grad_low_all, activated_all, core)
    down_held, down_leaving = halved(down_kept, down_sent, 0)
    down_arrived = send(down_leaving, flips[0])
    sums_own = after(sums_own, down_leaving, weight_up)

    def to_output(values_own, values_peer):
        stay = jnp.where(same, values_own, values_peer)
        leave = jnp.where(same, values_peer, values_own)
        arrived = send(leave, cross)
        low = stay * first + arrived * (1.0 - first)
        high = arrived * first + stay * (1.0 - first)
        return jnp.concatenate([low, high], axis=0)

    buffers, gain_sums = (), []
    for number in range(2):
        *buffers, gain_sum = residual_chunk(
            where_own,
            number,
            back_parts[number],
            sums_own[number],
            hidden_own[number],
            attn_total[number],
            cotangent,
            there,
            norm_in_mlp,
            norm_out_attn,
            buffers,
        )
        gain_sums.append(gain_sum)
    grad_res, grad_attn = buffers
    gain_in_mlp = gain_sums[0][0] + gain_sums[1][0]
    gain_out_attn = gain_sums[0][1] + gain_sums[1][1]
    gain_out_mlp = gain_out_mlp[0] + gain_out_mlp[1]
    grad_attn_other = send(grad_attn, cross)
    grad_attn_low = jnp.concatenate(
        [
            grad_attn * first + grad_attn_other * (1.0 - first),
            grad_attn_other * first + grad_attn * (1.0 - first),
        ],
        axis=0,
    ).astype(bf16)
    grad_heads = jnp.einsum("td,ed->te", grad_attn_low, w_out_mine, preferred_element_type=f32).astype(bf16)
    weight_out = jnp.concatenate(
        [jnp.einsum("td,te->de", grad_attn_low, values, preferred_element_type=f32) for values in attended], axis=1
    )
    weight_out_sent = send(weight_out, swap)
    down_held, down_leaving = halved(down_held, down_arrived, 1)
    down_arrived = send(down_leaving, flips[1])
    grad_heads = after(grad_heads, down_leaving, weight_out)
    grads = attention_backward(ready, lengths_row, pad_row, grad_heads)
    down_held, down_leaving = halved(down_held, down_arrived, 2)
    down_arrived = send(down_leaving, flips[2])
    grads = jnp.concatenate(after(grads, down_leaving), axis=1)
    other_sent = send(input_other(where_own, grads, weights_mine), cross)
    pair = jnp.einsum("td,te->de", ready[4], grads[:, : 2 * wide], preferred_element_type=f32)
    pair_held, pair_leaving = halved(pair, None, 0)
    pair_arrived = send(pair_leaving, flips[0])
    value = jnp.einsum("td,te->de", ready[4], grads[:, 2 * wide :], preferred_element_type=f32)
    value_held, value_leaving = halved(value, None, 0)
    value_arrived = send(value_leaving, flips[0])
    other_sent = after(other_sent, value_leaving)
    grad_in_own, gain_in_attn = input_own(
        where_own, grads, weights_mine, other_sent, block_in, there, grad_res, norm_in_attn
    )
    grad_in = to_output(grad_in_own, send(grad_in_own, over))
    grad_down = to_core(to_chip(down_held, down_arrived, 3)).T
    gains = jnp.stack([gain_in_attn[0], gain_out_attn, gain_in_mlp, gain_out_mlp], axis=1)
    weight_out_sent, gains, pair_arrived = after((weight_out_sent, gains, pair_arrived), grad_up, grad_down)
    others = lax.psum_scatter(
        jnp.concatenate([weight_out * keep + weight_out_sent, jnp.pad(gains, ((0, 0), (0, LANES - 4)))], axis=1),
        "dp",
        scatter_dimension=0,
        tiled=True,
    )
    held = jnp.concatenate([to_chip(pair_held, pair_arrived, 1), to_chip(value_held, value_arrived, 1)], axis=1)
    for_core = half_of(held, core, small)
    for_other = half_of(held, 1 - core, small)
    straight = send(for_core, flat_pairs(dp_size, lambda d, c, t: (d, 1 - t) if c != t else None))
    diagonal = send(for_other, swap)
    beside = send(for_other, flat_pairs(dp_size, lambda d, c, t: (d ^ 1, t) if c == t else None))
    heads = jnp.where(same, for_core + straight, beside + diagonal)
    gains = others[:, wide:]
    gains = gains + send(gains, over)
    block_out = to_output(jnp.concatenate(blocks[:2], axis=0), jnp.concatenate(blocks[2:], axis=0)).astype(bf16)
    return (
        block_out,
        grad_in,
        gains[:, 0],
        heads[:, :wide],
        heads[:, wide : 2 * wide],
        heads[:, 2 * wide : 3 * wide],
        others[:, :wide].T,
        gains[:, 1],
        gains[:, 2],
        grad_up,
        grad_down,
        gains[:, 3],
    )


def solution(mesh):
    placed = (
        P("dp", None),
        P("dp", None),
        P("dp", None),
        P("dp"),
        P(),
        P(None, "tensor"),
        P(None, "tensor"),
        P(None, "tensor"),
        P("tensor", None),
        P(),
        P(),
        P(None, "tensor"),
        P("tensor", None),
        P(),
    )
    return jax.shard_map(
        partial(body, mesh.shape["dp"]),
        mesh=mesh,
        in_specs=placed,
        out_specs=(
            P("dp", None),
            P("dp", None),
            P("dp"),
            P("dp", "tensor"),
            P("dp", "tensor"),
            P("dp", "tensor"),
            P("tensor", "dp"),
            P("dp"),
            P("dp"),
            P("dp", "tensor"),
            P("tensor", "dp"),
            P("dp"),
        ),
        check_vma=False,
    )
```

time: 1120 us -> 625 us (0.56)
  the two profiles are of different devices: /device:TPU:1 before, /device:TPU:0 now
where the time goes in v2:
time: 625 us; the launch traced here: 614 us
  waiting for transfers between devices  227 us (36%)
  Pallas kernels  193 us (31%)
  starting transfers between devices  61.2 us (10%)
  other arithmetic  60.9 us (10%)
  local copies, waits for them, and re-layouts  29.2 us (5%)
  matrix products  26.6 us (4%)
  between operations  16 us (3%)
    ppermute x39, waiting for transfers between devices, send(): return lax.ppermute(values, ('dp', 'tensor'), pairs)  227 us
    pallas_call x14, Pallas kernels, call(): pl.pallas_call(kernel, grid_spec=pltpu.PrefetchScalarGridSpec(num_scalar_...  115 us
    ppermute x39, starting transfers between devices, send(): return lax.ppermute(values, ('dp', 'tensor'), pairs)  61.1 us
    pallas_call x1, Pallas kernels, attention_backward(): pl.pallas_call(partial(backward_kernel, lengths.shape[1]), grid=(pairs,),...  26 us
    pallas_call x2, Pallas kernels, attention_forward(): pl.pallas_call(partial(forward_kernel, lengths.shape[1], first), grid=(1,...  23.7 us
    add x9, other arithmetic, halved(): sum((lax.dynamic_index_in_dim(part, which, 1, keepdims=False) for part in...  19.4 us
    unnamed x108, local copies, waits for them, and re-layouts  18.6 us
    pallas_call x1, Pallas kernels, attention_ready(): pl.pallas_call(partial(ready_kernel, lengths.shape[1]), grid=(wide // gro...  17.9 us
  transfers between devices with their start and end apart: 41, of which 15 were waited for; matrix products, arithmetic and copies ran while one was open for 15% of the time, Pallas kernels for 25%

profile of v2, /device:TPU:0, one launch (start us, length us, event | category | flops | bytes accessed | tf_op | source)
XLA Modules:
  0.0 613.9 jit_solution(8332204280693960330)
XLA Ops:
  11.0 12.0 %attention_forward.2 = (f32[1024,256]{1,0:T(8,128)}, bf16[1024,1024]{1,0:T(8,128)(2,1)}, f32[1024,128]{1,0:T(8,128)}, f32[1024,128]{1,0:T(8,128)}) custom-call(s32[1,4]{1,0:T(1,128)} %lengths_ref.3, s32[1]{0:T(128)S(6)} %copy.91.pad_ref, f32[32,1]{1,0:T(8,128)} %constant.135.clone.freq_ref, f32[1,1024]{1,0:T(1,128)} %bitcast.133, ...), custom_call_target="tpu_custom_call" | custom-call | flops 5905580032 | bytes 5767168 | tf_op jit(solution)/shard_map/attention_forward/pallas_call | solution.py:277
  23.1 11.7 %attention_forward.3 = f32[1024,256]{1,0:T(8,128)} custom-call(s32[1,4]{1,0:T(1,128)} %lengths_ref.3, s32[1]{0:T(128)S(6)} %copy.91.pad_ref, f32[32,1]{1,0:T(8,128)} %constant.135.clone.freq_ref, f32[1,1024]{1,0:T(1,128)} %bitcast.134, bf16[1024,1024]{1,0:T(8,128)(2,1)} %get-tuple-element.101.refs_0_, f32[1024,128]{1,0:T(8,128)} %get-tuple-element.102.refs_1_, ...), custom_call_target="tpu_custom_call" | custom-call | flops 5905580032 | bytes 5767168 | tf_op jit(solution)/shard_map/attention_forward/pallas_call | solution.py:277
  34.8 5.3 packed.1
  40.0 4.3 collective-permute-start.5
  51.8 2.1 add_convert_fusion.5.high_ref
  54.4 1.8 fusion.16
  56.1 19.6 %collective-permute-start.4 = (f32[512,1024]{1,0:T(8,128)}, f32[512,1024]{1,0:T(8,128)S(1)}, u32[]{:S(2)}, u32[]{:S(2)}) collective-permute-start(f32[512,1024]{1,0:T(8,128)} %fusion.16), channel_id=1, source_target_pairs={{0,2},{1,3},{2,0},{3,1},{4,6},{5,7},{6,4},{7,5},{8,10},{9,11},{10,... | collective-permute-start | bytes 6291464 | tf_op jit(solution)/shard_map/ppermute | solution.py:30
  77.8 2.2 collective-permute-start.9
  81.4 4.5 hidden.2
  87.5 4.5 hidden.3
  92.0 9.0 %mlp_forward.4 = (bf16[1024,1024]{1,0:T(8,128)(2,1)}, bf16[1024,2048]{1,0:T(8,128)(2,1)}, f32[256,2048]{1,0:T(8,128)}, f32[256,1024]{1,0:T(8,128)}) custom-call(f32[256,1024]{1,0:T(8,128)} %get-tuple-element.107.hidden_ref, f32[1,1024]{1,0:T(1,128)} %bitcast.119, bf16[1024,2048]{1,0:T(8,128)(2,1)} %up_ref.15, bf16[2048,1024]{1,0:T(8,128)(2,1)} %down_ref.15), custom_call_target="tpu_custom_call" | custom-call | flops 2147483648 | bytes 9441280 | tf_op jit(solution)/shard_map/mlp_forward/pallas_call | solution.py:532
  101.0 9.0 %mlp_forward.5 = (bf16[1024,1024]{1,0:T(8,128)(2,1)}, bf16[1024,2048]{1,0:T(8,128)(2,1)}, f32[256,2048]{1,0:T(8,128)}, f32[256,1024]{1,0:T(8,128)}) custom-call(f32[256,1024]{1,0:T(8,128)} %get-tuple-element.109.hidden_ref, f32[1,1024]{1,0:T(1,128)} %bitcast.120, bf16[1024,2048]{1,0:T(8,128)(2,1)} %up_ref.15, ...), custom_call_target="tpu_custom_call", output_to_operand_aliasing={{0}: (4, {}), {1}: (5, {})} | custom-call | flops 2147483648 | bytes 15732736 | tf_op jit(solution)/shard_map/mlp_forward/pallas_call | solution.py:532
  110.0 12.3 %collective-permute-done.6.hidden_ref = f32[256,1024]{1,0:T(8,128)S(1)} collective-permute-done((f32[256,1024]{1,0:T(8,128)}, f32[256,1024]{1,0:T(8,128)S(1)}, u32[]{:S(2)}, u32[]{:S(2)}) %collective-permute-start.6) | collective-permute-done | bytes 1048608 | tf_op jit(solution)/shard_map/ppermute | solution.py:30
  123.2 9.0 %mlp_forward.6 = (bf16[1024,1024]{1,0:T(8,128)(2,1)}, bf16[1024,2048]{1,0:T(8,128)(2,1)}, f32[256,2048]{1,0:T(8,128)}, f32[256,1024]{1,0:T(8,128)}) custom-call(f32[256,1024]{1,0:T(8,128)} %copy-done.20, f32[1,1024]{1,0:T(1,128)} %bitcast.121, bf16[1024,2048]{1,0:T(8,128)(2,1)} %up_ref.15, ...), custom_call_target="tpu_custom_call", output_to_operand_aliasing={{0}: (4, {}), {1}: (5, {})} | custom-call | flops 2147483648 | bytes 15732736 | tf_op jit(solution)/shard_map/mlp_forward/pallas_call | solution.py:532
  133.1 2.4 collective-permute-start.8
  137.3 21.0 %collective-permute-done.8.hidden_ref = f32[256,1024]{1,0:T(8,128)S(1)} collective-permute-done((f32[256,1024]{1,0:T(8,128)S(1)}, f32[256,1024]{1,0:T(8,128)S(1)}, u32[]{:S(2)}, u32[]{:S(2)}) %collective-permute-start.8) | collective-permute-done | bytes 1048608 | tf_op jit(solution)/shard_map/ppermute | solution.py:30
  159.2 8.9 %mlp_forward.7 = (bf16[1024,1024]{1,0:T(8,128)(2,1)}, bf16[1024,2048]{1,0:T(8,128)(2,1)}, f32[256,2048]{1,0:T(8,128)}, f32[256,1024]{1,0:T(8,128)}) custom-call(f32[256,1024]{1,0:T(8,128)} %copy-done.21, f32[1,1024]{1,0:T(1,128)} %bitcast.122, bf16[1024,2048]{1,0:T(8,128)(2,1)} %up_ref.15, ...), custom_call_target="tpu_custom_call", output_to_operand_aliasing={{0}: (4, {}), {1}: (5, {})} | custom-call | flops 2147483648 | bytes 15732736 | tf_op jit(solution)/shard_map/mlp_forward/pallas_call | solution.py:532
  168.2 2.8 collective-permute-start.14
  175.6 21.8 %collective-permute-done.7 = f32[256,1024]{1,0:T(8,128)} collective-permute-done((f32[256,1024]{1,0:T(8,128)}, f32[256,1024]{1,0:T(8,128)}, u32[]{:S(2)}, u32[]{:S(2)}) %collective-permute-start.7) | collective-permute-done | bytes 1048608 | tf_op jit(solution)/shard_map/ppermute | solution.py:30
  197.4 1.7 add.271.total_ref
  200.7 11.0 %mlp_backward.4 = (f32[256,1024]{1,0:T(8,128)}, bf16[1024,1024]{1,0:T(8,128)(2,1)}, f32[8,1024]{1,0:T(8,128)}, bf16[1024,2048]{1,0:T(8,128)(2,1)}, f32[256,1024]{1,0:T(8,128)}) custom-call(s32[2]{0:T(128)} %pad_add_fusion.where_ref, f32[256,1024]{1,0:T(8,128)} %get-tuple-element.107.hidden_ref, f32[256,1024]{1,0:T(8,128)} %copy-done.22, ...), custom_call_target="tpu_custom_call" | custom-call | flops 2147483648 | bytes 20975616 | tf_op jit(solution)/shard_map/mlp_backward/pallas_call | solution.py:532
  211.7 8.1 %collective-permute-done.11 = f32[256,1024]{1,0:T(8,128)} collective-permute-done((f32[256,1024]{1,0:T(8,128)}, f32[256,1024]{1,0:T(8,128)}, u32[]{:S(2)}, u32[]{:S(2)}) %collective-permute-start.11) | collective-permute-done | bytes 1048608 | tf_op jit(solution)/shard_map/ppermute | solution.py:30
  222.8 11.0 %mlp_backward.5 = (f32[256,1024]{1,0:T(8,128)}, bf16[1024,1024]{1,0:T(8,128)(2,1)}, f32[8,1024]{1,0:T(8,128)}, bf16[1024,2048]{1,0:T(8,128)(2,1)}, f32[256,1024]{1,0:T(8,128)}) custom-call(s32[2]{0:T(128)} %pad_add_fusion.where_ref, f32[256,1024]{1,0:T(8,128)} %get-tuple-element.109.hidden_ref, ...), custom_call_target="tpu_custom_call", output_to_operand_aliasing={{1}: (9, {}), {3}: (10, {})} | custom-call | flops 2147483648 | bytes 27267072 | tf_op jit(solution)/shard_map/mlp_backward/pallas_call | solution.py:532
  233.8 2.5 broadcast_select_fusion.1
  238.2 2.8 add_convert_fusion.wq_ref.wk_ref.wv_ref.weight_ref
  241.0 17.9 %attention_ready.1 = (bf16[1024,512]{1,0:T(8,128)(2,1)}, bf16[1024,512]{1,0:T(8,128)(2,1)}, bf16[1024,512]{1,0:T(8,128)(2,1)}, f32[2,4,1024]{2,1,0:T(4,128)}, bf...) custom-call(s32[2]{0:T(128)} %pad_add_fusion.where_ref, s32[1,4]{1,0:T(1,128)} %bitcast.137, ...), custom_call_target="tpu_custom_call" | custom-call | flops 7516192768 | bytes 12582912 | tf_op jit(solution)/shard_map/attention_ready/pallas_call | solution.py:307
  260.0 11.0 %mlp_backward.6 = (f32[256,1024]{1,0:T(8,128)}, bf16[1024,1024]{1,0:T(8,128)(2,1)}, f32[8,1024]{1,0:T(8,128)}, bf16[1024,2048]{1,0:T(8,128)(2,1)}, f32[256,1024]{1,0:T(8,128)}) custom-call(s32[2]{0:T(128)} %pad_add_fusion.1.where_ref, f32[256,1024]{1,0:T(8,128)} %copy-done.20, ...), custom_call_target="tpu_custom_call", output_to_operand_aliasing={{1}: (9, {}), {3}: (10, {})} | custom-call | flops 2147483648 | bytes 27267072 | tf_op jit(solution)/shard_map/mlp_backward/pallas_call | solution.py:532
  271.9 11.6 %mlp_backward.7 = (f32[256,1024]{1,0:T(8,128)}, bf16[1024,1024]{1,0:T(8,128)(2,1)}, f32[8,1024]{1,0:T(8,128)}, bf16[1024,2048]{1,0:T(8,128)(2,1)}, f32[256,1024]{1,0:T(8,128)}) custom-call(s32[2]{0:T(128)} %pad_add_fusion.1.where_ref, f32[256,1024]{1,0:T(8,128)} %copy-done.21, ...), custom_call_target="tpu_custom_call", output_to_operand_aliasing={{1}: (9, {}), {3}: (10, {})} | custom-call | flops 2147483648 | bytes 27267072 | tf_op jit(solution)/shard_map/mlp_backward/pallas_call | solution.py:532
  283.6 6.1 fusion.5
  289.7 6.9 %fusion.39 = f32[1024,2048]{1,0:T(8,128)} fusion(bf16[1024,1024]{1,0:T(8,128)(2,1)S(1)} %copy-done.3, bf16[1024,2048]{1,0:T(8,128)(2,1)S(1)} %copy-done.2), kind=kOutput, calls=%fused_computation.120 | convolution fusion | flops 4294967296 | bytes 14680064 | tf_op jit(solution)/shard_map/td,tf->df/dot_general | solution.py:863
  298.7 4.0 fusion.7
  302.8 5.7 dynamic-slice_add_fusion
  309.2 13.7 %collective-permute-done.18.arrived_ref = f32[256,1024]{1,0:T(8,128)S(1)} collective-permute-done((f32[256,1024]{1,0:T(8,128)}, f32[256,1024]{1,0:T(8,128)S(1)}, u32[]{:S(2)}, u32[]{:S(2)}) %collective-permute-start.18) | collective-permute-done | bytes 1048608 | tf_op jit(solution)/shard_map/ppermute | solution.py:30
  322.9 22.2 %collective-permute-done.17.arrived_ref = f32[256,1024]{1,0:T(8,128)} collective-permute-done((f32[256,1024]{1,0:T(8,128)}, f32[256,1024]{1,0:T(8,128)}, u32[]{:S(2)}, u32[]{:S(2)}) %collective-permute-start.17) | collective-permute-done | bytes 1048608 | tf_op jit(solution)/shard_map/ppermute | solution.py:30
  345.0 6.9 %residual.2 = (f32[512,1024]{1,0:T(8,128)}, f32[512,1024]{1,0:T(8,128)}, f32[8,1024]{1,0:T(8,128)}) custom-call(s32[2]{0:T(128)} %pad_add_fusion.where_ref, f32[256,1024]{1,0:T(8,128)} %get-tuple-element.124.part_ref, f32[256,1024]{1,0:T(8,128)} %collective-permute-done.17.arrived_ref, f32[256,1024]{1,0:T(8,128)} %get-tuple-element.107.hidden_ref, ...), custom_call_target="tpu_custom_call" | custom-call | flops 5242880 | bytes 12591104 | tf_op jit(solution)/shard_map/residual/pallas_call | solution.py:532
  351.9 6.6 %residual.3 = (f32[512,1024]{1,0:T(8,128)}, f32[512,1024]{1,0:T(8,128)}, f32[8,1024]{1,0:T(8,128)}) custom-call(s32[2]{0:T(128)} %pad_add_fusion.where_ref, f32[256,1024]{1,0:T(8,128)} %get-tuple-element.130.part_ref, f32[256,1024]{1,0:T(8,128)} %copy-done.36, ...), custom_call_target="tpu_custom_call", output_to_operand_aliasing={{0}: (9, {}), {1}: (10, {})} | custom-call | flops 5242880 | bytes 16785408 | tf_op jit(solution)/shard_map/residual/pallas_call | solution.py:532
  359.9 12.1 %collective-permute-done.21 = f32[4,128,1024]{2,1,0:T(8,128)} collective-permute-done((f32[4,128,1024]{2,1,0:T(8,128)}, f32[4,128,1024]{2,1,0:T(8,128)}, u32[]{:S(2)}, u32[]{:S(2)}) %collective-permute-start.21) | collective-permute-done | bytes 2097184 | tf_op jit(solution)/shard_map/ppermute | solution.py:30
  372.0 2.7 fusion.9
  375.6 2.2 add_convert_fusion.2
  381.8 2.3 convolution_convert_fusion.grad_ref
  384.1 26.0 %attention_backward.1 = (bf16[1024,512]{1,0:T(8,128)(2,1)}, bf16[1024,512]{1,0:T(8,128)(2,1)}, bf16[1024,512]{1,0:T(8,128)(2,1)}) custom-call(s32[1,4]{1,0:T(1,128)} %bitcast.138, s32[1]{0:T(128)} %bitcast.8.pad_ref, f32[1024,128]{1,0:T(8,128)} %get-tuple-element.139.cos_ref, f32[1024,128]{1,0:T(8,128)} %get-tuple-element.140.sin_ref, ...), custom_call_target="tpu_custom_call" | custom-call | flops 21474836480 | bytes 7340032 | tf_op jit(solution)/shard_map/attention_backward/pallas_call | solution.py:340
  411.6 1.9 collective-permute-done.22
  417.4 6.5 %input_other.1 = f32[512,1024]{1,0:T(8,128)} custom-call(s32[2]{0:T(128)} %pad_add_fusion.where_ref, bf16[1024,1536]{1,0:T(8,128)(2,1)} %copy-done.4, bf16[1024,1536]{1,0:T(8,128)(2,1)} %add_convert_fusion.wq_ref.wk_ref.wv_ref.weight_ref), custom_call_target="tpu_custom_call" | custom-call | flops 1610612736 | bytes 6291456 | tf_op jit(solution)/shard_map/input_other/pallas_call | solution.py:532
  426.5 2.3 collective-permute-start.26
  430.0 2.4 fusion.1
  432.4 2.3 constant_dynamic-slice_fusion
  436.2 2.1 collective-permute-start.33
  438.3 17.0 %collective-permute-done.28 = f32[1,128,1024]{2,1,0:T(8,128)S(1)} collective-permute-done((f32[1,128,1024]{2,1,0:T(8,128)S(1)}, f32[1,128,1024]{2,1,0:T(8,128)S(1)}, u32[]{:S(2)}, u32[]{:S(2)}) %collective-permute-start.28) | collective-permute-done | bytes 524320 | tf_op jit(solution)/shard_map/ppermute | solution.py:30
  455.6 10.5 %input_own.1 = (f32[512,1024]{1,0:T(8,128)}, f32[8,1024]{1,0:T(8,128)}) custom-call(s32[2]{0:T(128)} %pad_add_fusion.where_ref, bf16[1024,1536]{1,0:T(8,128)(2,1)} %copy-done.4, bf16[1024,1536]{1,0:T(8,128)(2,1)} %add_convert_fusion.wq_ref.wk_ref.wv_ref.weight_ref, f32[512,1024]{1,0:T(8,128)} %collective-permute-done.23.arrived_ref, ...), custom_call_target="tpu_custom_call" | custom-call | flops 1610612736 | bytes 18874368 | tf_op jit(solution)/shard_map/input_own/pallas_call | solution.py:687
  470.1 35.4 %collective-permute-done.33 = f32[4,128,512]{2,1,0:T(8,128)} collective-permute-done((f32[4,128,512]{2,1,0:T(8,128)S(1)}, f32[4,128,512]{2,1,0:T(8,128)}, u32[]{:S(2)}, u32[]{:S(2)}) %collective-permute-start.33) | collective-permute-done | bytes 1048608 | tf_op jit(solution)/shard_map/ppermute | solution.py:30
  505.5 1.9 fusion.19
  507.4 2.3 collective-permute-start.34
  510.5 4.2 dynamic-slice_add_fusion.1
  514.8 2.1 multiply_add_fusion
  516.8 1.8 select_maximum_fusion
  518.6 3.2 copy.60
  521.9 2.1 broadcast_select_fusion.2
  527.7 22.2 %collective-permute-done.31 = f32[2,128,1024]{2,1,0:T(8,128)} collective-permute-done((f32[2,128,1024]{2,1,0:T(8,128)}, f32[2,128,1024]{2,1,0:T(8,128)}, u32[]{:S(2)}, u32[]{:S(2)}) %collective-permute-start.31) | collective-permute-done | bytes 1048608 | tf_op jit(solution)/shard_map/ppermute | solution.py:30
  551.1 2.4 add_convert_fusion.4
  556.0 28.3 %collective-permute-done.32 = f32[1,128,1024]{2,1,0:T(8,128)S(1)} collective-permute-done((f32[1,128,1024]{2,1,0:T(8,128)S(1)}, f32[1,128,1024]{2,1,0:T(8,128)S(1)}, u32[]{:S(2)}, u32[]{:S(2)}) %collective-permute-start.32) | collective-permute-done | bytes 524320 | tf_op jit(solution)/shard_map/ppermute | solution.py:30
  585.6 1.8 collective-permute-start.37
  590.5 2.5 pad_maximum_fusion.1
  593.0 7.3 %collective-permute-done.36 = f32[64,1536]{1,0:T(8,128)S(1)} collective-permute-done((f32[64,1536]{1,0:T(8,128)S(1)}, f32[64,1536]{1,0:T(8,128)S(1)}, u32[]{:S(2)}, u32[]{:S(2)}) %collective-permute-start.36) | collective-permute-done | bytes 393248 | tf_op jit(solution)/shard_map/ppermute | solution.py:30
  603.7 2.7 collective-permute-done.30
  (219 shorter events, 73.8 us)
Async XLA Ops:
  7.2 503.3 %reduce-scatter.5.cloned.1.call-start = ((), (), s32[]{:S(2)}) async-start(), calls=%async_computation.2 | async-start | bytes 8912896 | tf_op jit(solution)/shard_map/reduce_scatter | solution.py:864
  8.4 14.7 %collective-permute-start.1 = (f32[256,1024]{1,0:T(8,128)S(1)}, f32[256,1024]{1,0:T(8,128)S(1)}, u32[]{:S(2)}, u32[]{:S(2)}) collective-permute-start(f32[256,1024]{1,0:T(8,128)S(1)} %dynamic-slice_convert_fusion.1), channel_id=1, source_target_pairs={{1,2},{2,1},{5,6},{6,5},{9,10},{10,9},{13,14},{14,13},{17,18},{18,... | collective-permute-start | bytes 3145736 | tf_op jit(solution)/shard_map/ppermute | solution.py:30
  34.8 9.5 %copy-start.47 = (f32[1024,256]{1,0:T(8,128)S(1)}, f32[1024,256]{1,0:T(8,128)}, u32[]{:S(2)}) copy-start(f32[1024,256]{1,0:T(8,128)} %get-tuple-element.97) | copy-start | bytes 3145732
  40.0 40.1 %collective-permute-start.5 = (f32[1536,1024]{1,0:T(8,128)}, f32[1536,1024]{1,0:T(8,128)}, u32[]{:S(2)}, u32[]{:S(2)}) collective-permute-start(f32[1536,1024]{1,0:T(8,128)} %packed.1), channel_id=1, source_target_pairs={{0,2},{1,3},{2,0},{3,1},{4,6},{5,7},{6,4},{7,5},{8,10},{9,11},{10,... | collective-permute-start | bytes 18874376 | tf_op jit(solution)/shard_map/ppermute | solution.py:30
  44.3 4.0 collective-permute-start
  45.9 4.1 collective-permute-start.3
  46.7 5.2 collective-permute-start.2
  50.0 4.4 copy-start.16
  56.1 23.9 %collective-permute-start.4 = (f32[512,1024]{1,0:T(8,128)}, f32[512,1024]{1,0:T(8,128)S(1)}, u32[]{:S(2)}, u32[]{:S(2)}) collective-permute-start(f32[512,1024]{1,0:T(8,128)} %fusion.16), channel_id=1, source_target_pairs={{0,2},{1,3},{2,0},{3,1},{4,6},{5,7},{6,4},{7,5},{8,10},{9,11},{10,... | collective-permute-start | bytes 6291464 | tf_op jit(solution)/shard_map/ppermute | solution.py:30
  77.8 54.4 %collective-permute-start.9 = (f32[256,1536]{1,0:T(8,128)S(1)}, f32[256,1536]{1,0:T(8,128)}, u32[]{:S(2)}, u32[]{:S(2)}) collective-permute-start(f32[256,1536]{1,0:T(8,128)S(1)} %dynamic-slice_convert_fusion), channel_id=1, source_target_pairs={{1,2},{2,1},{5,6},{6,5},{9,10},{10,9},{13,14},{14,13},{17,18},{18,... | collective-permute-start | bytes 4718600 | tf_op jit(solution)/shard_map/ppermute | solution.py:30
  85.9 36.3 %collective-permute-start.6 = (f32[256,1024]{1,0:T(8,128)}, f32[256,1024]{1,0:T(8,128)S(1)}, u32[]{:S(2)}, u32[]{:S(2)}) collective-permute-start(f32[256,1024]{1,0:T(8,128)} %get-tuple-element.107.hidden_ref), channel_id=1, source_target_pairs={{0,1},{1,0},{2,3},{3,2},{4,5},{5,4},{6,7},{7,6},{8,9},{9,8},{10,11... | collective-permute-start | bytes 3145736 | tf_op jit(solution)/shard_map/ppermute | solution.py:30
  123.2 9.8 %copy-start.9 = (f32[256,1024]{1,0:T(8,128)S(1)}, f32[256,1024]{1,0:T(8,128)}, u32[]{:S(2)}) copy-start(f32[256,1024]{1,0:T(8,128)} %get-tuple-element.109.hidden_ref) | copy-start | bytes 3145732
  132.3 3.1 collective-permute-start.10
  133.1 25.2 %collective-permute-start.8 = (f32[256,1024]{1,0:T(8,128)S(1)}, f32[256,1024]{1,0:T(8,128)S(1)}, u32[]{:S(2)}, u32[]{:S(2)}) collective-permute-start(f32[256,1024]{1,0:T(8,128)S(1)} %copy-done.9), channel_id=1, source_target_pairs={{0,1},{1,0},{2,3},{3,2},{4,5},{5,4},{6,7},{7,6},{8,9},{9,8},{10,11... | collective-permute-start | bytes 3145736 | tf_op jit(solution)/shard_map/ppermute | solution.py:30
  168.2 65.6 %collective-permute-start.14 = (f32[512,1536]{1,0:T(8,128)S(1)}, f32[512,1536]{1,0:T(8,128)}, u32[]{:S(2)}, u32[]{:S(2)}) collective-permute-start(f32[512,1536]{1,0:T(8,128)S(1)} %pad_maximum_fusion.2), channel_id=1, source_target_pairs={{1,9},{2,10},{5,13},{6,14},{9,1},{10,2},{13,5},{14,6},{17,25},{18,... | collective-permute-start | bytes 9437192 | tf_op jit(solution)/shard_map/ppermute | solution.py:30
  171.0 26.4 %collective-permute-start.7 = (f32[256,1024]{1,0:T(8,128)}, f32[256,1024]{1,0:T(8,128)}, u32[]{:S(2)}, u32[]{:S(2)}) collective-permute-start(f32[256,1024]{1,0:T(8,128)} %get-tuple-element.114), channel_id=1, source_target_pairs={{0,1},{1,0},{2,3},{3,2},{4,5},{5,4},{6,7},{7,6},{8,9},{9,8},{10,11... | collective-permute-start | bytes 3145736 | tf_op jit(solution)/shard_map/ppermute | solution.py:30
  172.5 47.4 %collective-permute-start.11 = (f32[256,1024]{1,0:T(8,128)}, f32[256,1024]{1,0:T(8,128)}, u32[]{:S(2)}, u32[]{:S(2)}) collective-permute-start(f32[256,1024]{1,0:T(8,128)} %get-tuple-element.123), channel_id=1, source_target_pairs={{0,1},{1,0},{2,3},{3,2},{4,5},{5,4},{6,7},{7,6},{8,9},{9,8},{10,11... | collective-permute-start | bytes 3145736 | tf_op jit(solution)/shard_map/ppermute | solution.py:30
  173.7 1.1 collective-permute-start.13
  174.9 36.8 %copy-start.49 = (s32[1,5]{1,0:T(1,128)}, s32[1,5]{1,0:T(1,128)S(1)}, u32[]{:S(2)}) copy-start(s32[1,5]{1,0:T(1,128)S(1)} %fusion.33) | copy-start | bytes 64
  199.1 59.8 %collective-permute-start.12 = (f32[256,1024]{1,0:T(8,128)S(1)}, f32[256,1024]{1,0:T(8,128)S(1)}, u32[]{:S(2)}, u32[]{:S(2)}) collective-permute-start(f32[256,1024]{1,0:T(8,128)S(1)} %add.271.total_ref), channel_id=1, source_target_pairs={{0,1},{1,0},{2,3},{3,2},{4,5},{5,4},{6,7},{7,6},{8,9},{9,8},{10,11... | collective-permute-start | bytes 3145736 | tf_op jit(solution)/shard_map/ppermute | solution.py:30
  200.7 19.2 %copy-start.34 = (f32[256,1024]{1,0:T(8,128)S(1)}, f32[256,1024]{1,0:T(8,128)}, u32[]{:S(2)}) copy-start(f32[256,1024]{1,0:T(8,128)} %get-tuple-element.117) | copy-start | bytes 3145732
  221.3 49.6 %collective-permute-start.15 = (f32[256,1024]{1,0:T(8,128)S(1)}, f32[256,1024]{1,0:T(8,128)S(1)}, u32[]{:S(2)}, u32[]{:S(2)}) collective-permute-start(f32[256,1024]{1,0:T(8,128)S(1)} %add.274.total_ref), channel_id=1, source_target_pairs={{0,1},{1,0},{2,3},{3,2},{4,5},{5,4},{6,7},{7,6},{8,9},{9,8},{10,11... | collective-permute-start | bytes 3145736 | tf_op jit(solution)/shard_map/ppermute | solution.py:30
  271.9 11.7 %copy-start = (bf16[1024,2048]{1,0:T(8,128)(2,1)S(1)}, bf16[1024,2048]{1,0:T(8,128)(2,1)}, u32[]{:S(2)}) copy-start(bf16[1024,2048]{1,0:T(8,128)(2,1)} %get-tuple-element.154) | copy-start | bytes 12582916
  283.6 6.1 copy-start.2
  283.6 6.1 copy-start.3
  289.7 13.1 %collective-permute-start.19 = (f32[1024,1024]{1,0:T(8,128)}, f32[1024,1024]{1,0:T(8,128)}, u32[]{:S(2)}, u32[]{:S(2)}) collective-permute-start(f32[1024,1024]{1,0:T(8,128)} %fusion.5), channel_id=1, source_target_pairs={{0,2},{1,3},{2,0},{3,1},{4,6},{5,7},{6,4},{7,5},{8,10},{9,11},{10,... | collective-permute-start | bytes 12582920 | tf_op jit(solution)/shard_map/ppermute | solution.py:30
  296.6 304.6 %reduce-scatter.7.cloned.1.call-start = ((), (), s32[]{:S(2)}) async-start(), calls=%async_computation.3 | async-start | bytes 2785280
  296.6 26.2 %collective-permute-start.18 = (f32[256,1024]{1,0:T(8,128)}, f32[256,1024]{1,0:T(8,128)S(1)}, u32[]{:S(2)}, u32[]{:S(2)}) collective-permute-start(f32[256,1024]{1,0:T(8,128)} %get-tuple-element.152), channel_id=1, source_target_pairs={{0,1},{1,0},{2,3},{3,2},{4,5},{5,4},{6,7},{7,6},{8,9},{9,8},{10,11... | collective-permute-start | bytes 3145736 | tf_op jit(solution)/shard_map/ppermute | solution.py:30
  297.6 47.5 %collective-permute-start.17 = (f32[256,1024]{1,0:T(8,128)}, f32[256,1024]{1,0:T(8,128)}, u32[]{:S(2)}, u32[]{:S(2)}) collective-permute-start(f32[256,1024]{1,0:T(8,128)} %get-tuple-element.146), channel_id=1, source_target_pairs={{0,1},{1,0},{2,3},{3,2},{4,5},{5,4},{6,7},{7,6},{8,9},{9,8},{10,11... | collective-permute-start | bytes 3145736 | tf_op jit(solution)/shard_map/ppermute | solution.py:30
  308.5 63.5 %collective-permute-start.21 = (f32[4,128,1024]{2,1,0:T(8,128)}, f32[4,128,1024]{2,1,0:T(8,128)}, u32[]{:S(2)}, u32[]{:S(2)}) collective-permute-start(f32[4,128,1024]{2,1,0:T(8,128)} %get-tuple-element.219), channel_id=1, source_target_pairs={{0,4},{1,5},{2,6},{3,7},{4,0},{5,1},{6,2},{7,3},{8,12},{9,13},{10,... | collective-permute-start | bytes 6291464 | tf_op jit(solution)/shard_map/ppermute | solution.py:30
  322.9 29.0 %copy-start.36 = (f32[256,1024]{1,0:T(8,128)}, f32[256,1024]{1,0:T(8,128)S(1)}, u32[]{:S(2)}) copy-start(f32[256,1024]{1,0:T(8,128)S(1)} %collective-permute-done.18.arrived_ref) | copy-start | bytes 3145732
  351.9 6.7 %copy-start.43 = (f32[256,1024]{1,0:T(8,128)S(1)}, f32[256,1024]{1,0:T(8,128)}, u32[]{:S(2)}) copy-start(f32[256,1024]{1,0:T(8,128)} %get-tuple-element.116) | copy-start | bytes 3145732
  358.5 17.1 %collective-permute-start.20 = (f32[512,1024]{1,0:T(8,128)}, f32[512,1024]{1,0:T(8,128)}, u32[]{:S(2)}, u32[]{:S(2)}) collective-permute-start(f32[512,1024]{1,0:T(8,128)} %get-tuple-element.163), channel_id=1, source_target_pairs={{0,2},{1,3},{2,0},{3,1},{4,6},{5,7},{6,4},{7,5},{8,10},{9,11},{10,... | collective-permute-start | bytes 6291464 | tf_op jit(solution)/shard_map/ppermute | solution.py:30
  359.9 15.7 %copy-start.11 = (f32[512,1024]{1,0:T(8,128)S(1)}, f32[512,1024]{1,0:T(8,128)}, u32[]{:S(2)}) copy-start(f32[512,1024]{1,0:T(8,128)} %get-tuple-element.163) | copy-start | bytes 6291460
  374.6 3.1 copy-start.17
  374.7 38.9 %collective-permute-start.22 = (f32[2,128,1024]{2,1,0:T(8,128)}, f32[2,128,1024]{2,1,0:T(8,128)S(1)}, u32[]{:S(2)}, u32[]{:S(2)}) collective-permute-start(f32[2,128,1024]{2,1,0:T(8,128)} %fusion.9), channel_id=1, source_target_pairs={{0,8},{1,9},{2,10},{3,11},{4,12},{5,13},{6,14},{7,15},{8,0},{9,1},... | collective-permute-start | bytes 3145736 | tf_op jit(solution)/shard_map/ppermute | solution.py:30
  384.1 26.0 %copy-start.10 = (f32[4,1,128,1024]{3,2,1,0:T(8,128)S(1)}, f32[4,1,128,1024]{3,2,1,0:T(8,128)}, u32[]{:S(2)}) copy-start(f32[4,1,128,1024]{3,2,1,0:T(8,128)} %get-tuple-element.218) | copy-start | bytes 6291460
  410.1 4.4 copy-start.29
  424.0 31.6 %collective-permute-start.23 = (f32[512,1024]{1,0:T(8,128)}, f32[512,1024]{1,0:T(8,128)}, u32[]{:S(2)}, u32[]{:S(2)}) collective-permute-start(f32[512,1024]{1,0:T(8,128)} %input_other.1), channel_id=1, source_target_pairs={{0,2},{1,3},{2,0},{3,1},{4,6},{5,7},{6,4},{7,5},{8,10},{9,11},{10,... | collective-permute-start | bytes 6291464 | tf_op jit(solution)/shard_map/ppermute | solution.py:30
  426.2 3.8 copy-start.31
  426.2 3.8 copy-start.33
  426.5 39.6 %copy-start.7 = (f32[512,1024]{1,0:T(8,128)}, f32[512,1024]{1,0:T(8,128)S(1)}, u32[]{:S(2)}) copy-start(f32[512,1024]{1,0:T(8,128)S(1)} %constant_dynamic-update-slice_fusion.5) | copy-start | bytes 6291460
  426.5 84.0 %collective-permute-start.26 = (f32[1024,512]{0,1:T(8,128)}, f32[1024,512]{0,1:T(8,128)}, u32[]{:S(2)}, u32[]{:S(2)}) collective-permute-start(f32[1024,512]{0,1:T(8,128)} %pad_maximum_fusion.5), channel_id=1, source_target_pairs={{1,2},{2,1},{5,6},{6,5},{9,10},{10,9},{13,14},{14,13},{17,18},{18,... | collective-permute-start | bytes 6291464 | tf_op jit(solution)/shard_map/ppermute | solution.py:30
  428.8 26.6 %collective-permute-start.28 = (f32[1,128,1024]{2,1,0:T(8,128)S(1)}, f32[1,128,1024]{2,1,0:T(8,128)S(1)}, u32[]{:S(2)}, u32[]{:S(2)}) collective-permute-start(f32[1,128,1024]{2,1,0:T(8,128)S(1)} %bitcast_add_fusion.5), channel_id=1, source_target_pairs={{0,16},{1,17},{2,18},{3,19},{4,20},{5,21},{6,22},{7,23},{8,24},{9,... | collective-permute-start | bytes 1572872 | tf_op jit(solution)/shard_map/ppermute | solution.py:30
  434.7 75.8 %collective-permute-start.27 = (f32[4,128,1024]{2,1,0:T(8,128)}, f32[4,128,1024]{2,1,0:T(8,128)}, u32[]{:S(2)}, u32[]{:S(2)}) collective-permute-start(f32[4,128,1024]{2,1,0:T(8,128)} %get-tuple-element.229), channel_id=1, source_target_pairs={{0,4},{1,5},{2,6},{3,7},{4,0},{5,1},{6,2},{7,3},{8,12},{9,13},{10,... | collective-permute-start | bytes 6291464 | tf_op jit(solution)/shard_map/ppermute | solution.py:30
  436.0 19.3 %copy-start.39 = (f32[2,128,1024]{2,1,0:T(8,128)S(1)}, f32[2,128,1024]{2,1,0:T(8,128)}, u32[]{:S(2)}) copy-start(f32[2,128,1024]{2,1,0:T(8,128)} %copy-done.38) | copy-start | bytes 3145732
  436.2 69.2 %collective-permute-start.33 = (f32[4,128,512]{2,1,0:T(8,128)S(1)}, f32[4,128,512]{2,1,0:T(8,128)}, u32[]{:S(2)}, u32[]{:S(2)}) collective-permute-start(f32[4,128,512]{2,1,0:T(8,128)S(1)} %get-tuple-element.235), channel_id=1, source_target_pairs={{0,4},{1,5},{2,6},{3,7},{4,0},{5,1},{6,2},{7,3},{8,12},{9,13},{10,... | collective-permute-start | bytes 3145736 | tf_op jit(solution)/shard_map/ppermute | solution.py:30
  455.5 13.2 %collective-permute-start.29 = (f32[64,1024]{1,0:T(8,128)S(1)}, f32[64,1024]{1,0:T(8,128)S(1)}, u32[]{:S(2)}, u32[]{:S(2)}) collective-permute-start(f32[64,1024]{1,0:T(8,128)S(1)} %dynamic-slice_bitcast_fusion.2), channel_id=1, source_target_pairs={{0,2},{1,3},{2,0},{3,1},{4,6},{5,7},{6,4},{7,5},{8,10},{9,11},{10,... | collective-permute-start | bytes 786440 | tf_op jit(solution)/shard_map/ppermute | solution.py:30
  466.1 55.8 %collective-permute-start.24 = (f32[512,1024]{1,0:T(8,128)}, f32[512,1024]{1,0:T(8,128)}, u32[]{:S(2)}, u32[]{:S(2)}) collective-permute-start(f32[512,1024]{1,0:T(8,128)} %get-tuple-element.173), channel_id=1, source_target_pairs={{0,1},{1,0},{2,3},{3,2},{4,5},{5,4},{6,7},{7,6},{8,9},{9,8},{10,11... | collective-permute-start | bytes 6291464 | tf_op jit(solution)/shard_map/ppermute | solution.py:30
  468.7 82.4 %collective-permute-start.16 = (f32[512,1024]{1,0:T(8,128)}, f32[512,1024]{1,0:T(8,128)}, u32[]{:S(2)}, u32[]{:S(2)}) collective-permute-start(f32[512,1024]{1,0:T(8,128)} %broadcast_select_fusion.4), channel_id=1, source_target_pairs={{0,2},{1,3},{2,0},{3,1},{4,6},{5,7},{6,4},{7,5},{8,10},{9,11},{10,... | collective-permute-start | bytes 6291464 | tf_op jit(solution)/shard_map/ppermute | solution.py:30
  507.4 18.0 %collective-permute-start.34 = (f32[2,128,512]{2,1,0:T(8,128)}, f32[2,128,512]{2,1,0:T(8,128)}, u32[]{:S(2)}, u32[]{:S(2)}) collective-permute-start(f32[2,128,512]{2,1,0:T(8,128)} %fusion.19), channel_id=1, source_target_pairs={{0,8},{1,9},{2,10},{3,11},{4,12},{5,13},{6,14},{7,15},{8,0},{9,1},... | collective-permute-start | bytes 1572872 | tf_op jit(solution)/shard_map/ppermute | solution.py:30
  510.5 4.2 copy-start.25
  510.5 4.2 copy-start.27
  514.7 35.1 %collective-permute-start.31 = (f32[2,128,1024]{2,1,0:T(8,128)}, f32[2,128,1024]{2,1,0:T(8,128)}, u32[]{:S(2)}, u32[]{:S(2)}) collective-permute-start(f32[2,128,1024]{2,1,0:T(8,128)} %get-tuple-element.227), channel_id=1, source_target_pairs={{0,8},{1,9},{2,10},{3,11},{4,12},{5,13},{6,14},{7,15},{8,0},{9,1},... | collective-permute-start | bytes 3145736 | tf_op jit(solution)/shard_map/ppermute | solution.py:30
  521.9 28.0 %copy-start.28 = (f32[2,1,128,1024]{3,2,1,0:T(8,128)S(1)}, f32[2,1,128,1024]{3,2,1,0:T(8,128)}, u32[]{:S(2)}) copy-start(f32[2,1,128,1024]{3,2,1,0:T(8,128)} %get-tuple-element.226) | copy-start | bytes 3145732
  524.0 27.1 %copy-start.8 = (f32[512,1024]{1,0:T(8,128)S(1)}, f32[512,1024]{1,0:T(8,128)}, u32[]{:S(2)}) copy-start(f32[512,1024]{1,0:T(8,128)} %copy-done.7) | copy-start | bytes 6291460
  524.0 65.4 %collective-permute-start.25 = (f32[512,1024]{1,0:T(8,128)S(1)}, f32[512,1024]{1,0:T(8,128)S(1)}, u32[]{:S(2)}, u32[]{:S(2)}) collective-permute-start(f32[512,1024]{1,0:T(8,128)S(1)} %broadcast_select_fusion.2), channel_id=1, source_target_pairs={{0,2},{1,3},{2,0},{3,1},{4,6},{5,7},{6,4},{7,5},{8,10},{9,11},{10,... | collective-permute-start | bytes 6291464 | tf_op jit(solution)/shard_map/ppermute | solution.py:30
  526.4 28.6 %collective-permute-start.35 = (f32[1,128,512]{2,1,0:T(8,128)S(1)}, f32[1,128,512]{2,1,0:T(8,128)S(1)}, u32[]{:S(2)}, u32[]{:S(2)}) collective-permute-start(f32[1,128,512]{2,1,0:T(8,128)S(1)} %bitcast_add_fusion.6), channel_id=1, source_target_pairs={{0,16},{1,17},{2,18},{3,19},{4,20},{5,21},{6,22},{7,23},{8,24},{9,... | collective-permute-start | bytes 786440 | tf_op jit(solution)/shard_map/ppermute | solution.py:30
  551.0 33.4 %collective-permute-start.32 = (f32[1,128,1024]{2,1,0:T(8,128)S(1)}, f32[1,128,1024]{2,1,0:T(8,128)S(1)}, u32[]{:S(2)}, u32[]{:S(2)}) collective-permute-start(f32[1,128,1024]{2,1,0:T(8,128)S(1)} %bitcast_add_fusion.2), channel_id=1, source_target_pairs={{0,16},{1,17},{2,18},{3,19},{4,20},{5,21},{6,22},{7,23},{8,24},{9,... | collective-permute-start | bytes 1572872 | tf_op jit(solution)/shard_map/ppermute | solution.py:30
  556.0 33.4 %copy-start.12 = (f32[512,1024]{1,0:T(8,128)S(1)}, f32[512,1024]{1,0:T(8,128)}, u32[]{:S(2)}) copy-start(f32[512,1024]{1,0:T(8,128)} %get-tuple-element.173) | copy-start | bytes 6291460
  585.6 14.7 %collective-permute-start.37 = (f32[64,1536]{1,0:T(8,128)S(1)}, f32[64,1536]{1,0:T(8,128)S(1)}, u32[]{:S(2)}, u32[]{:S(2)}) collective-permute-start(f32[64,1536]{1,0:T(8,128)S(1)} %get-tuple-element.239), channel_id=1, source_target_pairs={{0,2},{3,1},{4,6},{7,5},{8,10},{11,9},{12,14},{15,13},{16,18},{19,... | collective-permute-start | bytes 1179656 | tf_op jit(solution)/shard_map/ppermute | solution.py:30
  587.4 12.9 %collective-permute-start.38 = (f32[64,1536]{1,0:T(8,128)S(1)}, f32[64,1536]{1,0:T(8,128)S(1)}, u32[]{:S(2)}, u32[]{:S(2)}) collective-permute-start(f32[64,1536]{1,0:T(8,128)S(1)} %get-tuple-element.239), channel_id=1, source_target_pairs={{1,2},{2,1},{5,6},{6,5},{9,10},{10,9},{13,14},{14,13},{17,18},{18,... | collective-permute-start | bytes 1179656 | tf_op jit(solution)/shard_map/ppermute | solution.py:30
  588.1 12.2 %collective-permute-start.36 = (f32[64,1536]{1,0:T(8,128)S(1)}, f32[64,1536]{1,0:T(8,128)S(1)}, u32[]{:S(2)}, u32[]{:S(2)}) collective-permute-start(f32[64,1536]{1,0:T(8,128)S(1)} %get-tuple-element.238), channel_id=1, source_target_pairs={{1,0},{2,3},{5,4},{6,7},{9,8},{10,11},{13,12},{14,15},{17,16},{18,... | collective-permute-start | bytes 1179656 | tf_op jit(solution)/shard_map/ppermute | solution.py:30
  602.0 4.3 collective-permute-start.30
  (27 other events, 44.6 us)
Sparse Core Ops, SparseCore 0:
  296.7 117.7 reduce-scatter.4
  522.0 73.5 reduce-scatter.6

commit v3 on v2

--- a/solution.py
+++ b/solution.py
@@ -37,6 +37,7 @@
 BLOCK = 256
 LANES = 128
 VMEM_LIMIT = 56 * 1024 * 1024
+SMALL = pl.CostEstimate(flops=1, bytes_accessed=1, transcendentals=0)
 
 
 def doc_ends(lengths_ref, docs):
@@ -285,11 +286,7 @@
         out_shape=outs,
         scratch_shapes=[pltpu.VMEM((row_len, group), jnp.bfloat16)] * 3,
         compiler_params=pltpu.CompilerParams(vmem_limit_bytes=VMEM_LIMIT),
-        cost_estimate=pl.CostEstimate(
-            flops=6 * row_len * width * group + 16 * row_len * row_len * group,
-            bytes_accessed=4 * row_len * width + 6 * width * group,
-            transcendentals=row_len * row_len * group // HEAD_DIM,
-        ),
+        cost_estimate=SMALL,
         name="attention_forward",
     )(lengths, pad_count, jnp.asarray(frequencies()), gain[None], *sources, w_query, w_key, w_value)
 
@@ -321,11 +318,7 @@
             jax.ShapeDtypeStruct((row_len, width), jnp.bfloat16), table, table,
         ],
         compiler_params=pltpu.CompilerParams(vmem_limit_bytes=VMEM_LIMIT),
-        cost_estimate=pl.CostEstimate(
-            flops=6 * row_len * width * wide + 8 * row_len * row_len * wide,
-            bytes_accessed=6 * row_len * width + 6 * width * wide + 6 * row_len * wide,
-            transcendentals=row_len * row_len * wide // HEAD_DIM,
-        ),
+        cost_estimate=SMALL,
         name="attention_ready",
     )(where, lengths, pad_count, jnp.asarray(frequencies()), block_in, there, gain[None], weights, weights, weights)
 
@@ -348,18 +341,14 @@
         out_shape=[rows, rows, rows],
         scratch_shapes=[pltpu.VMEM((row_len, LANES), jnp.float32), pltpu.VMEM((row_len, LANES), jnp.float32)],
         compiler_params=pltpu.CompilerParams(vmem_limit_bytes=VMEM_LIMIT),
-        cost_estimate=pl.CostEstimate(
-            flops=40 * row_len * row_len * wide,
-            bytes_accessed=14 * row_len * wide,
-            transcendentals=row_len * row_len * wide // HEAD_DIM,
-        ),
+        cost_estimate=SMALL,
         name="attention_backward",
     )(lengths, pad_count, cosine, sine, query, key, value, logs, grad_heads)
 
 
 FF_STEPS = 4
 PARTS = 2
-TILE = 64
+TILE = 256
 
 
 def chosen_rows(flag, here_ref, there_ref):
@@ -540,7 +529,7 @@
         out_shape=[shape for shape, _ in outs],
         input_output_aliases=aliases,
         compiler_params=pltpu.CompilerParams(vmem_limit_bytes=VMEM_LIMIT),
-        cost_estimate=pl.CostEstimate(flops=flops, bytes_accessed=moved, transcendentals=0),
+        cost_estimate=SMALL,
         name=name,
     )(*(() if where is None else (where,)), *arrays)
 
@@ -662,6 +651,89 @@
     )[0]
 
 
+def outer_kernel(where_ref, left_ref, right_ref, out_ref, turned_ref):
+    @pl.when(pl.program_id(0) == 0)
+    def _():
+        turned_ref[...] = left_ref[...].T
+
+    out_ref[...] = jnp.dot(turned_ref[...], right_ref[...], preferred_element_type=jnp.float32)
+
+
+def outer(where, left, right, pick, columns):
+    tokens, width = left.shape
+    size = min(512, columns)
+    steps = columns // size
+    return pl.pallas_call(
+        outer_kernel,
+        grid_spec=pltpu.PrefetchScalarGridSpec(
+            num_scalar_prefetch=1,
+            grid=(steps,),
+            in_specs=[
+                fixed_spec((tokens, width)),
+                pl.BlockSpec((tokens, size), lambda step, where: (0, pick(where) * steps + step)),
+            ],
+            out_specs=pl.BlockSpec((width, size), lambda step, where: (0, step)),
+            scratch_shapes=[pltpu.VMEM((width, tokens), left.dtype)],
+        ),
+        out_shape=jax.ShapeDtypeStruct((width, columns), jnp.float32),
+        compiler_params=pltpu.CompilerParams(vmem_limit_bytes=VMEM_LIMIT),
+        cost_estimate=SMALL,
+        name="outer",
+    )(where, left, right)
+
+
+def halves_kernel(count, sources, where_ref, *refs):
+    stays, leaves = refs[:count], refs[count : 2 * count]
+    outs = refs[-count - 1 : -1]
+    leaving_ref = refs[-1]
+    start = 0
+    for stay_ref, leave_ref, out_ref, source in zip(stays, leaves, outs, sources):
+        columns = stay_ref.shape[-1]
+        stay, leave = stay_ref[0], leave_ref[0]
+        if source is not None:
+            number, first = source
+            stay += refs[2 * count + 2 * number][0, :, first : first + columns]
+            leave += refs[2 * count + 2 * number + 1][0, :, first : first + columns]
+        out_ref[0] = stay
+        leaving_ref[0, :, start : start + columns] = leave
+        start += columns
+
+
+def halves(where, step, held, arrived, sources):
+    blocks, rows = held[0].shape[0] // 2, held[0].shape[1]
+    widths = [part.shape[2] for part in held]
+
+    def spec(width, stays):
+        def place(index, where):
+            low, bit = where[2 + 2 * step], where[3 + 2 * step]
+            bit = bit if stays else 1 - bit
+            high = lax.shift_right_logical(index, low)
+            return (lax.shift_left(2 * high + bit, low) + index - lax.shift_left(high, low), 0, 0)
+
+        return pl.BlockSpec((1, rows, width), place)
+
+    arrays = list(held) * 2
+    specs = [spec(width, stays) for stays in (True, False) for width in widths]
+    for array in arrived:
+        arrays += [array] * 2
+        specs += [spec(array.shape[2], stays) for stays in (True, False)]
+    outs = [*widths, sum(widths)]
+    *staying, leaving = pl.pallas_call(
+        partial(halves_kernel, len(held), sources),
+        grid_spec=pltpu.PrefetchScalarGridSpec(
+            num_scalar_prefetch=1,
+            grid=(blocks,),
+            in_specs=specs,
+            out_specs=[pl.BlockSpec((1, rows, width), lambda index, where: (index, 0, 0)) for width in outs],
+        ),
+        out_shape=[jax.ShapeDtypeStruct((blocks, rows, width), jnp.float32) for width in outs],
+        compiler_params=pltpu.CompilerParams(vmem_limit_bytes=VMEM_LIMIT),
+        cost_estimate=SMALL,
+        name="halves",
+    )(where, *arrays)
+    return staying, leaving
+
+
 def input_specs(grads, weights, other):
     row_len, wide = grads.shape[0], grads.shape[1] // 3
     width = weights.shape[0]
@@ -695,7 +767,7 @@
         ),
         out_shape=[jax.ShapeDtypeStruct(shape, jnp.float32), jax.ShapeDtypeStruct((8, shape[1]), jnp.float32)],
         compiler_params=pltpu.CompilerParams(vmem_limit_bytes=VMEM_LIMIT),
-        cost_estimate=pl.CostEstimate(flops=2 * shape[0] * weights.size, bytes_accessed=moved, transcendentals=0),
+        cost_estimate=SMALL,
         name="input_own",
     )(where, grads, weights, arrived, block_in, there, res, gain[None])
 
@@ -749,29 +821,37 @@
     hidden = w_up.shape[1]
 
     shares = min(2, levels)
-    near = [flat_pairs(dp_size, lambda d, c, t: (d ^ (2 << level), t) if c != t else None) for level in range(shares)]
-
-    where_own = jnp.stack([core, same.astype(jnp.int32)])
+    near = flat_pairs(dp_size, lambda d, c, t: (d ^ 2, t) if c != t else None)
+
+    orders = (list(range(levels)), [*range(1, levels), 0])
+    hop_facts = []
+    for step in range(levels):
+        places = [sum(1 for later in order[step + 1 :] if later < order[step]) for order in orders]
+        hop_facts.append(jnp.where(core == 0, places[0], places[1]))
+        hop_facts.append(jnp.where(core == 0, bits[orders[0][step]], bits[orders[1][step]]))
+    hops = [flat_pairs(dp_size, lambda d, c, t: (d ^ (2 << orders[c][step]), t)) for step in range(levels)]
+    where_own = jnp.stack([core, same.astype(jnp.int32), *hop_facts])
     where_peer = jnp.stack([core, 1 - same.astype(jnp.int32)])
     out_rows = wide // 2
+    weights_here = (w_query, w_key, w_value)
+    part_rows = width >> shares
+    which = sum(bits[level] << level for level in range(shares))
+    parts_here = jnp.concatenate([half_of(weight, which, part_rows) for weight in weights_here], axis=1)
     w_out_sent = send(half_of(w_out, bits[0], out_rows).astype(f32), swap)
     attended_low, *sources = attention_forward(0, (block_in,), lengths, pad_count, norm_in_attn, w_query, w_key, w_value)
     low_sent = send(attended_low, swap)
     sources = after(sources, w_out_sent)
-    w_out_sent = ordered(w_out_sent, send(w_out_sent, near[0]), bits[0], 0)
+    w_out_sent = ordered(w_out_sent, send(w_out_sent, near), bits[0], 0)
     [attended_high] = attention_forward(1, sources, lengths, pad_count, norm_in_attn, w_query, w_key, w_value)
     high_sent = send(attended_high, swap)
-    block_late, cot_late, facts = after((block_in, cotangent, jnp.pad(lengths, ((0, 0), (0, 1)))), attended_high)
+    block_late, cot_late, facts = after((block_in, cotangent, jnp.pad(lengths, ((0, 0), (0, 1)))), low_sent, attended_high)
     facts = facts.astype(f32) + jnp.pad(pad_count.astype(f32)[:, None], ((0, 0), (lengths.shape[1], 0)))
     there = send(packed(where_own, block_late, cot_late), cross)
     facts_there = send(facts, cross)
     low_sent = after(low_sent, attended_high)
     attended = [(attended_low * keep + low_sent).astype(bf16), (attended_high * keep + high_sent).astype(bf16)]
-    weights_here = jnp.concatenate([w_query, w_key, w_value], axis=1)
-    part_rows = width >> shares
-    which = sum(bits[level] << level for level in range(shares))
-    weights_sent = send(half_of(after(weights_here, attended[1]), which, part_rows).astype(f32), swap)
     w_out_mine = (w_out.astype(f32) * keep + w_out_sent).astype(bf16)
+    parts_sent = send(after(parts_here, attended[0]).astype(f32), swap)
     facts_row = jnp.where(same, facts, facts_there).astype(jnp.int32)
     docs = lengths.shape[1]
     lengths_row, pad_row = facts_row[:, :docs], facts_row[:, docs]
@@ -787,40 +867,40 @@
         attn_total.append(total)
         hidden_peer.append(send(one, over))
 
+    gathered = 1 << shares
+    groups = [
+        [base + 2 * near_chip + one for near_chip in range(gathered)]
+        for base in range(0, dp_size, 2 * gathered)
+        for one in range(2)
+    ]
+    weights_sent = lax.all_gather(after(parts_sent, hidden_own[0]), "dp", axis=0, tiled=True, axis_index_groups=groups)
+
     buffers, slopes, parts, sums_own = (), [], [], []
     for number in range(4):
         piece = hidden_own[number] if number < 2 else hidden_peer[number - 2]
-        if number == 3:
-            piece = after(piece, parts[2], weights_sent)
+        if number > 1:
+            piece = after(piece, parts[number - 1])
         *buffers, slope, part = mlp_forward(number, piece, norm_in_mlp, w_up, w_down, buffers)
         slopes.append(slope)
         parts.append(part)
         if number >= 2:
             sums_own.append(send(part, over))
-            if number - 2 < shares:
-                weights_sent = after(weights_sent, part)
-                weights_sent = ordered(weights_sent, send(weights_sent, near[number - 2]), bits[number - 2], 0)
     mlp_in_all, activated_all = buffers
-    weights_late = after(weights_sent, parts[3])
-    weights_mine = (weights_here.astype(f32) * keep + weights_late).astype(bf16)
-    ready = attention_ready(where_own, block_in, there, lengths_row, pad_row, norm_in_attn, weights_mine)
-    totals, blocks, back_parts, gain_out_mlp = [], [], [], []
+    totals, blocks, back_parts, gain_out_mlp = [None] * 4, [None] * 4, [None] * 4, [None] * 4
     buffers = ()
+
+    def add_up(number, gate):
+        totals[number] = parts[number] + after(sums_own[number], gate)
+        totals[number + 2] = send(totals[number], over)
+
+    add_up(0, parts[3])
+    gate = totals[0]
     for number in range(4):
-        if number < 2:
-            total = parts[number] + (sums_own[0] if number == 0 else after(sums_own[1], back_parts[0]))
-            totals.append(total)
-            totals_peer = send(total, over)
-            totals.append(totals_peer)
-        total = totals[2 * number] if number < 2 else totals[2 * (number - 2) + 1]
-        if number >= 2:
-            total = after(total, back_parts[number - 1], ready)
-        hidden_piece = hidden_own[number] if number < 2 else hidden_peer[number - 2]
         block, low_all, gain_sum, up_all, part = mlp_backward(
             where_own if number < 2 else where_peer,
             number,
-            hidden_piece,
-            total,
+            hidden_own[number] if number < 2 else hidden_peer[number - 2],
+            after(totals[number], gate),
             cotangent,
             there,
             norm_out_mlp,
@@ -830,58 +910,20 @@
             buffers,
         )
         buffers = (low_all, up_all)
-        blocks.append(block)
-        back_parts.append(part)
-        gain_out_mlp.append(gain_sum[0])
+        blocks[number], back_parts[number], gain_out_mlp[number] = block, part, gain_sum[0]
+        gate = part
+        if number == 0:
+            add_up(1, part)
+            gate = totals[1]
     grad_low_all, grad_up_all = buffers
     sums_own = [send(part, over) for part in back_parts[2:]]
 
-    small = width // chips // 2
-
-    def halved(held, arrived, level):
-        group = (-1, 2, width // chips, held.shape[-1])
-        parts = [held.reshape(group)] + ([] if arrived is None else [arrived.reshape(group)])
-        results = []
-        for which in (bits[level], 1 - bits[level]):
-            results.append(sum(lax.dynamic_index_in_dim(part, which, 1, keepdims=False) for part in parts))
-        return results
-
-    def to_chip(held, arrived, level, gate=None):
-        for number in range(level, levels):
-            held, leaving = halved(held, arrived, number)
-            arrived = send(leaving, flips[number])
-        return (held + arrived).reshape(width // chips, -1)
-
-    def to_core(held):
-        arrived = send(half_of(held, 1 - core, small), cross)
-        return ordered(half_of(held, core, small), arrived, core, 1)
-
-    def weight_part(left, right, columns):
-        return jnp.einsum("td,tf->df", left, half_columns(right, columns, hidden // 2), preferred_element_type=f32)
-
-    down_sent = send(weight_part(grad_low_all, activated_all, 1 - core), cross)
-    weight_up = jnp.einsum("td,tf->df", mlp_in_all, grad_up_all, preferred_element_type=f32)
-    grad_up = lax.psum_scatter(weight_up, "dp", scatter_dimension=0, tiled=True)
-    down_kept = weight_part(grad_low_all, activated_all, core)
-    down_held, down_leaving = halved(down_kept, down_sent, 0)
-    down_arrived = send(down_leaving, flips[0])
-    sums_own = after(sums_own, down_leaving, weight_up)
-
-    def to_output(values_own, values_peer):
-        stay = jnp.where(same, values_own, values_peer)
-        leave = jnp.where(same, values_peer, values_own)
-        arrived = send(leave, cross)
-        low = stay * first + arrived * (1.0 - first)
-        high = arrived * first + stay * (1.0 - first)
-        return jnp.concatenate([low, high], axis=0)
-
-    buffers, gain_sums = (), []
-    for number in range(2):
-        *buffers, gain_sum = residual_chunk(
+    def residual(number, arrived, buffers):
+        return residual_chunk(
             where_own,
             number,
             back_parts[number],
-            sums_own[number],
+            arrived,
             hidden_own[number],
             attn_total[number],
             cotangent,
@@ -890,12 +932,63 @@
             norm_out_attn,
             buffers,
         )
-        gain_sums.append(gain_sum)
+
+    chip_rows = width // chips
+    small = chip_rows // 2
+
+    class Sum:
+        def __init__(self, held, arrived):
+            self.held = [part.reshape(chips, chip_rows, -1) for part in held]
+            self.arrived = [] if arrived is None else [arrived.reshape(chips, chip_rows, -1)]
+            self.sources = [None if arrived is None else (0, 0)] * len(held)
+            self.step = 0
+
+        def hop(self, *gates):
+            arrived = [after(array, *gates) for array in self.arrived]
+            self.held, leaving = halves(where_own, self.step, self.held, arrived, tuple(self.sources))
+            self.arrived = [send(leaving, hops[self.step])]
+            starts = np.cumsum([0, *(part.shape[2] for part in self.held)])
+            self.sources = [(0, int(start)) for start in starts[:-1]]
+            self.step += 1
+            return leaving
+
+        def result(self, *gates):
+            while self.step < levels:
+                gates = (self.hop(*gates),)
+            arrived = [after(array, *gates) for array in self.arrived]
+            return [
+                (part + arrived[number][:, :, start : start + part.shape[2]]).reshape(chip_rows, -1)
+                for part, (number, start) in zip(self.held, self.sources)
+            ]
+
+    down_other = outer(where_own, grad_low_all, activated_all, lambda where: 1 - where[0], hidden // 2)
+    down_kept = outer(where_own, grad_low_all, activated_all, lambda where: where[0], hidden // 2)
+    early = Sum([down_kept], send(down_other, cross))
+    mlp_in_all, grad_up_all = after((mlp_in_all, grad_up_all), early.hop(down_kept))
+    weight_up = outer(where_own, mlp_in_all, grad_up_all, lambda where: 0, hidden)
+    grad_up = lax.psum_scatter(weight_up, "dp", scatter_dimension=0, tiled=True)
+    weights_late = after(weights_sent, weight_up)
+    weights_mine = (jnp.concatenate(weights_here, axis=1).astype(f32) * keep + weights_late).astype(bf16)
+    ready = attention_ready(where_own, block_in, there, lengths_row, pad_row, norm_in_attn, weights_mine)
+    *buffers, gain_sum = residual(0, after(sums_own[0], ready[0]), ())
+    gain_sums = [gain_sum]
+    *buffers, gain_sum = residual(1, after(sums_own[1], gain_sum), buffers)
+    gain_sums.append(gain_sum)
     grad_res, grad_attn = buffers
     gain_in_mlp = gain_sums[0][0] + gain_sums[1][0]
     gain_out_attn = gain_sums[0][1] + gain_sums[1][1]
     gain_out_mlp = gain_out_mlp[0] + gain_out_mlp[1]
+
+    def to_output(values_own, values_peer):
+        stay = jnp.where(same, values_own, values_peer)
+        leave = jnp.where(same, values_peer, values_own)
+        arrived = send(leave, cross)
+        low = stay * first + arrived * (1.0 - first)
+        high = arrived * first + stay * (1.0 - first)
+        return jnp.concatenate([low, high], axis=0)
+
     grad_attn_other = send(grad_attn, cross)
+    gate = early.hop(gain_sum)
     grad_attn_low = jnp.concatenate(
         [
             grad_attn * first + grad_attn_other * (1.0 - first),
@@ -904,61 +997,69 @@
         axis=0,
     ).astype(bf16)
     grad_heads = jnp.einsum("td,ed->te", grad_attn_low, w_out_mine, preferred_element_type=f32).astype(bf16)
-    weight_out = jnp.concatenate(
-        [jnp.einsum("td,te->de", grad_attn_low, values, preferred_element_type=f32) for values in attended], axis=1
-    )
+    grads = attention_backward(ready, lengths_row, pad_row, after(grad_heads, gate))
+    grads = jnp.concatenate(after(grads, early.hop(grads)), axis=1)
+    late = Sum([jnp.einsum("td,te->de", ready[4], grads, preferred_element_type=f32)], None)
+    gate = late.hop()
+    other = input_other(where_own, after(grads, gate), weights_mine)
+    other_sent = send(other, cross)
+    attended_all = after(jnp.concatenate(attended, axis=1), other)
+    weight_out = jnp.einsum("td,te->de", grad_attn_low, attended_all, preferred_element_type=f32)
     weight_out_sent = send(weight_out, swap)
-    down_held, down_leaving = halved(down_held, down_arrived, 1)
-    down_arrived = send(down_leaving, flips[1])
-    grad_heads = after(grad_heads, down_leaving, weight_out)
-    grads = attention_backward(ready, lengths_row, pad_row, grad_heads)
-    down_held, down_leaving = halved(down_held, down_arrived, 2)
-    down_arrived = send(down_leaving, flips[2])
-    grads = jnp.concatenate(after(grads, down_leaving), axis=1)
-    other_sent = send(input_other(where_own, grads, weights_mine), cross)
-    pair = jnp.einsum("td,te->de", ready[4], grads[:, : 2 * wide], preferred_element_type=f32)
-    pair_held, pair_leaving = halved(pair, None, 0)
-    pair_arrived = send(pair_leaving, flips[0])
-    value = jnp.einsum("td,te->de", ready[4], grads[:, 2 * wide :], preferred_element_type=f32)
-    value_held, value_leaving = halved(value, None, 0)
-    value_arrived = send(value_leaving, flips[0])
-    other_sent = after(other_sent, value_leaving)
+    gate = weight_out
     grad_in_own, gain_in_attn = input_own(
-        where_own, grads, weights_mine, other_sent, block_in, there, grad_res, norm_in_attn
-    )
-    grad_in = to_output(grad_in_own, send(grad_in_own, over))
-    grad_down = to_core(to_chip(down_held, down_arrived, 3)).T
+        where_own, grads, weights_mine, after(other_sent, gate), block_in, there, grad_res, norm_in_attn
+    )
+    grad_in_sent = send(grad_in_own, over)
     gains = jnp.stack([gain_in_attn[0], gain_out_attn, gain_in_mlp, gain_out_mlp], axis=1)
-    weight_out_sent, gains, pair_arrived = after((weight_out_sent, gains, pair_arrived), grad_up, grad_down)
-    others = lax.psum_scatter(
-        jnp.concatenate([weight_out * keep + weight_out_sent, jnp.pad(gains, ((0, 0), (0, LANES - 4)))], axis=1),
-        "dp",
-        scatter_dimension=0,
-        tiled=True,
-    )
-    held = jnp.concatenate([to_chip(pair_held, pair_arrived, 1), to_chip(value_held, value_arrived, 1)], axis=1)
+    weight_out_sent, gains = after((weight_out_sent, gains), grad_up)
+    others = jnp.concatenate(
+        [weight_out * keep + weight_out_sent, jnp.pad(gains, ((0, 0), (0, LANES - gains.shape[1])))], axis=1
+    )
+    gate = late.hop(grad_in_own, others)
+    others = lax.psum_scatter(others, "dp", scatter_dimension=0, tiled=True)
+    gate = late.hop(gate)
+    [grad_down] = early.result(gate)
+    [held] = late.result(gate)
+
+    def to_core(held):
+        arrived = send(half_of(held, 1 - core, small), cross)
+        return ordered(half_of(held, core, small), arrived, core, 1)
+
+    def to_output(values_own, values_peer):
+        stay = jnp.where(same, values_own, values_peer)
+        leave = jnp.where(same, values_peer, values_own)
+        arrived = send(leave, cross)
+        low = stay * first + arrived * (1.0 - first)
+        high = arrived * first + stay * (1.0 - first)
+        return jnp.concatenate([low, high], axis=0)
+
+    grad_down = to_core(grad_down).T
+    grad_in = to_output(grad_in_own, after(grad_in_sent, gate))
     for_core = half_of(held, core, small)
     for_other = half_of(held, 1 - core, small)
-    straight = send(for_core, flat_pairs(dp_size, lambda d, c, t: (d, 1 - t) if c != t else None))
     diagonal = send(for_other, swap)
-    beside = send(for_other, flat_pairs(dp_size, lambda d, c, t: (d ^ 1, t) if c == t else None))
-    heads = jnp.where(same, for_core + straight, beside + diagonal)
-    gains = others[:, wide:]
+    straight = send(
+        jnp.where(same, for_other, for_core),
+        flat_pairs(dp_size, lambda d, c, t: (d, 1 - t) if c != t else (d ^ 1, t)),
+    )
+    heads = straight + jnp.where(same, for_core, diagonal)
+    gains = others[:, wide:].T
     gains = gains + send(gains, over)
     block_out = to_output(jnp.concatenate(blocks[:2], axis=0), jnp.concatenate(blocks[2:], axis=0)).astype(bf16)
     return (
         block_out,
         grad_in,
-        gains[:, 0],
+        gains[0],
         heads[:, :wide],
         heads[:, wide : 2 * wide],
         heads[:, 2 * wide : 3 * wide],
         others[:, :wide].T,
-        gains[:, 1],
-        gains[:, 2],
+        gains[1],
+        gains[2],
         grad_up,
         grad_down,
-        gains[:, 3],
+        gains[3],
     )
 
 

time: 625 us -> 570 us (0.912)
  the two profiles are of different devices: /device:TPU:0 before, /device:TPU:1 now
where the time goes in v3:
time: 570 us; the launch traced here: 559 us
  Pallas kernels  246 us (43%)
  waiting for transfers between devices  195 us (34%)
  other arithmetic  34 us (6%)
  starting transfers between devices  31.3 us (5%)
  local copies, waits for them, and re-layouts  24.8 us (4%)
  between operations  17.2 us (3%)
  matrix products  11.4 us (2%)
    ppermute x33, waiting for transfers between devices, send(): return lax.ppermute(values, ('dp', 'tensor'), pairs)  195 us
    pallas_call x14, Pallas kernels, call(): pl.pallas_call(kernel, grid_spec=pltpu.PrefetchScalarGridSpec(num_scalar_...  113 us
    ppermute x33, starting transfers between devices, send(): return lax.ppermute(values, ('dp', 'tensor'), pairs)  30.8 us
    pallas_call x6, Pallas kernels, halves(): pl.pallas_call(partial(halves_kernel, len(held), sources), grid_spec=pltp...  29.6 us
    pallas_call x1, Pallas kernels, attention_backward(): pl.pallas_call(partial(backward_kernel, lengths.shape[1]), grid=(pairs,),...  26 us
    pallas_call x3, Pallas kernels, outer(): pl.pallas_call(outer_kernel, grid_spec=pltpu.PrefetchScalarGridSpec(num_s...  24.7 us
    pallas_call x2, Pallas kernels, attention_forward(): pl.pallas_call(partial(forward_kernel, lengths.shape[1], first), grid=(1,...  23.5 us
    pallas_call x1, Pallas kernels, attention_ready(): pl.pallas_call(partial(ready_kernel, lengths.shape[1]), grid=(wide // gro...  18.5 us
  transfers between devices with their start and end apart: 36, of which 20 were waited for; matrix products, arithmetic and copies ran while one was open for 9% of the time, Pallas kernels for 43%

profile of v3, /device:TPU:1, one launch (start us, length us, event | category | flops | bytes accessed | tf_op | source)
XLA Modules:
  0.0 559.4 jit_solution(1920531703623586645)
XLA Ops:
  9.2 4.5 collective-permute-start.1
  14.4 12.0 %attention_forward.2 = (f32[1024,256]{1,0:T(8,128)}, bf16[1024,1024]{1,0:T(8,128)(2,1)}, f32[1024,128]{1,0:T(8,128)}, f32[1024,128]{1,0:T(8,128)}) custom-call(s32[1,4]{1,0:T(1,128)} %lengths_ref.3, s32[1]{0:T(128)S(6)} %copy.68.pad_ref, f32[32,1]{1,0:T(8,128)} %constant.51.clone.freq_ref, f32[1,1024]{1,0:T(1,128)} %bitcast.71, ...), custom_call_target="tpu_custom_call" | custom-call | flops 1 | bytes 1 | tf_op jit(solution)/shard_map/attention_forward/pallas_call | solution.py:278
  26.5 2.1 collective-permute-start
  29.3 11.5 %attention_forward.3 = f32[1024,256]{1,0:T(8,128)} custom-call(s32[1,4]{1,0:T(1,128)} %lengths_ref.3, s32[1]{0:T(128)S(6)} %copy.68.pad_ref, f32[32,1]{1,0:T(8,128)} %constant.51.clone.freq_ref, f32[1,1024]{1,0:T(1,128)} %bitcast.72, bf16[1024,1024]{1,0:T(8,128)(2,1)} %get-tuple-element.127.refs_0_, f32[1024,128]{1,0:T(8,128)} %get-tuple-element.128.refs_1_, ...), custom_call_target="tpu_custom_call" | custom-call | flops 1 | bytes 1 | tf_op jit(solution)/shard_map/attention_forward/pallas_call | solution.py:278
  40.7 2.0 collective-permute-done
  42.8 5.1 packed.1
  47.9 3.1 collective-permute-start.3
  51.1 2.2 collective-permute-start.2
  55.0 8.5 %collective-permute-done.3 = f32[256,1024]{1,0:T(8,128)S(1)} collective-permute-done((f32[256,1024]{1,0:T(8,128)S(1)}, f32[256,1024]{1,0:T(8,128)S(1)}, u32[]{:S(2)}, u32[]{:S(2)}) %collective-permute-start.3) | collective-permute-done | bytes 1048608 | tf_op jit(solution)/shard_map/ppermute | solution.py:30
  64.1 3.2 collective-permute-done.2
  69.2 1.8 fusion.6
  72.1 2.2 collective-permute-start.14
  75.5 4.6 hidden.2
  80.1 13.8 %collective-permute-done.14 = f32[256,1536]{1,0:T(8,128)} collective-permute-done((f32[256,1536]{1,0:T(8,128)S(1)}, f32[256,1536]{1,0:T(8,128)}, u32[]{:S(2)}, u32[]{:S(2)}) %collective-permute-start.14) | collective-permute-done | bytes 1572896 | tf_op jit(solution)/shard_map/ppermute | solution.py:30
  94.5 4.5 hidden.3
  100.5 9.4 %mlp_forward.4 = (bf16[1024,1024]{1,0:T(8,128)(2,1)}, bf16[1024,2048]{1,0:T(8,128)(2,1)}, f32[256,2048]{1,0:T(8,128)}, f32[256,1024]{1,0:T(8,128)}) custom-call(f32[256,1024]{1,0:T(8,128)} %get-tuple-element.133.hidden_ref, f32[1,1024]{1,0:T(1,128)} %bitcast.65, bf16[1024,2048]{1,0:T(8,128)(2,1)} %up_ref.15, bf16[2048,1024]{1,0:T(8,128)(2,1)} %down_ref.15), custom_call_target="tpu_custom_call" | custom-call | flops 1 | bytes 1 | tf_op jit(solution)/shard_map/mlp_forward/pallas_call | solution.py:521
  109.9 9.0 %mlp_forward.5 = (bf16[1024,1024]{1,0:T(8,128)(2,1)}, bf16[1024,2048]{1,0:T(8,128)(2,1)}, f32[256,2048]{1,0:T(8,128)}, f32[256,1024]{1,0:T(8,128)}) custom-call(f32[256,1024]{1,0:T(8,128)} %get-tuple-element.135.hidden_ref, f32[1,1024]{1,0:T(1,128)} %bitcast.66, bf16[1024,2048]{1,0:T(8,128)(2,1)} %up_ref.15, ...), custom_call_target="tpu_custom_call", output_to_operand_aliasing={{0}: (4, {}), {1}: (5, {})} | custom-call | flops 1 | bytes 1 | tf_op jit(solution)/shard_map/mlp_forward/pallas_call | solution.py:521
  121.0 9.0 %mlp_forward.6 = (bf16[1024,1024]{1,0:T(8,128)(2,1)}, bf16[1024,2048]{1,0:T(8,128)(2,1)}, f32[256,2048]{1,0:T(8,128)}, f32[256,1024]{1,0:T(8,128)}) custom-call(f32[256,1024]{1,0:T(8,128)} %copy-done.16, f32[1,1024]{1,0:T(1,128)} %bitcast.67, bf16[1024,2048]{1,0:T(8,128)(2,1)} %up_ref.15, ...), custom_call_target="tpu_custom_call", output_to_operand_aliasing={{0}: (4, {}), {1}: (5, {})} | custom-call | flops 1 | bytes 1 | tf_op jit(solution)/shard_map/mlp_forward/pallas_call | solution.py:521
  130.0 12.4 %collective-permute-done.8.hidden_ref = f32[256,1024]{1,0:T(8,128)S(1)} collective-permute-done((f32[256,1024]{1,0:T(8,128)}, f32[256,1024]{1,0:T(8,128)S(1)}, u32[]{:S(2)}, u32[]{:S(2)}) %collective-permute-start.8) | collective-permute-done | bytes 1048608 | tf_op jit(solution)/shard_map/ppermute | solution.py:30
  143.4 9.1 %mlp_forward.7 = (bf16[1024,1024]{1,0:T(8,128)(2,1)}, bf16[1024,2048]{1,0:T(8,128)(2,1)}, f32[256,2048]{1,0:T(8,128)}, f32[256,1024]{1,0:T(8,128)}) custom-call(f32[256,1024]{1,0:T(8,128)} %copy-done.15, f32[1,1024]{1,0:T(1,128)} %bitcast.68, bf16[1024,2048]{1,0:T(8,128)(2,1)} %up_ref.15, ...), custom_call_target="tpu_custom_call", output_to_operand_aliasing={{0}: (4, {}), {1}: (5, {})} | custom-call | flops 1 | bytes 1 | tf_op jit(solution)/shard_map/mlp_forward/pallas_call | solution.py:521
  152.6 12.3 %collective-permute-done.7 = f32[256,1024]{1,0:T(8,128)S(1)} collective-permute-done((f32[256,1024]{1,0:T(8,128)}, f32[256,1024]{1,0:T(8,128)S(1)}, u32[]{:S(2)}, u32[]{:S(2)}) %collective-permute-start.7) | collective-permute-done | bytes 1048608 | tf_op jit(solution)/shard_map/ppermute | solution.py:30
  166.1 11.1 %mlp_backward.4 = (f32[256,1024]{1,0:T(8,128)}, bf16[1024,1024]{1,0:T(8,128)(2,1)}, f32[8,1024]{1,0:T(8,128)}, bf16[1024,2048]{1,0:T(8,128)(2,1)}, f32[256,1024]{1,0:T(8,128)}) custom-call(s32[8]{0:T(128)} %stack.42.where_ref, f32[256,1024]{1,0:T(8,128)} %get-tuple-element.133.hidden_ref, f32[256,1024]{1,0:T(8,128)} %add.135.total_ref, ...), custom_call_target="tpu_custom_call" | custom-call | flops 1 | bytes 1 | tf_op jit(solution)/shard_map/mlp_backward/pallas_call | solution.py:521
  177.2 10.2 %collective-permute-done.9 = f32[256,1024]{1,0:T(8,128)S(1)} collective-permute-done((f32[256,1024]{1,0:T(8,128)}, f32[256,1024]{1,0:T(8,128)S(1)}, u32[]{:S(2)}, u32[]{:S(2)}) %collective-permute-start.9) | collective-permute-done | bytes 1048608 | tf_op jit(solution)/shard_map/ppermute | solution.py:30
  189.1 10.9 %mlp_backward.5 = (f32[256,1024]{1,0:T(8,128)}, bf16[1024,1024]{1,0:T(8,128)(2,1)}, f32[8,1024]{1,0:T(8,128)}, bf16[1024,2048]{1,0:T(8,128)(2,1)}, f32[256,1024]{1,0:T(8,128)}) custom-call(s32[8]{0:T(128)} %stack.42.where_ref, f32[256,1024]{1,0:T(8,128)} %get-tuple-element.135.hidden_ref, ...), custom_call_target="tpu_custom_call", output_to_operand_aliasing={{1}: (9, {}), {3}: (10, {})} | custom-call | flops 1 | bytes 1 | tf_op jit(solution)/shard_map/mlp_backward/pallas_call | solution.py:521
  200.0 9.8 %collective-permute-done.10.total_ref = f32[256,1024]{1,0:T(8,128)} collective-permute-done((f32[256,1024]{1,0:T(8,128)}, f32[256,1024]{1,0:T(8,128)}, u32[]{:S(2)}, u32[]{:S(2)}) %collective-permute-start.10) | collective-permute-done | bytes 1048608 | tf_op jit(solution)/shard_map/ppermute | solution.py:30
  209.8 10.9 %mlp_backward.6 = (f32[256,1024]{1,0:T(8,128)}, bf16[1024,1024]{1,0:T(8,128)(2,1)}, f32[8,1024]{1,0:T(8,128)}, bf16[1024,2048]{1,0:T(8,128)(2,1)}, f32[256,1024]{1,0:T(8,128)}) custom-call(s32[2]{0:T(128)} %pad_add_fusion.where_ref, f32[256,1024]{1,0:T(8,128)} %copy-done.16, ...), custom_call_target="tpu_custom_call", output_to_operand_aliasing={{1}: (9, {}), {3}: (10, {})} | custom-call | flops 1 | bytes 1 | tf_op jit(solution)/shard_map/mlp_backward/pallas_call | solution.py:521
  220.7 10.4 %collective-permute-done.11.total_ref = f32[256,1024]{1,0:T(8,128)} collective-permute-done((f32[256,1024]{1,0:T(8,128)}, f32[256,1024]{1,0:T(8,128)}, u32[]{:S(2)}, u32[]{:S(2)}) %collective-permute-start.11) | collective-permute-done | bytes 1048608 | tf_op jit(solution)/shard_map/ppermute | solution.py:30
  231.1 11.1 %mlp_backward.7 = (f32[256,1024]{1,0:T(8,128)}, bf16[1024,1024]{1,0:T(8,128)(2,1)}, f32[8,1024]{1,0:T(8,128)}, bf16[1024,2048]{1,0:T(8,128)(2,1)}, f32[256,1024]{1,0:T(8,128)}) custom-call(s32[2]{0:T(128)} %pad_add_fusion.where_ref, f32[256,1024]{1,0:T(8,128)} %copy-done.15, ...), custom_call_target="tpu_custom_call", output_to_operand_aliasing={{1}: (9, {}), {3}: (10, {})} | custom-call | flops 1 | bytes 1 | tf_op jit(solution)/shard_map/mlp_backward/pallas_call | solution.py:521
  242.2 7.1 %outer.4 = f32[1024,1024]{1,0:T(8,128)} custom-call(s32[8]{0:T(128)} %stack.42.where_ref, bf16[1024,1024]{1,0:T(8,128)(2,1)} %get-tuple-element.175.left_ref, bf16[1024,2048]{1,0:T(8,128)(2,1)} %get-tuple-element.176.right_ref), custom_call_target="tpu_custom_call" | custom-call | flops 1 | bytes 1 | tf_op jit(solution)/shard_map/outer/pallas_call | solution.py:666
  249.4 7.2 %outer.3 = f32[1024,1024]{1,0:T(8,128)} custom-call(s32[8]{0:T(128)} %stack.42.where_ref, bf16[1024,1024]{1,0:T(8,128)(2,1)} %get-tuple-element.175.left_ref, bf16[1024,2048]{1,0:T(8,128)(2,1)} %get-tuple-element.176.right_ref), custom_call_target="tpu_custom_call" | custom-call | flops 1 | bytes 1 | tf_op jit(solution)/shard_map/outer/pallas_call | solution.py:666
  256.7 2.0 copy-done.1
  258.8 6.4 %halves.6 = (f32[4,128,1024]{2,1,0:T(8,128)}, f32[4,128,1024]{2,1,0:T(8,128)}) custom-call(s32[8]{0:T(128)} %stack.42.where_ref, f32[8,128,1024]{2,1,0:T(8,128)} %bitcast.58, f32[8,128,1024]{2,1,0:T(8,128)} %bitcast.59, f32[8,128,1024]{2,1,0:T(8,128)} %bitcast.62, f32[8,128,1024]{2,1,0:T(8,128)} %bitcast.63), custom_call_target="tpu_custom_call" | custom-call | flops 1 | bytes 1 | tf_op jit(solution)/shard_map/halves/pallas_call | solution.py:721
  265.2 10.5 %outer.5 = f32[1024,2048]{1,0:T(8,128)} custom-call(s32[8]{0:T(128)} %stack.42.where_ref, bf16[1024,1024]{1,0:T(8,128)(2,1)} %get-tuple-element.179.left_ref, bf16[1024,2048]{1,0:T(8,128)(2,1)} %get-tuple-element.180.right_ref), custom_call_target="tpu_custom_call" | custom-call | flops 1 | bytes 1 | tf_op jit(solution)/shard_map/outer/pallas_call | solution.py:666
  281.0 4.8 add_convert_fusion.wq_ref.wk_ref.wv_ref.weight_ref
  285.8 18.5 %attention_ready.1 = (bf16[1024,512]{1,0:T(8,128)(2,1)}, bf16[1024,512]{1,0:T(8,128)(2,1)}, bf16[1024,512]{1,0:T(8,128)(2,1)}, f32[2,4,1024]{2,1,0:T(4,128)}, bf...) custom-call(s32[8]{0:T(128)} %stack.42.where_ref, s32[1,4]{1,0:T(1,128)} %bitcast.83, ...), custom_call_target="tpu_custom_call" | custom-call | flops 1 | bytes 1 | tf_op jit(solution)/shard_map/attention_ready/pallas_call | solution.py:304
  304.3 5.8 %residual.2 = (f32[512,1024]{1,0:T(8,128)}, f32[512,1024]{1,0:T(8,128)}, f32[8,1024]{1,0:T(8,128)}) custom-call(s32[8]{0:T(128)} %stack.42.where_ref, f32[256,1024]{1,0:T(8,128)} %get-tuple-element.151.part_ref, f32[256,1024]{1,0:T(8,128)} %collective-permute-done.17.arrived_ref, f32[256,1024]{1,0:T(8,128)} %get-tuple-element.133.hidden_ref, ...), custom_call_target="tpu_custom_call" | custom-call | flops 1 | bytes 1 | tf_op jit(solution)/shard_map/residual/pallas_call | solution.py:521
  310.1 12.9 %collective-permute-done.16.arrived_ref = f32[256,1024]{1,0:T(8,128)} collective-permute-done((f32[256,1024]{1,0:T(8,128)}, f32[256,1024]{1,0:T(8,128)}, u32[]{:S(2)}, u32[]{:S(2)}) %collective-permute-start.16) | collective-permute-done | bytes 1048608 | tf_op jit(solution)/shard_map/ppermute | solution.py:30
  323.0 5.9 %residual.3 = (f32[512,1024]{1,0:T(8,128)}, f32[512,1024]{1,0:T(8,128)}, f32[8,1024]{1,0:T(8,128)}) custom-call(s32[8]{0:T(128)} %stack.42.where_ref, f32[256,1024]{1,0:T(8,128)} %get-tuple-element.158.part_ref, f32[256,1024]{1,0:T(8,128)} %collective-permute-done.16.arrived_ref, ...), custom_call_target="tpu_custom_call", output_to_operand_aliasing={{0}: (9, {}), {1}: (10, {})} | custom-call | flops 1 | bytes 1 | tf_op jit(solution)/shard_map/residual/pallas_call | solution.py:521
  330.0 4.5 halves.7
  334.5 2.4 collective-permute-start.20
  337.5 2.3 add_convert_fusion.2
  339.8 2.3 convolution_convert_fusion.grad_ref
  342.1 26.0 %attention_backward.1 = (bf16[1024,512]{1,0:T(8,128)(2,1)}, bf16[1024,512]{1,0:T(8,128)(2,1)}, bf16[1024,512]{1,0:T(8,128)(2,1)}) custom-call(s32[1,4]{1,0:T(1,128)} %bitcast.84, s32[1]{0:T(128)} %bitcast.12.pad_ref, f32[1024,128]{1,0:T(8,128)} %get-tuple-element.182.cos_ref, f32[1024,128]{1,0:T(8,128)} %get-tuple-element.183.sin_ref, ...), custom_call_target="tpu_custom_call" | custom-call | flops 1 | bytes 1 | tf_op jit(solution)/shard_map/attention_backward/pallas_call | solution.py:333
  369.1 3.4 halves.8
  374.1 1.9 copy-done.41
  376.0 5.6 %fusion.18 = f32[1024,1536]{1,0:T(8,128)} fusion(bf16[1024,1024]{1,0:T(8,128)(2,1)S(1)} %copy-done.41, bf16[1024,1536]{1,0:T(8,128)(2,1)S(1)} %constant_dynamic-update-slice_fusion.4.grad_ref), kind=kOutput, calls=%fused_computation.73 | convolution fusion | flops 3221225472 | bytes 11534336 | tf_op jit(solution)/shard_map/td,te->de/dot_general | solution.py:1002
  381.6 6.5 %halves.9 = (f32[4,128,1536]{2,1,0:T(8,128)}, f32[4,128,1536]{2,1,0:T(8,128)}) custom-call(s32[8]{0:T(128)} %stack.42.where_ref, f32[8,128,1536]{2,1,0:T(8,128)} %bitcast.60, f32[8,128,1536]{2,1,0:T(8,128)} %bitcast.61), custom_call_target="tpu_custom_call" | custom-call | flops 1 | bytes 1 | tf_op jit(solution)/shard_map/halves/pallas_call | solution.py:721
  389.5 6.6 %input_other.1 = f32[512,1024]{1,0:T(8,128)} custom-call(s32[8]{0:T(128)} %stack.42.where_ref, bf16[1024,1536]{1,0:T(8,128)(2,1)} %copy-done, bf16[1024,1536]{1,0:T(8,128)(2,1)} %add_convert_fusion.wq_ref.wk_ref.wv_ref.weight_ref), custom_call_target="tpu_custom_call" | custom-call | flops 1 | bytes 1 | tf_op jit(solution)/shard_map/input_other/pallas_call | solution.py:521
  399.0 2.7 collective-permute-start.24
  408.1 10.5 %input_own.1 = (f32[512,1024]{1,0:T(8,128)}, f32[8,1024]{1,0:T(8,128)}) custom-call(s32[8]{0:T(128)} %stack.42.where_ref, bf16[1024,1536]{1,0:T(8,128)(2,1)} %copy-done, bf16[1024,1536]{1,0:T(8,128)(2,1)} %add_convert_fusion.wq_ref.wk_ref.wv_ref.weight_ref, f32[512,1024]{1,0:T(8,128)} %copy-done.21, bf16[1024,1024]{1,0:T(8,128)(2,1)} %here_ref.19, ...), custom_call_target="tpu_custom_call" | custom-call | flops 1 | bytes 1 | tf_op jit(solution)/shard_map/input_own/pallas_call | solution.py:759
  420.9 11.0 %collective-permute-done.24 = f32[1024,512]{0,1:T(8,128)} collective-permute-done((f32[1024,512]{0,1:T(8,128)S(1)}, f32[1024,512]{0,1:T(8,128)}, u32[]{:S(2)}, u32[]{:S(2)}) %collective-permute-start.24) | collective-permute-done | bytes 2097184 | tf_op jit(solution)/shard_map/ppermute | solution.py:30
  432.0 2.7 multiply_add_fusion.2
  434.6 1.8 select_maximum_fusion
  436.4 4.8 halves.10
  441.2 3.2 copy.45
  445.5 71.3 %collective-permute-done.25.refs_2_.refs_3_ = f32[2,128,1536]{2,1,0:T(8,128)} collective-permute-done((f32[2,128,1536]{2,1,0:T(8,128)}, f32[2,128,1536]{2,1,0:T(8,128)}, u32[]{:S(2)}, u32[]{:S(2)}) %collective-permute-start.25) | collective-permute-done | bytes 1572896 | tf_op jit(solution)/shard_map/ppermute | solution.py:30
  516.9 3.9 halves.11
  522.3 2.4 add_convert_fusion.4
  526.5 5.6 %collective-permute-done.28 = f32[1,128,1536]{2,1,0:T(8,128)S(1)} collective-permute-done((f32[1,128,1536]{2,1,0:T(8,128)}, f32[1,128,1536]{2,1,0:T(8,128)S(1)}, u32[]{:S(2)}, u32[]{:S(2)}) %collective-permute-start.28) | collective-permute-done | bytes 786464 | tf_op jit(solution)/shard_map/ppermute | solution.py:30
  532.3 1.9 collective-permute-start.30
  535.1 1.9 collective-permute-done.29
  537.0 4.4 collective-permute-done.30
  542.2 2.4 multiply_add_fusion.1
  544.6 2.5 pad_maximum_fusion
  (184 shorter events, 49.8 us)
Async XLA Ops:
  8.0 273.0 %all-gather.2.cloned.1.call-start = ((), (), s32[]{:S(2)}) async-start(), calls=%async_computation.2 | async-start | bytes 7864320 | tf_op jit(solution)/shard_map/all_gather | solution.py:876
  9.2 20.0 %collective-permute-start.1 = (f32[256,1024]{1,0:T(8,128)S(1)}, f32[256,1024]{1,0:T(8,128)S(1)}, u32[]{:S(2)}, u32[]{:S(2)}) collective-permute-start(f32[256,1024]{1,0:T(8,128)S(1)} %dynamic-slice_convert_fusion), channel_id=1, source_target_pairs={{1,2},{2,1},{5,6},{6,5},{9,10},{10,9},{13,14},{14,13},{17,18},{18,... | collective-permute-start | bytes 3145736 | tf_op jit(solution)/shard_map/ppermute | solution.py:30
  14.4 14.2 %copy-start.40 = (s32[1,4]{1,0:T(1,128)S(1)}, s32[1,4]{1,0:T(1,128)}, u32[]{:S(2)}) copy-start(s32[1,4]{1,0:T(1,128)} %lengths_ref.3) | copy-start | bytes 52
  26.5 16.3 %collective-permute-start = (f32[1024,256]{1,0:T(8,128)}, f32[1024,256]{1,0:T(8,128)S(1)}, u32[]{:S(2)}, u32[]{:S(2)}) collective-permute-start(f32[1024,256]{1,0:T(8,128)} %get-tuple-element.123), channel_id=1, source_target_pairs={{1,2},{2,1},{5,6},{6,5},{9,10},{10,9},{13,14},{14,13},{17,18},{18,... | collective-permute-start | bytes 3145736 | tf_op jit(solution)/shard_map/ppermute | solution.py:30
  40.7 10.3 %copy-start.18 = (f32[1024,256]{1,0:T(8,128)S(1)}, f32[1024,256]{1,0:T(8,128)}, u32[]{:S(2)}) copy-start(f32[1024,256]{1,0:T(8,128)} %attention_forward.3) | copy-start | bytes 3145732
  42.8 5.1 copy-start.28
  47.9 27.6 %collective-permute-start.5 = (f32[1536,1024]{1,0:T(8,128)}, f32[1536,1024]{1,0:T(8,128)}, u32[]{:S(2)}, u32[]{:S(2)}) collective-permute-start(f32[1536,1024]{1,0:T(8,128)} %packed.1), channel_id=1, source_target_pairs={{0,2},{1,3},{2,0},{3,1},{4,6},{5,7},{6,4},{7,5},{8,10},{9,11},{10,... | collective-permute-start | bytes 18874376 | tf_op jit(solution)/shard_map/ppermute | solution.py:30
  47.9 15.5 %collective-permute-start.3 = (f32[256,1024]{1,0:T(8,128)S(1)}, f32[256,1024]{1,0:T(8,128)S(1)}, u32[]{:S(2)}, u32[]{:S(2)}) collective-permute-start(f32[256,1024]{1,0:T(8,128)S(1)} %collective-permute-done.1), channel_id=1, source_target_pairs={{1,5},{2,6},{5,1},{6,2},{9,13},{10,14},{13,9},{14,10},{17,21},{18,... | collective-permute-start | bytes 3145736 | tf_op jit(solution)/shard_map/ppermute | solution.py:30
  51.1 16.2 %collective-permute-start.2 = (f32[1024,256]{1,0:T(8,128)S(1)}, f32[1024,256]{1,0:T(8,128)}, u32[]{:S(2)}, u32[]{:S(2)}) collective-permute-start(f32[1024,256]{1,0:T(8,128)S(1)} %copy-done.18), channel_id=1, source_target_pairs={{1,2},{2,1},{5,6},{6,5},{9,10},{10,9},{13,14},{14,13},{17,18},{18,... | collective-permute-start | bytes 3145736 | tf_op jit(solution)/shard_map/ppermute | solution.py:30
  55.0 14.1 %copy-start.9 = (bf16[1024,256]{1,0:T(8,128)(2,1)}, bf16[1024,256]{1,0:T(8,128)(2,1)S(1)}, u32[]{:S(2)}) copy-start(bf16[1024,256]{1,0:T(8,128)(2,1)S(1)} %add_convert_fusion.6.low_ref) | copy-start | bytes 1572868
  55.0 8.6 %copy-start.19 = (bf16[512,1024]{1,0:T(8,128)(2,1)S(1)}, bf16[512,1024]{1,0:T(8,128)(2,1)}, u32[]{:S(2)}) copy-start(bf16[512,1024]{1,0:T(8,128)(2,1)} %param.25) | copy-start | bytes 3145732
  64.1 5.1 copy-start.2
  68.7 2.3 copy-start.11
  69.2 2.6 copy-start.8
  71.0 4.5 collective-permute-start.4
  72.1 21.8 %collective-permute-start.14 = (f32[256,1536]{1,0:T(8,128)S(1)}, f32[256,1536]{1,0:T(8,128)}, u32[]{:S(2)}, u32[]{:S(2)}) collective-permute-start(f32[256,1536]{1,0:T(8,128)S(1)} %convert_element_type.64), channel_id=1, source_target_pairs={{1,2},{2,1},{5,6},{6,5},{9,10},{10,9},{13,14},{14,13},{17,18},{18,... | collective-permute-start | bytes 4718600 | tf_op jit(solution)/shard_map/ppermute | solution.py:30
  93.9 338.0 %reduce-scatter.5.cloned.1.call-start = ((), (), s32[]{:S(2)}) async-start(), calls=%async_computation.3 | async-start | bytes 8912896 | tf_op jit(solution)/shard_map/reduce_scatter | solution.py:969
  94.4 25.5 %collective-permute-start.6 = (f32[256,1024]{1,0:T(8,128)}, f32[256,1024]{1,0:T(8,128)S(1)}, u32[]{:S(2)}, u32[]{:S(2)}) collective-permute-start(f32[256,1024]{1,0:T(8,128)} %get-tuple-element.133.hidden_ref), channel_id=1, source_target_pairs={{0,1},{1,0},{2,3},{3,2},{4,5},{5,4},{6,7},{7,6},{8,9},{9,8},{10,11... | collective-permute-start | bytes 3145736 | tf_op jit(solution)/shard_map/ppermute | solution.py:30
  99.0 43.4 %collective-permute-start.8 = (f32[256,1024]{1,0:T(8,128)}, f32[256,1024]{1,0:T(8,128)S(1)}, u32[]{:S(2)}, u32[]{:S(2)}) collective-permute-start(f32[256,1024]{1,0:T(8,128)} %get-tuple-element.135.hidden_ref), channel_id=1, source_target_pairs={{0,1},{1,0},{2,3},{3,2},{4,5},{5,4},{6,7},{7,6},{8,9},{9,8},{10,11... | collective-permute-start | bytes 3145736 | tf_op jit(solution)/shard_map/ppermute | solution.py:30
  130.0 34.9 %collective-permute-start.7 = (f32[256,1024]{1,0:T(8,128)}, f32[256,1024]{1,0:T(8,128)S(1)}, u32[]{:S(2)}, u32[]{:S(2)}) collective-permute-start(f32[256,1024]{1,0:T(8,128)} %get-tuple-element.142), channel_id=1, source_target_pairs={{0,1},{1,0},{2,3},{3,2},{4,5},{5,4},{6,7},{7,6},{8,9},{9,8},{10,11... | collective-permute-start | bytes 3145736 | tf_op jit(solution)/shard_map/ppermute | solution.py:30
  143.4 21.5 %copy-start.23 = (f32[256,1024]{1,0:T(8,128)S(1)}, f32[256,1024]{1,0:T(8,128)}, u32[]{:S(2)}) copy-start(f32[256,1024]{1,0:T(8,128)} %get-tuple-element.134) | copy-start | bytes 3145732
  152.5 34.8 %collective-permute-start.9 = (f32[256,1024]{1,0:T(8,128)}, f32[256,1024]{1,0:T(8,128)S(1)}, u32[]{:S(2)}, u32[]{:S(2)}) collective-permute-start(f32[256,1024]{1,0:T(8,128)} %get-tuple-element.146), channel_id=1, source_target_pairs={{0,1},{1,0},{2,3},{3,2},{4,5},{5,4},{6,7},{7,6},{8,9},{9,8},{10,11... | collective-permute-start | bytes 3145736 | tf_op jit(solution)/shard_map/ppermute | solution.py:30
  166.1 43.7 %collective-permute-start.10 = (f32[256,1024]{1,0:T(8,128)}, f32[256,1024]{1,0:T(8,128)}, u32[]{:S(2)}, u32[]{:S(2)}) collective-permute-start(f32[256,1024]{1,0:T(8,128)} %add.135.total_ref), channel_id=1, source_target_pairs={{0,1},{1,0},{2,3},{3,2},{4,5},{5,4},{6,7},{7,6},{8,9},{9,8},{10,11... | collective-permute-start | bytes 3145736 | tf_op jit(solution)/shard_map/ppermute | solution.py:30
  166.1 21.3 %copy-start.22 = (f32[256,1024]{1,0:T(8,128)S(1)}, f32[256,1024]{1,0:T(8,128)}, u32[]{:S(2)}) copy-start(f32[256,1024]{1,0:T(8,128)} %get-tuple-element.138) | copy-start | bytes 3145732
  188.5 42.6 %collective-permute-start.11 = (f32[256,1024]{1,0:T(8,128)}, f32[256,1024]{1,0:T(8,128)}, u32[]{:S(2)}, u32[]{:S(2)}) collective-permute-start(f32[256,1024]{1,0:T(8,128)} %add.136.total_ref), channel_id=1, source_target_pairs={{0,1},{1,0},{2,3},{3,2},{4,5},{5,4},{6,7},{7,6},{8,9},{9,8},{10,11... | collective-permute-start | bytes 3145736 | tf_op jit(solution)/shard_map/ppermute | solution.py:30
  249.4 7.4 %collective-permute-start.15 = (f32[1024,1024]{1,0:T(8,128)}, f32[1024,1024]{1,0:T(8,128)S(1)}, u32[]{:S(2)}, u32[]{:S(2)}) collective-permute-start(f32[1024,1024]{1,0:T(8,128)} %outer.4), channel_id=1, source_target_pairs={{0,2},{1,3},{2,0},{3,1},{4,6},{5,7},{6,4},{7,5},{8,10},{9,11},{10,... | collective-permute-start | bytes 12582920 | tf_op jit(solution)/shard_map/ppermute | solution.py:30
  275.7 271.5 %reduce-scatter.7.cloned.1.call-start = ((), (), s32[]{:S(2)}) async-start(), calls=%async_computation.4 | async-start | bytes 2785280
  275.7 28.6 %collective-permute-start.17 = (f32[256,1024]{1,0:T(8,128)}, f32[256,1024]{1,0:T(8,128)}, u32[]{:S(2)}, u32[]{:S(2)}) collective-permute-start(f32[256,1024]{1,0:T(8,128)} %get-tuple-element.164), channel_id=1, source_target_pairs={{0,1},{1,0},{2,3},{3,2},{4,5},{5,4},{6,7},{7,6},{8,9},{9,8},{10,11... | collective-permute-start | bytes 3145736 | tf_op jit(solution)/shard_map/ppermute | solution.py:30
  277.2 45.9 %collective-permute-start.16 = (f32[256,1024]{1,0:T(8,128)}, f32[256,1024]{1,0:T(8,128)}, u32[]{:S(2)}, u32[]{:S(2)}) collective-permute-start(f32[256,1024]{1,0:T(8,128)} %get-tuple-element.188), channel_id=1, source_target_pairs={{0,1},{1,0},{2,3},{3,2},{4,5},{5,4},{6,7},{7,6},{8,9},{9,8},{10,11... | collective-permute-start | bytes 3145736 | tf_op jit(solution)/shard_map/ppermute | solution.py:30
  277.4 1.7 collective-permute-start.13
  279.1 6.7 %copy-start.39 = (s32[1,5]{1,0:T(1,128)}, s32[1,5]{1,0:T(1,128)S(1)}, u32[]{:S(2)}) copy-start(s32[1,5]{1,0:T(1,128)S(1)} %fusion.14) | copy-start | bytes 64
  279.7 50.3 %collective-permute-start.19 = (f32[4,128,1024]{2,1,0:T(8,128)}, f32[4,128,1024]{2,1,0:T(8,128)}, u32[]{:S(2)}, u32[]{:S(2)}) collective-permute-start(f32[4,128,1024]{2,1,0:T(8,128)} %get-tuple-element.178), channel_id=1, source_target_pairs={{0,4},{1,5},{2,10},{3,11},{4,0},{5,1},{6,14},{7,15},{8,12},{9,13},... | collective-permute-start | bytes 6291464 | tf_op jit(solution)/shard_map/ppermute | solution.py:30
  328.9 8.6 %collective-permute-start.18 = (f32[512,1024]{1,0:T(8,128)}, f32[512,1024]{1,0:T(8,128)}, u32[]{:S(2)}, u32[]{:S(2)}) collective-permute-start(f32[512,1024]{1,0:T(8,128)} %get-tuple-element.196), channel_id=1, source_target_pairs={{0,2},{1,3},{2,0},{3,1},{4,6},{5,7},{6,4},{7,5},{8,10},{9,11},{10,... | collective-permute-start | bytes 6291464 | tf_op jit(solution)/shard_map/ppermute | solution.py:30
  330.0 6.9 %copy-start.38 = (f32[2,4,1024]{2,1,0:T(4,128)S(1)}, f32[2,4,1024]{2,1,0:T(4,128)}, u32[]{:S(2)}) copy-start(f32[2,4,1024]{2,1,0:T(4,128)} %get-tuple-element.187) | copy-start | bytes 98308
  330.0 7.5 %copy-start.13 = (f32[512,1024]{1,0:T(8,128)S(1)}, f32[512,1024]{1,0:T(8,128)}, u32[]{:S(2)}) copy-start(f32[512,1024]{1,0:T(8,128)} %get-tuple-element.196) | copy-start | bytes 6291460
  334.5 33.5 %collective-permute-start.20 = (f32[2,128,1024]{2,1,0:T(8,128)}, f32[2,128,1024]{2,1,0:T(8,128)S(1)}, u32[]{:S(2)}, u32[]{:S(2)}) collective-permute-start(f32[2,128,1024]{2,1,0:T(8,128)} %get-tuple-element.200), channel_id=1, source_target_pairs={{0,8},{1,9},{2,18},{3,19},{4,12},{5,13},{6,22},{7,23},{8,0},{9,1},... | collective-permute-start | bytes 3145736 | tf_op jit(solution)/shard_map/ppermute | solution.py:30
  337.5 2.3 copy-start.3
  339.8 2.3 copy-start.32
  339.8 2.3 copy-start.34
  369.1 3.4 copy-start.31
  373.7 2.3 copy-start.41
  374.1 7.5 %copy-start = (bf16[1024,1536]{1,0:T(8,128)(2,1)}, bf16[1024,1536]{1,0:T(8,128)(2,1)S(1)}, u32[]{:S(2)}) copy-start(bf16[1024,1536]{1,0:T(8,128)(2,1)S(1)} %constant_dynamic-update-slice_fusion.4.grad_ref) | copy-start | bytes 9437188
  388.2 8.0 %copy-start.10 = (bf16[1024,256]{1,0:T(8,128)(2,1)S(1)}, bf16[1024,256]{1,0:T(8,128)(2,1)}, u32[]{:S(2)}) copy-start(bf16[1024,256]{1,0:T(8,128)(2,1)} %copy-done.9) | copy-start | bytes 1572868
  388.2 8.0 %copy-start.12 = (bf16[1024,256]{1,0:T(8,128)(2,1)S(1)}, bf16[1024,256]{1,0:T(8,128)(2,1)}, u32[]{:S(2)}) copy-start(bf16[1024,256]{1,0:T(8,128)(2,1)} %copy-done.11) | copy-start | bytes 1572868
  388.2 48.2 %collective-permute-start.23 = (f32[4,128,1536]{2,1,0:T(8,128)}, f32[4,128,1536]{2,1,0:T(8,128)}, u32[]{:S(2)}, u32[]{:S(2)}) collective-permute-start(f32[4,128,1536]{2,1,0:T(8,128)} %get-tuple-element.212), channel_id=1, source_target_pairs={{0,4},{1,5},{2,10},{3,11},{4,0},{5,1},{6,14},{7,15},{8,12},{9,13},... | collective-permute-start | bytes 9437192 | tf_op jit(solution)/shard_map/ppermute | solution.py:30
  396.1 10.6 %collective-permute-start.21 = (f32[512,1024]{1,0:T(8,128)}, f32[512,1024]{1,0:T(8,128)S(1)}, u32[]{:S(2)}, u32[]{:S(2)}) collective-permute-start(f32[512,1024]{1,0:T(8,128)} %input_other.1), channel_id=1, source_target_pairs={{0,2},{1,3},{2,0},{3,1},{4,6},{5,7},{6,4},{7,5},{8,10},{9,11},{10,... | collective-permute-start | bytes 6291464 | tf_op jit(solution)/shard_map/ppermute | solution.py:30
  397.7 4.0 copy-start.24
  399.0 2.9 copy-start.20
  399.0 2.8 copy-start.25
  399.0 33.0 %collective-permute-start.24 = (f32[1024,512]{0,1:T(8,128)S(1)}, f32[1024,512]{0,1:T(8,128)}, u32[]{:S(2)}, u32[]{:S(2)}) collective-permute-start(f32[1024,512]{0,1:T(8,128)S(1)} %fusion.1), channel_id=1, source_target_pairs={{1,2},{2,1},{5,6},{6,5},{9,10},{10,9},{13,14},{14,13},{17,18},{18,... | collective-permute-start | bytes 6291464 | tf_op jit(solution)/shard_map/ppermute | solution.py:30
  401.8 2.3 copy-start.27
  405.8 115.7 %collective-permute-start.12 = (f32[512,1024]{1,0:T(8,128)}, f32[512,1024]{1,0:T(8,128)}, u32[]{:S(2)}, u32[]{:S(2)}) collective-permute-start(f32[512,1024]{1,0:T(8,128)} %broadcast_select_fusion.2), channel_id=1, source_target_pairs={{0,2},{1,3},{2,0},{3,1},{4,6},{5,7},{6,4},{7,5},{8,10},{9,11},{10,... | collective-permute-start | bytes 6291464 | tf_op jit(solution)/shard_map/ppermute | solution.py:30
  418.6 102.2 %collective-permute-start.22 = (f32[512,1024]{1,0:T(8,128)}, f32[512,1024]{1,0:T(8,128)}, u32[]{:S(2)}, u32[]{:S(2)}) collective-permute-start(f32[512,1024]{1,0:T(8,128)} %get-tuple-element.217), channel_id=1, source_target_pairs={{0,1},{1,0},{2,3},{3,2},{4,5},{5,4},{6,7},{7,6},{8,9},{9,8},{10,11... | collective-permute-start | bytes 6291464 | tf_op jit(solution)/shard_map/ppermute | solution.py:30
  441.2 75.6 %collective-permute-start.25 = (f32[2,128,1536]{2,1,0:T(8,128)}, f32[2,128,1536]{2,1,0:T(8,128)}, u32[]{:S(2)}, u32[]{:S(2)}) collective-permute-start(f32[2,128,1536]{2,1,0:T(8,128)} %get-tuple-element.226), channel_id=1, source_target_pairs={{0,8},{1,9},{2,18},{3,19},{4,12},{5,13},{6,22},{7,23},{8,0},{9,1},... | collective-permute-start | bytes 4718600 | tf_op jit(solution)/shard_map/ppermute | solution.py:30
  445.5 79.2 %collective-permute-start.31 = (f32[1,128,1024]{2,1,0:T(8,128)S(1)}, f32[1,128,1024]{2,1,0:T(8,128)S(1)}, u32[]{:S(2)}, u32[]{:S(2)}) collective-permute-start(f32[1,128,1024]{2,1,0:T(8,128)S(1)} %copy-done.42), channel_id=1, source_target_pairs={{0,16},{1,17},{2,6},{3,7},{4,20},{5,21},{6,2},{7,3},{8,24},{9,25},... | collective-permute-start | bytes 1572872 | tf_op jit(solution)/shard_map/ppermute | solution.py:30
  516.9 4.0 copy-start.14
  520.7 11.3 %collective-permute-start.28 = (f32[1,128,1536]{2,1,0:T(8,128)}, f32[1,128,1536]{2,1,0:T(8,128)S(1)}, u32[]{:S(2)}, u32[]{:S(2)}) collective-permute-start(f32[1,128,1536]{2,1,0:T(8,128)} %get-tuple-element.228), channel_id=1, source_target_pairs={{0,16},{1,17},{2,6},{3,7},{4,20},{5,21},{6,2},{7,3},{8,24},{9,25},... | collective-permute-start | bytes 2359304 | tf_op jit(solution)/shard_map/ppermute | solution.py:30
  521.4 3.4 copy-start.37
  521.4 20.8 %collective-permute-start.26 = (f32[512,1024]{1,0:T(8,128)S(1)}, f32[512,1024]{1,0:T(8,128)S(1)}, u32[]{:S(2)}, u32[]{:S(2)}) collective-permute-start(f32[512,1024]{1,0:T(8,128)S(1)} %broadcast_select_fusion), channel_id=1, source_target_pairs={{0,2},{1,3},{2,0},{3,1},{4,6},{5,7},{6,4},{7,5},{8,10},{9,11},{10,... | collective-permute-start | bytes 6291464 | tf_op jit(solution)/shard_map/ppermute | solution.py:30
  524.9 9.4 %collective-permute-start.32 = (f32[64,1024]{1,0:T(8,128)S(1)}, f32[64,1024]{1,0:T(8,128)S(1)}, u32[]{:S(2)}, u32[]{:S(2)}) collective-permute-start(f32[64,1024]{1,0:T(8,128)S(1)} %dynamic-slice_bitcast_fusion.1), channel_id=1, source_target_pairs={{0,2},{1,3},{2,0},{3,1},{4,6},{5,7},{6,4},{7,5},{8,10},{9,11},{10,... | collective-permute-start | bytes 786440 | tf_op jit(solution)/shard_map/ppermute | solution.py:30
  524.9 7.1 %copy-start.36 = (f32[1,128,1536]{2,1,0:T(8,128)S(1)}, f32[1,128,1536]{2,1,0:T(8,128)}, u32[]{:S(2)}) copy-start(f32[1,128,1536]{2,1,0:T(8,128)} %get-tuple-element.230) | copy-start | bytes 2359300
  532.3 4.7 collective-permute-start.29
  532.3 9.1 %collective-permute-start.30 = (f32[64,1536]{1,0:T(8,128)S(1)}, f32[64,1536]{1,0:T(8,128)S(1)}, u32[]{:S(2)}, u32[]{:S(2)}) collective-permute-start(f32[64,1536]{1,0:T(8,128)S(1)} %get-tuple-element.259), channel_id=1, source_target_pairs={{1,2},{2,1},{5,6},{6,5},{9,10},{10,9},{13,14},{14,13},{17,18},{18,... | collective-permute-start | bytes 1179656 | tf_op jit(solution)/shard_map/ppermute | solution.py:30
  548.0 3.2 collective-permute-start.27
  (15 other events, 22.0 us)
Sparse Core Ops, SparseCore 0:
  94.0 112.4 all-gather.1
Sparse Core Ops, SparseCore 1:
  275.8 108.5 reduce-scatter.4
  444.6 71.8 reduce-scatter.6

commit v4 on v3

--- a/solution.py
+++ b/solution.py
@@ -820,7 +820,7 @@
     wide = w_query.shape[1]
     hidden = w_up.shape[1]
 
-    shares = min(2, levels)
+    shares = min(3, levels)
     near = flat_pairs(dp_size, lambda d, c, t: (d ^ 2, t) if c != t else None)
 
     orders = (list(range(levels)), [*range(1, levels), 0])
@@ -830,6 +830,8 @@
         hop_facts.append(jnp.where(core == 0, places[0], places[1]))
         hop_facts.append(jnp.where(core == 0, bits[orders[0][step]], bits[orders[1][step]]))
     hops = [flat_pairs(dp_size, lambda d, c, t: (d ^ (2 << orders[c][step]), t)) for step in range(levels)]
+    for bit in bits:
+        hop_facts += [jnp.zeros_like(bit), bit]
     where_own = jnp.stack([core, same.astype(jnp.int32), *hop_facts])
     where_peer = jnp.stack([core, 1 - same.astype(jnp.int32)])
     out_rows = wide // 2
@@ -937,16 +939,17 @@
     small = chip_rows // 2
 
     class Sum:
-        def __init__(self, held, arrived):
+        def __init__(self, held, arrived, plain=False):
+            self.plain = plain
             self.held = [part.reshape(chips, chip_rows, -1) for part in held]
             self.arrived = [] if arrived is None else [arrived.reshape(chips, chip_rows, -1)]
-            self.sources = [None if arrived is None else (0, 0)] * len(held)
+            self.sources = [None if arrived is None or number else (0, 0) for number in range(len(held))]
             self.step = 0
 
         def hop(self, *gates):
             arrived = [after(array, *gates) for array in self.arrived]
-            self.held, leaving = halves(where_own, self.step, self.held, arrived, tuple(self.sources))
-            self.arrived = [send(leaving, hops[self.step])]
+            self.held, leaving = halves(where_own, self.step + levels * self.plain, self.held, arrived, tuple(self.sources))
+            self.arrived = [send(leaving, (flips if self.plain else hops)[self.step])]
             starts = np.cumsum([0, *(part.shape[2] for part in self.held)])
             self.sources = [(0, int(start)) for start in starts[:-1]]
             self.step += 1
@@ -1011,20 +1014,29 @@
         where_own, grads, weights_mine, after(other_sent, gate), block_in, there, grad_res, norm_in_attn
     )
     grad_in_sent = send(grad_in_own, over)
-    gains = jnp.stack([gain_in_attn[0], gain_out_attn, gain_in_mlp, gain_out_mlp], axis=1)
+    gains = jnp.stack([gain_in_attn[0], gain_out_attn, gain_in_mlp, gain_out_mlp], axis=0)
     weight_out_sent, gains = after((weight_out_sent, gains), grad_up)
-    others = jnp.concatenate(
-        [weight_out * keep + weight_out_sent, jnp.pad(gains, ((0, 0), (0, LANES - gains.shape[1])))], axis=1
-    )
-    gate = late.hop(grad_in_own, others)
-    others = lax.psum_scatter(others, "dp", scatter_dimension=0, tiled=True)
+    gains = jnp.pad((gains + send(gains, cross)).T, ((0, 0), (0, LANES - 4)))
+    weight_out = weight_out * keep + weight_out_sent
+    out_sent = send(half_columns(weight_out, 1 - core, out_rows), cross)
+    extra = Sum([half_columns(weight_out, core, out_rows), gains], out_sent, plain=True)
+    gate = late.hop(weight_out)
+    gate = extra.hop(gate)
+    gate = extra.hop(gate)
     gate = late.hop(gate)
+    gate = extra.hop(gate)
     [grad_down] = early.result(gate)
     [held] = late.result(gate)
-
-    def to_core(held):
-        arrived = send(half_of(held, 1 - core, small), cross)
-        return ordered(half_of(held, core, small), arrived, core, 1)
+    grad_out, gains = extra.result()
+
+    def to_core(*parts):
+        leaving = jnp.concatenate([half_of(part, 1 - core, small) for part in parts], axis=1)
+        arrived, start, results = send(leaving, cross), 0, []
+        for part in parts:
+            columns = part.shape[1]
+            results.append(ordered(half_of(part, core, small), arrived[:, start : start + columns], core, 1))
+            start += columns
+        return results
 
     def to_output(values_own, values_peer):
         stay = jnp.where(same, values_own, values_peer)
@@ -1034,7 +1046,7 @@
         high = arrived * first + stay * (1.0 - first)
         return jnp.concatenate([low, high], axis=0)
 
-    grad_down = to_core(grad_down).T
+    grad_down, grad_out = to_core(grad_down, grad_out)
     grad_in = to_output(grad_in_own, after(grad_in_sent, gate))
     for_core = half_of(held, core, small)
     for_other = half_of(held, 1 - core, small)
@@ -1044,7 +1056,7 @@
         flat_pairs(dp_size, lambda d, c, t: (d, 1 - t) if c != t else (d ^ 1, t)),
     )
     heads = straight + jnp.where(same, for_core, diagonal)
-    gains = others[:, wide:].T
+    gains = half_of(gains, core, small)[:, :4].T
     gains = gains + send(gains, over)
     block_out = to_output(jnp.concatenate(blocks[:2], axis=0), jnp.concatenate(blocks[2:], axis=0)).astype(bf16)
     return (
@@ -1054,11 +1066,11 @@
         heads[:, :wide],
         heads[:, wide : 2 * wide],
         heads[:, 2 * wide : 3 * wide],
-        others[:, :wide].T,
+        grad_out.T,
         gains[1],
         gains[2],
         grad_up,
-        grad_down,
+        grad_down.T,
         gains[3],
     )
 

time: 570 us -> 550 us (0.965)
  waiting for transfers between devices: 195 us -> 148 us
  starting transfers between devices: 31.3 us -> 52.2 us
  Pallas kernels: 246 us -> 256 us
    ppermute x33 -> x38, waiting for transfers between devices: 195 us -> 147 us  [send(): return lax.ppermute(values, ('dp', 'tensor'), pairs)]
    ppermute x33 -> x38, starting transfers between devices: 30.8 us -> 51.9 us  [send(): return lax.ppermute(values, ('dp', 'tensor'), pairs)]
    pallas_call x6 -> x9, Pallas kernels: 29.6 us -> 39.3 us  [halves(): pl.pallas_call(partial(halves_kernel, len(held), sources), grid_spec=pltp...]
    unnamed x92 -> x87, local copies, waits for them, and re-layouts: 18.3 us -> 12.9 us
  transfers between devices with their start and end apart: 36 -> 40, of which waited for: 20 -> 20; matrix products, arithmetic and copies ran while one was open for 9% -> 9% of each run, Pallas kernels for 43% -> 46%
where the time goes in v4:
time: 550 us; the launch traced here: 542 us
  Pallas kernels  256 us (47%)
  waiting for transfers between devices  148 us (27%)
  starting transfers between devices  52.2 us (9%)
  other arithmetic  35.5 us (6%)
  local copies, waits for them, and re-layouts  20.8 us (4%)
  between operations  17.3 us (3%)
  matrix products  12.6 us (2%)
    ppermute x38, waiting for transfers between devices, send(): return lax.ppermute(values, ('dp', 'tensor'), pairs)  147 us
    pallas_call x14, Pallas kernels, call(): pl.pallas_call(kernel, grid_spec=pltpu.PrefetchScalarGridSpec(num_scalar_...  113 us
    ppermute x38, starting transfers between devices, send(): return lax.ppermute(values, ('dp', 'tensor'), pairs)  51.9 us
    pallas_call x9, Pallas kernels, halves(): pl.pallas_call(partial(halves_kernel, len(held), sources), grid_spec=pltp...  39.3 us
    pallas_call x1, Pallas kernels, attention_backward(): pl.pallas_call(partial(backward_kernel, lengths.shape[1]), grid=(pairs,),...  25.8 us
    pallas_call x3, Pallas kernels, outer(): pl.pallas_call(outer_kernel, grid_spec=pltpu.PrefetchScalarGridSpec(num_s...  24.8 us
    pallas_call x2, Pallas kernels, attention_forward(): pl.pallas_call(partial(forward_kernel, lengths.shape[1], first), grid=(1,...  23.5 us
    pallas_call x1, Pallas kernels, attention_ready(): pl.pallas_call(partial(ready_kernel, lengths.shape[1]), grid=(wide // gro...  18.6 us
  transfers between devices with their start and end apart: 40, of which 20 were waited for; matrix products, arithmetic and copies ran while one was open for 9% of the time, Pallas kernels for 46%

profile of v4, /device:TPU:1, one launch (start us, length us, event | category | flops | bytes accessed | tf_op | source)
XLA Modules:
  0.0 541.9 jit_solution(3694189340532089283)
XLA Ops:
  9.2 4.5 collective-permute-start.1
  14.4 12.0 %attention_forward.2 = (f32[1024,256]{1,0:T(8,128)}, bf16[1024,1024]{1,0:T(8,128)(2,1)}, f32[1024,128]{1,0:T(8,128)}, f32[1024,128]{1,0:T(8,128)}) custom-call(s32[1,4]{1,0:T(1,128)} %lengths_ref.3, s32[1]{0:T(128)S(6)} %copy.65.pad_ref, f32[32,1]{1,0:T(8,128)} %constant.55.clone.freq_ref, f32[1,1024]{1,0:T(1,128)} %bitcast.75, ...), custom_call_target="tpu_custom_call" | custom-call | flops 1 | bytes 1 | tf_op jit(solution)/shard_map/attention_forward/pallas_call | solution.py:278
  26.5 2.1 collective-permute-start
  29.2 11.5 %attention_forward.3 = f32[1024,256]{1,0:T(8,128)} custom-call(s32[1,4]{1,0:T(1,128)} %lengths_ref.3, s32[1]{0:T(128)S(6)} %copy.65.pad_ref, f32[32,1]{1,0:T(8,128)} %constant.55.clone.freq_ref, f32[1,1024]{1,0:T(1,128)} %bitcast.76, bf16[1024,1024]{1,0:T(8,128)(2,1)} %get-tuple-element.139.refs_0_, f32[1024,128]{1,0:T(8,128)} %get-tuple-element.140.refs_1_, ...), custom_call_target="tpu_custom_call" | custom-call | flops 1 | bytes 1 | tf_op jit(solution)/shard_map/attention_forward/pallas_call | solution.py:278
  42.8 5.1 packed.1
  47.9 3.1 collective-permute-start.3
  51.1 2.2 collective-permute-start.2
  55.0 8.5 %collective-permute-done.3 = f32[256,1024]{1,0:T(8,128)S(1)} collective-permute-done((f32[256,1024]{1,0:T(8,128)S(1)}, f32[256,1024]{1,0:T(8,128)S(1)}, u32[]{:S(2)}, u32[]{:S(2)}) %collective-permute-start.3) | collective-permute-done | bytes 1048608 | tf_op jit(solution)/shard_map/ppermute | solution.py:30
  64.1 3.2 collective-permute-done.2
  71.9 2.2 collective-permute-start.14
  75.5 4.5 hidden.2
  80.0 5.3 collective-permute-done.14
  85.7 4.5 hidden.3
  91.7 9.3 %mlp_forward.4 = (bf16[1024,1024]{1,0:T(8,128)(2,1)}, bf16[1024,2048]{1,0:T(8,128)(2,1)}, f32[256,2048]{1,0:T(8,128)}, f32[256,1024]{1,0:T(8,128)}) custom-call(f32[256,1024]{1,0:T(8,128)} %get-tuple-element.145.hidden_ref, f32[1,1024]{1,0:T(1,128)} %bitcast.69, bf16[1024,2048]{1,0:T(8,128)(2,1)} %up_ref.15, bf16[2048,1024]{1,0:T(8,128)(2,1)} %down_ref.15), custom_call_target="tpu_custom_call" | custom-call | flops 1 | bytes 1 | tf_op jit(solution)/shard_map/mlp_forward/pallas_call | solution.py:521
  101.0 9.1 %mlp_forward.5 = (bf16[1024,1024]{1,0:T(8,128)(2,1)}, bf16[1024,2048]{1,0:T(8,128)(2,1)}, f32[256,2048]{1,0:T(8,128)}, f32[256,1024]{1,0:T(8,128)}) custom-call(f32[256,1024]{1,0:T(8,128)} %get-tuple-element.147.hidden_ref, f32[1,1024]{1,0:T(1,128)} %bitcast.70, bf16[1024,2048]{1,0:T(8,128)(2,1)} %up_ref.15, ...), custom_call_target="tpu_custom_call", output_to_operand_aliasing={{0}: (4, {}), {1}: (5, {})} | custom-call | flops 1 | bytes 1 | tf_op jit(solution)/shard_map/mlp_forward/pallas_call | solution.py:521
  112.1 9.0 %mlp_forward.6 = (bf16[1024,1024]{1,0:T(8,128)(2,1)}, bf16[1024,2048]{1,0:T(8,128)(2,1)}, f32[256,2048]{1,0:T(8,128)}, f32[256,1024]{1,0:T(8,128)}) custom-call(f32[256,1024]{1,0:T(8,128)} %copy-done.15, f32[1,1024]{1,0:T(1,128)} %bitcast.71, bf16[1024,2048]{1,0:T(8,128)(2,1)} %up_ref.15, ...), custom_call_target="tpu_custom_call", output_to_operand_aliasing={{0}: (4, {}), {1}: (5, {})} | custom-call | flops 1 | bytes 1 | tf_op jit(solution)/shard_map/mlp_forward/pallas_call | solution.py:521
  121.2 12.5 %collective-permute-done.8.hidden_ref = f32[256,1024]{1,0:T(8,128)S(1)} collective-permute-done((f32[256,1024]{1,0:T(8,128)}, f32[256,1024]{1,0:T(8,128)S(1)}, u32[]{:S(2)}, u32[]{:S(2)}) %collective-permute-start.8) | collective-permute-done | bytes 1048608 | tf_op jit(solution)/shard_map/ppermute | solution.py:30
  134.6 9.1 %mlp_forward.7 = (bf16[1024,1024]{1,0:T(8,128)(2,1)}, bf16[1024,2048]{1,0:T(8,128)(2,1)}, f32[256,2048]{1,0:T(8,128)}, f32[256,1024]{1,0:T(8,128)}) custom-call(f32[256,1024]{1,0:T(8,128)} %copy-done.14, f32[1,1024]{1,0:T(1,128)} %bitcast.72, bf16[1024,2048]{1,0:T(8,128)(2,1)} %up_ref.15, ...), custom_call_target="tpu_custom_call", output_to_operand_aliasing={{0}: (4, {}), {1}: (5, {})} | custom-call | flops 1 | bytes 1 | tf_op jit(solution)/shard_map/mlp_forward/pallas_call | solution.py:521
  143.9 12.3 %collective-permute-done.7 = f32[256,1024]{1,0:T(8,128)S(1)} collective-permute-done((f32[256,1024]{1,0:T(8,128)}, f32[256,1024]{1,0:T(8,128)S(1)}, u32[]{:S(2)}, u32[]{:S(2)}) %collective-permute-start.7) | collective-permute-done | bytes 1048608 | tf_op jit(solution)/shard_map/ppermute | solution.py:30
  157.3 11.2 %mlp_backward.4 = (f32[256,1024]{1,0:T(8,128)}, bf16[1024,1024]{1,0:T(8,128)(2,1)}, f32[8,1024]{1,0:T(8,128)}, bf16[1024,2048]{1,0:T(8,128)(2,1)}, f32[256,1024]{1,0:T(8,128)}) custom-call(s32[14]{0:T(128)} %stack.54.where_ref, f32[256,1024]{1,0:T(8,128)} %get-tuple-element.145.hidden_ref, f32[256,1024]{1,0:T(8,128)} %add.127.total_ref, ...), custom_call_target="tpu_custom_call" | custom-call | flops 1 | bytes 1 | tf_op jit(solution)/shard_map/mlp_backward/pallas_call | solution.py:521
  168.5 10.1 %collective-permute-done.9 = f32[256,1024]{1,0:T(8,128)S(1)} collective-permute-done((f32[256,1024]{1,0:T(8,128)}, f32[256,1024]{1,0:T(8,128)S(1)}, u32[]{:S(2)}, u32[]{:S(2)}) %collective-permute-start.9) | collective-permute-done | bytes 1048608 | tf_op jit(solution)/shard_map/ppermute | solution.py:30
  180.4 11.0 %mlp_backward.5 = (f32[256,1024]{1,0:T(8,128)}, bf16[1024,1024]{1,0:T(8,128)(2,1)}, f32[8,1024]{1,0:T(8,128)}, bf16[1024,2048]{1,0:T(8,128)(2,1)}, f32[256,1024]{1,0:T(8,128)}) custom-call(s32[14]{0:T(128)} %stack.54.where_ref, f32[256,1024]{1,0:T(8,128)} %get-tuple-element.147.hidden_ref, ...), custom_call_target="tpu_custom_call", output_to_operand_aliasing={{1}: (9, {}), {3}: (10, {})} | custom-call | flops 1 | bytes 1 | tf_op jit(solution)/shard_map/mlp_backward/pallas_call | solution.py:521
  191.4 9.7 %collective-permute-done.10.total_ref = f32[256,1024]{1,0:T(8,128)} collective-permute-done((f32[256,1024]{1,0:T(8,128)}, f32[256,1024]{1,0:T(8,128)}, u32[]{:S(2)}, u32[]{:S(2)}) %collective-permute-start.10) | collective-permute-done | bytes 1048608 | tf_op jit(solution)/shard_map/ppermute | solution.py:30
  201.0 11.0 %mlp_backward.6 = (f32[256,1024]{1,0:T(8,128)}, bf16[1024,1024]{1,0:T(8,128)(2,1)}, f32[8,1024]{1,0:T(8,128)}, bf16[1024,2048]{1,0:T(8,128)(2,1)}, f32[256,1024]{1,0:T(8,128)}) custom-call(s32[2]{0:T(128)} %pad_add_fusion.where_ref, f32[256,1024]{1,0:T(8,128)} %copy-done.15, ...), custom_call_target="tpu_custom_call", output_to_operand_aliasing={{1}: (9, {}), {3}: (10, {})} | custom-call | flops 1 | bytes 1 | tf_op jit(solution)/shard_map/mlp_backward/pallas_call | solution.py:521
  212.0 10.4 %collective-permute-done.11.total_ref = f32[256,1024]{1,0:T(8,128)} collective-permute-done((f32[256,1024]{1,0:T(8,128)}, f32[256,1024]{1,0:T(8,128)}, u32[]{:S(2)}, u32[]{:S(2)}) %collective-permute-start.11) | collective-permute-done | bytes 1048608 | tf_op jit(solution)/shard_map/ppermute | solution.py:30
  222.4 11.3 %mlp_backward.7 = (f32[256,1024]{1,0:T(8,128)}, bf16[1024,1024]{1,0:T(8,128)(2,1)}, f32[8,1024]{1,0:T(8,128)}, bf16[1024,2048]{1,0:T(8,128)(2,1)}, f32[256,1024]{1,0:T(8,128)}) custom-call(s32[2]{0:T(128)} %pad_add_fusion.where_ref, f32[256,1024]{1,0:T(8,128)} %copy-done.14, ...), custom_call_target="tpu_custom_call", output_to_operand_aliasing={{1}: (9, {}), {3}: (10, {})} | custom-call | flops 1 | bytes 1 | tf_op jit(solution)/shard_map/mlp_backward/pallas_call | solution.py:521
  233.7 7.1 %outer.4 = f32[1024,1024]{1,0:T(8,128)} custom-call(s32[14]{0:T(128)} %stack.54.where_ref, bf16[1024,1024]{1,0:T(8,128)(2,1)} %get-tuple-element.187.left_ref, bf16[1024,2048]{1,0:T(8,128)(2,1)} %get-tuple-element.188.right_ref), custom_call_target="tpu_custom_call" | custom-call | flops 1 | bytes 1 | tf_op jit(solution)/shard_map/outer/pallas_call | solution.py:666
  240.8 7.2 %outer.3 = f32[1024,1024]{1,0:T(8,128)} custom-call(s32[14]{0:T(128)} %stack.54.where_ref, bf16[1024,1024]{1,0:T(8,128)(2,1)} %get-tuple-element.187.left_ref, bf16[1024,2048]{1,0:T(8,128)(2,1)} %get-tuple-element.188.right_ref), custom_call_target="tpu_custom_call" | custom-call | flops 1 | bytes 1 | tf_op jit(solution)/shard_map/outer/pallas_call | solution.py:666
  250.2 6.4 %halves.9 = (f32[4,128,1024]{2,1,0:T(8,128)}, f32[4,128,1024]{2,1,0:T(8,128)}) custom-call(s32[14]{0:T(128)} %stack.54.where_ref, f32[8,128,1024]{2,1,0:T(8,128)} %bitcast.57, f32[8,128,1024]{2,1,0:T(8,128)} %bitcast.58, f32[8,128,1024]{2,1,0:T(8,128)} %bitcast.61, f32[8,128,1024]{2,1,0:T(8,128)} %bitcast.62), custom_call_target="tpu_custom_call" | custom-call | flops 1 | bytes 1 | tf_op jit(solution)/shard_map/halves/pallas_call | solution.py:721
  256.6 10.5 %outer.5 = f32[1024,2048]{1,0:T(8,128)} custom-call(s32[14]{0:T(128)} %stack.54.where_ref, bf16[1024,1024]{1,0:T(8,128)(2,1)} %get-tuple-element.191.left_ref, bf16[1024,2048]{1,0:T(8,128)(2,1)} %get-tuple-element.192.right_ref), custom_call_target="tpu_custom_call" | custom-call | flops 1 | bytes 1 | tf_op jit(solution)/shard_map/outer/pallas_call | solution.py:666
  272.4 4.8 add_convert_fusion.wq_ref.wk_ref.wv_ref.weight_ref
  277.2 18.6 %attention_ready.1 = (bf16[1024,512]{1,0:T(8,128)(2,1)}, bf16[1024,512]{1,0:T(8,128)(2,1)}, bf16[1024,512]{1,0:T(8,128)(2,1)}, f32[2,4,1024]{2,1,0:T(4,128)}, bf...) custom-call(s32[14]{0:T(128)} %stack.54.where_ref, s32[1,4]{1,0:T(1,128)} %bitcast.87, ...), custom_call_target="tpu_custom_call" | custom-call | flops 1 | bytes 1 | tf_op jit(solution)/shard_map/attention_ready/pallas_call | solution.py:304
  295.9 5.9 %residual.2 = (f32[512,1024]{1,0:T(8,128)}, f32[512,1024]{1,0:T(8,128)}, f32[8,1024]{1,0:T(8,128)}) custom-call(s32[14]{0:T(128)} %stack.54.where_ref, f32[256,1024]{1,0:T(8,128)} %get-tuple-element.163.part_ref, f32[256,1024]{1,0:T(8,128)} %collective-permute-done.17.arrived_ref, f32[256,1024]{1,0:T(8,128)} %get-tuple-element.145.hidden_ref, ...), custom_call_target="tpu_custom_call" | custom-call | flops 1 | bytes 1 | tf_op jit(solution)/shard_map/residual/pallas_call | solution.py:521
  301.8 12.7 %collective-permute-done.16.arrived_ref = f32[256,1024]{1,0:T(8,128)} collective-permute-done((f32[256,1024]{1,0:T(8,128)}, f32[256,1024]{1,0:T(8,128)}, u32[]{:S(2)}, u32[]{:S(2)}) %collective-permute-start.16) | collective-permute-done | bytes 1048608 | tf_op jit(solution)/shard_map/ppermute | solution.py:30
  314.4 5.8 %residual.3 = (f32[512,1024]{1,0:T(8,128)}, f32[512,1024]{1,0:T(8,128)}, f32[8,1024]{1,0:T(8,128)}) custom-call(s32[14]{0:T(128)} %stack.54.where_ref, f32[256,1024]{1,0:T(8,128)} %get-tuple-element.170.part_ref, f32[256,1024]{1,0:T(8,128)} %collective-permute-done.16.arrived_ref, ...), custom_call_target="tpu_custom_call", output_to_operand_aliasing={{0}: (9, {}), {1}: (10, {})} | custom-call | flops 1 | bytes 1 | tf_op jit(solution)/shard_map/residual/pallas_call | solution.py:521
  321.4 4.4 halves.10
  325.8 2.4 collective-permute-start.20
  329.9 2.4 add_convert_fusion.2
  332.2 2.3 convolution_convert_fusion.grad_ref
  334.5 25.8 %attention_backward.1 = (bf16[1024,512]{1,0:T(8,128)(2,1)}, bf16[1024,512]{1,0:T(8,128)(2,1)}, bf16[1024,512]{1,0:T(8,128)(2,1)}) custom-call(s32[1,4]{1,0:T(1,128)} %bitcast.88, s32[1]{0:T(128)} %bitcast.15.pad_ref, f32[1024,128]{1,0:T(8,128)} %get-tuple-element.194.cos_ref, f32[1024,128]{1,0:T(8,128)} %get-tuple-element.195.sin_ref, ...), custom_call_target="tpu_custom_call" | custom-call | flops 1 | bytes 1 | tf_op jit(solution)/shard_map/attention_backward/pallas_call | solution.py:333
  360.3 3.4 halves.11
  367.2 5.5 %fusion.20 = f32[1024,1536]{1,0:T(8,128)} fusion(bf16[1024,1024]{1,0:T(8,128)(2,1)S(1)} %copy-done.39, bf16[1024,1536]{1,0:T(8,128)(2,1)S(1)} %constant_dynamic-update-slice_fusion.4.grad_ref), kind=kOutput, calls=%fused_computation.81 | convolution fusion | flops 3221225472 | bytes 11534336 | tf_op jit(solution)/shard_map/td,te->de/dot_general | solution.py:1005
  372.7 6.5 %halves.12 = (f32[4,128,1536]{2,1,0:T(8,128)}, f32[4,128,1536]{2,1,0:T(8,128)}) custom-call(s32[14]{0:T(128)} %stack.54.where_ref, f32[8,128,1536]{2,1,0:T(8,128)} %bitcast.59, f32[8,128,1536]{2,1,0:T(8,128)} %bitcast.60), custom_call_target="tpu_custom_call" | custom-call | flops 1 | bytes 1 | tf_op jit(solution)/shard_map/halves/pallas_call | solution.py:721
  379.3 6.7 %input_other.1 = f32[512,1024]{1,0:T(8,128)} custom-call(s32[14]{0:T(128)} %stack.54.where_ref, bf16[1024,1536]{1,0:T(8,128)(2,1)} %copy-done, bf16[1024,1536]{1,0:T(8,128)(2,1)} %add_convert_fusion.wq_ref.wk_ref.wv_ref.weight_ref), custom_call_target="tpu_custom_call" | custom-call | flops 1 | bytes 1 | tf_op jit(solution)/shard_map/input_other/pallas_call | solution.py:521
  386.0 2.6 fusion.1
  388.6 4.2 collective-permute-start.23
  399.0 10.5 %input_own.1 = (f32[512,1024]{1,0:T(8,128)}, f32[8,1024]{1,0:T(8,128)}) custom-call(s32[14]{0:T(128)} %stack.54.where_ref, bf16[1024,1536]{1,0:T(8,128)(2,1)} %copy-done, bf16[1024,1536]{1,0:T(8,128)(2,1)} %add_convert_fusion.wq_ref.wk_ref.wv_ref.weight_ref, f32[512,1024]{1,0:T(8,128)} %collective-permute-done.21.arrived_ref, bf16[1024,1024]{1,0:T(8,128)(2,1)} %here_ref.19, ...), custom_call_target="tpu_custom_call" | custom-call | flops 1 | bytes 1 | tf_op jit(solution)/shard_map/input_own/pallas_call | solution.py:759
  410.3 6.5 %collective-permute-done.23 = f32[1024,512]{1,0:T(8,128)} collective-permute-done((f32[1024,512]{1,0:T(8,128)}, f32[1024,512]{1,0:T(8,128)}, u32[]{:S(2)}, u32[]{:S(2)}) %collective-permute-start.23) | collective-permute-done | bytes 2097184 | tf_op jit(solution)/shard_map/ppermute | solution.py:30
  416.8 2.7 multiply_add_fusion.2
  422.9 6.6 %collective-permute-done.26.refs_2_.refs_3_ = f32[4,128,1536]{2,1,0:T(8,128)} collective-permute-done((f32[4,128,1536]{2,1,0:T(8,128)}, f32[4,128,1536]{2,1,0:T(8,128)}, u32[]{:S(2)}, u32[]{:S(2)}) %collective-permute-start.26) | collective-permute-done | bytes 3145760 | tf_op jit(solution)/shard_map/ppermute | solution.py:30
  429.5 4.8 halves.13
  439.1 4.5 halves.14
  443.9 19.1 %collective-permute-done.27.refs_4_.refs_5_ = f32[4,128,384]{2,1,0:T(8,128)S(1)} collective-permute-done((f32[4,128,384]{2,1,0:T(8,128)}, f32[4,128,384]{2,1,0:T(8,128)S(1)}, u32[]{:S(2)}, u32[]{:S(2)}) %collective-permute-start.27) | collective-permute-done | bytes 786464 | tf_op jit(solution)/shard_map/ppermute | solution.py:30
  463.8 2.9 halves.15
  467.6 2.4 add_convert_fusion.4
  471.6 3.8 halves.16
  476.8 7.2 %collective-permute-done.28.refs_4_.refs_5_ = f32[2,128,384]{2,1,0:T(8,128)S(1)} collective-permute-done((f32[2,128,384]{2,1,0:T(8,128)}, f32[2,128,384]{2,1,0:T(8,128)S(1)}, u32[]{:S(2)}, u32[]{:S(2)}) %collective-permute-start.28) | collective-permute-done | bytes 393248 | tf_op jit(solution)/shard_map/ppermute | solution.py:30
  484.7 2.6 halves.17
  490.9 11.9 %collective-permute-done.31 = f32[1,128,384]{2,1,0:T(8,128)S(1)} collective-permute-done((f32[1,128,384]{2,1,0:T(8,128)}, f32[1,128,384]{2,1,0:T(8,128)S(1)}, u32[]{:S(2)}, u32[]{:S(2)}) %collective-permute-start.31) | collective-permute-done | bytes 196640 | tf_op jit(solution)/shard_map/ppermute | solution.py:30
  503.7 9.1 %collective-permute-start.37 = (f32[64,1280]{1,0:T(8,128)S(1)}, f32[64,1280]{1,0:T(8,128)S(1)}, u32[]{:S(2)}, u32[]{:S(2)}) collective-permute-start(f32[64,1280]{1,0:T(8,128)S(1)} %pad_maximum_fusion.7), channel_id=1, source_target_pairs={{0,2},{1,3},{2,0},{3,1},{4,6},{5,7},{6,4},{7,5},{8,10},{9,11},{10,... | collective-permute-start | bytes 983048 | tf_op jit(solution)/shard_map/ppermute | solution.py:30
  514.9 5.5 %collective-permute-start.35 = (f32[64,1536]{1,0:T(8,128)S(1)}, f32[64,1536]{1,0:T(8,128)S(1)}, u32[]{:S(2)}, u32[]{:S(2)}) collective-permute-start(f32[64,1536]{1,0:T(8,128)S(1)} %get-tuple-element.263), channel_id=1, source_target_pairs={{1,2},{2,1},{5,6},{6,5},{9,10},{10,9},{13,14},{14,13},{17,18},{18,... | collective-permute-start | bytes 1179656 | tf_op jit(solution)/shard_map/ppermute | solution.py:30
  522.1 6.2 %collective-permute-done.35 = f32[64,1536]{1,0:T(8,128)S(1)} collective-permute-done((f32[64,1536]{1,0:T(8,128)S(1)}, f32[64,1536]{1,0:T(8,128)S(1)}, u32[]{:S(2)}, u32[]{:S(2)}) %collective-permute-start.35) | collective-permute-done | bytes 393248 | tf_op jit(solution)/shard_map/ppermute | solution.py:30
  529.1 2.4 multiply_add_fusion.1
  531.5 2.5 pad_maximum_fusion
  (197 shorter events, 63.8 us)
Async XLA Ops:
  8.0 264.4 %all-gather.2.cloned.1.call-start = ((), (), s32[]{:S(2)}) async-start(), calls=%async_computation.1 | async-start | bytes 7077888 | tf_op jit(solution)/shard_map/all_gather | solution.py:878
  9.2 20.0 %collective-permute-start.1 = (f32[256,1024]{1,0:T(8,128)S(1)}, f32[256,1024]{1,0:T(8,128)S(1)}, u32[]{:S(2)}, u32[]{:S(2)}) collective-permute-start(f32[256,1024]{1,0:T(8,128)S(1)} %dynamic-slice_convert_fusion), channel_id=1, source_target_pairs={{1,2},{2,1},{5,6},{6,5},{9,10},{10,9},{13,14},{14,13},{17,18},{18,... | collective-permute-start | bytes 3145736 | tf_op jit(solution)/shard_map/ppermute | solution.py:30
  14.4 14.2 %copy-start.38 = (s32[1,4]{1,0:T(1,128)S(1)}, s32[1,4]{1,0:T(1,128)}, u32[]{:S(2)}) copy-start(s32[1,4]{1,0:T(1,128)} %lengths_ref.3) | copy-start | bytes 52
  26.5 16.3 %collective-permute-start = (f32[1024,256]{1,0:T(8,128)}, f32[1024,256]{1,0:T(8,128)S(1)}, u32[]{:S(2)}, u32[]{:S(2)}) collective-permute-start(f32[1024,256]{1,0:T(8,128)} %get-tuple-element.135), channel_id=1, source_target_pairs={{1,2},{2,1},{5,6},{6,5},{9,10},{10,9},{13,14},{14,13},{17,18},{18,... | collective-permute-start | bytes 3145736 | tf_op jit(solution)/shard_map/ppermute | solution.py:30
  40.7 10.3 %copy-start.16 = (f32[1024,256]{1,0:T(8,128)S(1)}, f32[1024,256]{1,0:T(8,128)}, u32[]{:S(2)}) copy-start(f32[1024,256]{1,0:T(8,128)} %attention_forward.3) | copy-start | bytes 3145732
  42.8 5.2 copy-start.27
  47.9 27.6 %collective-permute-start.5 = (f32[1536,1024]{1,0:T(8,128)}, f32[1536,1024]{1,0:T(8,128)}, u32[]{:S(2)}, u32[]{:S(2)}) collective-permute-start(f32[1536,1024]{1,0:T(8,128)} %packed.1), channel_id=1, source_target_pairs={{0,2},{1,3},{2,0},{3,1},{4,6},{5,7},{6,4},{7,5},{8,10},{9,11},{10,... | collective-permute-start | bytes 18874376 | tf_op jit(solution)/shard_map/ppermute | solution.py:30
  47.9 15.5 %collective-permute-start.3 = (f32[256,1024]{1,0:T(8,128)S(1)}, f32[256,1024]{1,0:T(8,128)S(1)}, u32[]{:S(2)}, u32[]{:S(2)}) collective-permute-start(f32[256,1024]{1,0:T(8,128)S(1)} %collective-permute-done.1), channel_id=1, source_target_pairs={{1,5},{2,6},{5,1},{6,2},{9,13},{10,14},{13,9},{14,10},{17,21},{18,... | collective-permute-start | bytes 3145736 | tf_op jit(solution)/shard_map/ppermute | solution.py:30
  51.1 16.2 %collective-permute-start.2 = (f32[1024,256]{1,0:T(8,128)S(1)}, f32[1024,256]{1,0:T(8,128)}, u32[]{:S(2)}, u32[]{:S(2)}) collective-permute-start(f32[1024,256]{1,0:T(8,128)S(1)} %copy-done.16), channel_id=1, source_target_pairs={{1,2},{2,1},{5,6},{6,5},{9,10},{10,9},{13,14},{14,13},{17,18},{18,... | collective-permute-start | bytes 3145736 | tf_op jit(solution)/shard_map/ppermute | solution.py:30
  55.0 14.1 %copy-start.6 = (bf16[1024,256]{1,0:T(8,128)(2,1)}, bf16[1024,256]{1,0:T(8,128)(2,1)S(1)}, u32[]{:S(2)}) copy-start(bf16[1024,256]{1,0:T(8,128)(2,1)S(1)} %add_convert_fusion.6.low_ref) | copy-start | bytes 1572868
  55.0 8.6 %copy-start.19 = (bf16[512,1024]{1,0:T(8,128)(2,1)S(1)}, bf16[512,1024]{1,0:T(8,128)(2,1)}, u32[]{:S(2)}) copy-start(bf16[512,1024]{1,0:T(8,128)(2,1)} %param.25) | copy-start | bytes 3145732
  64.1 5.1 copy-start.2
  71.0 4.5 collective-permute-start.4
  71.9 13.4 %collective-permute-start.14 = (f32[128,1536]{1,0:T(8,128)S(1)}, f32[128,1536]{1,0:T(8,128)}, u32[]{:S(2)}, u32[]{:S(2)}) collective-permute-start(f32[128,1536]{1,0:T(8,128)S(1)} %convert_element_type.64), channel_id=1, source_target_pairs={{1,2},{2,1},{5,6},{6,5},{9,10},{10,9},{13,14},{14,13},{17,18},{18,... | collective-permute-start | bytes 2359304 | tf_op jit(solution)/shard_map/ppermute | solution.py:30
  85.4 331.4 %reduce-scatter.2.cloned.1.call-start = ((), (), s32[]{:S(2)}) async-start(), calls=%async_computation.2 | async-start | bytes 8912896 | tf_op jit(solution)/shard_map/reduce_scatter | solution.py:972
  85.6 25.5 %collective-permute-start.6 = (f32[256,1024]{1,0:T(8,128)}, f32[256,1024]{1,0:T(8,128)S(1)}, u32[]{:S(2)}, u32[]{:S(2)}) collective-permute-start(f32[256,1024]{1,0:T(8,128)} %get-tuple-element.145.hidden_ref), channel_id=1, source_target_pairs={{0,1},{1,0},{2,3},{3,2},{4,5},{5,4},{6,7},{7,6},{8,9},{9,8},{10,11... | collective-permute-start | bytes 3145736 | tf_op jit(solution)/shard_map/ppermute | solution.py:30
  90.2 43.4 %collective-permute-start.8 = (f32[256,1024]{1,0:T(8,128)}, f32[256,1024]{1,0:T(8,128)S(1)}, u32[]{:S(2)}, u32[]{:S(2)}) collective-permute-start(f32[256,1024]{1,0:T(8,128)} %get-tuple-element.147.hidden_ref), channel_id=1, source_target_pairs={{0,1},{1,0},{2,3},{3,2},{4,5},{5,4},{6,7},{7,6},{8,9},{9,8},{10,11... | collective-permute-start | bytes 3145736 | tf_op jit(solution)/shard_map/ppermute | solution.py:30
  121.1 35.0 %collective-permute-start.7 = (f32[256,1024]{1,0:T(8,128)}, f32[256,1024]{1,0:T(8,128)S(1)}, u32[]{:S(2)}, u32[]{:S(2)}) collective-permute-start(f32[256,1024]{1,0:T(8,128)} %get-tuple-element.154), channel_id=1, source_target_pairs={{0,1},{1,0},{2,3},{3,2},{4,5},{5,4},{6,7},{7,6},{8,9},{9,8},{10,11... | collective-permute-start | bytes 3145736 | tf_op jit(solution)/shard_map/ppermute | solution.py:30
  134.6 21.5 %copy-start.22 = (f32[256,1024]{1,0:T(8,128)S(1)}, f32[256,1024]{1,0:T(8,128)}, u32[]{:S(2)}) copy-start(f32[256,1024]{1,0:T(8,128)} %get-tuple-element.146) | copy-start | bytes 3145732
  143.8 34.8 %collective-permute-start.9 = (f32[256,1024]{1,0:T(8,128)}, f32[256,1024]{1,0:T(8,128)S(1)}, u32[]{:S(2)}, u32[]{:S(2)}) collective-permute-start(f32[256,1024]{1,0:T(8,128)} %get-tuple-element.158), channel_id=1, source_target_pairs={{0,1},{1,0},{2,3},{3,2},{4,5},{5,4},{6,7},{7,6},{8,9},{9,8},{10,11... | collective-permute-start | bytes 3145736 | tf_op jit(solution)/shard_map/ppermute | solution.py:30
  157.3 43.8 %collective-permute-start.10 = (f32[256,1024]{1,0:T(8,128)}, f32[256,1024]{1,0:T(8,128)}, u32[]{:S(2)}, u32[]{:S(2)}) collective-permute-start(f32[256,1024]{1,0:T(8,128)} %add.127.total_ref), channel_id=1, source_target_pairs={{0,1},{1,0},{2,3},{3,2},{4,5},{5,4},{6,7},{7,6},{8,9},{9,8},{10,11... | collective-permute-start | bytes 3145736 | tf_op jit(solution)/shard_map/ppermute | solution.py:30
  157.3 21.3 %copy-start.21 = (f32[256,1024]{1,0:T(8,128)S(1)}, f32[256,1024]{1,0:T(8,128)}, u32[]{:S(2)}) copy-start(f32[256,1024]{1,0:T(8,128)} %get-tuple-element.150) | copy-start | bytes 3145732
  179.8 42.5 %collective-permute-start.11 = (f32[256,1024]{1,0:T(8,128)}, f32[256,1024]{1,0:T(8,128)}, u32[]{:S(2)}, u32[]{:S(2)}) collective-permute-start(f32[256,1024]{1,0:T(8,128)} %add.128.total_ref), channel_id=1, source_target_pairs={{0,1},{1,0},{2,3},{3,2},{4,5},{5,4},{6,7},{7,6},{8,9},{9,8},{10,11... | collective-permute-start | bytes 3145736 | tf_op jit(solution)/shard_map/ppermute | solution.py:30
  240.8 7.4 %collective-permute-start.15 = (f32[1024,1024]{1,0:T(8,128)}, f32[1024,1024]{1,0:T(8,128)S(1)}, u32[]{:S(2)}, u32[]{:S(2)}) collective-permute-start(f32[1024,1024]{1,0:T(8,128)} %outer.4), channel_id=1, source_target_pairs={{0,2},{1,3},{2,0},{3,1},{4,6},{5,7},{6,4},{7,5},{8,10},{9,11},{10,... | collective-permute-start | bytes 12582920 | tf_op jit(solution)/shard_map/ppermute | solution.py:30
  267.1 28.8 %collective-permute-start.17 = (f32[256,1024]{1,0:T(8,128)}, f32[256,1024]{1,0:T(8,128)}, u32[]{:S(2)}, u32[]{:S(2)}) collective-permute-start(f32[256,1024]{1,0:T(8,128)} %get-tuple-element.176), channel_id=1, source_target_pairs={{0,1},{1,0},{2,3},{3,2},{4,5},{5,4},{6,7},{7,6},{8,9},{9,8},{10,11... | collective-permute-start | bytes 3145736 | tf_op jit(solution)/shard_map/ppermute | solution.py:30
  268.6 45.8 %collective-permute-start.16 = (f32[256,1024]{1,0:T(8,128)}, f32[256,1024]{1,0:T(8,128)}, u32[]{:S(2)}, u32[]{:S(2)}) collective-permute-start(f32[256,1024]{1,0:T(8,128)} %get-tuple-element.200), channel_id=1, source_target_pairs={{0,1},{1,0},{2,3},{3,2},{4,5},{5,4},{6,7},{7,6},{8,9},{9,8},{10,11... | collective-permute-start | bytes 3145736 | tf_op jit(solution)/shard_map/ppermute | solution.py:30
  268.8 1.7 collective-permute-start.13
  270.5 6.7 %copy-start.37 = (s32[1,5]{1,0:T(1,128)}, s32[1,5]{1,0:T(1,128)S(1)}, u32[]{:S(2)}) copy-start(s32[1,5]{1,0:T(1,128)S(1)} %fusion.15) | copy-start | bytes 64
  271.1 50.3 %collective-permute-start.19 = (f32[4,128,1024]{2,1,0:T(8,128)}, f32[4,128,1024]{2,1,0:T(8,128)}, u32[]{:S(2)}, u32[]{:S(2)}) collective-permute-start(f32[4,128,1024]{2,1,0:T(8,128)} %get-tuple-element.190), channel_id=1, source_target_pairs={{0,4},{1,5},{2,10},{3,11},{4,0},{5,1},{6,14},{7,15},{8,12},{9,13},... | collective-permute-start | bytes 6291464 | tf_op jit(solution)/shard_map/ppermute | solution.py:30
  320.3 9.6 %collective-permute-start.18 = (f32[512,1024]{1,0:T(8,128)}, f32[512,1024]{1,0:T(8,128)}, u32[]{:S(2)}, u32[]{:S(2)}) collective-permute-start(f32[512,1024]{1,0:T(8,128)} %get-tuple-element.208), channel_id=1, source_target_pairs={{0,2},{1,3},{2,0},{3,1},{4,6},{5,7},{6,4},{7,5},{8,10},{9,11},{10,... | collective-permute-start | bytes 6291464 | tf_op jit(solution)/shard_map/ppermute | solution.py:30
  321.4 6.7 %copy-start.7 = (bf16[1024,256]{1,0:T(8,128)(2,1)S(1)}, bf16[1024,256]{1,0:T(8,128)(2,1)}, u32[]{:S(2)}) copy-start(bf16[1024,256]{1,0:T(8,128)(2,1)} %copy-done.6) | copy-start | bytes 1572868
  321.4 6.7 %copy-start.9 = (bf16[1024,256]{1,0:T(8,128)(2,1)S(1)}, bf16[1024,256]{1,0:T(8,128)(2,1)}, u32[]{:S(2)}) copy-start(bf16[1024,256]{1,0:T(8,128)(2,1)} %copy-done.8) | copy-start | bytes 1572868
  321.4 7.8 %copy-start.35 = (f32[2,4,1024]{2,1,0:T(4,128)S(1)}, f32[2,4,1024]{2,1,0:T(4,128)}, u32[]{:S(2)}) copy-start(f32[2,4,1024]{2,1,0:T(4,128)} %get-tuple-element.199) | copy-start | bytes 98308
  325.8 4.1 copy-start.13
  325.8 34.5 %collective-permute-start.20 = (f32[2,128,1024]{2,1,0:T(8,128)}, f32[2,128,1024]{2,1,0:T(8,128)}, u32[]{:S(2)}, u32[]{:S(2)}) collective-permute-start(f32[2,128,1024]{2,1,0:T(8,128)} %get-tuple-element.212), channel_id=1, source_target_pairs={{0,8},{1,9},{2,18},{3,19},{4,12},{5,13},{6,22},{7,23},{8,0},{9,1},... | collective-permute-start | bytes 3145736 | tf_op jit(solution)/shard_map/ppermute | solution.py:30
  360.3 3.4 copy-start.31
  365.3 7.4 %copy-start = (bf16[1024,1536]{1,0:T(8,128)(2,1)}, bf16[1024,1536]{1,0:T(8,128)(2,1)S(1)}, u32[]{:S(2)}) copy-start(bf16[1024,1536]{1,0:T(8,128)(2,1)S(1)} %constant_dynamic-update-slice_fusion.4.grad_ref) | copy-start | bytes 9437188
  379.3 6.7 %copy-start.28 = (bf16[1024,512]{1,0:T(8,128)(2,1)S(1)}, bf16[1024,512]{1,0:T(8,128)(2,1)}, u32[]{:S(2)}) copy-start(bf16[1024,512]{1,0:T(8,128)(2,1)} %pad_maximum_fusion.5) | copy-start | bytes 3145732
  386.0 8.0 %copy-start.23 = (f32[256,1024]{1,0:T(8,128)S(1)}, f32[256,1024]{1,0:T(8,128)}, u32[]{:S(2)}) copy-start(f32[256,1024]{1,0:T(8,128)} %get-tuple-element.162) | copy-start | bytes 3145732
  386.0 13.0 %collective-permute-start.21 = (f32[512,1024]{1,0:T(8,128)}, f32[512,1024]{1,0:T(8,128)}, u32[]{:S(2)}, u32[]{:S(2)}) collective-permute-start(f32[512,1024]{1,0:T(8,128)} %input_other.1), channel_id=1, source_target_pairs={{0,2},{1,3},{2,0},{3,1},{4,6},{5,7},{6,4},{7,5},{8,10},{9,11},{10,... | collective-permute-start | bytes 6291464 | tf_op jit(solution)/shard_map/ppermute | solution.py:30
  388.5 5.5 %copy-start.24 = (f32[256,1024]{1,0:T(8,128)S(1)}, f32[256,1024]{1,0:T(8,128)}, u32[]{:S(2)}) copy-start(f32[256,1024]{1,0:T(8,128)} %get-tuple-element.169) | copy-start | bytes 3145732
  388.6 28.2 %collective-permute-start.23 = (f32[1024,512]{1,0:T(8,128)}, f32[1024,512]{1,0:T(8,128)}, u32[]{:S(2)}, u32[]{:S(2)}) collective-permute-start(f32[1024,512]{1,0:T(8,128)} %fusion.1), channel_id=1, source_target_pairs={{1,2},{2,1},{5,6},{6,5},{9,10},{10,9},{13,14},{14,13},{17,18},{18,... | collective-permute-start | bytes 6291464 | tf_op jit(solution)/shard_map/ppermute | solution.py:30
  392.7 36.8 %collective-permute-start.26 = (f32[4,128,1536]{2,1,0:T(8,128)}, f32[4,128,1536]{2,1,0:T(8,128)}, u32[]{:S(2)}, u32[]{:S(2)}) collective-permute-start(f32[4,128,1536]{2,1,0:T(8,128)} %get-tuple-element.224), channel_id=1, source_target_pairs={{0,4},{1,5},{2,10},{3,11},{4,0},{5,1},{6,14},{7,15},{8,12},{9,13},... | collective-permute-start | bytes 9437192 | tf_op jit(solution)/shard_map/ppermute | solution.py:30
  398.1 69.5 %collective-permute-start.12 = (f32[512,1024]{1,0:T(8,128)}, f32[512,1024]{1,0:T(8,128)}, u32[]{:S(2)}, u32[]{:S(2)}) collective-permute-start(f32[512,1024]{1,0:T(8,128)} %broadcast_select_fusion.2), channel_id=1, source_target_pairs={{0,2},{1,3},{2,0},{3,1},{4,6},{5,7},{6,4},{7,5},{8,10},{9,11},{10,... | collective-permute-start | bytes 6291464 | tf_op jit(solution)/shard_map/ppermute | solution.py:30
  421.1 17.1 %collective-permute-start.25 = (f32[1024,256]{1,0:T(8,128)}, f32[1024,256]{1,0:T(8,128)S(1)}, u32[]{:S(2)}, u32[]{:S(2)}) collective-permute-start(f32[1024,256]{1,0:T(8,128)} %get-tuple-element.270), channel_id=1, source_target_pairs={{0,2},{1,3},{2,0},{3,1},{4,6},{5,7},{6,4},{7,5},{8,10},{9,11},{10,... | collective-permute-start | bytes 3145736 | tf_op jit(solution)/shard_map/ppermute | solution.py:30
  421.1 66.9 %collective-permute-start.22 = (f32[512,1024]{1,0:T(8,128)}, f32[512,1024]{1,0:T(8,128)}, u32[]{:S(2)}, u32[]{:S(2)}) collective-permute-start(f32[512,1024]{1,0:T(8,128)} %get-tuple-element.229), channel_id=1, source_target_pairs={{0,1},{1,0},{2,3},{3,2},{4,5},{5,4},{6,7},{7,6},{8,9},{9,8},{10,11... | collective-permute-start | bytes 6291464 | tf_op jit(solution)/shard_map/ppermute | solution.py:30
  422.6 12.6 %collective-permute-start.24 = (f32[4,1024]{1,0:T(4,128)S(1)}, f32[4,1024]{1,0:T(4,128)S(1)}, u32[]{:S(2)}, u32[]{:S(2)}) collective-permute-start(f32[4,1024]{1,0:T(4,128)S(1)} %pad_maximum_fusion.8), channel_id=1, source_target_pairs={{0,2},{1,3},{2,0},{3,1},{4,6},{5,7},{6,4},{7,5},{8,10},{9,11},{10,... | collective-permute-start | bytes 49160 | tf_op jit(solution)/shard_map/ppermute | solution.py:30
  434.3 37.3 %collective-permute-start.29 = (f32[2,128,1536]{2,1,0:T(8,128)}, f32[2,128,1536]{2,1,0:T(8,128)}, u32[]{:S(2)}, u32[]{:S(2)}) collective-permute-start(f32[2,128,1536]{2,1,0:T(8,128)} %get-tuple-element.237), channel_id=1, source_target_pairs={{0,8},{1,9},{2,18},{3,19},{4,12},{5,13},{6,22},{7,23},{8,0},{9,1},... | collective-permute-start | bytes 4718600 | tf_op jit(solution)/shard_map/ppermute | solution.py:30
  443.6 19.3 %collective-permute-start.27 = (f32[4,128,384]{2,1,0:T(8,128)}, f32[4,128,384]{2,1,0:T(8,128)S(1)}, u32[]{:S(2)}, u32[]{:S(2)}) collective-permute-start(f32[4,128,384]{2,1,0:T(8,128)} %get-tuple-element.241), channel_id=1, source_target_pairs={{0,4},{1,5},{2,6},{3,7},{4,0},{5,1},{6,2},{7,3},{8,12},{9,13},{10,... | collective-permute-start | bytes 2359304 | tf_op jit(solution)/shard_map/ppermute | solution.py:30
  443.9 23.8 %copy-start.5 = (f32[512,1024]{1,0:T(8,128)S(1)}, f32[512,1024]{1,0:T(8,128)}, u32[]{:S(2)}) copy-start(f32[512,1024]{1,0:T(8,128)} %copy-done.4) | copy-start | bytes 6291460
  466.8 3.3 copy-start.40
  466.8 17.2 %collective-permute-start.28 = (f32[2,128,384]{2,1,0:T(8,128)}, f32[2,128,384]{2,1,0:T(8,128)S(1)}, u32[]{:S(2)}, u32[]{:S(2)}) collective-permute-start(f32[2,128,384]{2,1,0:T(8,128)} %get-tuple-element.245), channel_id=1, source_target_pairs={{0,8},{1,9},{2,10},{3,11},{4,12},{5,13},{6,14},{7,15},{8,0},{9,1},... | collective-permute-start | bytes 1179656 | tf_op jit(solution)/shard_map/ppermute | solution.py:30
  470.0 20.8 %collective-permute-start.36 = (f32[1,128,1024]{2,1,0:T(8,128)S(1)}, f32[1,128,1024]{2,1,0:T(8,128)S(1)}, u32[]{:S(2)}, u32[]{:S(2)}) collective-permute-start(f32[1,128,1024]{2,1,0:T(8,128)S(1)} %copy-done.40), channel_id=1, source_target_pairs={{0,16},{1,17},{2,6},{3,7},{4,20},{5,21},{6,2},{7,3},{8,24},{9,25},... | collective-permute-start | bytes 1572872 | tf_op jit(solution)/shard_map/ppermute | solution.py:30
  475.4 38.1 %collective-permute-start.33 = (f32[1,128,1536]{2,1,0:T(8,128)}, f32[1,128,1536]{2,1,0:T(8,128)S(1)}, u32[]{:S(2)}, u32[]{:S(2)}) collective-permute-start(f32[1,128,1536]{2,1,0:T(8,128)} %get-tuple-element.248), channel_id=1, source_target_pairs={{0,16},{1,17},{2,6},{3,7},{4,20},{5,21},{6,2},{7,3},{8,24},{9,25},... | collective-permute-start | bytes 2359304 | tf_op jit(solution)/shard_map/ppermute | solution.py:30
  487.4 3.4 copy-start.33
  487.4 15.4 %collective-permute-start.31 = (f32[1,128,384]{2,1,0:T(8,128)}, f32[1,128,384]{2,1,0:T(8,128)S(1)}, u32[]{:S(2)}, u32[]{:S(2)}) collective-permute-start(f32[1,128,384]{2,1,0:T(8,128)} %get-tuple-element.250), channel_id=1, source_target_pairs={{0,16},{1,17},{2,18},{3,19},{4,20},{5,21},{6,22},{7,23},{8,24},{9,... | collective-permute-start | bytes 589832 | tf_op jit(solution)/shard_map/ppermute | solution.py:30
  490.0 12.8 %copy-start.36 = (f32[1,128,128]{2,1,0:T(8,128)S(1)}, f32[1,128,128]{2,1,0:T(8,128)}, u32[]{:S(2)}) copy-start(f32[1,128,128]{2,1,0:T(8,128)} %get-tuple-element.252) | copy-start | bytes 196612
  490.0 13.6 %copy-start.34 = (f32[1,128,256]{2,1,0:T(8,128)S(1)}, f32[1,128,256]{2,1,0:T(8,128)}, u32[]{:S(2)}) copy-start(f32[1,128,256]{2,1,0:T(8,128)} %get-tuple-element.255) | copy-start | bytes 393220
  490.0 23.5 %copy-start.32 = (f32[1,128,1536]{2,1,0:T(8,128)S(1)}, f32[1,128,1536]{2,1,0:T(8,128)}, u32[]{:S(2)}) copy-start(f32[1,128,1536]{2,1,0:T(8,128)} %get-tuple-element.253) | copy-start | bytes 2359300
  490.0 39.0 %collective-permute-start.30 = (f32[512,1024]{1,0:T(8,128)S(1)}, f32[512,1024]{1,0:T(8,128)S(1)}, u32[]{:S(2)}, u32[]{:S(2)}) collective-permute-start(f32[512,1024]{1,0:T(8,128)S(1)} %broadcast_select_fusion), channel_id=1, source_target_pairs={{0,2},{1,3},{2,0},{3,1},{4,6},{5,7},{6,4},{7,5},{8,10},{9,11},{10,... | collective-permute-start | bytes 6291464 | tf_op jit(solution)/shard_map/ppermute | solution.py:30
  502.8 9.9 %collective-permute-start.32 = (f32[4,64]{0,1:T(8,128)S(1)}, f32[4,64]{0,1:T(8,128)S(1)}, u32[]{:S(2)}, u32[]{:S(2)}) collective-permute-start(f32[4,64]{0,1:T(8,128)S(1)} %slice_bitcast_fusion), channel_id=1, source_target_pairs={{0,1},{1,0},{2,3},{3,2},{4,5},{5,4},{6,7},{7,6},{8,9},{9,8},{10,11... | collective-permute-start | bytes 3080 | tf_op jit(solution)/shard_map/ppermute | solution.py:30
  503.7 16.8 %collective-permute-start.37 = (f32[64,1280]{1,0:T(8,128)S(1)}, f32[64,1280]{1,0:T(8,128)S(1)}, u32[]{:S(2)}, u32[]{:S(2)}) collective-permute-start(f32[64,1280]{1,0:T(8,128)S(1)} %pad_maximum_fusion.7), channel_id=1, source_target_pairs={{0,2},{1,3},{2,0},{3,1},{4,6},{5,7},{6,4},{7,5},{8,10},{9,11},{10,... | collective-permute-start | bytes 983048 | tf_op jit(solution)/shard_map/ppermute | solution.py:30
  513.7 8.4 %collective-permute-start.34 = (f32[64,1536]{1,0:T(8,128)S(1)}, f32[64,1536]{1,0:T(8,128)S(1)}, u32[]{:S(2)}, u32[]{:S(2)}) collective-permute-start(f32[64,1536]{1,0:T(8,128)S(1)} %get-tuple-element.262), channel_id=1, source_target_pairs={{0,2},{1,0},{2,3},{3,1},{4,6},{5,4},{6,7},{7,5},{8,10},{9,8},{10,1... | collective-permute-start | bytes 1179656 | tf_op jit(solution)/shard_map/ppermute | solution.py:30
  514.9 13.3 %collective-permute-start.35 = (f32[64,1536]{1,0:T(8,128)S(1)}, f32[64,1536]{1,0:T(8,128)S(1)}, u32[]{:S(2)}, u32[]{:S(2)}) collective-permute-start(f32[64,1536]{1,0:T(8,128)S(1)} %get-tuple-element.263), channel_id=1, source_target_pairs={{1,2},{2,1},{5,6},{6,5},{9,10},{10,9},{13,14},{14,13},{17,18},{18,... | collective-permute-start | bytes 1179656 | tf_op jit(solution)/shard_map/ppermute | solution.py:30
  (17 other events, 28.8 us)
Sparse Core Ops, SparseCore 0:
  85.5 97.3 all-gather.1
Sparse Core Ops, SparseCore 1:
  267.2 108.5 reduce-scatter.1

commit v5 on v4

--- a/solution.py
+++ b/solution.py
@@ -964,11 +964,15 @@
                 for part, (number, start) in zip(self.held, self.sources)
             ]
 
-    down_other = outer(where_own, grad_low_all, activated_all, lambda where: 1 - where[0], hidden // 2)
-    down_kept = outer(where_own, grad_low_all, activated_all, lambda where: where[0], hidden // 2)
+    def weight_part(columns):
+        chosen = half_columns(activated_all, columns, hidden // 2)
+        return jnp.einsum("td,tf->df", grad_low_all, chosen, preferred_element_type=f32)
+
+    down_other = weight_part(1 - core)
+    down_kept = weight_part(core)
     early = Sum([down_kept], send(down_other, cross))
     mlp_in_all, grad_up_all = after((mlp_in_all, grad_up_all), early.hop(down_kept))
-    weight_up = outer(where_own, mlp_in_all, grad_up_all, lambda where: 0, hidden)
+    weight_up = jnp.einsum("td,tf->df", mlp_in_all, grad_up_all, preferred_element_type=f32)
     grad_up = lax.psum_scatter(weight_up, "dp", scatter_dimension=0, tiled=True)
     weights_late = after(weights_sent, weight_up)
     weights_mine = (jnp.concatenate(weights_here, axis=1).astype(f32) * keep + weights_late).astype(bf16)
@@ -1027,7 +1031,15 @@
     gate = extra.hop(gate)
     [grad_down] = early.result(gate)
     [held] = late.result(gate)
-    grad_out, gains = extra.result()
+    for_core = half_of(held, core, small)
+    for_other = half_of(held, 1 - core, small)
+    for_other, leaving = lax.optimization_barrier((for_other, jnp.where(same, for_other, for_core)))
+    diagonal = send(for_other, swap)
+    straight = send(
+        leaving,
+        flat_pairs(dp_size, lambda d, c, t: (d, 1 - t) if c != t else (d ^ 1, t)),
+    )
+    grad_out, gains = extra.result(leaving)
 
     def to_core(*parts):
         leaving = jnp.concatenate([half_of(part, 1 - core, small) for part in parts], axis=1)
@@ -1048,13 +1060,6 @@
 
     grad_down, grad_out = to_core(grad_down, grad_out)
     grad_in = to_output(grad_in_own, after(grad_in_sent, gate))
-    for_core = half_of(held, core, small)
-    for_other = half_of(held, 1 - core, small)
-    diagonal = send(for_other, swap)
-    straight = send(
-        jnp.where(same, for_other, for_core),
-        flat_pairs(dp_size, lambda d, c, t: (d, 1 - t) if c != t else (d ^ 1, t)),
-    )
     heads = straight + jnp.where(same, for_core, diagonal)
     gains = half_of(gains, core, small)[:, :4].T
     gains = gains + send(gains, over)

time: 550 us -> 538 us (0.978)
  Pallas kernels: 256 us -> 232 us
  matrix products: 12.6 us -> 31.5 us
  waiting for transfers between devices: 148 us -> 135 us
    pallas_call x3 -> x0, Pallas kernels: 24.8 us -> none  [outer(): pl.pallas_call(outer_kernel, grid_spec=pltpu.PrefetchScalarGridSpec(num_s...]
    dot_general x0 -> x3, matrix products: none -> 18.9 us  [the longest x2 12 us: weight_part(): jnp.einsum('td,tf->df', grad_low_all, chosen, preferred_element_type=f32)]
    ppermute x38, waiting for transfers between devices: 147 us -> 135 us  [send(): return lax.ppermute(values, ('dp', 'tensor'), pairs)]
    unnamed x87 -> x103, local copies, waits for them, and re-layouts: 12.9 us -> 14.5 us
  transfers between devices with their start and end apart: 40 -> 40, of which waited for: 20 -> 21; matrix products, arithmetic and copies ran while one was open for 9% -> 13% of each run, Pallas kernels for 46% -> 43%
where the time goes in v5:
time: 538 us; the launch traced here: 529 us
  Pallas kernels  232 us (43%)
  waiting for transfers between devices  135 us (25%)
  starting transfers between devices  55.1 us (10%)
  other arithmetic  33.6 us (6%)
  matrix products  31.5 us (6%)
  local copies, waits for them, and re-layouts  24.3 us (5%)
  between operations  17.4 us (3%)
    ppermute x38, waiting for transfers between devices, send(): return lax.ppermute(values, ('dp', 'tensor'), pairs)  135 us
    pallas_call x14, Pallas kernels, call(): pl.pallas_call(kernel, grid_spec=pltpu.PrefetchScalarGridSpec(num_scalar_...  113 us
    ppermute x38, starting transfers between devices, send(): return lax.ppermute(values, ('dp', 'tensor'), pairs)  54.8 us
    pallas_call x9, Pallas kernels, halves(): pl.pallas_call(partial(halves_kernel, len(held), sources), grid_spec=pltp...  40.1 us
    pallas_call x1, Pallas kernels, attention_backward(): pl.pallas_call(partial(backward_kernel, lengths.shape[1]), grid=(pairs,),...  25.8 us
    pallas_call x2, Pallas kernels, attention_forward(): pl.pallas_call(partial(forward_kernel, lengths.shape[1], first), grid=(1,...  23.5 us
    pallas_call x1, Pallas kernels, attention_ready(): pl.pallas_call(partial(ready_kernel, lengths.shape[1]), grid=(wide // gro...  18.6 us
    unnamed x103, local copies, waits for them, and re-layouts  14.5 us
  transfers between devices with their start and end apart: 40, of which 21 were waited for; matrix products, arithmetic and copies ran while one was open for 13% of the time, Pallas kernels for 43%

profile of v5, /device:TPU:1, one launch (start us, length us, event | category | flops | bytes accessed | tf_op | source)
XLA Modules:
  0.0 529.3 jit_solution(6537115545263239410)
XLA Ops:
  9.2 4.5 collective-permute-start.1
  14.4 12.0 %attention_forward.2 = (f32[1024,256]{1,0:T(8,128)}, bf16[1024,1024]{1,0:T(8,128)(2,1)}, f32[1024,128]{1,0:T(8,128)}, f32[1024,128]{1,0:T(8,128)}) custom-call(s32[1,4]{1,0:T(1,128)} %lengths_ref.3, s32[1]{0:T(128)S(6)} %copy.65.pad_ref, f32[32,1]{1,0:T(8,128)} %constant.57.clone.freq_ref, f32[1,1024]{1,0:T(1,128)} %bitcast.77, ...), custom_call_target="tpu_custom_call" | custom-call | flops 1 | bytes 1 | tf_op jit(solution)/shard_map/attention_forward/pallas_call | solution.py:278
  26.5 2.1 collective-permute-start
  29.3 11.5 %attention_forward.3 = f32[1024,256]{1,0:T(8,128)} custom-call(s32[1,4]{1,0:T(1,128)} %lengths_ref.3, s32[1]{0:T(128)S(6)} %copy.65.pad_ref, f32[32,1]{1,0:T(8,128)} %constant.57.clone.freq_ref, f32[1,1024]{1,0:T(1,128)} %bitcast.78, bf16[1024,1024]{1,0:T(8,128)(2,1)} %get-tuple-element.142.refs_0_, f32[1024,128]{1,0:T(8,128)} %get-tuple-element.143.refs_1_, ...), custom_call_target="tpu_custom_call" | custom-call | flops 1 | bytes 1 | tf_op jit(solution)/shard_map/attention_forward/pallas_call | solution.py:278
  42.8 5.3 packed.1
  48.1 3.1 collective-permute-start.3
  51.2 2.3 collective-permute-start.2
  55.3 8.3 %collective-permute-done.3 = f32[256,1024]{1,0:T(8,128)S(1)} collective-permute-done((f32[256,1024]{1,0:T(8,128)S(1)}, f32[256,1024]{1,0:T(8,128)S(1)}, u32[]{:S(2)}, u32[]{:S(2)}) %collective-permute-start.3) | collective-permute-done | bytes 1048608 | tf_op jit(solution)/shard_map/ppermute | solution.py:30
  64.2 3.2 collective-permute-done.2
  73.1 2.3 collective-permute-start.14
  76.8 4.6 hidden.2
  81.3 5.1 collective-permute-done.14
  87.7 4.5 hidden.3
  93.6 9.3 %mlp_forward.4 = (bf16[1024,1024]{1,0:T(8,128)(2,1)}, bf16[1024,2048]{1,0:T(8,128)(2,1)}, f32[256,2048]{1,0:T(8,128)}, f32[256,1024]{1,0:T(8,128)}) custom-call(f32[256,1024]{1,0:T(8,128)} %get-tuple-element.148.hidden_ref, f32[1,1024]{1,0:T(1,128)} %bitcast.71, bf16[1024,2048]{1,0:T(8,128)(2,1)} %up_ref.15, bf16[2048,1024]{1,0:T(8,128)(2,1)} %down_ref.15), custom_call_target="tpu_custom_call" | custom-call | flops 1 | bytes 1 | tf_op jit(solution)/shard_map/mlp_forward/pallas_call | solution.py:521
  103.0 9.0 %mlp_forward.5 = (bf16[1024,1024]{1,0:T(8,128)(2,1)}, bf16[1024,2048]{1,0:T(8,128)(2,1)}, f32[256,2048]{1,0:T(8,128)}, f32[256,1024]{1,0:T(8,128)}) custom-call(f32[256,1024]{1,0:T(8,128)} %get-tuple-element.150.hidden_ref, f32[1,1024]{1,0:T(1,128)} %bitcast.72, bf16[1024,2048]{1,0:T(8,128)(2,1)} %up_ref.15, ...), custom_call_target="tpu_custom_call", output_to_operand_aliasing={{0}: (4, {}), {1}: (5, {})} | custom-call | flops 1 | bytes 1 | tf_op jit(solution)/shard_map/mlp_forward/pallas_call | solution.py:521
  114.1 9.0 %mlp_forward.6 = (bf16[1024,1024]{1,0:T(8,128)(2,1)}, bf16[1024,2048]{1,0:T(8,128)(2,1)}, f32[256,2048]{1,0:T(8,128)}, f32[256,1024]{1,0:T(8,128)}) custom-call(f32[256,1024]{1,0:T(8,128)} %copy-done.19, f32[1,1024]{1,0:T(1,128)} %bitcast.73, bf16[1024,2048]{1,0:T(8,128)(2,1)} %up_ref.15, ...), custom_call_target="tpu_custom_call", output_to_operand_aliasing={{0}: (4, {}), {1}: (5, {})} | custom-call | flops 1 | bytes 1 | tf_op jit(solution)/shard_map/mlp_forward/pallas_call | solution.py:521
  123.2 12.4 %collective-permute-done.8.hidden_ref = f32[256,1024]{1,0:T(8,128)S(1)} collective-permute-done((f32[256,1024]{1,0:T(8,128)}, f32[256,1024]{1,0:T(8,128)S(1)}, u32[]{:S(2)}, u32[]{:S(2)}) %collective-permute-start.8) | collective-permute-done | bytes 1048608 | tf_op jit(solution)/shard_map/ppermute | solution.py:30
  136.6 9.1 %mlp_forward.7 = (bf16[1024,1024]{1,0:T(8,128)(2,1)}, bf16[1024,2048]{1,0:T(8,128)(2,1)}, f32[256,2048]{1,0:T(8,128)}, f32[256,1024]{1,0:T(8,128)}) custom-call(f32[256,1024]{1,0:T(8,128)} %copy-done.18, f32[1,1024]{1,0:T(1,128)} %bitcast.74, bf16[1024,2048]{1,0:T(8,128)(2,1)} %up_ref.15, ...), custom_call_target="tpu_custom_call", output_to_operand_aliasing={{0}: (4, {}), {1}: (5, {})} | custom-call | flops 1 | bytes 1 | tf_op jit(solution)/shard_map/mlp_forward/pallas_call | solution.py:521
  145.8 12.3 %collective-permute-done.7 = f32[256,1024]{1,0:T(8,128)S(1)} collective-permute-done((f32[256,1024]{1,0:T(8,128)}, f32[256,1024]{1,0:T(8,128)S(1)}, u32[]{:S(2)}, u32[]{:S(2)}) %collective-permute-start.7) | collective-permute-done | bytes 1048608 | tf_op jit(solution)/shard_map/ppermute | solution.py:30
  159.2 11.2 %mlp_backward.4 = (f32[256,1024]{1,0:T(8,128)}, bf16[1024,1024]{1,0:T(8,128)(2,1)}, f32[8,1024]{1,0:T(8,128)}, bf16[1024,2048]{1,0:T(8,128)(2,1)}, f32[256,1024]{1,0:T(8,128)}) custom-call(s32[14]{0:T(128)} %stack.54.where_ref, f32[256,1024]{1,0:T(8,128)} %get-tuple-element.148.hidden_ref, f32[256,1024]{1,0:T(8,128)} %copy-done.20, ...), custom_call_target="tpu_custom_call" | custom-call | flops 1 | bytes 1 | tf_op jit(solution)/shard_map/mlp_backward/pallas_call | solution.py:521
  170.4 10.2 %collective-permute-done.9 = f32[256,1024]{1,0:T(8,128)S(1)} collective-permute-done((f32[256,1024]{1,0:T(8,128)}, f32[256,1024]{1,0:T(8,128)S(1)}, u32[]{:S(2)}, u32[]{:S(2)}) %collective-permute-start.9) | collective-permute-done | bytes 1048608 | tf_op jit(solution)/shard_map/ppermute | solution.py:30
  181.7 11.0 %mlp_backward.5 = (f32[256,1024]{1,0:T(8,128)}, bf16[1024,1024]{1,0:T(8,128)(2,1)}, f32[8,1024]{1,0:T(8,128)}, bf16[1024,2048]{1,0:T(8,128)(2,1)}, f32[256,1024]{1,0:T(8,128)}) custom-call(s32[14]{0:T(128)} %stack.54.where_ref, f32[256,1024]{1,0:T(8,128)} %get-tuple-element.150.hidden_ref, ...), custom_call_target="tpu_custom_call", output_to_operand_aliasing={{1}: (9, {}), {3}: (10, {})} | custom-call | flops 1 | bytes 1 | tf_op jit(solution)/shard_map/mlp_backward/pallas_call | solution.py:521
  192.7 10.3 %collective-permute-done.10.total_ref = f32[256,1024]{1,0:T(8,128)S(1)} collective-permute-done((f32[256,1024]{1,0:T(8,128)S(1)}, f32[256,1024]{1,0:T(8,128)S(1)}, u32[]{:S(2)}, u32[]{:S(2)}) %collective-permute-start.10) | collective-permute-done | bytes 1048608 | tf_op jit(solution)/shard_map/ppermute | solution.py:30
  204.0 10.9 %mlp_backward.6 = (f32[256,1024]{1,0:T(8,128)}, bf16[1024,1024]{1,0:T(8,128)(2,1)}, f32[8,1024]{1,0:T(8,128)}, bf16[1024,2048]{1,0:T(8,128)(2,1)}, f32[256,1024]{1,0:T(8,128)}) custom-call(s32[2]{0:T(128)} %pad_add_fusion.where_ref, f32[256,1024]{1,0:T(8,128)} %copy-done.19, f32[256,1024]{1,0:T(8,128)} %copy-done.28, ...), custom_call_target="tpu_custom_call", output_to_operand_aliasing={{1}: (9, {}), {3}: (10, {})} | custom-call | flops 1 | bytes 1 | tf_op jit(solution)/shard_map/mlp_backward/pallas_call | solution.py:521
  214.9 9.6 %collective-permute-done.11.total_ref = f32[256,1024]{1,0:T(8,128)} collective-permute-done((f32[256,1024]{1,0:T(8,128)S(1)}, f32[256,1024]{1,0:T(8,128)}, u32[]{:S(2)}, u32[]{:S(2)}) %collective-permute-start.11) | collective-permute-done | bytes 1048608 | tf_op jit(solution)/shard_map/ppermute | solution.py:30
  224.5 11.5 %mlp_backward.7 = (f32[256,1024]{1,0:T(8,128)}, bf16[1024,1024]{1,0:T(8,128)(2,1)}, f32[8,1024]{1,0:T(8,128)}, bf16[1024,2048]{1,0:T(8,128)(2,1)}, f32[256,1024]{1,0:T(8,128)}) custom-call(s32[2]{0:T(128)} %pad_add_fusion.where_ref, f32[256,1024]{1,0:T(8,128)} %copy-done.18, ...), custom_call_target="tpu_custom_call", output_to_operand_aliasing={{1}: (9, {}), {3}: (10, {})} | custom-call | flops 1 | bytes 1 | tf_op jit(solution)/shard_map/mlp_backward/pallas_call | solution.py:521
  236.0 6.1 %fusion.1 = f32[1024,1024]{1,0:T(8,128)} fusion(bf16[1024,1024]{1,0:T(8,128)(2,1)} %get-tuple-element.190, bf16[1024,2048]{1,0:T(8,128)(2,1)S(1)} %copy-done, s32[]{:T(128)S(6)} %select_n.143), kind=kOutput, calls=%fused_computation.11 | convolution fusion | flops 2147483648 | bytes 8388612 | tf_op jit(solution)/shard_map/td,tf->df/dot_general | solution.py:969
  242.0 6.0 %fusion.3 = f32[1024,1024]{1,0:T(8,128)} fusion(bf16[1024,1024]{1,0:T(8,128)(2,1)S(1)} %copy-done.1, bf16[1024,2048]{1,0:T(8,128)(2,1)} %get-tuple-element.191, s32[]{:T(128)S(6)} %select_n.142), kind=kOutput, calls=%fused_computation.13 | convolution fusion | flops 2147483648 | bytes 8388612 | tf_op jit(solution)/shard_map/td,tf->df/dot_general | solution.py:969
  249.5 7.1 %halves.9 = (f32[4,128,1024]{2,1,0:T(8,128)}, f32[4,128,1024]{2,1,0:T(8,128)}) custom-call(s32[14]{0:T(128)} %stack.54.where_ref, f32[8,128,1024]{2,1,0:T(8,128)} %bitcast.61, f32[8,128,1024]{2,1,0:T(8,128)} %bitcast.62, f32[8,128,1024]{2,1,0:T(8,128)} %bitcast.17.refs_2_.refs_3_, f32[8,128,1024]{2,1,0:T(8,128)} %bitcast.17.refs_2_.refs_3_), custom_call_target="tpu_custom_call" | custom-call | flops 1 | bytes 1 | tf_op jit(solution)/shard_map/halves/pallas_call | solution.py:721
  256.6 6.8 %fusion.26 = f32[1024,2048]{1,0:T(8,128)} fusion(bf16[1024,1024]{1,0:T(8,128)(2,1)S(1)} %copy-done.3, bf16[1024,2048]{1,0:T(8,128)(2,1)S(1)} %copy-done.2), kind=kOutput, calls=%fused_computation.87 | convolution fusion | flops 4294967296 | bytes 14680064 | tf_op jit(solution)/shard_map/td,tf->df/dot_general | solution.py:975
  268.6 4.9 add_convert_fusion.wq_ref.wk_ref.wv_ref.weight_ref
  273.5 18.6 %attention_ready.1 = (bf16[1024,512]{1,0:T(8,128)(2,1)}, bf16[1024,512]{1,0:T(8,128)(2,1)}, bf16[1024,512]{1,0:T(8,128)(2,1)}, f32[2,4,1024]{2,1,0:T(4,128)}, bf...) custom-call(s32[14]{0:T(128)} %stack.54.where_ref, s32[1,4]{1,0:T(1,128)} %bitcast.89, ...), custom_call_target="tpu_custom_call" | custom-call | flops 1 | bytes 1 | tf_op jit(solution)/shard_map/attention_ready/pallas_call | solution.py:304
  292.1 5.8 %residual.2 = (f32[512,1024]{1,0:T(8,128)}, f32[512,1024]{1,0:T(8,128)}, f32[8,1024]{1,0:T(8,128)}) custom-call(s32[14]{0:T(128)} %stack.54.where_ref, f32[256,1024]{1,0:T(8,128)} %get-tuple-element.166.part_ref, f32[256,1024]{1,0:T(8,128)} %collective-permute-done.17.arrived_ref, f32[256,1024]{1,0:T(8,128)} %get-tuple-element.148.hidden_ref, ...), custom_call_target="tpu_custom_call" | custom-call | flops 1 | bytes 1 | tf_op jit(solution)/shard_map/residual/pallas_call | solution.py:521
  297.9 13.1 %collective-permute-done.16.arrived_ref = f32[256,1024]{1,0:T(8,128)} collective-permute-done((f32[256,1024]{1,0:T(8,128)}, f32[256,1024]{1,0:T(8,128)}, u32[]{:S(2)}, u32[]{:S(2)}) %collective-permute-start.16) | collective-permute-done | bytes 1048608 | tf_op jit(solution)/shard_map/ppermute | solution.py:30
  311.0 5.8 %residual.3 = (f32[512,1024]{1,0:T(8,128)}, f32[512,1024]{1,0:T(8,128)}, f32[8,1024]{1,0:T(8,128)}) custom-call(s32[14]{0:T(128)} %stack.54.where_ref, f32[256,1024]{1,0:T(8,128)} %get-tuple-element.173.part_ref, f32[256,1024]{1,0:T(8,128)} %collective-permute-done.16.arrived_ref, ...), custom_call_target="tpu_custom_call", output_to_operand_aliasing={{0}: (9, {}), {1}: (10, {})} | custom-call | flops 1 | bytes 1 | tf_op jit(solution)/shard_map/residual/pallas_call | solution.py:521
  317.8 4.3 halves.10
  322.1 2.4 collective-permute-start.20
  326.2 2.4 add_convert_fusion.2
  328.6 2.2 convolution_convert_fusion.grad_ref
  330.9 25.8 %attention_backward.1 = (bf16[1024,512]{1,0:T(8,128)(2,1)}, bf16[1024,512]{1,0:T(8,128)(2,1)}, bf16[1024,512]{1,0:T(8,128)(2,1)}) custom-call(s32[1,4]{1,0:T(1,128)} %bitcast.90, s32[1]{0:T(128)} %bitcast.15.pad_ref, f32[1024,128]{1,0:T(8,128)} %get-tuple-element.197.cos_ref, f32[1024,128]{1,0:T(8,128)} %get-tuple-element.198.sin_ref, ...), custom_call_target="tpu_custom_call" | custom-call | flops 1 | bytes 1 | tf_op jit(solution)/shard_map/attention_backward/pallas_call | solution.py:333
  356.7 3.4 halves.11
  363.6 5.6 %fusion.27 = f32[1024,1536]{1,0:T(8,128)} fusion(bf16[1024,1024]{1,0:T(8,128)(2,1)S(1)} %copy-done.47, bf16[1024,1536]{1,0:T(8,128)(2,1)S(1)} %constant_dynamic-update-slice_fusion.4.grad_ref), kind=kOutput, calls=%fused_computation.88 | convolution fusion | flops 3221225472 | bytes 11534336 | tf_op jit(solution)/shard_map/td,te->de/dot_general | solution.py:1009
  369.1 6.5 %halves.12 = (f32[4,128,1536]{2,1,0:T(8,128)}, f32[4,128,1536]{2,1,0:T(8,128)}) custom-call(s32[14]{0:T(128)} %stack.54.where_ref, f32[8,128,1536]{2,1,0:T(8,128)} %bitcast.63, f32[8,128,1536]{2,1,0:T(8,128)} %bitcast.64), custom_call_target="tpu_custom_call" | custom-call | flops 1 | bytes 1 | tf_op jit(solution)/shard_map/halves/pallas_call | solution.py:721
  376.9 6.5 %input_other.1 = f32[512,1024]{1,0:T(8,128)} custom-call(s32[14]{0:T(128)} %stack.54.where_ref, bf16[1024,1536]{1,0:T(8,128)(2,1)} %copy-done.4, bf16[1024,1536]{1,0:T(8,128)(2,1)} %add_convert_fusion.wq_ref.wk_ref.wv_ref.weight_ref), custom_call_target="tpu_custom_call" | custom-call | flops 1 | bytes 1 | tf_op jit(solution)/shard_map/input_other/pallas_call | solution.py:521
  383.4 2.6 fusion.5
  386.0 3.8 collective-permute-start.23
  394.8 10.6 %input_own.1 = (f32[512,1024]{1,0:T(8,128)}, f32[8,1024]{1,0:T(8,128)}) custom-call(s32[14]{0:T(128)} %stack.54.where_ref, bf16[1024,1536]{1,0:T(8,128)(2,1)} %copy-done.4, bf16[1024,1536]{1,0:T(8,128)(2,1)} %add_convert_fusion.wq_ref.wk_ref.wv_ref.weight_ref, f32[512,1024]{1,0:T(8,128)} %collective-permute-done.21.arrived_ref, ...), custom_call_target="tpu_custom_call" | custom-call | flops 1 | bytes 1 | tf_op jit(solution)/shard_map/input_own/pallas_call | solution.py:759
  406.1 7.6 %collective-permute-done.23 = f32[1024,512]{1,0:T(8,128)} collective-permute-done((f32[1024,512]{1,0:T(8,128)}, f32[1024,512]{1,0:T(8,128)}, u32[]{:S(2)}, u32[]{:S(2)}) %collective-permute-start.23) | collective-permute-done | bytes 2097184 | tf_op jit(solution)/shard_map/ppermute | solution.py:30
  413.8 2.7 multiply_add_fusion.2
  418.1 4.8 halves.13
  430.2 4.5 halves.14
  435.6 18.2 %collective-permute-done.27.refs_4_.refs_5_ = f32[4,128,384]{2,1,0:T(8,128)S(1)} collective-permute-done((f32[4,128,384]{2,1,0:T(8,128)}, f32[4,128,384]{2,1,0:T(8,128)S(1)}, u32[]{:S(2)}, u32[]{:S(2)}) %collective-permute-start.27) | collective-permute-done | bytes 786464 | tf_op jit(solution)/shard_map/ppermute | solution.py:30
  454.7 3.0 halves.15
  460.2 3.9 halves.16
  464.5 2.4 add_convert_fusion.4
  470.3 2.6 halves.17
  475.2 2.6 collective-permute-start.30
  477.8 3.2 collective-permute-done.36
  483.1 10.3 %collective-permute-done.31 = f32[1,128,384]{2,1,0:T(8,128)S(1)} collective-permute-done((f32[1,128,384]{2,1,0:T(8,128)}, f32[1,128,384]{2,1,0:T(8,128)S(1)}, u32[]{:S(2)}, u32[]{:S(2)}) %collective-permute-start.31) | collective-permute-done | bytes 196640 | tf_op jit(solution)/shard_map/ppermute | solution.py:30
  493.4 11.7 %collective-permute-start.33 = (f32[4,64]{0,1:T(8,128)S(1)}, f32[4,64]{0,1:T(8,128)S(1)}, u32[]{:S(2)}, u32[]{:S(2)}) collective-permute-start(f32[4,64]{0,1:T(8,128)S(1)} %slice_bitcast_fusion), channel_id=1, source_target_pairs={{0,1},{1,0},{2,3},{3,2},{4,5},{5,4},{6,7},{7,6},{8,9},{9,8},{10,11... | collective-permute-start | bytes 3080 | tf_op jit(solution)/shard_map/ppermute | solution.py:30
  505.0 4.3 collective-permute-start.35
  512.8 2.9 collective-permute-done.35
  516.5 2.4 multiply_add_fusion.1
  518.8 2.5 pad_maximum_fusion
  (213 shorter events, 67.5 us)
Async XLA Ops:
  8.0 260.6 %all-gather.2.cloned.1.call-start = ((), (), s32[]{:S(2)}) async-start(), calls=%async_computation.1 | async-start | bytes 7077888 | tf_op jit(solution)/shard_map/all_gather | solution.py:878
  9.2 20.1 %collective-permute-start.1 = (f32[256,1024]{1,0:T(8,128)S(1)}, f32[256,1024]{1,0:T(8,128)S(1)}, u32[]{:S(2)}, u32[]{:S(2)}) collective-permute-start(f32[256,1024]{1,0:T(8,128)S(1)} %dynamic-slice_convert_fusion), channel_id=1, source_target_pairs={{1,2},{2,1},{5,6},{6,5},{9,10},{10,9},{13,14},{14,13},{17,18},{18,... | collective-permute-start | bytes 3145736 | tf_op jit(solution)/shard_map/ppermute | solution.py:30
  14.4 14.2 %copy-start.46 = (s32[1,4]{1,0:T(1,128)S(1)}, s32[1,4]{1,0:T(1,128)}, u32[]{:S(2)}) copy-start(s32[1,4]{1,0:T(1,128)} %lengths_ref.3) | copy-start | bytes 52
  26.5 16.3 %collective-permute-start = (f32[1024,256]{1,0:T(8,128)}, f32[1024,256]{1,0:T(8,128)S(1)}, u32[]{:S(2)}, u32[]{:S(2)}) collective-permute-start(f32[1024,256]{1,0:T(8,128)} %get-tuple-element.138), channel_id=1, source_target_pairs={{1,2},{2,1},{5,6},{6,5},{9,10},{10,9},{13,14},{14,13},{17,18},{18,... | collective-permute-start | bytes 3145736 | tf_op jit(solution)/shard_map/ppermute | solution.py:30
  40.8 10.4 %copy-start.22 = (f32[1024,256]{1,0:T(8,128)S(1)}, f32[1024,256]{1,0:T(8,128)}, u32[]{:S(2)}) copy-start(f32[1024,256]{1,0:T(8,128)} %attention_forward.3) | copy-start | bytes 3145732
  42.8 5.3 copy-start.34
  48.0 27.4 %collective-permute-start.5 = (f32[1536,1024]{1,0:T(8,128)}, f32[1536,1024]{1,0:T(8,128)}, u32[]{:S(2)}, u32[]{:S(2)}) collective-permute-start(f32[1536,1024]{1,0:T(8,128)} %packed.1), channel_id=1, source_target_pairs={{0,2},{1,3},{2,0},{3,1},{4,6},{5,7},{6,4},{7,5},{8,10},{9,11},{10,... | collective-permute-start | bytes 18874376 | tf_op jit(solution)/shard_map/ppermute | solution.py:30
  48.1 15.5 %collective-permute-start.3 = (f32[256,1024]{1,0:T(8,128)S(1)}, f32[256,1024]{1,0:T(8,128)S(1)}, u32[]{:S(2)}, u32[]{:S(2)}) collective-permute-start(f32[256,1024]{1,0:T(8,128)S(1)} %collective-permute-done.1), channel_id=1, source_target_pairs={{1,5},{2,6},{5,1},{6,2},{9,13},{10,14},{13,9},{14,10},{17,21},{18,... | collective-permute-start | bytes 3145736 | tf_op jit(solution)/shard_map/ppermute | solution.py:30
  51.2 16.2 %collective-permute-start.2 = (f32[1024,256]{1,0:T(8,128)S(1)}, f32[1024,256]{1,0:T(8,128)}, u32[]{:S(2)}, u32[]{:S(2)}) collective-permute-start(f32[1024,256]{1,0:T(8,128)S(1)} %copy-done.22), channel_id=1, source_target_pairs={{1,2},{2,1},{5,6},{6,5},{9,10},{10,9},{13,14},{14,13},{17,18},{18,... | collective-permute-start | bytes 3145736 | tf_op jit(solution)/shard_map/ppermute | solution.py:30
  55.2 14.0 %copy-start.9 = (bf16[1024,256]{1,0:T(8,128)(2,1)}, bf16[1024,256]{1,0:T(8,128)(2,1)S(1)}, u32[]{:S(2)}) copy-start(bf16[1024,256]{1,0:T(8,128)(2,1)S(1)} %add_convert_fusion.6.low_ref) | copy-start | bytes 1572868
  55.3 8.5 %copy-start.25 = (bf16[512,1024]{1,0:T(8,128)(2,1)S(1)}, bf16[512,1024]{1,0:T(8,128)(2,1)}, u32[]{:S(2)}) copy-start(bf16[512,1024]{1,0:T(8,128)(2,1)} %param.25) | copy-start | bytes 3145732
  71.1 4.4 collective-permute-start.4
  73.1 13.3 %collective-permute-start.14 = (f32[128,1536]{1,0:T(8,128)S(1)}, f32[128,1536]{1,0:T(8,128)S(1)}, u32[]{:S(2)}, u32[]{:S(2)}) collective-permute-start(f32[128,1536]{1,0:T(8,128)S(1)} %convert_element_type.64), channel_id=1, source_target_pairs={{1,2},{2,1},{5,6},{6,5},{9,10},{10,9},{13,14},{14,13},{17,18},{18,... | collective-permute-start | bytes 2359304 | tf_op jit(solution)/shard_map/ppermute | solution.py:30
  87.3 326.4 %reduce-scatter.2.cloned.1.call-start = ((), (), s32[]{:S(2)}) async-start(), calls=%async_computation.2 | async-start | bytes 8912896 | tf_op jit(solution)/shard_map/reduce_scatter | solution.py:976
  87.6 25.5 %collective-permute-start.6 = (f32[256,1024]{1,0:T(8,128)}, f32[256,1024]{1,0:T(8,128)S(1)}, u32[]{:S(2)}, u32[]{:S(2)}) collective-permute-start(f32[256,1024]{1,0:T(8,128)} %get-tuple-element.148.hidden_ref), channel_id=1, source_target_pairs={{0,1},{1,0},{2,3},{3,2},{4,5},{5,4},{6,7},{7,6},{8,9},{9,8},{10,11... | collective-permute-start | bytes 3145736 | tf_op jit(solution)/shard_map/ppermute | solution.py:30
  92.2 43.4 %collective-permute-start.8 = (f32[256,1024]{1,0:T(8,128)}, f32[256,1024]{1,0:T(8,128)S(1)}, u32[]{:S(2)}, u32[]{:S(2)}) collective-permute-start(f32[256,1024]{1,0:T(8,128)} %get-tuple-element.150.hidden_ref), channel_id=1, source_target_pairs={{0,1},{1,0},{2,3},{3,2},{4,5},{5,4},{6,7},{7,6},{8,9},{9,8},{10,11... | collective-permute-start | bytes 3145736 | tf_op jit(solution)/shard_map/ppermute | solution.py:30
  123.1 34.9 %collective-permute-start.7 = (f32[256,1024]{1,0:T(8,128)}, f32[256,1024]{1,0:T(8,128)S(1)}, u32[]{:S(2)}, u32[]{:S(2)}) collective-permute-start(f32[256,1024]{1,0:T(8,128)} %get-tuple-element.157), channel_id=1, source_target_pairs={{0,1},{1,0},{2,3},{3,2},{4,5},{5,4},{6,7},{7,6},{8,9},{9,8},{10,11... | collective-permute-start | bytes 3145736 | tf_op jit(solution)/shard_map/ppermute | solution.py:30
  136.6 21.5 %copy-start.29 = (f32[256,1024]{1,0:T(8,128)S(1)}, f32[256,1024]{1,0:T(8,128)}, u32[]{:S(2)}) copy-start(f32[256,1024]{1,0:T(8,128)} %get-tuple-element.149) | copy-start | bytes 3145732
  145.7 34.8 %collective-permute-start.9 = (f32[256,1024]{1,0:T(8,128)}, f32[256,1024]{1,0:T(8,128)S(1)}, u32[]{:S(2)}, u32[]{:S(2)}) collective-permute-start(f32[256,1024]{1,0:T(8,128)} %get-tuple-element.161), channel_id=1, source_target_pairs={{0,1},{1,0},{2,3},{3,2},{4,5},{5,4},{6,7},{7,6},{8,9},{9,8},{10,11... | collective-permute-start | bytes 3145736 | tf_op jit(solution)/shard_map/ppermute | solution.py:30
  158.2 44.8 %collective-permute-start.10 = (f32[256,1024]{1,0:T(8,128)S(1)}, f32[256,1024]{1,0:T(8,128)S(1)}, u32[]{:S(2)}, u32[]{:S(2)}) collective-permute-start(f32[256,1024]{1,0:T(8,128)S(1)} %add.133.total_ref), channel_id=1, source_target_pairs={{0,1},{1,0},{2,3},{3,2},{4,5},{5,4},{6,7},{7,6},{8,9},{9,8},{10,11... | collective-permute-start | bytes 3145736 | tf_op jit(solution)/shard_map/ppermute | solution.py:30
  159.2 21.3 %copy-start.27 = (f32[256,1024]{1,0:T(8,128)S(1)}, f32[256,1024]{1,0:T(8,128)}, u32[]{:S(2)}) copy-start(f32[256,1024]{1,0:T(8,128)} %get-tuple-element.153) | copy-start | bytes 3145732
  180.7 43.8 %collective-permute-start.11 = (f32[256,1024]{1,0:T(8,128)S(1)}, f32[256,1024]{1,0:T(8,128)}, u32[]{:S(2)}, u32[]{:S(2)}) collective-permute-start(f32[256,1024]{1,0:T(8,128)S(1)} %add.134.total_ref), channel_id=1, source_target_pairs={{0,1},{1,0},{2,3},{3,2},{4,5},{5,4},{6,7},{7,6},{8,9},{9,8},{10,11... | collective-permute-start | bytes 3145736 | tf_op jit(solution)/shard_map/ppermute | solution.py:30
  224.5 11.5 %copy-start = (bf16[1024,2048]{1,0:T(8,128)(2,1)S(1)}, bf16[1024,2048]{1,0:T(8,128)(2,1)}, u32[]{:S(2)}) copy-start(bf16[1024,2048]{1,0:T(8,128)(2,1)} %get-tuple-element.191) | copy-start | bytes 12582916
  236.0 6.1 %copy-start.1 = (bf16[1024,1024]{1,0:T(8,128)(2,1)S(1)}, bf16[1024,1024]{1,0:T(8,128)(2,1)}, u32[]{:S(2)}) copy-start(bf16[1024,1024]{1,0:T(8,128)(2,1)} %get-tuple-element.190) | copy-start | bytes 6291460
  242.0 7.5 %collective-permute-start.15 = (f32[1024,1024]{1,0:T(8,128)}, f32[1024,1024]{1,0:T(8,128)}, u32[]{:S(2)}, u32[]{:S(2)}) collective-permute-start(f32[1024,1024]{1,0:T(8,128)} %fusion.1), channel_id=1, source_target_pairs={{0,2},{1,3},{2,0},{3,1},{4,6},{5,7},{6,4},{7,5},{8,10},{9,11},{10,... | collective-permute-start | bytes 12582920 | tf_op jit(solution)/shard_map/ppermute | solution.py:30
  249.5 7.1 %copy-start.2 = (bf16[1024,2048]{1,0:T(8,128)(2,1)S(1)}, bf16[1024,2048]{1,0:T(8,128)(2,1)}, u32[]{:S(2)}) copy-start(bf16[1024,2048]{1,0:T(8,128)(2,1)} %get-tuple-element.195) | copy-start | bytes 12582916
  249.5 7.1 %copy-start.3 = (bf16[1024,1024]{1,0:T(8,128)(2,1)S(1)}, bf16[1024,1024]{1,0:T(8,128)(2,1)}, u32[]{:S(2)}) copy-start(bf16[1024,1024]{1,0:T(8,128)(2,1)} %get-tuple-element.194) | copy-start | bytes 6291460
  263.5 5.1 copy-start.14
  263.5 5.1 copy-start.15
  263.5 28.6 %collective-permute-start.17 = (f32[256,1024]{1,0:T(8,128)}, f32[256,1024]{1,0:T(8,128)}, u32[]{:S(2)}, u32[]{:S(2)}) collective-permute-start(f32[256,1024]{1,0:T(8,128)} %get-tuple-element.179), channel_id=1, source_target_pairs={{0,1},{1,0},{2,3},{3,2},{4,5},{5,4},{6,7},{7,6},{8,9},{9,8},{10,11... | collective-permute-start | bytes 3145736 | tf_op jit(solution)/shard_map/ppermute | solution.py:30
  264.6 46.4 %collective-permute-start.16 = (f32[256,1024]{1,0:T(8,128)}, f32[256,1024]{1,0:T(8,128)}, u32[]{:S(2)}, u32[]{:S(2)}) collective-permute-start(f32[256,1024]{1,0:T(8,128)} %get-tuple-element.203), channel_id=1, source_target_pairs={{0,1},{1,0},{2,3},{3,2},{4,5},{5,4},{6,7},{7,6},{8,9},{9,8},{10,11... | collective-permute-start | bytes 3145736 | tf_op jit(solution)/shard_map/ppermute | solution.py:30
  265.1 1.5 collective-permute-start.13
  266.7 6.8 %copy-start.45 = (s32[1,5]{1,0:T(1,128)}, s32[1,5]{1,0:T(1,128)S(1)}, u32[]{:S(2)}) copy-start(s32[1,5]{1,0:T(1,128)S(1)} %fusion.21) | copy-start | bytes 64
  267.3 50.5 %collective-permute-start.19 = (f32[4,128,1024]{2,1,0:T(8,128)}, f32[4,128,1024]{2,1,0:T(8,128)}, u32[]{:S(2)}, u32[]{:S(2)}) collective-permute-start(f32[4,128,1024]{2,1,0:T(8,128)} %get-tuple-element.193), channel_id=1, source_target_pairs={{0,4},{1,5},{2,10},{3,11},{4,0},{5,1},{6,14},{7,15},{8,12},{9,13},... | collective-permute-start | bytes 6291464 | tf_op jit(solution)/shard_map/ppermute | solution.py:30
  316.8 9.4 %collective-permute-start.18 = (f32[512,1024]{1,0:T(8,128)}, f32[512,1024]{1,0:T(8,128)}, u32[]{:S(2)}, u32[]{:S(2)}) collective-permute-start(f32[512,1024]{1,0:T(8,128)} %get-tuple-element.211), channel_id=1, source_target_pairs={{0,2},{1,3},{2,0},{3,1},{4,6},{5,7},{6,4},{7,5},{8,10},{9,11},{10,... | collective-permute-start | bytes 6291464 | tf_op jit(solution)/shard_map/ppermute | solution.py:30
  317.8 6.7 %copy-start.10 = (bf16[1024,256]{1,0:T(8,128)(2,1)S(1)}, bf16[1024,256]{1,0:T(8,128)(2,1)}, u32[]{:S(2)}) copy-start(bf16[1024,256]{1,0:T(8,128)(2,1)} %copy-done.9) | copy-start | bytes 1572868
  317.8 6.7 %copy-start.12 = (bf16[1024,256]{1,0:T(8,128)(2,1)S(1)}, bf16[1024,256]{1,0:T(8,128)(2,1)}, u32[]{:S(2)}) copy-start(bf16[1024,256]{1,0:T(8,128)(2,1)} %copy-done.11) | copy-start | bytes 1572868
  317.8 7.8 %copy-start.43 = (f32[2,4,1024]{2,1,0:T(4,128)S(1)}, f32[2,4,1024]{2,1,0:T(4,128)}, u32[]{:S(2)}) copy-start(f32[2,4,1024]{2,1,0:T(4,128)} %get-tuple-element.202) | copy-start | bytes 98308
  322.1 34.6 %collective-permute-start.20 = (f32[2,128,1024]{2,1,0:T(8,128)}, f32[2,128,1024]{2,1,0:T(8,128)}, u32[]{:S(2)}, u32[]{:S(2)}) collective-permute-start(f32[2,128,1024]{2,1,0:T(8,128)} %get-tuple-element.215), channel_id=1, source_target_pairs={{0,8},{1,9},{2,18},{3,19},{4,12},{5,13},{6,22},{7,23},{8,0},{9,1},... | collective-permute-start | bytes 3145736 | tf_op jit(solution)/shard_map/ppermute | solution.py:30
  361.7 7.4 %copy-start.4 = (bf16[1024,1536]{1,0:T(8,128)(2,1)}, bf16[1024,1536]{1,0:T(8,128)(2,1)S(1)}, u32[]{:S(2)}) copy-start(bf16[1024,1536]{1,0:T(8,128)(2,1)S(1)} %constant_dynamic-update-slice_fusion.4.grad_ref) | copy-start | bytes 9437188
  375.7 7.7 %copy-start.35 = (bf16[1024,512]{1,0:T(8,128)(2,1)S(1)}, bf16[1024,512]{1,0:T(8,128)(2,1)}, u32[]{:S(2)}) copy-start(bf16[1024,512]{1,0:T(8,128)(2,1)} %pad_maximum_fusion.5) | copy-start | bytes 3145732
  375.7 42.4 %collective-permute-start.26 = (f32[4,128,1536]{2,1,0:T(8,128)}, f32[4,128,1536]{2,1,0:T(8,128)}, u32[]{:S(2)}, u32[]{:S(2)}) collective-permute-start(f32[4,128,1536]{2,1,0:T(8,128)} %get-tuple-element.227), channel_id=1, source_target_pairs={{0,4},{1,5},{2,10},{3,11},{4,0},{5,1},{6,14},{7,15},{8,12},{9,13},... | collective-permute-start | bytes 9437192 | tf_op jit(solution)/shard_map/ppermute | solution.py:30
  383.4 6.4 %copy-start.30 = (f32[256,1024]{1,0:T(8,128)S(1)}, f32[256,1024]{1,0:T(8,128)}, u32[]{:S(2)}) copy-start(f32[256,1024]{1,0:T(8,128)} %get-tuple-element.165) | copy-start | bytes 3145732
  383.4 11.4 %collective-permute-start.21 = (f32[512,1024]{1,0:T(8,128)}, f32[512,1024]{1,0:T(8,128)}, u32[]{:S(2)}, u32[]{:S(2)}) collective-permute-start(f32[512,1024]{1,0:T(8,128)} %input_other.1), channel_id=1, source_target_pairs={{0,2},{1,3},{2,0},{3,1},{4,6},{5,7},{6,4},{7,5},{8,10},{9,11},{10,... | collective-permute-start | bytes 6291464 | tf_op jit(solution)/shard_map/ppermute | solution.py:30
  386.0 27.8 %collective-permute-start.23 = (f32[1024,512]{1,0:T(8,128)}, f32[1024,512]{1,0:T(8,128)}, u32[]{:S(2)}, u32[]{:S(2)}) collective-permute-start(f32[1024,512]{1,0:T(8,128)} %fusion.5), channel_id=1, source_target_pairs={{1,2},{2,1},{5,6},{6,5},{9,10},{10,9},{13,14},{14,13},{17,18},{18,... | collective-permute-start | bytes 6291464 | tf_op jit(solution)/shard_map/ppermute | solution.py:30
  393.9 70.6 %collective-permute-start.12 = (f32[512,1024]{1,0:T(8,128)}, f32[512,1024]{1,0:T(8,128)}, u32[]{:S(2)}, u32[]{:S(2)}) collective-permute-start(f32[512,1024]{1,0:T(8,128)} %broadcast_select_fusion.2), channel_id=1, source_target_pairs={{0,2},{1,3},{2,0},{3,1},{4,6},{5,7},{6,4},{7,5},{8,10},{9,11},{10,... | collective-permute-start | bytes 6291464 | tf_op jit(solution)/shard_map/ppermute | solution.py:30
  418.1 11.1 %collective-permute-start.25 = (f32[1024,256]{1,0:T(8,128)}, f32[1024,256]{1,0:T(8,128)S(1)}, u32[]{:S(2)}, u32[]{:S(2)}) collective-permute-start(f32[1024,256]{1,0:T(8,128)} %get-tuple-element.276), channel_id=1, source_target_pairs={{0,2},{1,3},{2,0},{3,1},{4,6},{5,7},{6,4},{7,5},{8,10},{9,11},{10,... | collective-permute-start | bytes 3145736 | tf_op jit(solution)/shard_map/ppermute | solution.py:30
  422.9 37.3 %collective-permute-start.29 = (f32[2,128,1536]{2,1,0:T(8,128)}, f32[2,128,1536]{2,1,0:T(8,128)}, u32[]{:S(2)}, u32[]{:S(2)}) collective-permute-start(f32[2,128,1536]{2,1,0:T(8,128)} %get-tuple-element.240), channel_id=1, source_target_pairs={{0,8},{1,9},{2,18},{3,19},{4,12},{5,13},{6,22},{7,23},{8,0},{9,1},... | collective-permute-start | bytes 4718600 | tf_op jit(solution)/shard_map/ppermute | solution.py:30
  423.7 49.6 %collective-permute-start.22 = (f32[512,1024]{1,0:T(8,128)}, f32[512,1024]{1,0:T(8,128)}, u32[]{:S(2)}, u32[]{:S(2)}) collective-permute-start(f32[512,1024]{1,0:T(8,128)} %get-tuple-element.232), channel_id=1, source_target_pairs={{0,1},{1,0},{2,3},{3,2},{4,5},{5,4},{6,7},{7,6},{8,9},{9,8},{10,11... | collective-permute-start | bytes 6291464 | tf_op jit(solution)/shard_map/ppermute | solution.py:30
  424.8 1.5 collective-permute-start.24
  434.7 19.1 %collective-permute-start.27 = (f32[4,128,384]{2,1,0:T(8,128)}, f32[4,128,384]{2,1,0:T(8,128)S(1)}, u32[]{:S(2)}, u32[]{:S(2)}) collective-permute-start(f32[4,128,384]{2,1,0:T(8,128)} %get-tuple-element.244), channel_id=1, source_target_pairs={{0,4},{1,5},{2,6},{3,7},{4,0},{5,1},{6,2},{7,3},{8,12},{9,13},{10,... | collective-permute-start | bytes 2359304 | tf_op jit(solution)/shard_map/ppermute | solution.py:30
  457.7 11.9 %collective-permute-start.28 = (f32[2,128,384]{2,1,0:T(8,128)}, f32[2,128,384]{2,1,0:T(8,128)S(1)}, u32[]{:S(2)}, u32[]{:S(2)}) collective-permute-start(f32[2,128,384]{2,1,0:T(8,128)} %get-tuple-element.248), channel_id=1, source_target_pairs={{0,8},{1,9},{2,10},{3,11},{4,12},{5,13},{6,14},{7,15},{8,0},{9,1},... | collective-permute-start | bytes 1179656 | tf_op jit(solution)/shard_map/ppermute | solution.py:30
  464.1 17.1 %collective-permute-start.32 = (f32[1,128,1536]{2,1,0:T(8,128)}, f32[1,128,1536]{2,1,0:T(8,128)S(1)}, u32[]{:S(2)}, u32[]{:S(2)}) collective-permute-start(f32[1,128,1536]{2,1,0:T(8,128)} %get-tuple-element.251), channel_id=1, source_target_pairs={{0,16},{1,17},{2,6},{3,7},{4,20},{5,21},{6,2},{7,3},{8,24},{9,25},... | collective-permute-start | bytes 2359304 | tf_op jit(solution)/shard_map/ppermute | solution.py:30
  466.9 14.1 %collective-permute-start.36 = (f32[1,128,1024]{2,1,0:T(8,128)S(1)}, f32[1,128,1024]{2,1,0:T(8,128)S(1)}, u32[]{:S(2)}, u32[]{:S(2)}) collective-permute-start(f32[1,128,1024]{2,1,0:T(8,128)S(1)} %copy-done.48), channel_id=1, source_target_pairs={{0,16},{1,17},{2,6},{3,7},{4,20},{5,21},{6,2},{7,3},{8,24},{9,25},... | collective-permute-start | bytes 1572872 | tf_op jit(solution)/shard_map/ppermute | solution.py:30
  472.9 8.1 %copy-start.41 = (f32[1,128,1024]{2,1,0:T(8,128)S(1)}, f32[1,128,1024]{2,1,0:T(8,128)}, u32[]{:S(2)}) copy-start(f32[1,128,1024]{2,1,0:T(8,128)} %get-tuple-element.262) | copy-start | bytes 1572868
  472.9 20.4 %collective-permute-start.31 = (f32[1,128,384]{2,1,0:T(8,128)}, f32[1,128,384]{2,1,0:T(8,128)S(1)}, u32[]{:S(2)}, u32[]{:S(2)}) collective-permute-start(f32[1,128,384]{2,1,0:T(8,128)} %get-tuple-element.253), channel_id=1, source_target_pairs={{0,16},{1,17},{2,18},{3,19},{4,20},{5,21},{6,22},{7,23},{8,24},{9,... | collective-permute-start | bytes 589832 | tf_op jit(solution)/shard_map/ppermute | solution.py:30
  475.2 6.0 %copy-start.40 = (f32[1,128,1536]{2,1,0:T(8,128)S(1)}, f32[1,128,1536]{2,1,0:T(8,128)}, u32[]{:S(2)}) copy-start(f32[1,128,1536]{2,1,0:T(8,128)} %get-tuple-element.256) | copy-start | bytes 2359300
  475.2 41.3 %collective-permute-start.30 = (f32[512,1024]{1,0:T(8,128)S(1)}, f32[512,1024]{1,0:T(8,128)S(1)}, u32[]{:S(2)}, u32[]{:S(2)}) collective-permute-start(f32[512,1024]{1,0:T(8,128)S(1)} %broadcast_select_fusion), channel_id=1, source_target_pairs={{0,2},{1,3},{2,0},{3,1},{4,6},{5,7},{6,4},{7,5},{8,10},{9,11},{10,... | collective-permute-start | bytes 6291464 | tf_op jit(solution)/shard_map/ppermute | solution.py:30
  481.1 12.2 %copy-start.44 = (f32[1,128,128]{2,1,0:T(8,128)S(1)}, f32[1,128,128]{2,1,0:T(8,128)}, u32[]{:S(2)}) copy-start(f32[1,128,128]{2,1,0:T(8,128)} %get-tuple-element.255) | copy-start | bytes 196612
  481.2 28.2 %copy-start.42 = (f32[1,128,256]{2,1,0:T(8,128)S(1)}, f32[1,128,256]{2,1,0:T(8,128)}, u32[]{:S(2)}) copy-start(f32[1,128,256]{2,1,0:T(8,128)} %get-tuple-element.261) | copy-start | bytes 393220
  481.4 31.4 %collective-permute-start.34 = (f32[64,1536]{1,0:T(8,128)S(1)}, f32[64,1536]{1,0:T(8,128)S(1)}, u32[]{:S(2)}, u32[]{:S(2)}) collective-permute-start(f32[64,1536]{1,0:T(8,128)S(1)} %get-tuple-element.258), channel_id=1, source_target_pairs={{0,2},{1,0},{2,3},{3,1},{4,6},{5,4},{6,7},{7,5},{8,10},{9,8},{10,1... | collective-permute-start | bytes 1179656 | tf_op jit(solution)/shard_map/ppermute | solution.py:30
  493.4 16.2 %collective-permute-start.33 = (f32[4,64]{0,1:T(8,128)S(1)}, f32[4,64]{0,1:T(8,128)S(1)}, u32[]{:S(2)}, u32[]{:S(2)}) collective-permute-start(f32[4,64]{0,1:T(8,128)S(1)} %slice_bitcast_fusion), channel_id=1, source_target_pairs={{0,1},{1,0},{2,3},{3,2},{4,5},{5,4},{6,7},{7,6},{8,9},{9,8},{10,11... | collective-permute-start | bytes 3080 | tf_op jit(solution)/shard_map/ppermute | solution.py:30
  505.0 10.6 %collective-permute-start.35 = (f32[64,1536]{1,0:T(8,128)S(1)}, f32[64,1536]{1,0:T(8,128)S(1)}, u32[]{:S(2)}, u32[]{:S(2)}) collective-permute-start(f32[64,1536]{1,0:T(8,128)S(1)} %get-tuple-element.260), channel_id=1, source_target_pairs={{1,2},{2,1},{5,6},{6,5},{9,10},{10,9},{13,14},{14,13},{17,18},{18,... | collective-permute-start | bytes 1179656 | tf_op jit(solution)/shard_map/ppermute | solution.py:30
  509.5 1.7 collective-permute-start.37
  (25 other events, 54.4 us)
Sparse Core Ops, SparseCore 0:
  87.5 97.4 all-gather.1
Sparse Core Ops, SparseCore 1:
  263.6 108.7 reduce-scatter.1

commit v6 on v5

--- a/solution.py
+++ b/solution.py
@@ -1019,12 +1019,12 @@
     )
     grad_in_sent = send(grad_in_own, over)
     gains = jnp.stack([gain_in_attn[0], gain_out_attn, gain_in_mlp, gain_out_mlp], axis=0)
-    weight_out_sent, gains = after((weight_out_sent, gains), grad_up)
+    gate = late.hop(grad_in_own)
+    weight_out_sent, gains = after((weight_out_sent, gains), grad_up, gate)
     gains = jnp.pad((gains + send(gains, cross)).T, ((0, 0), (0, LANES - 4)))
     weight_out = weight_out * keep + weight_out_sent
     out_sent = send(half_columns(weight_out, 1 - core, out_rows), cross)
     extra = Sum([half_columns(weight_out, core, out_rows), gains], out_sent, plain=True)
-    gate = late.hop(weight_out)
     gate = extra.hop(gate)
     gate = extra.hop(gate)
     gate = late.hop(gate)

time: 538 us -> 536 us (level)
  transfers between devices with their start and end apart: 40 -> 40, of which waited for: 21 -> 23; matrix products, arithmetic and copies ran while one was open for 13% -> 13% of each run, Pallas kernels for 43% -> 43%
where the time goes in v6:
time: 536 us; the launch traced here: 528 us
  Pallas kernels  232 us (43%)
  waiting for transfers between devices  136 us (25%)
  starting transfers between devices  53 us (10%)
  other arithmetic  32.5 us (6%)
  matrix products  31.8 us (6%)
  local copies, waits for them, and re-layouts  25.1 us (5%)
  between operations  17.4 us (3%)
    ppermute x38, waiting for transfers between devices, send(): return lax.ppermute(values, ('dp', 'tensor'), pairs)  136 us
    pallas_call x14, Pallas kernels, call(): pl.pallas_call(kernel, grid_spec=pltpu.PrefetchScalarGridSpec(num_scalar_...  113 us
    ppermute x38, starting transfers between devices, send(): return lax.ppermute(values, ('dp', 'tensor'), pairs)  52.8 us
    pallas_call x9, Pallas kernels, halves(): pl.pallas_call(partial(halves_kernel, len(held), sources), grid_spec=pltp...  40.2 us
    pallas_call x1, Pallas kernels, attention_backward(): pl.pallas_call(partial(backward_kernel, lengths.shape[1]), grid=(pairs,),...  25.9 us
    pallas_call x2, Pallas kernels, attention_forward(): pl.pallas_call(partial(forward_kernel, lengths.shape[1], first), grid=(1,...  23.5 us
    pallas_call x1, Pallas kernels, attention_ready(): pl.pallas_call(partial(ready_kernel, lengths.shape[1]), grid=(wide // gro...  18.6 us
    unnamed x103, local copies, waits for them, and re-layouts  15.3 us
  transfers between devices with their start and end apart: 40, of which 23 were waited for; matrix products, arithmetic and copies ran while one was open for 13% of the time, Pallas kernels for 43%

profile of v6, /device:TPU:1, one launch (start us, length us, event | category | flops | bytes accessed | tf_op | source)
XLA Modules:
  0.0 527.9 jit_solution(7987131712682838311)
XLA Ops:
  9.2 4.5 collective-permute-start.1
  14.4 12.0 %attention_forward.2 = (f32[1024,256]{1,0:T(8,128)}, bf16[1024,1024]{1,0:T(8,128)(2,1)}, f32[1024,128]{1,0:T(8,128)}, f32[1024,128]{1,0:T(8,128)}) custom-call(s32[1,4]{1,0:T(1,128)} %lengths_ref.3, s32[1]{0:T(128)S(6)} %copy.65.pad_ref, f32[32,1]{1,0:T(8,128)} %constant.57.clone.freq_ref, f32[1,1024]{1,0:T(1,128)} %bitcast.77, ...), custom_call_target="tpu_custom_call" | custom-call | flops 1 | bytes 1 | tf_op jit(solution)/shard_map/attention_forward/pallas_call | solution.py:278
  26.5 2.1 collective-permute-start
  29.3 11.4 %attention_forward.3 = f32[1024,256]{1,0:T(8,128)} custom-call(s32[1,4]{1,0:T(1,128)} %lengths_ref.3, s32[1]{0:T(128)S(6)} %copy.65.pad_ref, f32[32,1]{1,0:T(8,128)} %constant.57.clone.freq_ref, f32[1,1024]{1,0:T(1,128)} %bitcast.78, bf16[1024,1024]{1,0:T(8,128)(2,1)} %get-tuple-element.142.refs_0_, f32[1024,128]{1,0:T(8,128)} %get-tuple-element.143.refs_1_, ...), custom_call_target="tpu_custom_call" | custom-call | flops 1 | bytes 1 | tf_op jit(solution)/shard_map/attention_forward/pallas_call | solution.py:278
  42.8 5.1 packed.1
  47.9 3.1 collective-permute-start.3
  51.0 2.2 collective-permute-start.2
  55.0 8.5 %collective-permute-done.3 = f32[256,1024]{1,0:T(8,128)S(1)} collective-permute-done((f32[256,1024]{1,0:T(8,128)S(1)}, f32[256,1024]{1,0:T(8,128)S(1)}, u32[]{:S(2)}, u32[]{:S(2)}) %collective-permute-start.3) | collective-permute-done | bytes 1048608 | tf_op jit(solution)/shard_map/ppermute | solution.py:30
  64.0 3.2 collective-permute-done.2
  73.0 2.2 collective-permute-start.14
  76.6 4.5 hidden.2
  81.1 5.2 collective-permute-done.14
  87.5 4.5 hidden.3
  93.5 9.3 %mlp_forward.4 = (bf16[1024,1024]{1,0:T(8,128)(2,1)}, bf16[1024,2048]{1,0:T(8,128)(2,1)}, f32[256,2048]{1,0:T(8,128)}, f32[256,1024]{1,0:T(8,128)}) custom-call(f32[256,1024]{1,0:T(8,128)} %get-tuple-element.148.hidden_ref, f32[1,1024]{1,0:T(1,128)} %bitcast.71, bf16[1024,2048]{1,0:T(8,128)(2,1)} %up_ref.15, bf16[2048,1024]{1,0:T(8,128)(2,1)} %down_ref.15), custom_call_target="tpu_custom_call" | custom-call | flops 1 | bytes 1 | tf_op jit(solution)/shard_map/mlp_forward/pallas_call | solution.py:521
  102.8 9.0 %mlp_forward.5 = (bf16[1024,1024]{1,0:T(8,128)(2,1)}, bf16[1024,2048]{1,0:T(8,128)(2,1)}, f32[256,2048]{1,0:T(8,128)}, f32[256,1024]{1,0:T(8,128)}) custom-call(f32[256,1024]{1,0:T(8,128)} %get-tuple-element.150.hidden_ref, f32[1,1024]{1,0:T(1,128)} %bitcast.72, bf16[1024,2048]{1,0:T(8,128)(2,1)} %up_ref.15, ...), custom_call_target="tpu_custom_call", output_to_operand_aliasing={{0}: (4, {}), {1}: (5, {})} | custom-call | flops 1 | bytes 1 | tf_op jit(solution)/shard_map/mlp_forward/pallas_call | solution.py:521
  113.9 9.0 %mlp_forward.6 = (bf16[1024,1024]{1,0:T(8,128)(2,1)}, bf16[1024,2048]{1,0:T(8,128)(2,1)}, f32[256,2048]{1,0:T(8,128)}, f32[256,1024]{1,0:T(8,128)}) custom-call(f32[256,1024]{1,0:T(8,128)} %copy-done.19, f32[1,1024]{1,0:T(1,128)} %bitcast.73, bf16[1024,2048]{1,0:T(8,128)(2,1)} %up_ref.15, ...), custom_call_target="tpu_custom_call", output_to_operand_aliasing={{0}: (4, {}), {1}: (5, {})} | custom-call | flops 1 | bytes 1 | tf_op jit(solution)/shard_map/mlp_forward/pallas_call | solution.py:521
  123.0 12.4 %collective-permute-done.8.hidden_ref = f32[256,1024]{1,0:T(8,128)S(1)} collective-permute-done((f32[256,1024]{1,0:T(8,128)}, f32[256,1024]{1,0:T(8,128)S(1)}, u32[]{:S(2)}, u32[]{:S(2)}) %collective-permute-start.8) | collective-permute-done | bytes 1048608 | tf_op jit(solution)/shard_map/ppermute | solution.py:30
  136.4 9.1 %mlp_forward.7 = (bf16[1024,1024]{1,0:T(8,128)(2,1)}, bf16[1024,2048]{1,0:T(8,128)(2,1)}, f32[256,2048]{1,0:T(8,128)}, f32[256,1024]{1,0:T(8,128)}) custom-call(f32[256,1024]{1,0:T(8,128)} %copy-done.18, f32[1,1024]{1,0:T(1,128)} %bitcast.74, bf16[1024,2048]{1,0:T(8,128)(2,1)} %up_ref.15, ...), custom_call_target="tpu_custom_call", output_to_operand_aliasing={{0}: (4, {}), {1}: (5, {})} | custom-call | flops 1 | bytes 1 | tf_op jit(solution)/shard_map/mlp_forward/pallas_call | solution.py:521
  145.6 12.3 %collective-permute-done.7 = f32[256,1024]{1,0:T(8,128)S(1)} collective-permute-done((f32[256,1024]{1,0:T(8,128)}, f32[256,1024]{1,0:T(8,128)S(1)}, u32[]{:S(2)}, u32[]{:S(2)}) %collective-permute-start.7) | collective-permute-done | bytes 1048608 | tf_op jit(solution)/shard_map/ppermute | solution.py:30
  159.0 11.2 %mlp_backward.4 = (f32[256,1024]{1,0:T(8,128)}, bf16[1024,1024]{1,0:T(8,128)(2,1)}, f32[8,1024]{1,0:T(8,128)}, bf16[1024,2048]{1,0:T(8,128)(2,1)}, f32[256,1024]{1,0:T(8,128)}) custom-call(s32[14]{0:T(128)} %stack.54.where_ref, f32[256,1024]{1,0:T(8,128)} %get-tuple-element.148.hidden_ref, f32[256,1024]{1,0:T(8,128)} %copy-done.20, ...), custom_call_target="tpu_custom_call" | custom-call | flops 1 | bytes 1 | tf_op jit(solution)/shard_map/mlp_backward/pallas_call | solution.py:521
  170.2 10.2 %collective-permute-done.9 = f32[256,1024]{1,0:T(8,128)S(1)} collective-permute-done((f32[256,1024]{1,0:T(8,128)}, f32[256,1024]{1,0:T(8,128)S(1)}, u32[]{:S(2)}, u32[]{:S(2)}) %collective-permute-start.9) | collective-permute-done | bytes 1048608 | tf_op jit(solution)/shard_map/ppermute | solution.py:30
  181.5 10.9 %mlp_backward.5 = (f32[256,1024]{1,0:T(8,128)}, bf16[1024,1024]{1,0:T(8,128)(2,1)}, f32[8,1024]{1,0:T(8,128)}, bf16[1024,2048]{1,0:T(8,128)(2,1)}, f32[256,1024]{1,0:T(8,128)}) custom-call(s32[14]{0:T(128)} %stack.54.where_ref, f32[256,1024]{1,0:T(8,128)} %get-tuple-element.150.hidden_ref, ...), custom_call_target="tpu_custom_call", output_to_operand_aliasing={{1}: (9, {}), {3}: (10, {})} | custom-call | flops 1 | bytes 1 | tf_op jit(solution)/shard_map/mlp_backward/pallas_call | solution.py:521
  192.4 10.4 %collective-permute-done.10.total_ref = f32[256,1024]{1,0:T(8,128)S(1)} collective-permute-done((f32[256,1024]{1,0:T(8,128)S(1)}, f32[256,1024]{1,0:T(8,128)S(1)}, u32[]{:S(2)}, u32[]{:S(2)}) %collective-permute-start.10) | collective-permute-done | bytes 1048608 | tf_op jit(solution)/shard_map/ppermute | solution.py:30
  203.8 10.9 %mlp_backward.6 = (f32[256,1024]{1,0:T(8,128)}, bf16[1024,1024]{1,0:T(8,128)(2,1)}, f32[8,1024]{1,0:T(8,128)}, bf16[1024,2048]{1,0:T(8,128)(2,1)}, f32[256,1024]{1,0:T(8,128)}) custom-call(s32[2]{0:T(128)} %pad_add_fusion.where_ref, f32[256,1024]{1,0:T(8,128)} %copy-done.19, f32[256,1024]{1,0:T(8,128)} %copy-done.29, ...), custom_call_target="tpu_custom_call", output_to_operand_aliasing={{1}: (9, {}), {3}: (10, {})} | custom-call | flops 1 | bytes 1 | tf_op jit(solution)/shard_map/mlp_backward/pallas_call | solution.py:521
  214.8 9.4 %collective-permute-done.11.total_ref = f32[256,1024]{1,0:T(8,128)} collective-permute-done((f32[256,1024]{1,0:T(8,128)S(1)}, f32[256,1024]{1,0:T(8,128)}, u32[]{:S(2)}, u32[]{:S(2)}) %collective-permute-start.11) | collective-permute-done | bytes 1048608 | tf_op jit(solution)/shard_map/ppermute | solution.py:30
  224.2 11.5 %mlp_backward.7 = (f32[256,1024]{1,0:T(8,128)}, bf16[1024,1024]{1,0:T(8,128)(2,1)}, f32[8,1024]{1,0:T(8,128)}, bf16[1024,2048]{1,0:T(8,128)(2,1)}, f32[256,1024]{1,0:T(8,128)}) custom-call(s32[2]{0:T(128)} %pad_add_fusion.where_ref, f32[256,1024]{1,0:T(8,128)} %copy-done.18, ...), custom_call_target="tpu_custom_call", output_to_operand_aliasing={{1}: (9, {}), {3}: (10, {})} | custom-call | flops 1 | bytes 1 | tf_op jit(solution)/shard_map/mlp_backward/pallas_call | solution.py:521
  235.7 6.2 %fusion.1 = f32[1024,1024]{1,0:T(8,128)} fusion(bf16[1024,1024]{1,0:T(8,128)(2,1)} %get-tuple-element.190, bf16[1024,2048]{1,0:T(8,128)(2,1)S(1)} %copy-done, s32[]{:T(128)S(6)} %select_n.143), kind=kOutput, calls=%fused_computation.11 | convolution fusion | flops 2147483648 | bytes 8388612 | tf_op jit(solution)/shard_map/td,tf->df/dot_general | solution.py:969
  242.0 6.0 %fusion.3 = f32[1024,1024]{1,0:T(8,128)} fusion(bf16[1024,1024]{1,0:T(8,128)(2,1)S(1)} %copy-done.1, bf16[1024,2048]{1,0:T(8,128)(2,1)} %get-tuple-element.191, s32[]{:T(128)S(6)} %select_n.142), kind=kOutput, calls=%fused_computation.13 | convolution fusion | flops 2147483648 | bytes 8388612 | tf_op jit(solution)/shard_map/td,tf->df/dot_general | solution.py:969
  249.5 7.1 %halves.9 = (f32[4,128,1024]{2,1,0:T(8,128)}, f32[4,128,1024]{2,1,0:T(8,128)}) custom-call(s32[14]{0:T(128)} %stack.54.where_ref, f32[8,128,1024]{2,1,0:T(8,128)} %bitcast.61, f32[8,128,1024]{2,1,0:T(8,128)} %bitcast.62, f32[8,128,1024]{2,1,0:T(8,128)} %bitcast.17.refs_2_.refs_3_, f32[8,128,1024]{2,1,0:T(8,128)} %bitcast.17.refs_2_.refs_3_), custom_call_target="tpu_custom_call" | custom-call | flops 1 | bytes 1 | tf_op jit(solution)/shard_map/halves/pallas_call | solution.py:721
  256.6 6.8 %fusion.26 = f32[1024,2048]{1,0:T(8,128)} fusion(bf16[1024,1024]{1,0:T(8,128)(2,1)S(1)} %copy-done.3, bf16[1024,2048]{1,0:T(8,128)(2,1)S(1)} %copy-done.2), kind=kOutput, calls=%fused_computation.87 | convolution fusion | flops 4294967296 | bytes 14680064 | tf_op jit(solution)/shard_map/td,tf->df/dot_general | solution.py:975
  268.5 5.0 add_convert_fusion.wq_ref.wk_ref.wv_ref.weight_ref
  273.5 18.6 %attention_ready.1 = (bf16[1024,512]{1,0:T(8,128)(2,1)}, bf16[1024,512]{1,0:T(8,128)(2,1)}, bf16[1024,512]{1,0:T(8,128)(2,1)}, f32[2,4,1024]{2,1,0:T(4,128)}, bf...) custom-call(s32[14]{0:T(128)} %stack.54.where_ref, s32[1,4]{1,0:T(1,128)} %bitcast.89, ...), custom_call_target="tpu_custom_call" | custom-call | flops 1 | bytes 1 | tf_op jit(solution)/shard_map/attention_ready/pallas_call | solution.py:304
  292.1 5.8 %residual.2 = (f32[512,1024]{1,0:T(8,128)}, f32[512,1024]{1,0:T(8,128)}, f32[8,1024]{1,0:T(8,128)}) custom-call(s32[14]{0:T(128)} %stack.54.where_ref, f32[256,1024]{1,0:T(8,128)} %get-tuple-element.166.part_ref, f32[256,1024]{1,0:T(8,128)} %collective-permute-done.17.arrived_ref, f32[256,1024]{1,0:T(8,128)} %get-tuple-element.148.hidden_ref, ...), custom_call_target="tpu_custom_call" | custom-call | flops 1 | bytes 1 | tf_op jit(solution)/shard_map/residual/pallas_call | solution.py:521
  298.0 12.9 %collective-permute-done.16.arrived_ref = f32[256,1024]{1,0:T(8,128)} collective-permute-done((f32[256,1024]{1,0:T(8,128)}, f32[256,1024]{1,0:T(8,128)}, u32[]{:S(2)}, u32[]{:S(2)}) %collective-permute-start.16) | collective-permute-done | bytes 1048608 | tf_op jit(solution)/shard_map/ppermute | solution.py:30
  310.9 5.9 %residual.3 = (f32[512,1024]{1,0:T(8,128)}, f32[512,1024]{1,0:T(8,128)}, f32[8,1024]{1,0:T(8,128)}) custom-call(s32[14]{0:T(128)} %stack.54.where_ref, f32[256,1024]{1,0:T(8,128)} %get-tuple-element.173.part_ref, f32[256,1024]{1,0:T(8,128)} %collective-permute-done.16.arrived_ref, ...), custom_call_target="tpu_custom_call", output_to_operand_aliasing={{0}: (9, {}), {1}: (10, {})} | custom-call | flops 1 | bytes 1 | tf_op jit(solution)/shard_map/residual/pallas_call | solution.py:521
  317.7 4.3 halves.10
  322.0 2.4 collective-permute-start.20
  325.0 2.3 add_convert_fusion.2
  327.3 2.3 convolution_convert_fusion.grad_ref
  329.6 25.9 %attention_backward.1 = (bf16[1024,512]{1,0:T(8,128)(2,1)}, bf16[1024,512]{1,0:T(8,128)(2,1)}, bf16[1024,512]{1,0:T(8,128)(2,1)}) custom-call(s32[1,4]{1,0:T(1,128)} %bitcast.90, s32[1]{0:T(128)} %bitcast.15.pad_ref, f32[1024,128]{1,0:T(8,128)} %get-tuple-element.197.cos_ref, f32[1024,128]{1,0:T(8,128)} %get-tuple-element.198.sin_ref, ...), custom_call_target="tpu_custom_call" | custom-call | flops 1 | bytes 1 | tf_op jit(solution)/shard_map/attention_backward/pallas_call | solution.py:333
  356.5 3.4 halves.11
  363.4 5.6 %fusion.27 = f32[1024,1536]{1,0:T(8,128)} fusion(bf16[1024,1024]{1,0:T(8,128)(2,1)S(1)} %copy-done.47, bf16[1024,1536]{1,0:T(8,128)(2,1)S(1)} %constant_dynamic-update-slice_fusion.4.grad_ref), kind=kOutput, calls=%fused_computation.88 | convolution fusion | flops 3221225472 | bytes 11534336 | tf_op jit(solution)/shard_map/td,te->de/dot_general | solution.py:1009
  369.0 6.7 %halves.12 = (f32[4,128,1536]{2,1,0:T(8,128)}, f32[4,128,1536]{2,1,0:T(8,128)}) custom-call(s32[14]{0:T(128)} %stack.54.where_ref, f32[8,128,1536]{2,1,0:T(8,128)} %bitcast.63, f32[8,128,1536]{2,1,0:T(8,128)} %bitcast.64), custom_call_target="tpu_custom_call" | custom-call | flops 1 | bytes 1 | tf_op jit(solution)/shard_map/halves/pallas_call | solution.py:721
  377.1 6.6 %input_other.1 = f32[512,1024]{1,0:T(8,128)} custom-call(s32[14]{0:T(128)} %stack.54.where_ref, bf16[1024,1536]{1,0:T(8,128)(2,1)} %copy-done.4, bf16[1024,1536]{1,0:T(8,128)(2,1)} %add_convert_fusion.wq_ref.wk_ref.wv_ref.weight_ref), custom_call_target="tpu_custom_call" | custom-call | flops 1 | bytes 1 | tf_op jit(solution)/shard_map/input_other/pallas_call | solution.py:521
  383.7 2.6 fusion.5
  386.3 3.8 collective-permute-start.23
  395.2 10.5 %input_own.1 = (f32[512,1024]{1,0:T(8,128)}, f32[8,1024]{1,0:T(8,128)}) custom-call(s32[14]{0:T(128)} %stack.54.where_ref, bf16[1024,1536]{1,0:T(8,128)(2,1)} %copy-done.4, bf16[1024,1536]{1,0:T(8,128)(2,1)} %add_convert_fusion.wq_ref.wk_ref.wv_ref.weight_ref, f32[512,1024]{1,0:T(8,128)} %collective-permute-done.21.arrived_ref, ...), custom_call_target="tpu_custom_call" | custom-call | flops 1 | bytes 1 | tf_op jit(solution)/shard_map/input_own/pallas_call | solution.py:759
  406.5 5.6 %collective-permute-done.24.refs_2_.refs_3_ = f32[4,128,1536]{2,1,0:T(8,128)} collective-permute-done((f32[4,128,1536]{2,1,0:T(8,128)}, f32[4,128,1536]{2,1,0:T(8,128)}, u32[]{:S(2)}, u32[]{:S(2)}) %collective-permute-start.24) | collective-permute-done | bytes 3145760 | tf_op jit(solution)/shard_map/ppermute | solution.py:30
  412.1 4.8 halves.13
  417.0 2.7 multiply_add_fusion.2
  421.5 2.4 collective-permute-start.29
  430.2 4.5 halves.14
  435.0 19.1 %collective-permute-done.27.refs_4_.refs_5_ = f32[4,128,384]{2,1,0:T(8,128)S(1)} collective-permute-done((f32[4,128,384]{2,1,0:T(8,128)}, f32[4,128,384]{2,1,0:T(8,128)S(1)}, u32[]{:S(2)}, u32[]{:S(2)}) %collective-permute-start.27) | collective-permute-done | bytes 786464 | tf_op jit(solution)/shard_map/ppermute | solution.py:30
  454.9 3.0 halves.15
  458.9 3.8 halves.16
  463.1 2.4 add_convert_fusion.4
  470.5 2.6 halves.17
  477.2 2.5 collective-permute-done.36
  480.9 10.8 %collective-permute-done.31 = f32[1,128,384]{2,1,0:T(8,128)S(1)} collective-permute-done((f32[1,128,384]{2,1,0:T(8,128)}, f32[1,128,384]{2,1,0:T(8,128)S(1)}, u32[]{:S(2)}, u32[]{:S(2)}) %collective-permute-start.31) | collective-permute-done | bytes 196640 | tf_op jit(solution)/shard_map/ppermute | solution.py:30
  491.7 12.4 %collective-permute-start.33 = (f32[4,64]{0,1:T(8,128)S(1)}, f32[4,64]{0,1:T(8,128)S(1)}, u32[]{:S(2)}, u32[]{:S(2)}) collective-permute-start(f32[4,64]{0,1:T(8,128)S(1)} %slice_bitcast_fusion), channel_id=1, source_target_pairs={{0,1},{1,0},{2,3},{3,2},{4,5},{5,4},{6,7},{7,6},{8,9},{9,8},{10,11... | collective-permute-start | bytes 3080 | tf_op jit(solution)/shard_map/ppermute | solution.py:30
  504.2 3.7 collective-permute-start.35
  511.2 3.0 collective-permute-done.35
  515.1 2.4 multiply_add_fusion.1
  517.5 2.5 pad_maximum_fusion
  (213 shorter events, 67.1 us)
Async XLA Ops:
  8.0 260.5 %all-gather.2.cloned.1.call-start = ((), (), s32[]{:S(2)}) async-start(), calls=%async_computation.1 | async-start | bytes 7077888 | tf_op jit(solution)/shard_map/all_gather | solution.py:878
  9.2 20.0 %collective-permute-start.1 = (f32[256,1024]{1,0:T(8,128)S(1)}, f32[256,1024]{1,0:T(8,128)S(1)}, u32[]{:S(2)}, u32[]{:S(2)}) collective-permute-start(f32[256,1024]{1,0:T(8,128)S(1)} %dynamic-slice_convert_fusion), channel_id=1, source_target_pairs={{1,2},{2,1},{5,6},{6,5},{9,10},{10,9},{13,14},{14,13},{17,18},{18,... | collective-permute-start | bytes 3145736 | tf_op jit(solution)/shard_map/ppermute | solution.py:30
  14.4 14.2 %copy-start.46 = (s32[1,4]{1,0:T(1,128)S(1)}, s32[1,4]{1,0:T(1,128)}, u32[]{:S(2)}) copy-start(s32[1,4]{1,0:T(1,128)} %lengths_ref.3) | copy-start | bytes 52
  26.5 16.3 %collective-permute-start = (f32[1024,256]{1,0:T(8,128)}, f32[1024,256]{1,0:T(8,128)S(1)}, u32[]{:S(2)}, u32[]{:S(2)}) collective-permute-start(f32[1024,256]{1,0:T(8,128)} %get-tuple-element.138), channel_id=1, source_target_pairs={{1,2},{2,1},{5,6},{6,5},{9,10},{10,9},{13,14},{14,13},{17,18},{18,... | collective-permute-start | bytes 3145736 | tf_op jit(solution)/shard_map/ppermute | solution.py:30
  40.7 10.3 %copy-start.23 = (f32[1024,256]{1,0:T(8,128)S(1)}, f32[1024,256]{1,0:T(8,128)}, u32[]{:S(2)}) copy-start(f32[1024,256]{1,0:T(8,128)} %attention_forward.3) | copy-start | bytes 3145732
  42.8 5.1 copy-start.35
  47.9 27.4 %collective-permute-start.5 = (f32[1536,1024]{1,0:T(8,128)}, f32[1536,1024]{1,0:T(8,128)}, u32[]{:S(2)}, u32[]{:S(2)}) collective-permute-start(f32[1536,1024]{1,0:T(8,128)} %packed.1), channel_id=1, source_target_pairs={{0,2},{1,3},{2,0},{3,1},{4,6},{5,7},{6,4},{7,5},{8,10},{9,11},{10,... | collective-permute-start | bytes 18874376 | tf_op jit(solution)/shard_map/ppermute | solution.py:30
  47.9 15.5 %collective-permute-start.3 = (f32[256,1024]{1,0:T(8,128)S(1)}, f32[256,1024]{1,0:T(8,128)S(1)}, u32[]{:S(2)}, u32[]{:S(2)}) collective-permute-start(f32[256,1024]{1,0:T(8,128)S(1)} %collective-permute-done.1), channel_id=1, source_target_pairs={{1,5},{2,6},{5,1},{6,2},{9,13},{10,14},{13,9},{14,10},{17,21},{18,... | collective-permute-start | bytes 3145736 | tf_op jit(solution)/shard_map/ppermute | solution.py:30
  51.0 16.2 %collective-permute-start.2 = (f32[1024,256]{1,0:T(8,128)S(1)}, f32[1024,256]{1,0:T(8,128)}, u32[]{:S(2)}, u32[]{:S(2)}) collective-permute-start(f32[1024,256]{1,0:T(8,128)S(1)} %copy-done.23), channel_id=1, source_target_pairs={{1,2},{2,1},{5,6},{6,5},{9,10},{10,9},{13,14},{14,13},{17,18},{18,... | collective-permute-start | bytes 3145736 | tf_op jit(solution)/shard_map/ppermute | solution.py:30
  55.0 14.1 %copy-start.9 = (bf16[1024,256]{1,0:T(8,128)(2,1)}, bf16[1024,256]{1,0:T(8,128)(2,1)S(1)}, u32[]{:S(2)}) copy-start(bf16[1024,256]{1,0:T(8,128)(2,1)S(1)} %add_convert_fusion.6.low_ref) | copy-start | bytes 1572868
  55.0 8.6 %copy-start.26 = (bf16[512,1024]{1,0:T(8,128)(2,1)S(1)}, bf16[512,1024]{1,0:T(8,128)(2,1)}, u32[]{:S(2)}) copy-start(bf16[512,1024]{1,0:T(8,128)(2,1)} %param.25) | copy-start | bytes 3145732
  70.9 4.4 collective-permute-start.4
  73.0 13.3 %collective-permute-start.14 = (f32[128,1536]{1,0:T(8,128)S(1)}, f32[128,1536]{1,0:T(8,128)S(1)}, u32[]{:S(2)}, u32[]{:S(2)}) collective-permute-start(f32[128,1536]{1,0:T(8,128)S(1)} %convert_element_type.64), channel_id=1, source_target_pairs={{1,2},{2,1},{5,6},{6,5},{9,10},{10,9},{13,14},{14,13},{17,18},{18,... | collective-permute-start | bytes 2359304 | tf_op jit(solution)/shard_map/ppermute | solution.py:30
  87.2 329.8 %reduce-scatter.2.cloned.1.call-start = ((), (), s32[]{:S(2)}) async-start(), calls=%async_computation.2 | async-start | bytes 8912896 | tf_op jit(solution)/shard_map/reduce_scatter | solution.py:976
  87.4 25.5 %collective-permute-start.6 = (f32[256,1024]{1,0:T(8,128)}, f32[256,1024]{1,0:T(8,128)S(1)}, u32[]{:S(2)}, u32[]{:S(2)}) collective-permute-start(f32[256,1024]{1,0:T(8,128)} %get-tuple-element.148.hidden_ref), channel_id=1, source_target_pairs={{0,1},{1,0},{2,3},{3,2},{4,5},{5,4},{6,7},{7,6},{8,9},{9,8},{10,11... | collective-permute-start | bytes 3145736 | tf_op jit(solution)/shard_map/ppermute | solution.py:30
  92.0 43.4 %collective-permute-start.8 = (f32[256,1024]{1,0:T(8,128)}, f32[256,1024]{1,0:T(8,128)S(1)}, u32[]{:S(2)}, u32[]{:S(2)}) collective-permute-start(f32[256,1024]{1,0:T(8,128)} %get-tuple-element.150.hidden_ref), channel_id=1, source_target_pairs={{0,1},{1,0},{2,3},{3,2},{4,5},{5,4},{6,7},{7,6},{8,9},{9,8},{10,11... | collective-permute-start | bytes 3145736 | tf_op jit(solution)/shard_map/ppermute | solution.py:30
  122.9 35.0 %collective-permute-start.7 = (f32[256,1024]{1,0:T(8,128)}, f32[256,1024]{1,0:T(8,128)S(1)}, u32[]{:S(2)}, u32[]{:S(2)}) collective-permute-start(f32[256,1024]{1,0:T(8,128)} %get-tuple-element.157), channel_id=1, source_target_pairs={{0,1},{1,0},{2,3},{3,2},{4,5},{5,4},{6,7},{7,6},{8,9},{9,8},{10,11... | collective-permute-start | bytes 3145736 | tf_op jit(solution)/shard_map/ppermute | solution.py:30
  136.4 21.5 %copy-start.30 = (f32[256,1024]{1,0:T(8,128)S(1)}, f32[256,1024]{1,0:T(8,128)}, u32[]{:S(2)}) copy-start(f32[256,1024]{1,0:T(8,128)} %get-tuple-element.149) | copy-start | bytes 3145732
  145.5 34.9 %collective-permute-start.9 = (f32[256,1024]{1,0:T(8,128)}, f32[256,1024]{1,0:T(8,128)S(1)}, u32[]{:S(2)}, u32[]{:S(2)}) collective-permute-start(f32[256,1024]{1,0:T(8,128)} %get-tuple-element.161), channel_id=1, source_target_pairs={{0,1},{1,0},{2,3},{3,2},{4,5},{5,4},{6,7},{7,6},{8,9},{9,8},{10,11... | collective-permute-start | bytes 3145736 | tf_op jit(solution)/shard_map/ppermute | solution.py:30
  158.1 44.8 %collective-permute-start.10 = (f32[256,1024]{1,0:T(8,128)S(1)}, f32[256,1024]{1,0:T(8,128)S(1)}, u32[]{:S(2)}, u32[]{:S(2)}) collective-permute-start(f32[256,1024]{1,0:T(8,128)S(1)} %add.133.total_ref), channel_id=1, source_target_pairs={{0,1},{1,0},{2,3},{3,2},{4,5},{5,4},{6,7},{7,6},{8,9},{9,8},{10,11... | collective-permute-start | bytes 3145736 | tf_op jit(solution)/shard_map/ppermute | solution.py:30
  159.0 21.4 %copy-start.28 = (f32[256,1024]{1,0:T(8,128)S(1)}, f32[256,1024]{1,0:T(8,128)}, u32[]{:S(2)}) copy-start(f32[256,1024]{1,0:T(8,128)} %get-tuple-element.153) | copy-start | bytes 3145732
  180.5 43.6 %collective-permute-start.11 = (f32[256,1024]{1,0:T(8,128)S(1)}, f32[256,1024]{1,0:T(8,128)}, u32[]{:S(2)}, u32[]{:S(2)}) collective-permute-start(f32[256,1024]{1,0:T(8,128)S(1)} %add.134.total_ref), channel_id=1, source_target_pairs={{0,1},{1,0},{2,3},{3,2},{4,5},{5,4},{6,7},{7,6},{8,9},{9,8},{10,11... | collective-permute-start | bytes 3145736 | tf_op jit(solution)/shard_map/ppermute | solution.py:30
  224.2 11.5 %copy-start = (bf16[1024,2048]{1,0:T(8,128)(2,1)S(1)}, bf16[1024,2048]{1,0:T(8,128)(2,1)}, u32[]{:S(2)}) copy-start(bf16[1024,2048]{1,0:T(8,128)(2,1)} %get-tuple-element.191) | copy-start | bytes 12582916
  235.7 6.2 %copy-start.1 = (bf16[1024,1024]{1,0:T(8,128)(2,1)S(1)}, bf16[1024,1024]{1,0:T(8,128)(2,1)}, u32[]{:S(2)}) copy-start(bf16[1024,1024]{1,0:T(8,128)(2,1)} %get-tuple-element.190) | copy-start | bytes 6291460
  241.9 7.5 %collective-permute-start.15 = (f32[1024,1024]{1,0:T(8,128)}, f32[1024,1024]{1,0:T(8,128)}, u32[]{:S(2)}, u32[]{:S(2)}) collective-permute-start(f32[1024,1024]{1,0:T(8,128)} %fusion.1), channel_id=1, source_target_pairs={{0,2},{1,3},{2,0},{3,1},{4,6},{5,7},{6,4},{7,5},{8,10},{9,11},{10,... | collective-permute-start | bytes 12582920 | tf_op jit(solution)/shard_map/ppermute | solution.py:30
  249.5 7.1 %copy-start.2 = (bf16[1024,2048]{1,0:T(8,128)(2,1)S(1)}, bf16[1024,2048]{1,0:T(8,128)(2,1)}, u32[]{:S(2)}) copy-start(bf16[1024,2048]{1,0:T(8,128)(2,1)} %get-tuple-element.195) | copy-start | bytes 12582916
  249.5 7.1 %copy-start.3 = (bf16[1024,1024]{1,0:T(8,128)(2,1)S(1)}, bf16[1024,1024]{1,0:T(8,128)(2,1)}, u32[]{:S(2)}) copy-start(bf16[1024,1024]{1,0:T(8,128)(2,1)} %get-tuple-element.194) | copy-start | bytes 6291460
  263.4 5.1 copy-start.13
  263.4 5.1 copy-start.14
  263.4 5.1 copy-start.15
  263.4 28.7 %collective-permute-start.17 = (f32[256,1024]{1,0:T(8,128)}, f32[256,1024]{1,0:T(8,128)}, u32[]{:S(2)}, u32[]{:S(2)}) collective-permute-start(f32[256,1024]{1,0:T(8,128)} %get-tuple-element.179), channel_id=1, source_target_pairs={{0,1},{1,0},{2,3},{3,2},{4,5},{5,4},{6,7},{7,6},{8,9},{9,8},{10,11... | collective-permute-start | bytes 3145736 | tf_op jit(solution)/shard_map/ppermute | solution.py:30
  264.7 46.2 %collective-permute-start.16 = (f32[256,1024]{1,0:T(8,128)}, f32[256,1024]{1,0:T(8,128)}, u32[]{:S(2)}, u32[]{:S(2)}) collective-permute-start(f32[256,1024]{1,0:T(8,128)} %get-tuple-element.203), channel_id=1, source_target_pairs={{0,1},{1,0},{2,3},{3,2},{4,5},{5,4},{6,7},{7,6},{8,9},{9,8},{10,11... | collective-permute-start | bytes 3145736 | tf_op jit(solution)/shard_map/ppermute | solution.py:30
  265.0 1.5 collective-permute-start.13
  266.6 6.9 %copy-start.45 = (s32[1,5]{1,0:T(1,128)}, s32[1,5]{1,0:T(1,128)S(1)}, u32[]{:S(2)}) copy-start(s32[1,5]{1,0:T(1,128)S(1)} %fusion.21) | copy-start | bytes 64
  267.2 50.5 %collective-permute-start.19 = (f32[4,128,1024]{2,1,0:T(8,128)}, f32[4,128,1024]{2,1,0:T(8,128)}, u32[]{:S(2)}, u32[]{:S(2)}) collective-permute-start(f32[4,128,1024]{2,1,0:T(8,128)} %get-tuple-element.193), channel_id=1, source_target_pairs={{0,4},{1,5},{2,10},{3,11},{4,0},{5,1},{6,14},{7,15},{8,12},{9,13},... | collective-permute-start | bytes 6291464 | tf_op jit(solution)/shard_map/ppermute | solution.py:30
  316.7 8.3 %collective-permute-start.18 = (f32[512,1024]{1,0:T(8,128)}, f32[512,1024]{1,0:T(8,128)}, u32[]{:S(2)}, u32[]{:S(2)}) collective-permute-start(f32[512,1024]{1,0:T(8,128)} %get-tuple-element.211), channel_id=1, source_target_pairs={{0,2},{1,3},{2,0},{3,1},{4,6},{5,7},{6,4},{7,5},{8,10},{9,11},{10,... | collective-permute-start | bytes 6291464 | tf_op jit(solution)/shard_map/ppermute | solution.py:30
  317.7 6.7 %copy-start.43 = (f32[2,4,1024]{2,1,0:T(4,128)S(1)}, f32[2,4,1024]{2,1,0:T(4,128)}, u32[]{:S(2)}) copy-start(f32[2,4,1024]{2,1,0:T(4,128)} %get-tuple-element.202) | copy-start | bytes 98308
  317.7 7.3 %copy-start.16 = (f32[512,1024]{1,0:T(8,128)S(1)}, f32[512,1024]{1,0:T(8,128)}, u32[]{:S(2)}) copy-start(f32[512,1024]{1,0:T(8,128)} %get-tuple-element.211) | copy-start | bytes 6291460
  322.0 33.5 %collective-permute-start.20 = (f32[2,128,1024]{2,1,0:T(8,128)}, f32[2,128,1024]{2,1,0:T(8,128)S(1)}, u32[]{:S(2)}, u32[]{:S(2)}) collective-permute-start(f32[2,128,1024]{2,1,0:T(8,128)} %get-tuple-element.215), channel_id=1, source_target_pairs={{0,8},{1,9},{2,18},{3,19},{4,12},{5,13},{6,22},{7,23},{8,0},{9,1},... | collective-permute-start | bytes 3145736 | tf_op jit(solution)/shard_map/ppermute | solution.py:30
  361.5 7.5 %copy-start.4 = (bf16[1024,1536]{1,0:T(8,128)(2,1)}, bf16[1024,1536]{1,0:T(8,128)(2,1)S(1)}, u32[]{:S(2)}) copy-start(bf16[1024,1536]{1,0:T(8,128)(2,1)S(1)} %constant_dynamic-update-slice_fusion.4.grad_ref) | copy-start | bytes 9437188
  369.0 8.0 %copy-start.10 = (bf16[1024,256]{1,0:T(8,128)(2,1)S(1)}, bf16[1024,256]{1,0:T(8,128)(2,1)}, u32[]{:S(2)}) copy-start(bf16[1024,256]{1,0:T(8,128)(2,1)} %copy-done.9) | copy-start | bytes 1572868
  369.0 8.0 %copy-start.12 = (bf16[1024,256]{1,0:T(8,128)(2,1)S(1)}, bf16[1024,256]{1,0:T(8,128)(2,1)}, u32[]{:S(2)}) copy-start(bf16[1024,256]{1,0:T(8,128)(2,1)} %copy-done.11) | copy-start | bytes 1572868
  375.7 36.4 %collective-permute-start.24 = (f32[4,128,1536]{2,1,0:T(8,128)}, f32[4,128,1536]{2,1,0:T(8,128)}, u32[]{:S(2)}, u32[]{:S(2)}) collective-permute-start(f32[4,128,1536]{2,1,0:T(8,128)} %get-tuple-element.227), channel_id=1, source_target_pairs={{0,4},{1,5},{2,10},{3,11},{4,0},{5,1},{6,14},{7,15},{8,12},{9,13},... | collective-permute-start | bytes 9437192 | tf_op jit(solution)/shard_map/ppermute | solution.py:30
  383.7 6.5 %copy-start.31 = (f32[256,1024]{1,0:T(8,128)S(1)}, f32[256,1024]{1,0:T(8,128)}, u32[]{:S(2)}) copy-start(f32[256,1024]{1,0:T(8,128)} %get-tuple-element.165) | copy-start | bytes 3145732
  383.7 11.5 %collective-permute-start.21 = (f32[512,1024]{1,0:T(8,128)}, f32[512,1024]{1,0:T(8,128)}, u32[]{:S(2)}, u32[]{:S(2)}) collective-permute-start(f32[512,1024]{1,0:T(8,128)} %input_other.1), channel_id=1, source_target_pairs={{0,2},{1,3},{2,0},{3,1},{4,6},{5,7},{6,4},{7,5},{8,10},{9,11},{10,... | collective-permute-start | bytes 6291464 | tf_op jit(solution)/shard_map/ppermute | solution.py:30
  386.3 30.6 %collective-permute-start.23 = (f32[1024,512]{1,0:T(8,128)}, f32[1024,512]{1,0:T(8,128)}, u32[]{:S(2)}, u32[]{:S(2)}) collective-permute-start(f32[1024,512]{1,0:T(8,128)} %fusion.5), channel_id=1, source_target_pairs={{1,2},{2,1},{5,6},{6,5},{9,10},{10,9},{13,14},{14,13},{17,18},{18,... | collective-permute-start | bytes 6291464 | tf_op jit(solution)/shard_map/ppermute | solution.py:30
  394.4 68.8 %collective-permute-start.12 = (f32[512,1024]{1,0:T(8,128)}, f32[512,1024]{1,0:T(8,128)}, u32[]{:S(2)}, u32[]{:S(2)}) collective-permute-start(f32[512,1024]{1,0:T(8,128)} %broadcast_select_fusion.2), channel_id=1, source_target_pairs={{0,2},{1,3},{2,0},{3,1},{4,6},{5,7},{6,4},{7,5},{8,10},{9,11},{10,... | collective-permute-start | bytes 6291464 | tf_op jit(solution)/shard_map/ppermute | solution.py:30
  421.2 8.0 %collective-permute-start.26 = (f32[1024,256]{1,0:T(8,128)}, f32[1024,256]{1,0:T(8,128)S(1)}, u32[]{:S(2)}, u32[]{:S(2)}) collective-permute-start(f32[1024,256]{1,0:T(8,128)} %get-tuple-element.276), channel_id=1, source_target_pairs={{0,2},{1,3},{2,0},{3,1},{4,6},{5,7},{6,4},{7,5},{8,10},{9,11},{10,... | collective-permute-start | bytes 3145736 | tf_op jit(solution)/shard_map/ppermute | solution.py:30
  421.5 37.4 %collective-permute-start.29 = (f32[2,128,1536]{2,1,0:T(8,128)}, f32[2,128,1536]{2,1,0:T(8,128)}, u32[]{:S(2)}, u32[]{:S(2)}) collective-permute-start(f32[2,128,1536]{2,1,0:T(8,128)} %get-tuple-element.238), channel_id=1, source_target_pairs={{0,8},{1,9},{2,18},{3,19},{4,12},{5,13},{6,22},{7,23},{8,0},{9,1},... | collective-permute-start | bytes 4718600 | tf_op jit(solution)/shard_map/ppermute | solution.py:30
  423.9 49.6 %collective-permute-start.22 = (f32[512,1024]{1,0:T(8,128)}, f32[512,1024]{1,0:T(8,128)}, u32[]{:S(2)}, u32[]{:S(2)}) collective-permute-start(f32[512,1024]{1,0:T(8,128)} %get-tuple-element.232), channel_id=1, source_target_pairs={{0,1},{1,0},{2,3},{3,2},{4,5},{5,4},{6,7},{7,6},{8,9},{9,8},{10,11... | collective-permute-start | bytes 6291464 | tf_op jit(solution)/shard_map/ppermute | solution.py:30
  425.1 1.2 collective-permute-start.25
  434.7 19.3 %collective-permute-start.27 = (f32[4,128,384]{2,1,0:T(8,128)}, f32[4,128,384]{2,1,0:T(8,128)S(1)}, u32[]{:S(2)}, u32[]{:S(2)}) collective-permute-start(f32[4,128,384]{2,1,0:T(8,128)} %get-tuple-element.244), channel_id=1, source_target_pairs={{0,4},{1,5},{2,6},{3,7},{4,0},{5,1},{6,2},{7,3},{8,12},{9,13},{10,... | collective-permute-start | bytes 2359304 | tf_op jit(solution)/shard_map/ppermute | solution.py:30
  457.9 11.9 %collective-permute-start.28 = (f32[2,128,384]{2,1,0:T(8,128)}, f32[2,128,384]{2,1,0:T(8,128)S(1)}, u32[]{:S(2)}, u32[]{:S(2)}) collective-permute-start(f32[2,128,384]{2,1,0:T(8,128)} %get-tuple-element.248), channel_id=1, source_target_pairs={{0,8},{1,9},{2,10},{3,11},{4,12},{5,13},{6,14},{7,15},{8,0},{9,1},... | collective-permute-start | bytes 1179656 | tf_op jit(solution)/shard_map/ppermute | solution.py:30
  462.8 17.1 %collective-permute-start.32 = (f32[1,128,1536]{2,1,0:T(8,128)}, f32[1,128,1536]{2,1,0:T(8,128)S(1)}, u32[]{:S(2)}, u32[]{:S(2)}) collective-permute-start(f32[1,128,1536]{2,1,0:T(8,128)} %get-tuple-element.251), channel_id=1, source_target_pairs={{0,16},{1,17},{2,6},{3,7},{4,20},{5,21},{6,2},{7,3},{8,24},{9,25},... | collective-permute-start | bytes 2359304 | tf_op jit(solution)/shard_map/ppermute | solution.py:30
  465.5 14.2 %collective-permute-start.36 = (f32[1,128,1024]{2,1,0:T(8,128)S(1)}, f32[1,128,1024]{2,1,0:T(8,128)S(1)}, u32[]{:S(2)}, u32[]{:S(2)}) collective-permute-start(f32[1,128,1024]{2,1,0:T(8,128)S(1)} %copy-done.48), channel_id=1, source_target_pairs={{0,16},{1,17},{2,6},{3,7},{4,20},{5,21},{6,2},{7,3},{8,24},{9,25},... | collective-permute-start | bytes 1572872 | tf_op jit(solution)/shard_map/ppermute | solution.py:30
  473.2 6.5 %copy-start.41 = (f32[1,128,1024]{2,1,0:T(8,128)S(1)}, f32[1,128,1024]{2,1,0:T(8,128)}, u32[]{:S(2)}) copy-start(f32[1,128,1024]{2,1,0:T(8,128)} %get-tuple-element.262) | copy-start | bytes 1572868
  473.2 18.5 %collective-permute-start.31 = (f32[1,128,384]{2,1,0:T(8,128)}, f32[1,128,384]{2,1,0:T(8,128)S(1)}, u32[]{:S(2)}, u32[]{:S(2)}) collective-permute-start(f32[1,128,384]{2,1,0:T(8,128)} %get-tuple-element.253), channel_id=1, source_target_pairs={{0,16},{1,17},{2,18},{3,19},{4,20},{5,21},{6,22},{7,23},{8,24},{9,... | collective-permute-start | bytes 589832 | tf_op jit(solution)/shard_map/ppermute | solution.py:30
  475.6 39.5 %collective-permute-start.30 = (f32[512,1024]{1,0:T(8,128)S(1)}, f32[512,1024]{1,0:T(8,128)S(1)}, u32[]{:S(2)}, u32[]{:S(2)}) collective-permute-start(f32[512,1024]{1,0:T(8,128)S(1)} %broadcast_select_fusion), channel_id=1, source_target_pairs={{0,2},{1,3},{2,0},{3,1},{4,6},{5,7},{6,4},{7,5},{8,10},{9,11},{10,... | collective-permute-start | bytes 6291464 | tf_op jit(solution)/shard_map/ppermute | solution.py:30
  479.8 11.9 %copy-start.44 = (f32[1,128,128]{2,1,0:T(8,128)S(1)}, f32[1,128,128]{2,1,0:T(8,128)}, u32[]{:S(2)}) copy-start(f32[1,128,128]{2,1,0:T(8,128)} %get-tuple-element.255) | copy-start | bytes 196612
  479.9 28.0 %copy-start.42 = (f32[1,128,256]{2,1,0:T(8,128)S(1)}, f32[1,128,256]{2,1,0:T(8,128)}, u32[]{:S(2)}) copy-start(f32[1,128,256]{2,1,0:T(8,128)} %get-tuple-element.261) | copy-start | bytes 393220
  480.0 31.2 %collective-permute-start.34 = (f32[64,1536]{1,0:T(8,128)S(1)}, f32[64,1536]{1,0:T(8,128)S(1)}, u32[]{:S(2)}, u32[]{:S(2)}) collective-permute-start(f32[64,1536]{1,0:T(8,128)S(1)} %get-tuple-element.258), channel_id=1, source_target_pairs={{0,2},{1,0},{2,3},{3,1},{4,6},{5,4},{6,7},{7,5},{8,10},{9,8},{10,1... | collective-permute-start | bytes 1179656 | tf_op jit(solution)/shard_map/ppermute | solution.py:30
  491.7 16.3 %collective-permute-start.33 = (f32[4,64]{0,1:T(8,128)S(1)}, f32[4,64]{0,1:T(8,128)S(1)}, u32[]{:S(2)}, u32[]{:S(2)}) collective-permute-start(f32[4,64]{0,1:T(8,128)S(1)} %slice_bitcast_fusion), channel_id=1, source_target_pairs={{0,1},{1,0},{2,3},{3,2},{4,5},{5,4},{6,7},{7,6},{8,9},{9,8},{10,11... | collective-permute-start | bytes 3080 | tf_op jit(solution)/shard_map/ppermute | solution.py:30
  504.2 10.1 %collective-permute-start.35 = (f32[64,1536]{1,0:T(8,128)S(1)}, f32[64,1536]{1,0:T(8,128)S(1)}, u32[]{:S(2)}, u32[]{:S(2)}) collective-permute-start(f32[64,1536]{1,0:T(8,128)S(1)} %get-tuple-element.260), channel_id=1, source_target_pairs={{1,2},{2,1},{5,6},{6,5},{9,10},{10,9},{13,14},{14,13},{17,18},{18,... | collective-permute-start | bytes 1179656 | tf_op jit(solution)/shard_map/ppermute | solution.py:30
  508.0 1.7 collective-permute-start.37
  (25 other events, 50.1 us)
Sparse Core Ops, SparseCore 0:
  87.3 97.2 all-gather.1
Sparse Core Ops, SparseCore 1:
  263.5 108.7 reduce-scatter.1

commit v7 on v6

--- a/solution.py
+++ b/solution.py
@@ -1017,8 +1017,9 @@
     grad_in_own, gain_in_attn = input_own(
         where_own, grads, weights_mine, after(other_sent, gate), block_in, there, grad_res, norm_in_attn
     )
-    grad_in_sent = send(grad_in_own, over)
     gains = jnp.stack([gain_in_attn[0], gain_out_attn, gain_in_mlp, gain_out_mlp], axis=0)
+    gains = gains + send(gains, over)
+    grad_in_sent = send(after(grad_in_own, gains), over)
     gate = late.hop(grad_in_own)
     weight_out_sent, gains = after((weight_out_sent, gains), grad_up, gate)
     gains = jnp.pad((gains + send(gains, cross)).T, ((0, 0), (0, LANES - 4)))
@@ -1062,7 +1063,6 @@
     grad_in = to_output(grad_in_own, after(grad_in_sent, gate))
     heads = straight + jnp.where(same, for_core, diagonal)
     gains = half_of(gains, core, small)[:, :4].T
-    gains = gains + send(gains, over)
     block_out = to_output(jnp.concatenate(blocks[:2], axis=0), jnp.concatenate(blocks[2:], axis=0)).astype(bf16)
     return (
         block_out,

time: 536 us -> 538 us (level)
  transfers between devices with their start and end apart: 40 -> 40, of which waited for: 23 -> 21; matrix products, arithmetic and copies ran while one was open for 13% -> 13% of each run, Pallas kernels for 43% -> 43%
where the time goes in v7:
time: 538 us; the launch traced here: 530 us
  Pallas kernels  232 us (43%)
  waiting for transfers between devices  135 us (25%)
  starting transfers between devices  54.9 us (10%)
  other arithmetic  32.5 us (6%)
  matrix products  31.6 us (6%)
  local copies, waits for them, and re-layouts  25.4 us (5%)
  between operations  17.5 us (3%)
    ppermute x38, waiting for transfers between devices, send(): return lax.ppermute(values, ('dp', 'tensor'), pairs)  135 us
    pallas_call x14, Pallas kernels, call(): pl.pallas_call(kernel, grid_spec=pltpu.PrefetchScalarGridSpec(num_scalar_...  113 us
    ppermute x38, starting transfers between devices, send(): return lax.ppermute(values, ('dp', 'tensor'), pairs)  54.6 us
    pallas_call x9, Pallas kernels, halves(): pl.pallas_call(partial(halves_kernel, len(held), sources), grid_spec=pltp...  40.2 us
    pallas_call x1, Pallas kernels, attention_backward(): pl.pallas_call(partial(backward_kernel, lengths.shape[1]), grid=(pairs,),...  26 us
    pallas_call x2, Pallas kernels, attention_forward(): pl.pallas_call(partial(forward_kernel, lengths.shape[1], first), grid=(1,...  23.5 us
    pallas_call x1, Pallas kernels, attention_ready(): pl.pallas_call(partial(ready_kernel, lengths.shape[1]), grid=(wide // gro...  18.7 us
    unnamed x103, local copies, waits for them, and re-layouts  15.6 us
  transfers between devices with their start and end apart: 40, of which 21 were waited for; matrix products, arithmetic and copies ran while one was open for 13% of the time, Pallas kernels for 43%

profile of v7, /device:TPU:1, one launch (start us, length us, event | category | flops | bytes accessed | tf_op | source)
XLA Modules:
  0.0 529.6 jit_solution(2885691390624882695)
XLA Ops:
  9.2 4.5 collective-permute-start.1
  14.4 12.0 %attention_forward.2 = (f32[1024,256]{1,0:T(8,128)}, bf16[1024,1024]{1,0:T(8,128)(2,1)}, f32[1024,128]{1,0:T(8,128)}, f32[1024,128]{1,0:T(8,128)}) custom-call(s32[1,4]{1,0:T(1,128)} %lengths_ref.3, s32[1]{0:T(128)S(6)} %copy.65.pad_ref, f32[32,1]{1,0:T(8,128)} %constant.57.clone.freq_ref, f32[1,1024]{1,0:T(1,128)} %bitcast.75, ...), custom_call_target="tpu_custom_call" | custom-call | flops 1 | bytes 1 | tf_op jit(solution)/shard_map/attention_forward/pallas_call | solution.py:278
  26.5 2.1 collective-permute-start
  29.3 11.5 %attention_forward.3 = f32[1024,256]{1,0:T(8,128)} custom-call(s32[1,4]{1,0:T(1,128)} %lengths_ref.3, s32[1]{0:T(128)S(6)} %copy.65.pad_ref, f32[32,1]{1,0:T(8,128)} %constant.57.clone.freq_ref, f32[1,1024]{1,0:T(1,128)} %bitcast.76, bf16[1024,1024]{1,0:T(8,128)(2,1)} %get-tuple-element.143.refs_0_, f32[1024,128]{1,0:T(8,128)} %get-tuple-element.144.refs_1_, ...), custom_call_target="tpu_custom_call" | custom-call | flops 1 | bytes 1 | tf_op jit(solution)/shard_map/attention_forward/pallas_call | solution.py:278
  42.8 5.1 packed.1
  47.9 3.1 collective-permute-start.3
  51.1 2.3 collective-permute-start.2
  55.1 8.3 %collective-permute-done.3 = f32[256,1024]{1,0:T(8,128)S(1)} collective-permute-done((f32[256,1024]{1,0:T(8,128)S(1)}, f32[256,1024]{1,0:T(8,128)S(1)}, u32[]{:S(2)}, u32[]{:S(2)}) %collective-permute-start.3) | collective-permute-done | bytes 1048608 | tf_op jit(solution)/shard_map/ppermute | solution.py:30
  64.1 3.2 collective-permute-done.2
  73.0 2.3 collective-permute-start.14
  76.7 4.6 hidden.2
  81.2 5.1 collective-permute-done.14
  87.6 4.5 hidden.3
  93.5 9.4 %mlp_forward.4 = (bf16[1024,1024]{1,0:T(8,128)(2,1)}, bf16[1024,2048]{1,0:T(8,128)(2,1)}, f32[256,2048]{1,0:T(8,128)}, f32[256,1024]{1,0:T(8,128)}) custom-call(f32[256,1024]{1,0:T(8,128)} %get-tuple-element.149.hidden_ref, f32[1,1024]{1,0:T(1,128)} %bitcast.69, bf16[1024,2048]{1,0:T(8,128)(2,1)} %up_ref.15, bf16[2048,1024]{1,0:T(8,128)(2,1)} %down_ref.15), custom_call_target="tpu_custom_call" | custom-call | flops 1 | bytes 1 | tf_op jit(solution)/shard_map/mlp_forward/pallas_call | solution.py:521
  102.9 9.0 %mlp_forward.5 = (bf16[1024,1024]{1,0:T(8,128)(2,1)}, bf16[1024,2048]{1,0:T(8,128)(2,1)}, f32[256,2048]{1,0:T(8,128)}, f32[256,1024]{1,0:T(8,128)}) custom-call(f32[256,1024]{1,0:T(8,128)} %get-tuple-element.151.hidden_ref, f32[1,1024]{1,0:T(1,128)} %bitcast.70, bf16[1024,2048]{1,0:T(8,128)(2,1)} %up_ref.15, ...), custom_call_target="tpu_custom_call", output_to_operand_aliasing={{0}: (4, {}), {1}: (5, {})} | custom-call | flops 1 | bytes 1 | tf_op jit(solution)/shard_map/mlp_forward/pallas_call | solution.py:521
  114.0 9.0 %mlp_forward.6 = (bf16[1024,1024]{1,0:T(8,128)(2,1)}, bf16[1024,2048]{1,0:T(8,128)(2,1)}, f32[256,2048]{1,0:T(8,128)}, f32[256,1024]{1,0:T(8,128)}) custom-call(f32[256,1024]{1,0:T(8,128)} %copy-done.19, f32[1,1024]{1,0:T(1,128)} %bitcast.71, bf16[1024,2048]{1,0:T(8,128)(2,1)} %up_ref.15, ...), custom_call_target="tpu_custom_call", output_to_operand_aliasing={{0}: (4, {}), {1}: (5, {})} | custom-call | flops 1 | bytes 1 | tf_op jit(solution)/shard_map/mlp_forward/pallas_call | solution.py:521
  123.1 12.4 %collective-permute-done.8.hidden_ref = f32[256,1024]{1,0:T(8,128)S(1)} collective-permute-done((f32[256,1024]{1,0:T(8,128)}, f32[256,1024]{1,0:T(8,128)S(1)}, u32[]{:S(2)}, u32[]{:S(2)}) %collective-permute-start.8) | collective-permute-done | bytes 1048608 | tf_op jit(solution)/shard_map/ppermute | solution.py:30
  136.5 9.1 %mlp_forward.7 = (bf16[1024,1024]{1,0:T(8,128)(2,1)}, bf16[1024,2048]{1,0:T(8,128)(2,1)}, f32[256,2048]{1,0:T(8,128)}, f32[256,1024]{1,0:T(8,128)}) custom-call(f32[256,1024]{1,0:T(8,128)} %copy-done.18, f32[1,1024]{1,0:T(1,128)} %bitcast.72, bf16[1024,2048]{1,0:T(8,128)(2,1)} %up_ref.15, ...), custom_call_target="tpu_custom_call", output_to_operand_aliasing={{0}: (4, {}), {1}: (5, {})} | custom-call | flops 1 | bytes 1 | tf_op jit(solution)/shard_map/mlp_forward/pallas_call | solution.py:521
  145.7 12.2 %collective-permute-done.7 = f32[256,1024]{1,0:T(8,128)S(1)} collective-permute-done((f32[256,1024]{1,0:T(8,128)}, f32[256,1024]{1,0:T(8,128)S(1)}, u32[]{:S(2)}, u32[]{:S(2)}) %collective-permute-start.7) | collective-permute-done | bytes 1048608 | tf_op jit(solution)/shard_map/ppermute | solution.py:30
  159.0 11.2 %mlp_backward.4 = (f32[256,1024]{1,0:T(8,128)}, bf16[1024,1024]{1,0:T(8,128)(2,1)}, f32[8,1024]{1,0:T(8,128)}, bf16[1024,2048]{1,0:T(8,128)(2,1)}, f32[256,1024]{1,0:T(8,128)}) custom-call(s32[14]{0:T(128)} %stack.54.where_ref, f32[256,1024]{1,0:T(8,128)} %get-tuple-element.149.hidden_ref, f32[256,1024]{1,0:T(8,128)} %copy-done.20, ...), custom_call_target="tpu_custom_call" | custom-call | flops 1 | bytes 1 | tf_op jit(solution)/shard_map/mlp_backward/pallas_call | solution.py:521
  170.2 10.2 %collective-permute-done.9 = f32[256,1024]{1,0:T(8,128)S(1)} collective-permute-done((f32[256,1024]{1,0:T(8,128)}, f32[256,1024]{1,0:T(8,128)S(1)}, u32[]{:S(2)}, u32[]{:S(2)}) %collective-permute-start.9) | collective-permute-done | bytes 1048608 | tf_op jit(solution)/shard_map/ppermute | solution.py:30
  181.6 11.0 %mlp_backward.5 = (f32[256,1024]{1,0:T(8,128)}, bf16[1024,1024]{1,0:T(8,128)(2,1)}, f32[8,1024]{1,0:T(8,128)}, bf16[1024,2048]{1,0:T(8,128)(2,1)}, f32[256,1024]{1,0:T(8,128)}) custom-call(s32[14]{0:T(128)} %stack.54.where_ref, f32[256,1024]{1,0:T(8,128)} %get-tuple-element.151.hidden_ref, ...), custom_call_target="tpu_custom_call", output_to_operand_aliasing={{1}: (9, {}), {3}: (10, {})} | custom-call | flops 1 | bytes 1 | tf_op jit(solution)/shard_map/mlp_backward/pallas_call | solution.py:521
  192.5 10.3 %collective-permute-done.10.total_ref = f32[256,1024]{1,0:T(8,128)S(1)} collective-permute-done((f32[256,1024]{1,0:T(8,128)S(1)}, f32[256,1024]{1,0:T(8,128)S(1)}, u32[]{:S(2)}, u32[]{:S(2)}) %collective-permute-start.10) | collective-permute-done | bytes 1048608 | tf_op jit(solution)/shard_map/ppermute | solution.py:30
  203.9 10.9 %mlp_backward.6 = (f32[256,1024]{1,0:T(8,128)}, bf16[1024,1024]{1,0:T(8,128)(2,1)}, f32[8,1024]{1,0:T(8,128)}, bf16[1024,2048]{1,0:T(8,128)(2,1)}, f32[256,1024]{1,0:T(8,128)}) custom-call(s32[2]{0:T(128)} %pad_add_fusion.where_ref, f32[256,1024]{1,0:T(8,128)} %copy-done.19, f32[256,1024]{1,0:T(8,128)} %copy-done.29, ...), custom_call_target="tpu_custom_call", output_to_operand_aliasing={{1}: (9, {}), {3}: (10, {})} | custom-call | flops 1 | bytes 1 | tf_op jit(solution)/shard_map/mlp_backward/pallas_call | solution.py:521
  214.8 9.6 %collective-permute-done.11.total_ref = f32[256,1024]{1,0:T(8,128)} collective-permute-done((f32[256,1024]{1,0:T(8,128)S(1)}, f32[256,1024]{1,0:T(8,128)}, u32[]{:S(2)}, u32[]{:S(2)}) %collective-permute-start.11) | collective-permute-done | bytes 1048608 | tf_op jit(solution)/shard_map/ppermute | solution.py:30
  224.4 11.5 %mlp_backward.7 = (f32[256,1024]{1,0:T(8,128)}, bf16[1024,1024]{1,0:T(8,128)(2,1)}, f32[8,1024]{1,0:T(8,128)}, bf16[1024,2048]{1,0:T(8,128)(2,1)}, f32[256,1024]{1,0:T(8,128)}) custom-call(s32[2]{0:T(128)} %pad_add_fusion.where_ref, f32[256,1024]{1,0:T(8,128)} %copy-done.18, ...), custom_call_target="tpu_custom_call", output_to_operand_aliasing={{1}: (9, {}), {3}: (10, {})} | custom-call | flops 1 | bytes 1 | tf_op jit(solution)/shard_map/mlp_backward/pallas_call | solution.py:521
  235.8 6.1 %fusion.1 = f32[1024,1024]{1,0:T(8,128)} fusion(bf16[1024,1024]{1,0:T(8,128)(2,1)} %get-tuple-element.191, bf16[1024,2048]{1,0:T(8,128)(2,1)S(1)} %copy-done, s32[]{:T(128)S(6)} %select_n.143), kind=kOutput, calls=%fused_computation.11 | convolution fusion | flops 2147483648 | bytes 8388612 | tf_op jit(solution)/shard_map/td,tf->df/dot_general | solution.py:969
  241.9 6.0 %fusion.3 = f32[1024,1024]{1,0:T(8,128)} fusion(bf16[1024,1024]{1,0:T(8,128)(2,1)S(1)} %copy-done.1, bf16[1024,2048]{1,0:T(8,128)(2,1)} %get-tuple-element.192, s32[]{:T(128)S(6)} %select_n.142), kind=kOutput, calls=%fused_computation.13 | convolution fusion | flops 2147483648 | bytes 8388612 | tf_op jit(solution)/shard_map/td,tf->df/dot_general | solution.py:969
  249.4 7.1 %halves.9 = (f32[4,128,1024]{2,1,0:T(8,128)}, f32[4,128,1024]{2,1,0:T(8,128)}) custom-call(s32[14]{0:T(128)} %stack.54.where_ref, f32[8,128,1024]{2,1,0:T(8,128)} %bitcast.59, f32[8,128,1024]{2,1,0:T(8,128)} %bitcast.60, f32[8,128,1024]{2,1,0:T(8,128)} %bitcast.17.refs_2_.refs_3_, f32[8,128,1024]{2,1,0:T(8,128)} %bitcast.17.refs_2_.refs_3_), custom_call_target="tpu_custom_call" | custom-call | flops 1 | bytes 1 | tf_op jit(solution)/shard_map/halves/pallas_call | solution.py:721
  256.5 6.8 %fusion.26 = f32[1024,2048]{1,0:T(8,128)} fusion(bf16[1024,1024]{1,0:T(8,128)(2,1)S(1)} %copy-done.3, bf16[1024,2048]{1,0:T(8,128)(2,1)S(1)} %copy-done.2), kind=kOutput, calls=%fused_computation.87 | convolution fusion | flops 4294967296 | bytes 14680064 | tf_op jit(solution)/shard_map/td,tf->df/dot_general | solution.py:975
  268.5 4.9 add_convert_fusion.wq_ref.wk_ref.wv_ref.weight_ref
  273.4 18.7 %attention_ready.1 = (bf16[1024,512]{1,0:T(8,128)(2,1)}, bf16[1024,512]{1,0:T(8,128)(2,1)}, bf16[1024,512]{1,0:T(8,128)(2,1)}, f32[2,4,1024]{2,1,0:T(4,128)}, bf...) custom-call(s32[14]{0:T(128)} %stack.54.where_ref, s32[1,4]{1,0:T(1,128)} %bitcast.87, ...), custom_call_target="tpu_custom_call" | custom-call | flops 1 | bytes 1 | tf_op jit(solution)/shard_map/attention_ready/pallas_call | solution.py:304
  292.0 5.8 %residual.2 = (f32[512,1024]{1,0:T(8,128)}, f32[512,1024]{1,0:T(8,128)}, f32[8,1024]{1,0:T(8,128)}) custom-call(s32[14]{0:T(128)} %stack.54.where_ref, f32[256,1024]{1,0:T(8,128)} %get-tuple-element.167.part_ref, f32[256,1024]{1,0:T(8,128)} %collective-permute-done.17.arrived_ref, f32[256,1024]{1,0:T(8,128)} %get-tuple-element.149.hidden_ref, ...), custom_call_target="tpu_custom_call" | custom-call | flops 1 | bytes 1 | tf_op jit(solution)/shard_map/residual/pallas_call | solution.py:521
  297.8 13.1 %collective-permute-done.16.arrived_ref = f32[256,1024]{1,0:T(8,128)} collective-permute-done((f32[256,1024]{1,0:T(8,128)}, f32[256,1024]{1,0:T(8,128)}, u32[]{:S(2)}, u32[]{:S(2)}) %collective-permute-start.16) | collective-permute-done | bytes 1048608 | tf_op jit(solution)/shard_map/ppermute | solution.py:30
  310.9 5.8 %residual.3 = (f32[512,1024]{1,0:T(8,128)}, f32[512,1024]{1,0:T(8,128)}, f32[8,1024]{1,0:T(8,128)}) custom-call(s32[14]{0:T(128)} %stack.54.where_ref, f32[256,1024]{1,0:T(8,128)} %get-tuple-element.174.part_ref, f32[256,1024]{1,0:T(8,128)} %collective-permute-done.16.arrived_ref, ...), custom_call_target="tpu_custom_call", output_to_operand_aliasing={{0}: (9, {}), {1}: (10, {})} | custom-call | flops 1 | bytes 1 | tf_op jit(solution)/shard_map/residual/pallas_call | solution.py:521
  317.7 4.3 halves.10
  322.0 2.4 collective-permute-start.20
  325.0 2.3 add_convert_fusion.2
  327.3 2.3 convolution_convert_fusion.grad_ref
  329.6 26.0 %attention_backward.1 = (bf16[1024,512]{1,0:T(8,128)(2,1)}, bf16[1024,512]{1,0:T(8,128)(2,1)}, bf16[1024,512]{1,0:T(8,128)(2,1)}) custom-call(s32[1,4]{1,0:T(1,128)} %bitcast.88, s32[1]{0:T(128)} %bitcast.15.pad_ref, f32[1024,128]{1,0:T(8,128)} %get-tuple-element.198.cos_ref, f32[1024,128]{1,0:T(8,128)} %get-tuple-element.199.sin_ref, ...), custom_call_target="tpu_custom_call" | custom-call | flops 1 | bytes 1 | tf_op jit(solution)/shard_map/attention_backward/pallas_call | solution.py:333
  356.6 3.4 halves.11
  363.5 5.5 %fusion.27 = f32[1024,1536]{1,0:T(8,128)} fusion(bf16[1024,1024]{1,0:T(8,128)(2,1)S(1)} %copy-done.47, bf16[1024,1536]{1,0:T(8,128)(2,1)S(1)} %constant_dynamic-update-slice_fusion.4.grad_ref), kind=kOutput, calls=%fused_computation.88 | convolution fusion | flops 3221225472 | bytes 11534336 | tf_op jit(solution)/shard_map/td,te->de/dot_general | solution.py:1009
  369.0 6.5 %halves.12 = (f32[4,128,1536]{2,1,0:T(8,128)}, f32[4,128,1536]{2,1,0:T(8,128)}) custom-call(s32[14]{0:T(128)} %stack.54.where_ref, f32[8,128,1536]{2,1,0:T(8,128)} %bitcast.61, f32[8,128,1536]{2,1,0:T(8,128)} %bitcast.62), custom_call_target="tpu_custom_call" | custom-call | flops 1 | bytes 1 | tf_op jit(solution)/shard_map/halves/pallas_call | solution.py:721
  377.0 6.5 %input_other.1 = f32[512,1024]{1,0:T(8,128)} custom-call(s32[14]{0:T(128)} %stack.54.where_ref, bf16[1024,1536]{1,0:T(8,128)(2,1)} %copy-done.4, bf16[1024,1536]{1,0:T(8,128)(2,1)} %add_convert_fusion.wq_ref.wk_ref.wv_ref.weight_ref), custom_call_target="tpu_custom_call" | custom-call | flops 1 | bytes 1 | tf_op jit(solution)/shard_map/input_other/pallas_call | solution.py:521
  383.6 2.6 fusion.5
  386.3 3.7 collective-permute-start.24
  393.3 10.6 %input_own.1 = (f32[512,1024]{1,0:T(8,128)}, f32[8,1024]{1,0:T(8,128)}) custom-call(s32[14]{0:T(128)} %stack.54.where_ref, bf16[1024,1536]{1,0:T(8,128)(2,1)} %copy-done.4, bf16[1024,1536]{1,0:T(8,128)(2,1)} %add_convert_fusion.wq_ref.wk_ref.wv_ref.weight_ref, f32[512,1024]{1,0:T(8,128)} %collective-permute-done.21.arrived_ref, ...), custom_call_target="tpu_custom_call" | custom-call | flops 1 | bytes 1 | tf_op jit(solution)/shard_map/input_own/pallas_call | solution.py:759
  407.1 6.1 %collective-permute-done.22 = f32[4,1024]{1,0:T(4,128)S(1)} collective-permute-done((f32[4,1024]{1,0:T(4,128)S(1)}, f32[4,1024]{1,0:T(4,128)S(1)}, u32[]{:S(2)}, u32[]{:S(2)}) %collective-permute-start.22) | collective-permute-done | bytes 16416 | tf_op jit(solution)/shard_map/ppermute | solution.py:30
  413.3 4.8 halves.13
  418.1 2.7 multiply_add_fusion.2
  430.8 4.5 halves.14
  435.9 18.5 %collective-permute-done.28.refs_4_.refs_5_ = f32[4,128,384]{2,1,0:T(8,128)S(1)} collective-permute-done((f32[4,128,384]{2,1,0:T(8,128)}, f32[4,128,384]{2,1,0:T(8,128)S(1)}, u32[]{:S(2)}, u32[]{:S(2)}) %collective-permute-start.28) | collective-permute-done | bytes 786464 | tf_op jit(solution)/shard_map/ppermute | solution.py:30
  455.3 3.0 halves.15
  459.4 2.2 collective-permute-done.30.refs_2_.refs_3_
  461.6 3.9 halves.16
  465.6 2.5 add_convert_fusion.4
  471.7 2.6 halves.17
  477.0 2.0 collective-permute-start.31
  479.0 3.4 collective-permute-done.36
  483.1 10.4 %collective-permute-done.32 = f32[1,128,384]{2,1,0:T(8,128)S(1)} collective-permute-done((f32[1,128,384]{2,1,0:T(8,128)}, f32[1,128,384]{2,1,0:T(8,128)S(1)}, u32[]{:S(2)}, u32[]{:S(2)}) %collective-permute-start.32) | collective-permute-done | bytes 196640 | tf_op jit(solution)/shard_map/ppermute | solution.py:30
  493.5 16.0 %collective-permute-start.35 = (f32[64,1536]{1,0:T(8,128)S(1)}, f32[64,1536]{1,0:T(8,128)S(1)}, u32[]{:S(2)}, u32[]{:S(2)}) collective-permute-start(f32[64,1536]{1,0:T(8,128)S(1)} %get-tuple-element.262), channel_id=1, source_target_pairs={{1,2},{2,1},{5,6},{6,5},{9,10},{10,9},{13,14},{14,13},{17,18},{18,... | collective-permute-start | bytes 1179656 | tf_op jit(solution)/shard_map/ppermute | solution.py:30
  512.9 3.1 collective-permute-done.35
  516.8 2.4 multiply_add_fusion.1
  519.2 2.5 pad_maximum_fusion
  (213 shorter events, 66.7 us)
Async XLA Ops:
  8.0 260.5 %all-gather.2.cloned.1.call-start = ((), (), s32[]{:S(2)}) async-start(), calls=%async_computation.1 | async-start | bytes 7077888 | tf_op jit(solution)/shard_map/all_gather | solution.py:878
  9.2 20.1 %collective-permute-start.1 = (f32[256,1024]{1,0:T(8,128)S(1)}, f32[256,1024]{1,0:T(8,128)S(1)}, u32[]{:S(2)}, u32[]{:S(2)}) collective-permute-start(f32[256,1024]{1,0:T(8,128)S(1)} %dynamic-slice_convert_fusion), channel_id=1, source_target_pairs={{1,2},{2,1},{5,6},{6,5},{9,10},{10,9},{13,14},{14,13},{17,18},{18,... | collective-permute-start | bytes 3145736 | tf_op jit(solution)/shard_map/ppermute | solution.py:30
  14.4 14.2 %copy-start.46 = (s32[1,4]{1,0:T(1,128)S(1)}, s32[1,4]{1,0:T(1,128)}, u32[]{:S(2)}) copy-start(s32[1,4]{1,0:T(1,128)} %lengths_ref.3) | copy-start | bytes 52
  26.5 16.3 %collective-permute-start = (f32[1024,256]{1,0:T(8,128)}, f32[1024,256]{1,0:T(8,128)S(1)}, u32[]{:S(2)}, u32[]{:S(2)}) collective-permute-start(f32[1024,256]{1,0:T(8,128)} %get-tuple-element.139), channel_id=1, source_target_pairs={{1,2},{2,1},{5,6},{6,5},{9,10},{10,9},{13,14},{14,13},{17,18},{18,... | collective-permute-start | bytes 3145736 | tf_op jit(solution)/shard_map/ppermute | solution.py:30
  40.8 10.3 %copy-start.23 = (f32[1024,256]{1,0:T(8,128)S(1)}, f32[1024,256]{1,0:T(8,128)}, u32[]{:S(2)}) copy-start(f32[1024,256]{1,0:T(8,128)} %attention_forward.3) | copy-start | bytes 3145732
  42.8 5.1 copy-start.35
  47.9 27.4 %collective-permute-start.5 = (f32[1536,1024]{1,0:T(8,128)}, f32[1536,1024]{1,0:T(8,128)}, u32[]{:S(2)}, u32[]{:S(2)}) collective-permute-start(f32[1536,1024]{1,0:T(8,128)} %packed.1), channel_id=1, source_target_pairs={{0,2},{1,3},{2,0},{3,1},{4,6},{5,7},{6,4},{7,5},{8,10},{9,11},{10,... | collective-permute-start | bytes 18874376 | tf_op jit(solution)/shard_map/ppermute | solution.py:30
  47.9 15.5 %collective-permute-start.3 = (f32[256,1024]{1,0:T(8,128)S(1)}, f32[256,1024]{1,0:T(8,128)S(1)}, u32[]{:S(2)}, u32[]{:S(2)}) collective-permute-start(f32[256,1024]{1,0:T(8,128)S(1)} %collective-permute-done.1), channel_id=1, source_target_pairs={{1,5},{2,6},{5,1},{6,2},{9,13},{10,14},{13,9},{14,10},{17,21},{18,... | collective-permute-start | bytes 3145736 | tf_op jit(solution)/shard_map/ppermute | solution.py:30
  51.1 16.2 %collective-permute-start.2 = (f32[1024,256]{1,0:T(8,128)S(1)}, f32[1024,256]{1,0:T(8,128)}, u32[]{:S(2)}, u32[]{:S(2)}) collective-permute-start(f32[1024,256]{1,0:T(8,128)S(1)} %copy-done.23), channel_id=1, source_target_pairs={{1,2},{2,1},{5,6},{6,5},{9,10},{10,9},{13,14},{14,13},{17,18},{18,... | collective-permute-start | bytes 3145736 | tf_op jit(solution)/shard_map/ppermute | solution.py:30
  55.1 14.0 %copy-start.9 = (bf16[1024,256]{1,0:T(8,128)(2,1)}, bf16[1024,256]{1,0:T(8,128)(2,1)S(1)}, u32[]{:S(2)}) copy-start(bf16[1024,256]{1,0:T(8,128)(2,1)S(1)} %add_convert_fusion.6.low_ref) | copy-start | bytes 1572868
  55.1 8.5 %copy-start.26 = (bf16[512,1024]{1,0:T(8,128)(2,1)S(1)}, bf16[512,1024]{1,0:T(8,128)(2,1)}, u32[]{:S(2)}) copy-start(bf16[512,1024]{1,0:T(8,128)(2,1)} %param.25) | copy-start | bytes 3145732
  71.0 4.4 collective-permute-start.4
  73.0 13.3 %collective-permute-start.14 = (f32[128,1536]{1,0:T(8,128)S(1)}, f32[128,1536]{1,0:T(8,128)S(1)}, u32[]{:S(2)}, u32[]{:S(2)}) collective-permute-start(f32[128,1536]{1,0:T(8,128)S(1)} %convert_element_type.64), channel_id=1, source_target_pairs={{1,2},{2,1},{5,6},{6,5},{9,10},{10,9},{13,14},{14,13},{17,18},{18,... | collective-permute-start | bytes 2359304 | tf_op jit(solution)/shard_map/ppermute | solution.py:30
  87.2 330.9 %reduce-scatter.2.cloned.1.call-start = ((), (), s32[]{:S(2)}) async-start(), calls=%async_computation.2 | async-start | bytes 8912896 | tf_op jit(solution)/shard_map/reduce_scatter | solution.py:976
  87.5 25.5 %collective-permute-start.6 = (f32[256,1024]{1,0:T(8,128)}, f32[256,1024]{1,0:T(8,128)S(1)}, u32[]{:S(2)}, u32[]{:S(2)}) collective-permute-start(f32[256,1024]{1,0:T(8,128)} %get-tuple-element.149.hidden_ref), channel_id=1, source_target_pairs={{0,1},{1,0},{2,3},{3,2},{4,5},{5,4},{6,7},{7,6},{8,9},{9,8},{10,11... | collective-permute-start | bytes 3145736 | tf_op jit(solution)/shard_map/ppermute | solution.py:30
  92.1 43.4 %collective-permute-start.8 = (f32[256,1024]{1,0:T(8,128)}, f32[256,1024]{1,0:T(8,128)S(1)}, u32[]{:S(2)}, u32[]{:S(2)}) collective-permute-start(f32[256,1024]{1,0:T(8,128)} %get-tuple-element.151.hidden_ref), channel_id=1, source_target_pairs={{0,1},{1,0},{2,3},{3,2},{4,5},{5,4},{6,7},{7,6},{8,9},{9,8},{10,11... | collective-permute-start | bytes 3145736 | tf_op jit(solution)/shard_map/ppermute | solution.py:30
  123.0 34.9 %collective-permute-start.7 = (f32[256,1024]{1,0:T(8,128)}, f32[256,1024]{1,0:T(8,128)S(1)}, u32[]{:S(2)}, u32[]{:S(2)}) collective-permute-start(f32[256,1024]{1,0:T(8,128)} %get-tuple-element.158), channel_id=1, source_target_pairs={{0,1},{1,0},{2,3},{3,2},{4,5},{5,4},{6,7},{7,6},{8,9},{9,8},{10,11... | collective-permute-start | bytes 3145736 | tf_op jit(solution)/shard_map/ppermute | solution.py:30
  136.5 21.5 %copy-start.30 = (f32[256,1024]{1,0:T(8,128)S(1)}, f32[256,1024]{1,0:T(8,128)}, u32[]{:S(2)}) copy-start(f32[256,1024]{1,0:T(8,128)} %get-tuple-element.150) | copy-start | bytes 3145732
  145.6 34.8 %collective-permute-start.9 = (f32[256,1024]{1,0:T(8,128)}, f32[256,1024]{1,0:T(8,128)S(1)}, u32[]{:S(2)}, u32[]{:S(2)}) collective-permute-start(f32[256,1024]{1,0:T(8,128)} %get-tuple-element.162), channel_id=1, source_target_pairs={{0,1},{1,0},{2,3},{3,2},{4,5},{5,4},{6,7},{7,6},{8,9},{9,8},{10,11... | collective-permute-start | bytes 3145736 | tf_op jit(solution)/shard_map/ppermute | solution.py:30
  158.1 44.8 %collective-permute-start.10 = (f32[256,1024]{1,0:T(8,128)S(1)}, f32[256,1024]{1,0:T(8,128)S(1)}, u32[]{:S(2)}, u32[]{:S(2)}) collective-permute-start(f32[256,1024]{1,0:T(8,128)S(1)} %add.133.total_ref), channel_id=1, source_target_pairs={{0,1},{1,0},{2,3},{3,2},{4,5},{5,4},{6,7},{7,6},{8,9},{9,8},{10,11... | collective-permute-start | bytes 3145736 | tf_op jit(solution)/shard_map/ppermute | solution.py:30
  159.0 21.4 %copy-start.28 = (f32[256,1024]{1,0:T(8,128)S(1)}, f32[256,1024]{1,0:T(8,128)}, u32[]{:S(2)}) copy-start(f32[256,1024]{1,0:T(8,128)} %get-tuple-element.154) | copy-start | bytes 3145732
  180.6 43.8 %collective-permute-start.11 = (f32[256,1024]{1,0:T(8,128)S(1)}, f32[256,1024]{1,0:T(8,128)}, u32[]{:S(2)}, u32[]{:S(2)}) collective-permute-start(f32[256,1024]{1,0:T(8,128)S(1)} %add.134.total_ref), channel_id=1, source_target_pairs={{0,1},{1,0},{2,3},{3,2},{4,5},{5,4},{6,7},{7,6},{8,9},{9,8},{10,11... | collective-permute-start | bytes 3145736 | tf_op jit(solution)/shard_map/ppermute | solution.py:30
  224.4 11.5 %copy-start = (bf16[1024,2048]{1,0:T(8,128)(2,1)S(1)}, bf16[1024,2048]{1,0:T(8,128)(2,1)}, u32[]{:S(2)}) copy-start(bf16[1024,2048]{1,0:T(8,128)(2,1)} %get-tuple-element.192) | copy-start | bytes 12582916
  235.8 6.1 %copy-start.1 = (bf16[1024,1024]{1,0:T(8,128)(2,1)S(1)}, bf16[1024,1024]{1,0:T(8,128)(2,1)}, u32[]{:S(2)}) copy-start(bf16[1024,1024]{1,0:T(8,128)(2,1)} %get-tuple-element.191) | copy-start | bytes 6291460
  241.9 7.5 %collective-permute-start.15 = (f32[1024,1024]{1,0:T(8,128)}, f32[1024,1024]{1,0:T(8,128)}, u32[]{:S(2)}, u32[]{:S(2)}) collective-permute-start(f32[1024,1024]{1,0:T(8,128)} %fusion.1), channel_id=1, source_target_pairs={{0,2},{1,3},{2,0},{3,1},{4,6},{5,7},{6,4},{7,5},{8,10},{9,11},{10,... | collective-permute-start | bytes 12582920 | tf_op jit(solution)/shard_map/ppermute | solution.py:30
  249.4 7.1 %copy-start.2 = (bf16[1024,2048]{1,0:T(8,128)(2,1)S(1)}, bf16[1024,2048]{1,0:T(8,128)(2,1)}, u32[]{:S(2)}) copy-start(bf16[1024,2048]{1,0:T(8,128)(2,1)} %get-tuple-element.196) | copy-start | bytes 12582916
  249.4 7.1 %copy-start.3 = (bf16[1024,1024]{1,0:T(8,128)(2,1)S(1)}, bf16[1024,1024]{1,0:T(8,128)(2,1)}, u32[]{:S(2)}) copy-start(bf16[1024,1024]{1,0:T(8,128)(2,1)} %get-tuple-element.195) | copy-start | bytes 6291460
  263.4 5.1 copy-start.15
  263.4 28.6 %collective-permute-start.17 = (f32[256,1024]{1,0:T(8,128)}, f32[256,1024]{1,0:T(8,128)}, u32[]{:S(2)}, u32[]{:S(2)}) collective-permute-start(f32[256,1024]{1,0:T(8,128)} %get-tuple-element.180), channel_id=1, source_target_pairs={{0,1},{1,0},{2,3},{3,2},{4,5},{5,4},{6,7},{7,6},{8,9},{9,8},{10,11... | collective-permute-start | bytes 3145736 | tf_op jit(solution)/shard_map/ppermute | solution.py:30
  264.5 46.3 %collective-permute-start.16 = (f32[256,1024]{1,0:T(8,128)}, f32[256,1024]{1,0:T(8,128)}, u32[]{:S(2)}, u32[]{:S(2)}) collective-permute-start(f32[256,1024]{1,0:T(8,128)} %get-tuple-element.204), channel_id=1, source_target_pairs={{0,1},{1,0},{2,3},{3,2},{4,5},{5,4},{6,7},{7,6},{8,9},{9,8},{10,11... | collective-permute-start | bytes 3145736 | tf_op jit(solution)/shard_map/ppermute | solution.py:30
  265.0 1.5 collective-permute-start.13
  266.6 6.8 %copy-start.45 = (s32[1,5]{1,0:T(1,128)}, s32[1,5]{1,0:T(1,128)S(1)}, u32[]{:S(2)}) copy-start(s32[1,5]{1,0:T(1,128)S(1)} %fusion.21) | copy-start | bytes 64
  267.2 50.5 %collective-permute-start.19 = (f32[4,128,1024]{2,1,0:T(8,128)}, f32[4,128,1024]{2,1,0:T(8,128)}, u32[]{:S(2)}, u32[]{:S(2)}) collective-permute-start(f32[4,128,1024]{2,1,0:T(8,128)} %get-tuple-element.194), channel_id=1, source_target_pairs={{0,4},{1,5},{2,10},{3,11},{4,0},{5,1},{6,14},{7,15},{8,12},{9,13},... | collective-permute-start | bytes 6291464 | tf_op jit(solution)/shard_map/ppermute | solution.py:30
  316.7 8.3 %collective-permute-start.18 = (f32[512,1024]{1,0:T(8,128)}, f32[512,1024]{1,0:T(8,128)}, u32[]{:S(2)}, u32[]{:S(2)}) collective-permute-start(f32[512,1024]{1,0:T(8,128)} %get-tuple-element.212), channel_id=1, source_target_pairs={{0,2},{1,3},{2,0},{3,1},{4,6},{5,7},{6,4},{7,5},{8,10},{9,11},{10,... | collective-permute-start | bytes 6291464 | tf_op jit(solution)/shard_map/ppermute | solution.py:30
  317.7 6.7 %copy-start.43 = (f32[2,4,1024]{2,1,0:T(4,128)S(1)}, f32[2,4,1024]{2,1,0:T(4,128)}, u32[]{:S(2)}) copy-start(f32[2,4,1024]{2,1,0:T(4,128)} %get-tuple-element.203) | copy-start | bytes 98308
  317.7 7.3 %copy-start.16 = (f32[512,1024]{1,0:T(8,128)S(1)}, f32[512,1024]{1,0:T(8,128)}, u32[]{:S(2)}) copy-start(f32[512,1024]{1,0:T(8,128)} %get-tuple-element.212) | copy-start | bytes 6291460
  322.0 33.6 %collective-permute-start.20 = (f32[2,128,1024]{2,1,0:T(8,128)}, f32[2,128,1024]{2,1,0:T(8,128)S(1)}, u32[]{:S(2)}, u32[]{:S(2)}) collective-permute-start(f32[2,128,1024]{2,1,0:T(8,128)} %get-tuple-element.216), channel_id=1, source_target_pairs={{0,8},{1,9},{2,18},{3,19},{4,12},{5,13},{6,22},{7,23},{8,0},{9,1},... | collective-permute-start | bytes 3145736 | tf_op jit(solution)/shard_map/ppermute | solution.py:30
  361.6 7.4 %copy-start.4 = (bf16[1024,1536]{1,0:T(8,128)(2,1)}, bf16[1024,1536]{1,0:T(8,128)(2,1)S(1)}, u32[]{:S(2)}) copy-start(bf16[1024,1536]{1,0:T(8,128)(2,1)S(1)} %constant_dynamic-update-slice_fusion.4.grad_ref) | copy-start | bytes 9437188
  375.6 7.9 %copy-start.10 = (bf16[1024,256]{1,0:T(8,128)(2,1)S(1)}, bf16[1024,256]{1,0:T(8,128)(2,1)}, u32[]{:S(2)}) copy-start(bf16[1024,256]{1,0:T(8,128)(2,1)} %copy-done.9) | copy-start | bytes 1572868
  375.6 7.9 %copy-start.12 = (bf16[1024,256]{1,0:T(8,128)(2,1)S(1)}, bf16[1024,256]{1,0:T(8,128)(2,1)}, u32[]{:S(2)}) copy-start(bf16[1024,256]{1,0:T(8,128)(2,1)} %copy-done.11) | copy-start | bytes 1572868
  375.6 37.7 %collective-permute-start.25 = (f32[4,128,1536]{2,1,0:T(8,128)}, f32[4,128,1536]{2,1,0:T(8,128)}, u32[]{:S(2)}, u32[]{:S(2)}) collective-permute-start(f32[4,128,1536]{2,1,0:T(8,128)} %get-tuple-element.228), channel_id=1, source_target_pairs={{0,4},{1,5},{2,10},{3,11},{4,0},{5,1},{6,14},{7,15},{8,12},{9,13},... | collective-permute-start | bytes 9437192 | tf_op jit(solution)/shard_map/ppermute | solution.py:30
  383.5 9.7 %collective-permute-start.21 = (f32[512,1024]{1,0:T(8,128)}, f32[512,1024]{1,0:T(8,128)}, u32[]{:S(2)}, u32[]{:S(2)}) collective-permute-start(f32[512,1024]{1,0:T(8,128)} %input_other.1), channel_id=1, source_target_pairs={{0,2},{1,3},{2,0},{3,1},{4,6},{5,7},{6,4},{7,5},{8,10},{9,11},{10,... | collective-permute-start | bytes 6291464 | tf_op jit(solution)/shard_map/ppermute | solution.py:30
  383.6 6.3 %copy-start.31 = (f32[256,1024]{1,0:T(8,128)S(1)}, f32[256,1024]{1,0:T(8,128)}, u32[]{:S(2)}) copy-start(f32[256,1024]{1,0:T(8,128)} %get-tuple-element.166) | copy-start | bytes 3145732
  386.3 31.8 %collective-permute-start.24 = (f32[1024,512]{1,0:T(8,128)}, f32[1024,512]{1,0:T(8,128)}, u32[]{:S(2)}, u32[]{:S(2)}) collective-permute-start(f32[1024,512]{1,0:T(8,128)} %fusion.5), channel_id=1, source_target_pairs={{1,2},{2,1},{5,6},{6,5},{9,10},{10,9},{13,14},{14,13},{17,18},{18,... | collective-permute-start | bytes 6291464 | tf_op jit(solution)/shard_map/ppermute | solution.py:30
  390.2 14.6 %copy-start.7 = (f32[512,1024]{1,0:T(8,128)}, f32[512,1024]{1,0:T(8,128)S(1)}, u32[]{:S(2)}) copy-start(f32[512,1024]{1,0:T(8,128)S(1)} %constant_dynamic-update-slice_fusion) | copy-start | bytes 6291460
  404.6 8.6 %collective-permute-start.22 = (f32[4,1024]{1,0:T(4,128)S(1)}, f32[4,1024]{1,0:T(4,128)S(1)}, u32[]{:S(2)}, u32[]{:S(2)}) collective-permute-start(f32[4,1024]{1,0:T(4,128)S(1)} %pad_maximum_fusion.8), channel_id=1, source_target_pairs={{0,1},{1,0},{2,3},{3,2},{4,5},{5,4},{6,7},{7,6},{8,9},{9,8},{10,11... | collective-permute-start | bytes 49160 | tf_op jit(solution)/shard_map/ppermute | solution.py:30
  406.4 59.2 %collective-permute-start.12 = (f32[512,1024]{1,0:T(8,128)}, f32[512,1024]{1,0:T(8,128)}, u32[]{:S(2)}, u32[]{:S(2)}) collective-permute-start(f32[512,1024]{1,0:T(8,128)} %broadcast_select_fusion.2), channel_id=1, source_target_pairs={{0,2},{1,3},{2,0},{3,1},{4,6},{5,7},{6,4},{7,5},{8,10},{9,11},{10,... | collective-permute-start | bytes 6291464 | tf_op jit(solution)/shard_map/ppermute | solution.py:30
  422.5 7.2 %collective-permute-start.27 = (f32[1024,256]{1,0:T(8,128)}, f32[1024,256]{1,0:T(8,128)S(1)}, u32[]{:S(2)}, u32[]{:S(2)}) collective-permute-start(f32[1024,256]{1,0:T(8,128)} %get-tuple-element.278), channel_id=1, source_target_pairs={{0,2},{1,3},{2,0},{3,1},{4,6},{5,7},{6,4},{7,5},{8,10},{9,11},{10,... | collective-permute-start | bytes 3145736 | tf_op jit(solution)/shard_map/ppermute | solution.py:30
  424.2 37.4 %collective-permute-start.30 = (f32[2,128,1536]{2,1,0:T(8,128)}, f32[2,128,1536]{2,1,0:T(8,128)}, u32[]{:S(2)}, u32[]{:S(2)}) collective-permute-start(f32[2,128,1536]{2,1,0:T(8,128)} %get-tuple-element.240), channel_id=1, source_target_pairs={{0,8},{1,9},{2,18},{3,19},{4,12},{5,13},{6,22},{7,23},{8,0},{9,1},... | collective-permute-start | bytes 4718600 | tf_op jit(solution)/shard_map/ppermute | solution.py:30
  425.0 50.0 %collective-permute-start.23 = (f32[512,1024]{1,0:T(8,128)}, f32[512,1024]{1,0:T(8,128)}, u32[]{:S(2)}, u32[]{:S(2)}) collective-permute-start(f32[512,1024]{1,0:T(8,128)} %get-tuple-element.237), channel_id=1, source_target_pairs={{0,1},{1,0},{2,3},{3,2},{4,5},{5,4},{6,7},{7,6},{8,9},{9,8},{10,11... | collective-permute-start | bytes 6291464 | tf_op jit(solution)/shard_map/ppermute | solution.py:30
  425.0 1.8 collective-permute-start.26
  435.3 19.1 %collective-permute-start.28 = (f32[4,128,384]{2,1,0:T(8,128)}, f32[4,128,384]{2,1,0:T(8,128)S(1)}, u32[]{:S(2)}, u32[]{:S(2)}) collective-permute-start(f32[4,128,384]{2,1,0:T(8,128)} %get-tuple-element.246), channel_id=1, source_target_pairs={{0,4},{1,5},{2,6},{3,7},{4,0},{5,1},{6,2},{7,3},{8,12},{9,13},{10,... | collective-permute-start | bytes 2359304 | tf_op jit(solution)/shard_map/ppermute | solution.py:30
  458.2 12.7 %collective-permute-start.29 = (f32[2,128,384]{2,1,0:T(8,128)}, f32[2,128,384]{2,1,0:T(8,128)S(1)}, u32[]{:S(2)}, u32[]{:S(2)}) collective-permute-start(f32[2,128,384]{2,1,0:T(8,128)} %get-tuple-element.250), channel_id=1, source_target_pairs={{0,8},{1,9},{2,10},{3,11},{4,12},{5,13},{6,14},{7,15},{8,0},{9,1},... | collective-permute-start | bytes 1179656 | tf_op jit(solution)/shard_map/ppermute | solution.py:30
  465.5 17.1 %collective-permute-start.33 = (f32[1,128,1536]{2,1,0:T(8,128)}, f32[1,128,1536]{2,1,0:T(8,128)S(1)}, u32[]{:S(2)}, u32[]{:S(2)}) collective-permute-start(f32[1,128,1536]{2,1,0:T(8,128)} %get-tuple-element.253), channel_id=1, source_target_pairs={{0,16},{1,17},{2,6},{3,7},{4,20},{5,21},{6,2},{7,3},{8,24},{9,25},... | collective-permute-start | bytes 2359304 | tf_op jit(solution)/shard_map/ppermute | solution.py:30
  468.1 14.4 %collective-permute-start.36 = (f32[1,128,1024]{2,1,0:T(8,128)S(1)}, f32[1,128,1024]{2,1,0:T(8,128)S(1)}, u32[]{:S(2)}, u32[]{:S(2)}) collective-permute-start(f32[1,128,1024]{2,1,0:T(8,128)S(1)} %copy-done.48), channel_id=1, source_target_pairs={{0,16},{1,17},{2,6},{3,7},{4,20},{5,21},{6,2},{7,3},{8,24},{9,25},... | collective-permute-start | bytes 1572872 | tf_op jit(solution)/shard_map/ppermute | solution.py:30
  474.4 8.1 %copy-start.41 = (f32[1,128,1024]{2,1,0:T(8,128)S(1)}, f32[1,128,1024]{2,1,0:T(8,128)}, u32[]{:S(2)}) copy-start(f32[1,128,1024]{2,1,0:T(8,128)} %get-tuple-element.264) | copy-start | bytes 1572868
  474.4 19.1 %collective-permute-start.32 = (f32[1,128,384]{2,1,0:T(8,128)}, f32[1,128,384]{2,1,0:T(8,128)S(1)}, u32[]{:S(2)}, u32[]{:S(2)}) collective-permute-start(f32[1,128,384]{2,1,0:T(8,128)} %get-tuple-element.255), channel_id=1, source_target_pairs={{0,16},{1,17},{2,18},{3,19},{4,20},{5,21},{6,22},{7,23},{8,24},{9,... | collective-permute-start | bytes 589832 | tf_op jit(solution)/shard_map/ppermute | solution.py:30
  477.0 5.6 %copy-start.40 = (f32[1,128,1536]{2,1,0:T(8,128)S(1)}, f32[1,128,1536]{2,1,0:T(8,128)}, u32[]{:S(2)}) copy-start(f32[1,128,1536]{2,1,0:T(8,128)} %get-tuple-element.258) | copy-start | bytes 2359300
  477.0 39.8 %collective-permute-start.31 = (f32[512,1024]{1,0:T(8,128)S(1)}, f32[512,1024]{1,0:T(8,128)S(1)}, u32[]{:S(2)}, u32[]{:S(2)}) collective-permute-start(f32[512,1024]{1,0:T(8,128)S(1)} %broadcast_select_fusion), channel_id=1, source_target_pairs={{0,2},{1,3},{2,0},{3,1},{4,6},{5,7},{6,4},{7,5},{8,10},{9,11},{10,... | collective-permute-start | bytes 6291464 | tf_op jit(solution)/shard_map/ppermute | solution.py:30
  482.6 26.9 %copy-start.42 = (f32[1,128,256]{2,1,0:T(8,128)S(1)}, f32[1,128,256]{2,1,0:T(8,128)}, u32[]{:S(2)}) copy-start(f32[1,128,256]{2,1,0:T(8,128)} %get-tuple-element.263) | copy-start | bytes 393220
  482.6 27.0 %copy-start.44 = (f32[1,128,128]{2,1,0:T(8,128)S(1)}, f32[1,128,128]{2,1,0:T(8,128)}, u32[]{:S(2)}) copy-start(f32[1,128,128]{2,1,0:T(8,128)} %get-tuple-element.257) | copy-start | bytes 196612
  482.8 30.0 %collective-permute-start.34 = (f32[64,1536]{1,0:T(8,128)S(1)}, f32[64,1536]{1,0:T(8,128)S(1)}, u32[]{:S(2)}, u32[]{:S(2)}) collective-permute-start(f32[64,1536]{1,0:T(8,128)S(1)} %get-tuple-element.260), channel_id=1, source_target_pairs={{0,2},{1,0},{2,3},{3,1},{4,6},{5,4},{6,7},{7,5},{8,10},{9,8},{10,1... | collective-permute-start | bytes 1179656 | tf_op jit(solution)/shard_map/ppermute | solution.py:30
  493.5 22.5 %collective-permute-start.35 = (f32[64,1536]{1,0:T(8,128)S(1)}, f32[64,1536]{1,0:T(8,128)S(1)}, u32[]{:S(2)}, u32[]{:S(2)}) collective-permute-start(f32[64,1536]{1,0:T(8,128)S(1)} %get-tuple-element.262), channel_id=1, source_target_pairs={{1,2},{2,1},{5,6},{6,5},{9,10},{10,9},{13,14},{14,13},{17,18},{18,... | collective-permute-start | bytes 1179656 | tf_op jit(solution)/shard_map/ppermute | solution.py:30
  509.6 1.7 collective-permute-start.37
  (25 other events, 53.5 us)
Sparse Core Ops, SparseCore 0:
  87.3 97.6 all-gather.1
Sparse Core Ops, SparseCore 1:
  263.5 108.6 reduce-scatter.1
